TPU v7x, 512 devices: a whole 4x8x8 slice. The times are simulated.
512 devices in a mesh: gx: 64 (over z, x, core), gz: 8 (over y).
Axes of the slice: x: 4, y: 8, z: 8, core: 2. Of those that a mesh axis runs over, the one named last changes fastest.
Arguments:
- right_side: float32 [3, 24, 512, 1024], P(None, 'gz', 'gx'), may hold values from -48 to 48
- density: float32 [24, 512, 1024], P('gz', 'gx'), may hold values from 0.5 to 4
Outputs:
- solution_field: float32 [3, 24, 512, 1024], P(None, 'gz', 'gx')
All inputs are finite; a program needn't handle non-finite values.
Results may differ from a plain program's by a relative error of at most 0.0001.
Values sent between devices are 32-bit elements; how exact they have to be, the bound alone decides.
No kernel may reach another device: no remote copies, remote signals or barrier semaphores. Data moves between devices by JAX's collectives and lax.ppermute only.
A program may use at most 128 MiB of HBM per device.

v0:
```python
import jax
import jax.numpy as jnp
from jax import lax
from jax.sharding import PartitionSpec as P

LEVELS = 4
PRE = 2
POST = 2
COARSE_SWEEPS = 3
CYCLES = 2


relaxation = 0.8
plane_coupling = 16.0
depth_coupling = 1.0


def extended(cells, sides, width, closed):
    for axis, dim in sides:
        count = lax.axis_size(axis)
        ends = count if closed else count - 1
        head = lax.slice_in_dim(cells, 0, width, axis=dim)
        tail = lax.slice_in_dim(cells, cells.shape[dim] - width, cells.shape[dim], axis=dim)
        cells = jnp.concatenate(
            [
                lax.ppermute(tail, axis, [(i, (i + 1) % count) for i in range(ends)]),
                cells,
                lax.ppermute(head, axis, [((i + 1) % count, i) for i in range(ends)]),
            ],
            axis=dim,
        )
    return cells


def diagonal_of(density_level, coupling):
    return density_level[None] + 4.0 * coupling + 2.0 * depth_coupling


def image_parts(field, x_plus, x_minus, z_minus, z_plus, density_level, coupling):
    diagonal = diagonal_of(density_level, coupling)
    y_padded = jnp.pad(field, ((0, 0), (0, 0), (0, 0), (1, 1)))
    lateral = x_plus + x_minus + y_padded[..., 2:] + y_padded[..., :-2]
    vertical = z_minus + z_plus
    return (diagonal * field - coupling * lateral - depth_coupling * vertical, diagonal)


def single_image(field, density_level, coupling):
    x_padded = extended(field, (("gx", 2),), 1, False)
    z_padded = extended(field, (("gz", 1),), 1, True)
    return image_parts(
        field,
        x_padded[:, :, 2:],
        x_padded[:, :, :-2],
        z_padded[:, :-2],
        z_padded[:, 2:],
        density_level,
        coupling,
    )


def single_sweep(field, source, density_level, coupling):
    image, diagonal = single_image(field, density_level, coupling)
    return field + relaxation * (source - image) / diagonal


def shrink(values):
    components, rows_z, rows_x, rows_y = values.shape
    return values.reshape(components, rows_z, rows_x // 2, 2, rows_y // 2, 2).mean(axis=(3, 5))


def shards(right_side, density):
    density_levels = [density]
    for level_index in range(1, LEVELS):
        density_levels.append(shrink(density_levels[-1][None])[0])

    def smooth(field, source, level_index, coupling, repeats):
        for repeat_index in range(repeats):
            field = single_sweep(field, source, density_levels[level_index], coupling)
        return field

    coarse_coupling = plane_coupling / 4.0 ** (LEVELS - 1)

    def coarse_solve(source):
        level_density = density_levels[-1]
        field = relaxation * source / diagonal_of(level_density, coarse_coupling)
        for sweep_index in range(COARSE_SWEEPS - 1):
            field = single_sweep(field, source, level_density, coarse_coupling)
        return field

    def vcycle(field, source, level_index, from_zero):
        if level_index == LEVELS - 1:
            return coarse_solve(source)
        coupling = plane_coupling / 4.0**level_index
        level_density = density_levels[level_index]
        if from_zero:
            field = relaxation * source / diagonal_of(level_density, coupling)
            field = single_sweep(field, source, level_density, coupling)
        else:
            field = smooth(field, source, level_index, coupling, PRE)
        image, diagonal = single_image(field, level_density, coupling)
        correction = vcycle(None, shrink(source - image), level_index + 1, True)
        field = field + jnp.repeat(jnp.repeat(correction, 2, axis=2), 2, axis=3)
        return smooth(field, source, level_index, coupling, POST)

    field = None
    for cycle_index in range(CYCLES):
        field = vcycle(field, right_side, 0, cycle_index == 0)
    return field


def solution(mesh):
    return jax.shard_map(
        shards,
        mesh=mesh,
        in_specs=(P(None, "gz", "gx", None), P("gz", "gx", None)),
        out_specs=P(None, "gz", "gx", None),
        check_vma=False,
    )
```

profile of v0, /device:TPU:256, one launch (start us, length us, event | category | flops | bytes accessed | tf_op | source)
XLA Modules:
  0.0 620.8 jit_solution(18530745360785249)
XLA Ops:
  5.4 3.8 collective-permute-start.3
  14.1 8.4 %reshape_broadcast_in_dim.3 = f32[3,4,2,512,2]{4,3,2,1,0:T(8,128)} reshape(f32[3,8,1024]{2,1,0:T(8,128)} %param.3) | data formatting | bytes 196608 | tf_op jit(solution)/shard_map/reshape;broadcast_in_dim | solution.py:68
  22.5 3.7 reduce_sum.103
  26.7 7.0 %collective-permute-start.4 = (f32[3,3,1,1024]{3,2,1,0:T(1,128)S(1)}, f32[3,3,1,1024]{3,2,1,0:T(1,128)S(1)}, u32[]{:S(2)}, u32[]{:S(2)}) collective-permute-start(f32[3,3,1,1024]{3,2,1,0:T(1,128)S(1)} %get-tuple-element.33), channel_id=1, source_target_pairs={{8,0},{16,8},{24,16},{32,24},{40,32},{48,40},{56,48},{64,56},{72,6... | collective-permute-start | bytes 110600 | tf_op jit(solution)/shard_map/ppermute | solution.py:28
  37.5 5.1 collective-permute-start.7
  45.1 20.2 %reshape.156 = f32[3,3,4,2,512,2]{5,4,3,2,1,0:T(8,128)} reshape(f32[3,3,8,1024]{3,2,1,0:T(8,128)S(1)} %fusion.14) | data formatting | bytes 589824 | tf_op jit(solution)/shard_map/reshape | solution.py:68
  65.3 7.8 %reduce_sum.102 = f32[3,3,4,512]{3,2,1,0:T(4,128)S(1)} reduce(f32[3,3,4,2,512,2]{5,4,3,2,1,0:T(8,128)} %reshape.156, f32[]{:T(128)} %constant.43.clone.1), dimensions={3,5}, to_apply=%region_0.0 | reduce | flops 55296 | bytes 368644 | tf_op jit(solution)/shard_map/reduce_sum | solution.py:68
  76.2 4.3 collective-permute-start.11
  80.6 5.3 collective-permute-start.8
  89.6 4.6 collective-permute-done.9
  101.6 4.3 collective-permute-start.15
  108.4 7.1 %reshape.157 = f32[3,3,2,2,256,2]{5,4,3,2,1,0:T(8,128)} reshape(f32[3,3,4,512]{3,2,1,0:T(4,128)S(1)} %fusion.105) | data formatting | bytes 147456 | tf_op jit(solution)/shard_map/reshape | solution.py:68
  118.5 5.8 collective-permute-start.16
  126.2 3.6 collective-permute-start.18
  135.6 4.3 collective-permute-start.22
  142.7 5.0 collective-permute-start.20
  150.1 5.9 collective-permute-done.21
  158.8 7.0 %collective-permute-start.24 = (f32[3,3,1,128]{3,1,0,2:T(4,128)S(1)}, f32[3,3,1,128]{3,1,0,2:T(4,128)S(1)}, u32[]{:S(2)}, u32[]{:S(2)}) collective-permute-start(f32[3,3,1,128]{3,1,0,2:T(4,128)S(1)} %bitcast_divide_fusion.1), channel_id=1, source_target_pairs={{8,0},{16,8},{24,16},{32,24},{40,32},{48,40},{56,48},{64,56},{72,6... | collective-permute-start | bytes 13832 | tf_op jit(solution)/shard_map/ppermute | solution.py:28
  169.2 3.6 collective-permute-start.27
  176.7 7.0 %collective-permute-start.28 = (f32[3,3,1,128]{3,1,0,2:T(4,128)S(1)}, f32[3,3,1,128]{3,1,0,2:T(4,128)S(1)}, u32[]{:S(2)}, u32[]{:S(2)}) collective-permute-start(f32[3,3,1,128]{3,1,0,2:T(4,128)S(1)} %divide_add_fusion.15), channel_id=1, source_target_pairs={{8,0},{16,8},{24,16},{32,24},{40,32},{48,40},{56,48},{64,56},{72,6... | collective-permute-start | bytes 13832 | tf_op jit(solution)/shard_map/ppermute | solution.py:28
  197.9 4.1 collective-permute-start.34
  207.7 5.3 collective-permute-start.36
  231.7 3.9 collective-permute-start.43
  235.7 5.0 collective-permute-start.40
  242.6 6.5 %collective-permute-done.41 = f32[3,3,1,512]{3,2,1,0:T(1,128)S(1)} collective-permute-done((f32[3,3,1,512]{3,2,1,0:T(1,128)S(1)}, f32[3,3,1,512]{3,2,1,0:T(1,128)S(1)}, u32[]{:S(2)}, u32[]{:S(2)}) %collective-permute-start.41) | collective-permute-done | bytes 18464 | tf_op jit(solution)/shard_map/ppermute | solution.py:26
  251.2 5.1 collective-permute-start.47
  260.7 6.0 collective-permute-done.45
  267.7 3.8 broadcast_in_dim.56
  276.5 5.1 collective-permute-start.51
  286.1 6.2 collective-permute-done.49
  294.5 5.1 collective-permute-start.55
  304.0 6.2 collective-permute-done.53
  312.4 5.1 collective-permute-start.59
  322.0 6.2 collective-permute-done.57
  330.4 5.1 collective-permute-start.63
  339.9 6.2 collective-permute-done.61
  348.3 5.1 collective-permute-start.67
  358.0 6.0 collective-permute-done.65
  364.3 20.2 %reshape.162 = f32[3,3,4,2,512,2]{5,4,3,2,1,0:T(8,128)} reshape(f32[3,3,8,1024]{3,2,1,0:T(8,128)S(1)} %fusion.56) | data formatting | bytes 589824 | tf_op jit(solution)/shard_map/reshape | solution.py:68
  384.5 7.8 %reduce_sum.112 = f32[3,3,4,512]{3,2,1,0:T(4,128)S(1)} reduce(f32[3,3,4,2,512,2]{5,4,3,2,1,0:T(8,128)} %reshape.162, f32[]{:T(128)} %constant.43.clone.1), dimensions={3,5}, to_apply=%region_8.9 | reduce | flops 55296 | bytes 368644 | tf_op jit(solution)/shard_map/reduce_sum | solution.py:68
  394.3 5.1 collective-permute-start.71
  403.8 6.0 collective-permute-done.69
  411.9 5.1 collective-permute-start.75
  421.4 6.0 collective-permute-done.73
  427.6 7.1 %reshape.163 = f32[3,3,2,2,256,2]{5,4,3,2,1,0:T(8,128)} reshape(f32[3,3,4,512]{3,2,1,0:T(4,128)S(1)} %fusion.132) | data formatting | bytes 147456 | tf_op jit(solution)/shard_map/reshape | solution.py:68
  444.0 5.1 collective-permute-start.79
  450.6 5.3 collective-permute-start.80
  459.8 5.1 collective-permute-start.83
  469.2 7.0 %collective-permute-start.84 = (f32[3,3,1,128]{3,1,0,2:T(4,128)S(1)}, f32[3,3,1,128]{3,1,0,2:T(4,128)S(1)}, u32[]{:S(2)}, u32[]{:S(2)}) collective-permute-start(f32[3,3,1,128]{3,1,0,2:T(4,128)S(1)} %bitcast_divide_fusion), channel_id=1, source_target_pairs={{8,0},{16,8},{24,16},{32,24},{40,32},{48,40},{56,48},{64,56},{72,6... | collective-permute-start | bytes 13832 | tf_op jit(solution)/shard_map/ppermute | solution.py:28
  479.6 3.9 collective-permute-start.87
  487.1 7.0 %collective-permute-start.88 = (f32[3,3,1,128]{3,1,0,2:T(4,128)S(1)}, f32[3,3,1,128]{3,1,0,2:T(4,128)S(1)}, u32[]{:S(2)}, u32[]{:S(2)}) collective-permute-start(f32[3,3,1,128]{3,1,0,2:T(4,128)S(1)} %divide_add_fusion.13), channel_id=1, source_target_pairs={{8,0},{16,8},{24,16},{32,24},{40,32},{48,40},{56,48},{64,56},{72,6... | collective-permute-start | bytes 13832 | tf_op jit(solution)/shard_map/ppermute | solution.py:28
  494.1 3.9 collective-permute-start.90
  511.7 3.9 collective-permute-start.95
  517.4 5.0 collective-permute-start.96
  527.5 3.9 collective-permute-start.99
  544.6 5.5 collective-permute-start.100
  552.0 6.5 %collective-permute-done.101 = f32[3,3,1,512]{3,2,1,0:T(1,128)S(1)} collective-permute-done((f32[3,3,1,512]{3,2,1,0:T(1,128)S(1)}, f32[3,3,1,512]{3,2,1,0:T(1,128)S(1)}, u32[]{:S(2)}, u32[]{:S(2)}) %collective-permute-start.101) | collective-permute-done | bytes 18464 | tf_op jit(solution)/shard_map/ppermute | solution.py:26
  560.7 5.1 collective-permute-start.107
  570.4 5.8 collective-permute-done.105
  577.1 3.8 broadcast_in_dim.63
  586.0 5.1 collective-permute-start.111
  595.5 6.2 collective-permute-done.109
  603.9 5.1 collective-permute-start.115
  613.5 6.2 collective-permute-done.113
  (312 shorter events, 242.1 us)
Async XLA Ops:
  1.9 24.4 %collective-permute-start.2 = (f32[3,1,8,1024]{3,2,1,0:T(8,128)S(1)}, f32[3,1,8,1024]{3,2,1,0:T(8,128)S(1)}, u32[]{:S(2)}, u32[]{:S(2)}) collective-permute-start(f32[3,1,8,1024]{3,2,1,0:T(8,128)S(1)} %get-tuple-element.39), channel_id=1, source_target_pairs={{0,1},{1,2},{2,3},{3,4},{4,5},{5,6},{6,7},{7,0},{8,9},{9,10},{10,1... | collective-permute-start | bytes 294920 | tf_op jit(solution)/shard_map/ppermute | solution.py:26
  5.4 20.9 %collective-permute-start.3 = (f32[3,1,8,1024]{3,2,1,0:T(8,128)S(1)}, f32[3,1,8,1024]{3,2,1,0:T(8,128)S(1)}, u32[]{:S(2)}, u32[]{:S(2)}) collective-permute-start(f32[3,1,8,1024]{3,2,1,0:T(8,128)S(1)} %get-tuple-element.40), channel_id=1, source_target_pairs={{1,0},{2,1},{3,2},{4,3},{5,4},{6,5},{7,6},{0,7},{9,8},{10,9},{11,1... | collective-permute-start | bytes 294920 | tf_op jit(solution)/shard_map/ppermute | solution.py:28
  9.3 17.0 %collective-permute-start = (f32[3,3,1,1024]{3,2,1,0:T(1,128)S(1)}, f32[3,3,1,1024]{3,2,1,0:T(1,128)S(1)}, u32[]{:S(2)}, u32[]{:S(2)}) collective-permute-start(f32[3,3,1,1024]{3,2,1,0:T(1,128)S(1)} %get-tuple-element.37), channel_id=1, source_target_pairs={{8,0},{16,8},{24,16},{32,24},{40,32},{48,40},{56,48},{64,56},{72,6... | collective-permute-start | bytes 110600 | tf_op jit(solution)/shard_map/ppermute | solution.py:28
  12.2 14.1 %collective-permute-start.1 = (f32[3,3,1,1024]{3,2,1,0:T(1,128)S(1)}, f32[3,3,1,1024]{3,2,1,0:T(1,128)S(1)}, u32[]{:S(2)}, u32[]{:S(2)}) collective-permute-start(f32[3,3,1,1024]{3,2,1,0:T(1,128)S(1)} %get-tuple-element.38), channel_id=1, source_target_pairs={{0,8},{8,16},{16,24},{24,32},{32,40},{40,48},{48,56},{56,64},{64,7... | collective-permute-start | bytes 110600 | tf_op jit(solution)/shard_map/ppermute | solution.py:26
  26.7 16.0 %collective-permute-start.4 = (f32[3,3,1,1024]{3,2,1,0:T(1,128)S(1)}, f32[3,3,1,1024]{3,2,1,0:T(1,128)S(1)}, u32[]{:S(2)}, u32[]{:S(2)}) collective-permute-start(f32[3,3,1,1024]{3,2,1,0:T(1,128)S(1)} %get-tuple-element.33), channel_id=1, source_target_pairs={{8,0},{16,8},{24,16},{32,24},{40,32},{48,40},{56,48},{64,56},{72,6... | collective-permute-start | bytes 110600 | tf_op jit(solution)/shard_map/ppermute | solution.py:28
  33.7 9.0 %collective-permute-start.5 = (f32[3,3,1,1024]{3,2,1,0:T(1,128)S(1)}, f32[3,3,1,1024]{3,2,1,0:T(1,128)S(1)}, u32[]{:S(2)}, u32[]{:S(2)}) collective-permute-start(f32[3,3,1,1024]{3,2,1,0:T(1,128)S(1)} %get-tuple-element.34), channel_id=1, source_target_pairs={{0,8},{8,16},{16,24},{24,32},{32,40},{40,48},{48,56},{56,64},{64,7... | collective-permute-start | bytes 110600 | tf_op jit(solution)/shard_map/ppermute | solution.py:26
  73.1 21.2 %collective-permute-start.10 = (f32[3,1,4,512]{3,2,1,0:T(4,128)S(1)}, f32[3,1,4,512]{3,2,1,0:T(4,128)S(1)}, u32[]{:S(2)}, u32[]{:S(2)}) collective-permute-start(f32[3,1,4,512]{3,2,1,0:T(4,128)S(1)} %get-tuple-element.71), channel_id=1, source_target_pairs={{0,1},{1,2},{2,3},{3,4},{4,5},{5,6},{6,7},{7,0},{8,9},{9,10},{10,1... | collective-permute-start | bytes 73736 | tf_op jit(solution)/shard_map/ppermute | solution.py:26
  76.2 18.0 %collective-permute-start.11 = (f32[3,1,4,512]{3,2,1,0:T(4,128)S(1)}, f32[3,1,4,512]{3,2,1,0:T(4,128)S(1)}, u32[]{:S(2)}, u32[]{:S(2)}) collective-permute-start(f32[3,1,4,512]{3,2,1,0:T(4,128)S(1)} %get-tuple-element.72), channel_id=1, source_target_pairs={{1,0},{2,1},{3,2},{4,3},{5,4},{6,5},{7,6},{0,7},{9,8},{10,9},{11,1... | collective-permute-start | bytes 73736 | tf_op jit(solution)/shard_map/ppermute | solution.py:28
  80.6 9.0 %collective-permute-start.8 = (f32[3,3,1,512]{3,2,1,0:T(1,128)S(1)}, f32[3,3,1,512]{3,2,1,0:T(1,128)S(1)}, u32[]{:S(2)}, u32[]{:S(2)}) collective-permute-start(f32[3,3,1,512]{3,2,1,0:T(1,128)S(1)} %get-tuple-element.69), channel_id=1, source_target_pairs={{8,0},{16,8},{24,16},{32,24},{40,32},{48,40},{56,48},{64,56},{72,6... | collective-permute-start | bytes 55304 | tf_op jit(solution)/shard_map/ppermute | solution.py:28
  94.5 11.4 %collective-permute-start.12 = (f32[3,3,1,512]{3,2,1,0:T(1,128)S(1)}, f32[3,3,1,512]{3,2,1,0:T(1,128)S(1)}, u32[]{:S(2)}, u32[]{:S(2)}) collective-permute-start(f32[3,3,1,512]{3,2,1,0:T(1,128)S(1)} %get-tuple-element.65), channel_id=1, source_target_pairs={{8,0},{16,8},{24,16},{32,24},{40,32},{48,40},{56,48},{64,56},{72,6... | collective-permute-start | bytes 55304 | tf_op jit(solution)/shard_map/ppermute | solution.py:28
  96.9 9.1 %collective-permute-start.13 = (f32[3,3,1,512]{3,2,1,0:T(1,128)S(1)}, f32[3,3,1,512]{3,2,1,0:T(1,128)S(1)}, u32[]{:S(2)}, u32[]{:S(2)}) collective-permute-start(f32[3,3,1,512]{3,2,1,0:T(1,128)S(1)} %get-tuple-element.66), channel_id=1, source_target_pairs={{0,8},{8,16},{16,24},{24,32},{32,40},{40,48},{48,56},{56,64},{64,7... | collective-permute-start | bytes 55304 | tf_op jit(solution)/shard_map/ppermute | solution.py:26
  118.5 16.9 %collective-permute-start.16 = (f32[3,3,1,256]{3,2,1,0:T(1,128)S(1)}, f32[3,3,1,256]{3,2,1,0:T(1,128)S(1)}, u32[]{:S(2)}, u32[]{:S(2)}) collective-permute-start(f32[3,3,1,256]{3,2,1,0:T(1,128)S(1)} %get-tuple-element.103), channel_id=1, source_target_pairs={{8,0},{16,8},{24,16},{32,24},{40,32},{48,40},{56,48},{64,56},{72,6... | collective-permute-start | bytes 27656 | tf_op jit(solution)/shard_map/ppermute | solution.py:28
  124.3 11.1 %collective-permute-start.17 = (f32[3,3,1,256]{3,2,1,0:T(1,128)S(1)}, f32[3,3,1,256]{3,2,1,0:T(1,128)S(1)}, u32[]{:S(2)}, u32[]{:S(2)}) collective-permute-start(f32[3,3,1,256]{3,2,1,0:T(1,128)S(1)} %get-tuple-element.104), channel_id=1, source_target_pairs={{0,8},{8,16},{16,24},{24,32},{32,40},{40,48},{48,56},{56,64},{64,7... | collective-permute-start | bytes 27656 | tf_op jit(solution)/shard_map/ppermute | solution.py:26
  135.6 14.5 %collective-permute-start.22 = (f32[3,1,2,256]{3,2,1,0:T(2,128)S(1)}, f32[3,1,2,256]{3,2,1,0:T(2,128)S(1)}, u32[]{:S(2)}, u32[]{:S(2)}) collective-permute-start(f32[3,1,2,256]{3,2,1,0:T(2,128)S(1)} %get-tuple-element.101), channel_id=1, source_target_pairs={{0,1},{1,2},{2,3},{3,4},{4,5},{5,6},{6,7},{7,0},{8,9},{9,10},{10,1... | collective-permute-start | bytes 18440 | tf_op jit(solution)/shard_map/ppermute | solution.py:26
  139.9 10.1 %collective-permute-start.23 = (f32[3,1,2,256]{3,2,1,0:T(2,128)S(1)}, f32[3,1,2,256]{3,2,1,0:T(2,128)S(1)}, u32[]{:S(2)}, u32[]{:S(2)}) collective-permute-start(f32[3,1,2,256]{3,2,1,0:T(2,128)S(1)} %get-tuple-element.102), channel_id=1, source_target_pairs={{1,0},{2,1},{3,2},{4,3},{5,4},{6,5},{7,6},{0,7},{9,8},{10,9},{11,1... | collective-permute-start | bytes 18440 | tf_op jit(solution)/shard_map/ppermute | solution.py:28
  156.9 17.8 %collective-permute-start.25 = (f32[3,3,1,128]{3,1,0,2:T(4,128)S(1)}, f32[3,3,1,128]{3,1,0,2:T(4,128)S(1)}, u32[]{:S(2)}, u32[]{:S(2)}) collective-permute-start(f32[3,3,1,128]{3,1,0,2:T(4,128)S(1)} %bitcast_divide_fusion.1), channel_id=1, source_target_pairs={{0,8},{8,16},{16,24},{24,32},{32,40},{40,48},{48,56},{56,64},{64,7... | collective-permute-start | bytes 13832 | tf_op jit(solution)/shard_map/ppermute | solution.py:26
  158.8 15.9 %collective-permute-start.24 = (f32[3,3,1,128]{3,1,0,2:T(4,128)S(1)}, f32[3,3,1,128]{3,1,0,2:T(4,128)S(1)}, u32[]{:S(2)}, u32[]{:S(2)}) collective-permute-start(f32[3,3,1,128]{3,1,0,2:T(4,128)S(1)} %bitcast_divide_fusion.1), channel_id=1, source_target_pairs={{8,0},{16,8},{24,16},{32,24},{40,32},{48,40},{56,48},{64,56},{72,6... | collective-permute-start | bytes 13832 | tf_op jit(solution)/shard_map/ppermute | solution.py:28
  174.8 18.0 %collective-permute-start.29 = (f32[3,3,1,128]{3,1,0,2:T(4,128)S(1)}, f32[3,3,1,128]{3,1,0,2:T(4,128)S(1)}, u32[]{:S(2)}, u32[]{:S(2)}) collective-permute-start(f32[3,3,1,128]{3,1,0,2:T(4,128)S(1)} %divide_add_fusion.15), channel_id=1, source_target_pairs={{0,8},{8,16},{16,24},{24,32},{32,40},{40,48},{48,56},{56,64},{64,7... | collective-permute-start | bytes 13832 | tf_op jit(solution)/shard_map/ppermute | solution.py:26
  176.7 16.1 %collective-permute-start.28 = (f32[3,3,1,128]{3,1,0,2:T(4,128)S(1)}, f32[3,3,1,128]{3,1,0,2:T(4,128)S(1)}, u32[]{:S(2)}, u32[]{:S(2)}) collective-permute-start(f32[3,3,1,128]{3,1,0,2:T(4,128)S(1)} %divide_add_fusion.15), channel_id=1, source_target_pairs={{8,0},{16,8},{24,16},{32,24},{40,32},{48,40},{56,48},{64,56},{72,6... | collective-permute-start | bytes 13832 | tf_op jit(solution)/shard_map/ppermute | solution.py:28
  193.5 14.0 %collective-permute-start.32 = (f32[3,3,1,256]{3,2,1,0:T(1,128)S(1)}, f32[3,3,1,256]{3,2,1,0:T(1,128)S(1)}, u32[]{:S(2)}, u32[]{:S(2)}) collective-permute-start(f32[3,3,1,256]{3,2,1,0:T(1,128)S(1)} %get-tuple-element.95), channel_id=1, source_target_pairs={{8,0},{16,8},{24,16},{32,24},{40,32},{48,40},{56,48},{64,56},{72,6... | collective-permute-start | bytes 27656 | tf_op jit(solution)/shard_map/ppermute | solution.py:28
  195.4 12.1 %collective-permute-start.33 = (f32[3,3,1,256]{3,2,1,0:T(1,128)S(1)}, f32[3,3,1,256]{3,2,1,0:T(1,128)S(1)}, u32[]{:S(2)}, u32[]{:S(2)}) collective-permute-start(f32[3,3,1,256]{3,2,1,0:T(1,128)S(1)} %get-tuple-element.96), channel_id=1, source_target_pairs={{0,8},{8,16},{16,24},{24,32},{32,40},{40,48},{48,56},{56,64},{64,7... | collective-permute-start | bytes 27656 | tf_op jit(solution)/shard_map/ppermute | solution.py:26
  207.7 16.5 %collective-permute-start.36 = (f32[3,3,1,256]{3,2,1,0:T(1,128)S(1)}, f32[3,3,1,256]{3,2,1,0:T(1,128)S(1)}, u32[]{:S(2)}, u32[]{:S(2)}) collective-permute-start(f32[3,3,1,256]{3,2,1,0:T(1,128)S(1)} %get-tuple-element.91), channel_id=1, source_target_pairs={{8,0},{16,8},{24,16},{32,24},{40,32},{48,40},{56,48},{64,56},{72,6... | collective-permute-start | bytes 27656 | tf_op jit(solution)/shard_map/ppermute | solution.py:28
  213.0 11.1 %collective-permute-start.37 = (f32[3,3,1,256]{3,2,1,0:T(1,128)S(1)}, f32[3,3,1,256]{3,2,1,0:T(1,128)S(1)}, u32[]{:S(2)}, u32[]{:S(2)}) collective-permute-start(f32[3,3,1,256]{3,2,1,0:T(1,128)S(1)} %get-tuple-element.92), channel_id=1, source_target_pairs={{0,8},{8,16},{16,24},{24,32},{32,40},{40,48},{48,56},{56,64},{64,7... | collective-permute-start | bytes 27656 | tf_op jit(solution)/shard_map/ppermute | solution.py:26
  228.6 20.5 %collective-permute-start.42 = (f32[3,1,4,512]{3,2,1,0:T(4,128)S(1)}, f32[3,1,4,512]{3,2,1,0:T(4,128)S(1)}, u32[]{:S(2)}, u32[]{:S(2)}) collective-permute-start(f32[3,1,4,512]{3,2,1,0:T(4,128)S(1)} %get-tuple-element.63), channel_id=1, source_target_pairs={{0,1},{1,2},{2,3},{3,4},{4,5},{5,6},{6,7},{7,0},{8,9},{9,10},{10,1... | collective-permute-start | bytes 73736 | tf_op jit(solution)/shard_map/ppermute | solution.py:26
  231.7 17.4 %collective-permute-start.43 = (f32[3,1,4,512]{3,2,1,0:T(4,128)S(1)}, f32[3,1,4,512]{3,2,1,0:T(4,128)S(1)}, u32[]{:S(2)}, u32[]{:S(2)}) collective-permute-start(f32[3,1,4,512]{3,2,1,0:T(4,128)S(1)} %get-tuple-element.64), channel_id=1, source_target_pairs={{1,0},{2,1},{3,2},{4,3},{5,4},{6,5},{7,6},{0,7},{9,8},{10,9},{11,1... | collective-permute-start | bytes 73736 | tf_op jit(solution)/shard_map/ppermute | solution.py:28
  249.2 17.4 %collective-permute-start.46 = (f32[3,1,4,512]{3,2,1,0:T(4,128)S(1)}, f32[3,1,4,512]{3,2,1,0:T(4,128)S(1)}, u32[]{:S(2)}, u32[]{:S(2)}) collective-permute-start(f32[3,1,4,512]{3,2,1,0:T(4,128)S(1)} %get-tuple-element.59), channel_id=1, source_target_pairs={{0,1},{1,2},{2,3},{3,4},{4,5},{5,6},{6,7},{7,0},{8,9},{9,10},{10,1... | collective-permute-start | bytes 73736 | tf_op jit(solution)/shard_map/ppermute | solution.py:26
  251.2 15.5 %collective-permute-start.47 = (f32[3,1,4,512]{3,2,1,0:T(4,128)S(1)}, f32[3,1,4,512]{3,2,1,0:T(4,128)S(1)}, u32[]{:S(2)}, u32[]{:S(2)}) collective-permute-start(f32[3,1,4,512]{3,2,1,0:T(4,128)S(1)} %get-tuple-element.60), channel_id=1, source_target_pairs={{1,0},{2,1},{3,2},{4,3},{5,4},{6,5},{7,6},{0,7},{9,8},{10,9},{11,1... | collective-permute-start | bytes 73736 | tf_op jit(solution)/shard_map/ppermute | solution.py:28
  274.6 17.7 %collective-permute-start.50 = (f32[3,1,8,1024]{3,2,1,0:T(8,128)S(1)}, f32[3,1,8,1024]{3,2,1,0:T(8,128)S(1)}, u32[]{:S(2)}, u32[]{:S(2)}) collective-permute-start(f32[3,1,8,1024]{3,2,1,0:T(8,128)S(1)} %get-tuple-element.31), channel_id=1, source_target_pairs={{0,1},{1,2},{2,3},{3,4},{4,5},{5,6},{6,7},{7,0},{8,9},{9,10},{10,1... | collective-permute-start | bytes 294920 | tf_op jit(solution)/shard_map/ppermute | solution.py:26
  276.5 15.7 %collective-permute-start.51 = (f32[3,1,8,1024]{3,2,1,0:T(8,128)S(1)}, f32[3,1,8,1024]{3,2,1,0:T(8,128)S(1)}, u32[]{:S(2)}, u32[]{:S(2)}) collective-permute-start(f32[3,1,8,1024]{3,2,1,0:T(8,128)S(1)} %get-tuple-element.32), channel_id=1, source_target_pairs={{1,0},{2,1},{3,2},{4,3},{5,4},{6,5},{7,6},{0,7},{9,8},{10,9},{11,1... | collective-permute-start | bytes 294920 | tf_op jit(solution)/shard_map/ppermute | solution.py:28
  283.6 8.6 %collective-permute-start.49 = (f32[3,3,1,1024]{3,2,1,0:T(1,128)S(1)}, f32[3,3,1,1024]{3,2,1,0:T(1,128)S(1)}, u32[]{:S(2)}, u32[]{:S(2)}) collective-permute-start(f32[3,3,1,1024]{3,2,1,0:T(1,128)S(1)} %get-tuple-element.30), channel_id=1, source_target_pairs={{0,8},{8,16},{16,24},{24,32},{32,40},{40,48},{48,56},{56,64},{64,7... | collective-permute-start | bytes 110600 | tf_op jit(solution)/shard_map/ppermute | solution.py:26
  292.5 17.7 %collective-permute-start.54 = (f32[3,1,8,1024]{3,2,1,0:T(8,128)S(1)}, f32[3,1,8,1024]{3,2,1,0:T(8,128)S(1)}, u32[]{:S(2)}, u32[]{:S(2)}) collective-permute-start(f32[3,1,8,1024]{3,2,1,0:T(8,128)S(1)} %get-tuple-element.27), channel_id=1, source_target_pairs={{0,1},{1,2},{2,3},{3,4},{4,5},{5,6},{6,7},{7,0},{8,9},{9,10},{10,1... | collective-permute-start | bytes 294920 | tf_op jit(solution)/shard_map/ppermute | solution.py:26
  294.5 15.7 %collective-permute-start.55 = (f32[3,1,8,1024]{3,2,1,0:T(8,128)S(1)}, f32[3,1,8,1024]{3,2,1,0:T(8,128)S(1)}, u32[]{:S(2)}, u32[]{:S(2)}) collective-permute-start(f32[3,1,8,1024]{3,2,1,0:T(8,128)S(1)} %get-tuple-element.28), channel_id=1, source_target_pairs={{1,0},{2,1},{3,2},{4,3},{5,4},{6,5},{7,6},{0,7},{9,8},{10,9},{11,1... | collective-permute-start | bytes 294920 | tf_op jit(solution)/shard_map/ppermute | solution.py:28
  301.6 8.6 %collective-permute-start.53 = (f32[3,3,1,1024]{3,2,1,0:T(1,128)S(1)}, f32[3,3,1,1024]{3,2,1,0:T(1,128)S(1)}, u32[]{:S(2)}, u32[]{:S(2)}) collective-permute-start(f32[3,3,1,1024]{3,2,1,0:T(1,128)S(1)} %get-tuple-element.26), channel_id=1, source_target_pairs={{0,8},{8,16},{16,24},{24,32},{32,40},{40,48},{48,56},{56,64},{64,7... | collective-permute-start | bytes 110600 | tf_op jit(solution)/shard_map/ppermute | solution.py:26
  310.5 17.7 %collective-permute-start.58 = (f32[3,1,8,1024]{3,2,1,0:T(8,128)S(1)}, f32[3,1,8,1024]{3,2,1,0:T(8,128)S(1)}, u32[]{:S(2)}, u32[]{:S(2)}) collective-permute-start(f32[3,1,8,1024]{3,2,1,0:T(8,128)S(1)} %get-tuple-element.23), channel_id=1, source_target_pairs={{0,1},{1,2},{2,3},{3,4},{4,5},{5,6},{6,7},{7,0},{8,9},{9,10},{10,1... | collective-permute-start | bytes 294920 | tf_op jit(solution)/shard_map/ppermute | solution.py:26
  312.4 15.7 %collective-permute-start.59 = (f32[3,1,8,1024]{3,2,1,0:T(8,128)S(1)}, f32[3,1,8,1024]{3,2,1,0:T(8,128)S(1)}, u32[]{:S(2)}, u32[]{:S(2)}) collective-permute-start(f32[3,1,8,1024]{3,2,1,0:T(8,128)S(1)} %get-tuple-element.24), channel_id=1, source_target_pairs={{1,0},{2,1},{3,2},{4,3},{5,4},{6,5},{7,6},{0,7},{9,8},{10,9},{11,1... | collective-permute-start | bytes 294920 | tf_op jit(solution)/shard_map/ppermute | solution.py:28
  319.5 8.6 %collective-permute-start.57 = (f32[3,3,1,1024]{3,2,1,0:T(1,128)S(1)}, f32[3,3,1,1024]{3,2,1,0:T(1,128)S(1)}, u32[]{:S(2)}, u32[]{:S(2)}) collective-permute-start(f32[3,3,1,1024]{3,2,1,0:T(1,128)S(1)} %get-tuple-element.22), channel_id=1, source_target_pairs={{0,8},{8,16},{16,24},{24,32},{32,40},{40,48},{48,56},{56,64},{64,7... | collective-permute-start | bytes 110600 | tf_op jit(solution)/shard_map/ppermute | solution.py:26
  328.4 17.7 %collective-permute-start.62 = (f32[3,1,8,1024]{3,2,1,0:T(8,128)S(1)}, f32[3,1,8,1024]{3,2,1,0:T(8,128)S(1)}, u32[]{:S(2)}, u32[]{:S(2)}) collective-permute-start(f32[3,1,8,1024]{3,2,1,0:T(8,128)S(1)} %get-tuple-element.19), channel_id=1, source_target_pairs={{0,1},{1,2},{2,3},{3,4},{4,5},{5,6},{6,7},{7,0},{8,9},{9,10},{10,1... | collective-permute-start | bytes 294920 | tf_op jit(solution)/shard_map/ppermute | solution.py:26
  330.4 15.7 %collective-permute-start.63 = (f32[3,1,8,1024]{3,2,1,0:T(8,128)S(1)}, f32[3,1,8,1024]{3,2,1,0:T(8,128)S(1)}, u32[]{:S(2)}, u32[]{:S(2)}) collective-permute-start(f32[3,1,8,1024]{3,2,1,0:T(8,128)S(1)} %get-tuple-element.20), channel_id=1, source_target_pairs={{1,0},{2,1},{3,2},{4,3},{5,4},{6,5},{7,6},{0,7},{9,8},{10,9},{11,1... | collective-permute-start | bytes 294920 | tf_op jit(solution)/shard_map/ppermute | solution.py:28
  346.4 17.7 %collective-permute-start.66 = (f32[3,1,8,1024]{3,2,1,0:T(8,128)S(1)}, f32[3,1,8,1024]{3,2,1,0:T(8,128)S(1)}, u32[]{:S(2)}, u32[]{:S(2)}) collective-permute-start(f32[3,1,8,1024]{3,2,1,0:T(8,128)S(1)} %get-tuple-element.15), channel_id=1, source_target_pairs={{0,1},{1,2},{2,3},{3,4},{4,5},{5,6},{6,7},{7,0},{8,9},{9,10},{10,1... | collective-permute-start | bytes 294920 | tf_op jit(solution)/shard_map/ppermute | solution.py:26
  348.3 15.7 %collective-permute-start.67 = (f32[3,1,8,1024]{3,2,1,0:T(8,128)S(1)}, f32[3,1,8,1024]{3,2,1,0:T(8,128)S(1)}, u32[]{:S(2)}, u32[]{:S(2)}) collective-permute-start(f32[3,1,8,1024]{3,2,1,0:T(8,128)S(1)} %get-tuple-element.16), channel_id=1, source_target_pairs={{1,0},{2,1},{3,2},{4,3},{5,4},{6,5},{7,6},{0,7},{9,8},{10,9},{11,1... | collective-permute-start | bytes 294920 | tf_op jit(solution)/shard_map/ppermute | solution.py:28
  392.3 17.4 %collective-permute-start.70 = (f32[3,1,4,512]{3,2,1,0:T(4,128)S(1)}, f32[3,1,4,512]{3,2,1,0:T(4,128)S(1)}, u32[]{:S(2)}, u32[]{:S(2)}) collective-permute-start(f32[3,1,4,512]{3,2,1,0:T(4,128)S(1)} %get-tuple-element.55), channel_id=1, source_target_pairs={{0,1},{1,2},{2,3},{3,4},{4,5},{5,6},{6,7},{7,0},{8,9},{9,10},{10,1... | collective-permute-start | bytes 73736 | tf_op jit(solution)/shard_map/ppermute | solution.py:26
  394.3 15.5 %collective-permute-start.71 = (f32[3,1,4,512]{3,2,1,0:T(4,128)S(1)}, f32[3,1,4,512]{3,2,1,0:T(4,128)S(1)}, u32[]{:S(2)}, u32[]{:S(2)}) collective-permute-start(f32[3,1,4,512]{3,2,1,0:T(4,128)S(1)} %get-tuple-element.56), channel_id=1, source_target_pairs={{1,0},{2,1},{3,2},{4,3},{5,4},{6,5},{7,6},{0,7},{9,8},{10,9},{11,1... | collective-permute-start | bytes 73736 | tf_op jit(solution)/shard_map/ppermute | solution.py:28
  410.0 17.4 %collective-permute-start.74 = (f32[3,1,4,512]{3,2,1,0:T(4,128)S(1)}, f32[3,1,4,512]{3,2,1,0:T(4,128)S(1)}, u32[]{:S(2)}, u32[]{:S(2)}) collective-permute-start(f32[3,1,4,512]{3,2,1,0:T(4,128)S(1)} %get-tuple-element.51), channel_id=1, source_target_pairs={{0,1},{1,2},{2,3},{3,4},{4,5},{5,6},{6,7},{7,0},{8,9},{9,10},{10,1... | collective-permute-start | bytes 73736 | tf_op jit(solution)/shard_map/ppermute | solution.py:26
  411.9 15.5 %collective-permute-start.75 = (f32[3,1,4,512]{3,2,1,0:T(4,128)S(1)}, f32[3,1,4,512]{3,2,1,0:T(4,128)S(1)}, u32[]{:S(2)}, u32[]{:S(2)}) collective-permute-start(f32[3,1,4,512]{3,2,1,0:T(4,128)S(1)} %get-tuple-element.52), channel_id=1, source_target_pairs={{1,0},{2,1},{3,2},{4,3},{5,4},{6,5},{7,6},{0,7},{9,8},{10,9},{11,1... | collective-permute-start | bytes 73736 | tf_op jit(solution)/shard_map/ppermute | solution.py:28
  437.7 12.8 %collective-permute-start.76 = (f32[3,3,1,256]{3,2,1,0:T(1,128)S(1)}, f32[3,3,1,256]{3,2,1,0:T(1,128)S(1)}, u32[]{:S(2)}, u32[]{:S(2)}) collective-permute-start(f32[3,3,1,256]{3,2,1,0:T(1,128)S(1)} %get-tuple-element.87), channel_id=1, source_target_pairs={{8,0},{16,8},{24,16},{32,24},{40,32},{48,40},{56,48},{64,56},{72,6... | collective-permute-start | bytes 27656 | tf_op jit(solution)/shard_map/ppermute | solution.py:28
  439.6 10.8 %collective-permute-start.77 = (f32[3,3,1,256]{3,2,1,0:T(1,128)S(1)}, f32[3,3,1,256]{3,2,1,0:T(1,128)S(1)}, u32[]{:S(2)}, u32[]{:S(2)}) collective-permute-start(f32[3,3,1,256]{3,2,1,0:T(1,128)S(1)} %get-tuple-element.88), channel_id=1, source_target_pairs={{0,8},{8,16},{16,24},{24,32},{32,40},{40,48},{48,56},{56,64},{64,7... | collective-permute-start | bytes 27656 | tf_op jit(solution)/shard_map/ppermute | solution.py:26
  450.6 15.7 %collective-permute-start.80 = (f32[3,3,1,256]{3,2,1,0:T(1,128)S(1)}, f32[3,3,1,256]{3,2,1,0:T(1,128)S(1)}, u32[]{:S(2)}, u32[]{:S(2)}) collective-permute-start(f32[3,3,1,256]{3,2,1,0:T(1,128)S(1)} %get-tuple-element.83), channel_id=1, source_target_pairs={{8,0},{16,8},{24,16},{32,24},{40,32},{48,40},{56,48},{64,56},{72,6... | collective-permute-start | bytes 27656 | tf_op jit(solution)/shard_map/ppermute | solution.py:28
  456.0 10.3 %collective-permute-start.81 = (f32[3,3,1,256]{3,2,1,0:T(1,128)S(1)}, f32[3,3,1,256]{3,2,1,0:T(1,128)S(1)}, u32[]{:S(2)}, u32[]{:S(2)}) collective-permute-start(f32[3,3,1,256]{3,2,1,0:T(1,128)S(1)} %get-tuple-element.84), channel_id=1, source_target_pairs={{0,8},{8,16},{16,24},{24,32},{32,40},{40,48},{48,56},{56,64},{64,7... | collective-permute-start | bytes 27656 | tf_op jit(solution)/shard_map/ppermute | solution.py:26
  467.2 17.8 %collective-permute-start.85 = (f32[3,3,1,128]{3,1,0,2:T(4,128)S(1)}, f32[3,3,1,128]{3,1,0,2:T(4,128)S(1)}, u32[]{:S(2)}, u32[]{:S(2)}) collective-permute-start(f32[3,3,1,128]{3,1,0,2:T(4,128)S(1)} %bitcast_divide_fusion), channel_id=1, source_target_pairs={{0,8},{8,16},{16,24},{24,32},{32,40},{40,48},{48,56},{56,64},{64,7... | collective-permute-start | bytes 13832 | tf_op jit(solution)/shard_map/ppermute | solution.py:26
  469.2 15.9 %collective-permute-start.84 = (f32[3,3,1,128]{3,1,0,2:T(4,128)S(1)}, f32[3,3,1,128]{3,1,0,2:T(4,128)S(1)}, u32[]{:S(2)}, u32[]{:S(2)}) collective-permute-start(f32[3,3,1,128]{3,1,0,2:T(4,128)S(1)} %bitcast_divide_fusion), channel_id=1, source_target_pairs={{8,0},{16,8},{24,16},{32,24},{40,32},{48,40},{56,48},{64,56},{72,6... | collective-permute-start | bytes 13832 | tf_op jit(solution)/shard_map/ppermute | solution.py:28
  485.2 18.3 %collective-permute-start.89 = (f32[3,3,1,128]{3,1,0,2:T(4,128)S(1)}, f32[3,3,1,128]{3,1,0,2:T(4,128)S(1)}, u32[]{:S(2)}, u32[]{:S(2)}) collective-permute-start(f32[3,3,1,128]{3,1,0,2:T(4,128)S(1)} %divide_add_fusion.13), channel_id=1, source_target_pairs={{0,8},{8,16},{16,24},{24,32},{32,40},{40,48},{48,56},{56,64},{64,7... | collective-permute-start | bytes 13832 | tf_op jit(solution)/shard_map/ppermute | solution.py:26
  487.1 16.4 %collective-permute-start.88 = (f32[3,3,1,128]{3,1,0,2:T(4,128)S(1)}, f32[3,3,1,128]{3,1,0,2:T(4,128)S(1)}, u32[]{:S(2)}, u32[]{:S(2)}) collective-permute-start(f32[3,3,1,128]{3,1,0,2:T(4,128)S(1)} %divide_add_fusion.13), channel_id=1, source_target_pairs={{8,0},{16,8},{24,16},{32,24},{40,32},{48,40},{56,48},{64,56},{72,6... | collective-permute-start | bytes 13832 | tf_op jit(solution)/shard_map/ppermute | solution.py:28
  504.2 13.0 %collective-permute-start.92 = (f32[3,3,1,256]{3,2,1,0:T(1,128)S(1)}, f32[3,3,1,256]{3,2,1,0:T(1,128)S(1)}, u32[]{:S(2)}, u32[]{:S(2)}) collective-permute-start(f32[3,3,1,256]{3,2,1,0:T(1,128)S(1)} %get-tuple-element.79), channel_id=1, source_target_pairs={{8,0},{16,8},{24,16},{32,24},{40,32},{48,40},{56,48},{64,56},{72,6... | collective-permute-start | bytes 27656 | tf_op jit(solution)/shard_map/ppermute | solution.py:28
  506.1 11.1 %collective-permute-start.93 = (f32[3,3,1,256]{3,2,1,0:T(1,128)S(1)}, f32[3,3,1,256]{3,2,1,0:T(1,128)S(1)}, u32[]{:S(2)}, u32[]{:S(2)}) collective-permute-start(f32[3,3,1,256]{3,2,1,0:T(1,128)S(1)} %get-tuple-element.80), channel_id=1, source_target_pairs={{0,8},{8,16},{16,24},{24,32},{32,40},{40,48},{48,56},{56,64},{64,7... | collective-permute-start | bytes 27656 | tf_op jit(solution)/shard_map/ppermute | solution.py:26
  517.4 15.7 %collective-permute-start.96 = (f32[3,3,1,256]{3,2,1,0:T(1,128)S(1)}, f32[3,3,1,256]{3,2,1,0:T(1,128)S(1)}, u32[]{:S(2)}, u32[]{:S(2)}) collective-permute-start(f32[3,3,1,256]{3,2,1,0:T(1,128)S(1)} %get-tuple-element.75), channel_id=1, source_target_pairs={{8,0},{16,8},{24,16},{32,24},{40,32},{48,40},{56,48},{64,56},{72,6... | collective-permute-start | bytes 27656 | tf_op jit(solution)/shard_map/ppermute | solution.py:28
  522.4 10.6 %collective-permute-start.97 = (f32[3,3,1,256]{3,2,1,0:T(1,128)S(1)}, f32[3,3,1,256]{3,2,1,0:T(1,128)S(1)}, u32[]{:S(2)}, u32[]{:S(2)}) collective-permute-start(f32[3,3,1,256]{3,2,1,0:T(1,128)S(1)} %get-tuple-element.76), channel_id=1, source_target_pairs={{0,8},{8,16},{16,24},{24,32},{32,40},{40,48},{48,56},{56,64},{64,7... | collective-permute-start | bytes 27656 | tf_op jit(solution)/shard_map/ppermute | solution.py:26
  537.5 21.0 %collective-permute-start.102 = (f32[3,1,4,512]{3,2,1,0:T(4,128)S(1)}, f32[3,1,4,512]{3,2,1,0:T(4,128)S(1)}, u32[]{:S(2)}, u32[]{:S(2)}) collective-permute-start(f32[3,1,4,512]{3,2,1,0:T(4,128)S(1)} %get-tuple-element.47), channel_id=1, source_target_pairs={{0,1},{1,2},{2,3},{3,4},{4,5},{5,6},{6,7},{7,0},{8,9},{9,10},{10,1... | collective-permute-start | bytes 73736 | tf_op jit(solution)/shard_map/ppermute | solution.py:26
  540.9 17.6 %collective-permute-start.103 = (f32[3,1,4,512]{3,2,1,0:T(4,128)S(1)}, f32[3,1,4,512]{3,2,1,0:T(4,128)S(1)}, u32[]{:S(2)}, u32[]{:S(2)}) collective-permute-start(f32[3,1,4,512]{3,2,1,0:T(4,128)S(1)} %get-tuple-element.48), channel_id=1, source_target_pairs={{1,0},{2,1},{3,2},{4,3},{5,4},{6,5},{7,6},{0,7},{9,8},{10,9},{11,1... | collective-permute-start | bytes 73736 | tf_op jit(solution)/shard_map/ppermute | solution.py:28
  558.7 17.4 %collective-permute-start.106 = (f32[3,1,4,512]{3,2,1,0:T(4,128)S(1)}, f32[3,1,4,512]{3,2,1,0:T(4,128)S(1)}, u32[]{:S(2)}, u32[]{:S(2)}) collective-permute-start(f32[3,1,4,512]{3,2,1,0:T(4,128)S(1)} %get-tuple-element.43), channel_id=1, source_target_pairs={{0,1},{1,2},{2,3},{3,4},{4,5},{5,6},{6,7},{7,0},{8,9},{9,10},{10,1... | collective-permute-start | bytes 73736 | tf_op jit(solution)/shard_map/ppermute | solution.py:26
  560.7 15.5 %collective-permute-start.107 = (f32[3,1,4,512]{3,2,1,0:T(4,128)S(1)}, f32[3,1,4,512]{3,2,1,0:T(4,128)S(1)}, u32[]{:S(2)}, u32[]{:S(2)}) collective-permute-start(f32[3,1,4,512]{3,2,1,0:T(4,128)S(1)} %get-tuple-element.44), channel_id=1, source_target_pairs={{1,0},{2,1},{3,2},{4,3},{5,4},{6,5},{7,6},{0,7},{9,8},{10,9},{11,1... | collective-permute-start | bytes 73736 | tf_op jit(solution)/shard_map/ppermute | solution.py:28
  584.0 17.7 %collective-permute-start.110 = (f32[3,1,8,1024]{3,2,1,0:T(8,128)S(1)}, f32[3,1,8,1024]{3,2,1,0:T(8,128)S(1)}, u32[]{:S(2)}, u32[]{:S(2)}) collective-permute-start(f32[3,1,8,1024]{3,2,1,0:T(8,128)S(1)} %get-tuple-element.11), channel_id=1, source_target_pairs={{0,1},{1,2},{2,3},{3,4},{4,5},{5,6},{6,7},{7,0},{8,9},{9,10},{10,1... | collective-permute-start | bytes 294920 | tf_op jit(solution)/shard_map/ppermute | solution.py:26
  586.0 15.7 %collective-permute-start.111 = (f32[3,1,8,1024]{3,2,1,0:T(8,128)S(1)}, f32[3,1,8,1024]{3,2,1,0:T(8,128)S(1)}, u32[]{:S(2)}, u32[]{:S(2)}) collective-permute-start(f32[3,1,8,1024]{3,2,1,0:T(8,128)S(1)} %get-tuple-element.12), channel_id=1, source_target_pairs={{1,0},{2,1},{3,2},{4,3},{5,4},{6,5},{7,6},{0,7},{9,8},{10,9},{11,1... | collective-permute-start | bytes 294920 | tf_op jit(solution)/shard_map/ppermute | solution.py:28
  602.0 17.7 %collective-permute-start.114 = (f32[3,1,8,1024]{3,2,1,0:T(8,128)S(1)}, f32[3,1,8,1024]{3,2,1,0:T(8,128)S(1)}, u32[]{:S(2)}, u32[]{:S(2)}) collective-permute-start(f32[3,1,8,1024]{3,2,1,0:T(8,128)S(1)} %get-tuple-element.7), channel_id=1, source_target_pairs={{0,1},{1,2},{2,3},{3,4},{4,5},{5,6},{6,7},{7,0},{8,9},{9,10},{10,1... | collective-permute-start | bytes 294920 | tf_op jit(solution)/shard_map/ppermute | solution.py:26
  603.9 15.7 %collective-permute-start.115 = (f32[3,1,8,1024]{3,2,1,0:T(8,128)S(1)}, f32[3,1,8,1024]{3,2,1,0:T(8,128)S(1)}, u32[]{:S(2)}, u32[]{:S(2)}) collective-permute-start(f32[3,1,8,1024]{3,2,1,0:T(8,128)S(1)} %get-tuple-element.8), channel_id=1, source_target_pairs={{1,0},{2,1},{3,2},{4,3},{5,4},{6,5},{7,6},{0,7},{9,8},{10,9},{11,1... | collective-permute-start | bytes 294920 | tf_op jit(solution)/shard_map/ppermute | solution.py:28
  (53 other events, 344.8 us)
where the time goes:
time: 633 us; the launch traced here: 621 us
  starting transfers between devices  378 us (60%)
  waiting for transfers between devices  115 us (18%)
  local copies, waits for them, and re-layouts  91.6 us (14%)
  other arithmetic  34.2 us (5%)
    ppermute x58, starting transfers between devices, extended(): lax.ppermute(head, axis, [((i + 1) % count, i) for i in range(ends)])  235 us
    ppermute x58, starting transfers between devices, extended(): lax.ppermute(tail, axis, [(i, (i + 1) % count) for i in range(ends)])  143 us
    ppermute x58, waiting for transfers between devices, extended(): lax.ppermute(tail, axis, [(i, (i + 1) % count) for i in range(ends)])  90.9 us
    reshape x4, local copies, waits for them, and re-layouts, shrink(): values.reshape(components, rows_z, rows_x // 2, 2, rows_y // 2, 2)  54.5 us
    reduce_sum x12, other arithmetic, shrink(): values.reshape(components, rows_z, rows_x // 2, 2, rows_y // 2, 2)  26.5 us
    ppermute x58, waiting for transfers between devices, extended(): lax.ppermute(head, axis, [((i + 1) % count, i) for i in range(ends)])  23.9 us
    broadcast_in_dim x12, local copies, waits for them, and re-layouts, vcycle(): field = field + jnp.repeat(jnp.repeat(correction, 2, axis=2), 2, axis=3)  13 us
  transfers between devices with their start and end apart: 116, of which 29 were waited for; matrix products, arithmetic and copies ran while one was open for 2% of the time, Pallas kernels for 0%

commit v1 on v0

v1 whole, which is shorter than its diff:
```python
import jax
import jax.numpy as jnp
from jax import lax
from jax.experimental import pallas as pl
from jax.experimental.pallas import tpu as pltpu
from jax.sharding import PartitionSpec as P

relaxation = 0.8
plane_coupling = 16.0
depth_coupling = 1.0
C = 3
NZ = 24
HALO = 6
LANES = 128
PARAMS = pltpu.CompilerParams(vmem_limit_bytes=28 << 20)


def coupling_of(level):
    return plane_coupling / 4.0**level


def base_of(level):
    return 4.0 * coupling_of(level) + 2.0 * depth_coupling


class Row:
    def __init__(self, base, shift):
        self.base, self.shift = base, shift

    def __add__(self, n):
        return Row(self.base, self.shift + n)

    def __sub__(self, n):
        return self + -n

    def double(self):
        return Row(2 * self.base, 2 * self.shift)


def index(field, r):
    return r.base + (r.shift - field[1]) if isinstance(r, Row) else r - field[1]


def row(field, c, r):
    return field[0][c, index(field, r)]


def shared(field, r):
    return field[0][index(field, r)]


def neighbours(field, c, r, level):
    mid = row(field, c, r)
    width = mid.shape[1]
    lateral = row(field, c, r - 1) + row(field, c, r + 1) + pltpu.roll(mid, 1, 1) + pltpu.roll(mid, width - 1, 1)
    vertical = pltpu.roll(mid, 1, 0) + pltpu.roll(mid, NZ - 1, 0)
    return mid, coupling_of(level) * lateral + depth_coupling * vertical


def each_row(low, high, body):
    def step(n, carry):
        body(Row(n, low))
        return carry

    lax.fori_loop(0, high - low, step, 0)


def sweep(target, field, source, factor, level, low, high):
    def body(r):
        f = shared(factor, r)
        for c in range(C):
            mid, around = neighbours(field, c, r, level)
            target[0][c, index(target, r)] = (1.0 - relaxation) * mid + f * (row(source, c, r) + around)

    each_row(low, high, body)


def first_sweep(target, source, factor, low, high):
    def body(r):
        f = shared(factor, r)
        for c in range(C):
            target[0][c, index(target, r)] = f * row(source, c, r)

    each_row(low, high, body)


def lane_index():
    return lax.broadcasted_iota(jnp.int32, (NZ, LANES), 1)


def take(values, index):
    return jnp.take_along_axis(values, index, axis=1, mode="promise_in_bounds")


def pair_sum(values, period):
    lane = lane_index()
    if values.shape[1] == 2 * LANES:
        even = (2 * lane) % LANES
        halves = [take(h + pltpu.roll(h, LANES - 1, 1), even) for h in (values[:, :LANES], values[:, LANES:])]
        return jnp.where(lane < LANES // 2, halves[0], halves[1])
    return take(values + pltpu.roll(values, LANES - 1, 1), (2 * lane) % period)


def spread(values, period):
    lane = lane_index()
    if period == 2 * LANES:
        return jnp.concatenate([take(values, lane // 2), take(values, LANES // 2 + lane // 2)], axis=1)
    return take(values, (lane % period) // 2)


def coarse_source(target, field, source, density, level, period, low, high):
    def body(q):
        for c in range(C):
            total = None
            for r in (q.double(), q.double() + 1):
                mid, around = neighbours(field, c, r, level)
                residual = row(source, c, r) + around - (shared(density, r) + base_of(level)) * mid
                total = residual if total is None else total + residual
            target[0][c, index(target, q)] = 0.25 * pair_sum(total, period)

    each_row(low, high, body)


def coarse_density(target, density, period, low, high):
    def body(q):
        total = shared(density, q.double()) + shared(density, q.double() + 1)
        target[0][index(target, q)] = 0.25 * pair_sum(total, period)

    each_row(low, high, body)


def factors(target, density, level, period, rows, position, low, high):
    i, j, count_x, count_y = position[0], position[1], position[2], position[3]
    width = target[0].shape[-1]
    lane = lax.broadcasted_iota(jnp.int32, (NZ, width), 1) % period
    inside_y = ((lane < 3 * period // 4) | (j > 0)) & ((lane < period // 2) | (lane >= 3 * period // 4) | (j < count_y - 1))

    def body(r):
        at = i * rows + r.base
        inside = inside_y & ((at >= -r.shift) & (at < count_x * rows - r.shift))
        target[0][index(target, r)] = jnp.where(inside, relaxation / (shared(density, r) + base_of(level)), 0.0)

    each_row(low, high, body)


def level_one_down(g1, v1, scratch, d1, f1, packed):
    first_sweep(scratch, g1, f1, -2, 6)
    sweep(v1, scratch, g1, f1, 1, -1, 5)
    lane = lane_index()
    for c in range(C + 1):
        pair = []
        for q in (0, 1):
            total = None
            for r in (2 * q, 2 * q + 1):
                if c == C:
                    part = shared(d1, r)
                else:
                    mid, around = neighbours(v1, c, r, 1)
                    part = row(g1, c, r) + around - (shared(d1, r) + base_of(1)) * mid
                total = part if total is None else total + part
            pair.append(0.25 * pair_sum(total, LANES))
        packed[c] = jnp.where(lane < LANES // 2, pair[0], pair[1])


def pack_kernel(source, density, out):
    blocks = out.shape[0]
    for ref, at, n in ((source, 0, source.shape[0]), (density, source.shape[0], density.shape[0])):
        for m in range(n):
            for b in range(blocks):
                out[b, at + m, :, :LANES] = ref[m, :, b * LANES : (b + 1) * LANES]
                zero = jnp.zeros((ref.shape[1], LANES), jnp.float32)
                after = ref[m, :, (b + 1) * LANES : (b + 2) * LANES] if b + 1 < blocks else zero
                before = ref[m, :, (b - 1) * LANES : b * LANES] if b else zero
                lane = lax.broadcasted_iota(jnp.int32, zero.shape, 1)
                out[b, at + m, :, LANES:] = jnp.where(lane < LANES // 2, after, before)


def unpack_kernel(taken, own, low, high, scratch):
    blocks, _, rows, _ = taken.shape
    depth = NZ // blocks
    for c in range(C + 1):
        for b in range(blocks):
            for z in range(depth):
                at = (b * depth + z) * rows
                for h in range(2):
                    scratch[c, h, at : at + rows] = taken[b, c * depth + z, :, h * LANES : (h + 1) * LANES]
    for c in range(C + 1):
        for r in range(rows):
            for h in range(2):
                part = scratch[c, h, pl.ds(r, NZ, stride=rows), :]
                lanes = slice(h * LANES, (h + 1) * LANES)
                own[c, r, :, lanes] = part
                if r < HALO:
                    low[c, r, :, lanes] = part
                if r >= rows - HALO:
                    high[c, r - rows + HALO, :, lanes] = part


def first_down_kernel(position, own, left, right, g0, d0, f0, v0, g1, d1, f1, v1, packed, field, field1):
    rows = own.shape[1]
    for c in range(C + 1):
        for piece, at, n in ((left, 0, HALO), (own, HALO, rows), (right, HALO + rows, HALO)):
            for r in range(n):
                if c < C:
                    g0[c, at + r] = piece[c, r]
                else:
                    d0[at + r] = piece[c, r]
    g, d, f, a, b = (g0, -HALO), (d0, -HALO), (f0, -HALO), (field, -HALO), (v0, -HALO)
    factors(f, d, 0, 2 * LANES, rows, position, -HALO, rows + HALO)
    coarse_density((d1, -3), d, 2 * LANES, -3, rows // 2 + 3)
    factors((f1, -3), (d1, -3), 1, LANES, rows // 2, position, -3, rows // 2 + 3)
    first_sweep(a, g, f, -6, rows + 6)
    sweep(b, a, g, f, 0, -5, rows + 5)
    coarse_source((g1, -2), b, g, d, 0, 2 * LANES, -2, rows // 2 + 2)
    level_one_down((g1, -2), (v1, -2), (field1, -2), (d1, -3), (f1, -3), packed)


def side_kernel(own, left, right, to_left, to_right):
    rows, halo = own.shape[1], left.shape[1]
    half = (rows + 2 * halo) // 2
    lane = lane_index()

    def at(c, r):
        if r < halo:
            return left[c, r]
        return own[c, r - halo] if r < halo + rows else right[c, r - halo - rows]

    for c in range(C):
        for r in range(half):
            one, two = at(c, r), pltpu.roll(at(c, r + half), LANES // 2, 1)
            to_left[c, r] = jnp.where(lane < LANES // 2, one, two)
            to_right[c, r] = jnp.where(lane < LANES // 2, two, one)


def second_down_kernel(own, left, right, after, before, g0, d0, f0, d1, f1, v0, g1, v1, packed, wide, field, field1):
    rows, halo = own.shape[1], left.shape[1]
    half = (rows + 2 * halo) // 2
    lane = lane_index()
    for c in range(C):
        for piece, at, n in ((left, 0, halo), (own, halo, rows), (right, halo + rows, halo)):
            for r in range(n):
                wide[c, at + r, :, :LANES] = piece[c, r]
        for r in range(half):
            wide[c, r, :, LANES:] = jnp.where(lane < LANES // 2, after[c, r], before[c, r])
            two = jnp.where(lane < LANES // 2, before[c, r], after[c, r])
            wide[c, r + half, :, LANES:] = pltpu.roll(two, LANES // 2, 1)
    g, d, f, a, b = (g0, -HALO), (d0, -HALO), (f0, -HALO), (field, -HALO), (v0, -HALO)
    sweep(a, (wide, -halo), g, f, 0, -6, rows + 6)
    sweep(b, a, g, f, 0, -5, rows + 5)
    coarse_source((g1, -2), b, g, d, 0, 2 * LANES, -2, rows // 2 + 2)
    level_one_down((g1, -2), (v1, -2), (field1, -2), (d1, -3), (f1, -3), packed)


def coarse_kernel(position, blocks, v1, out, g2, d2, f2, g3, d3, f3, a, b, a3, b3):
    lane = lane_index()
    count = blocks.shape[0]
    reach = count // 2 * 2
    for n in range(count):
        for c in range(C + 1):
            both = blocks[n, c]
            other = pltpu.roll(both, LANES // 2, 1)
            for q, value in ((0, jnp.where(lane < LANES // 2, both, other)), (1, jnp.where(lane < LANES // 2, other, both))):
                if c < C:
                    g2[c, 2 * n + q] = value
                else:
                    d2[2 * n + q] = value
    g, d, f, u, w = (g2, -reach), (d2, -reach), (f2, -reach), (a, -reach), (b, -reach)
    h, e, k, s, t = (g3, -reach // 2), (d3, -reach // 2), (f3, -reach // 2), (a3, -reach // 2), (b3, -reach // 2)
    factors(f, d, 2, LANES // 2, 2, position, -8, 10)
    coarse_density(e, d, LANES // 2, -3, 4)
    factors(k, e, 3, LANES // 4, 1, position, -3, 4)
    first_sweep(u, g, f, -8, 10)
    sweep(w, u, g, f, 2, -7, 9)
    coarse_source(h, w, g, d, 2, LANES // 2, -3, 4)
    first_sweep(s, h, k, -3, 4)
    sweep(t, s, h, k, 3, -2, 3)
    sweep(s, t, h, k, 3, -1, 2)

    def correct(q):
        for c in range(C):
            fine = spread(row(s, c, q), LANES // 2)
            for r in (q.double(), q.double() + 1):
                b[c, index(w, r)] = row(w, c, r) + fine

    each_row(-1, 2, correct)
    sweep(u, w, g, f, 2, -1, 3)
    sweep(w, u, g, f, 2, 0, 2)
    for c in range(C):
        for q in (0, 1):
            fine = spread(row(w, c, q), LANES)
            for r in (2 * q, 2 * q + 1):
                out[c, r] = v1[c, r + 2] + fine


def climb(own, left, right, g0, f0, v0, g1, f1, wide, u, w, field, emit):
    rows1, halo = own.shape[1], left.shape[1]
    for c in range(C):
        for piece, at, n in ((left, 0, halo), (own, halo, rows1), (right, halo + rows1, halo)):
            for r in range(n):
                wide[c, at + r] = piece[c, r]
    sweep((u, -3), (wide, -halo), (g1, -2), (f1, -3), 1, -2, rows1 + 2)
    sweep((w, -3), (u, -3), (g1, -2), (f1, -3), 1, -1, rows1 + 1)

    def correct(q):
        for c in range(C):
            fine = spread(row((w, -3), c, q), 2 * LANES)
            for r in (q.double(), q.double() + 1):
                field[c, index((field, -HALO), r)] = row((v0, -HALO), c, r) + fine

    each_row(-1, rows1 + 1, correct)
    rows = 2 * rows1
    sweep((emit, -HALO), (field, -HALO), (g0, -HALO), (f0, -HALO), 0, -1, rows + 1)
    sweep((field, -HALO), (emit, -HALO), (g0, -HALO), (f0, -HALO), 0, 0, rows)


def first_up_kernel(own, left, right, g0, f0, v0, g1, f1, out, low, high, wide, u, w, field, other):
    climb(own, left, right, g0, f0, v0, g1, f1, wide, u, w, field, other)
    rows, halo = out.shape[1], low.shape[1]
    for c in range(C):
        for r in range(rows):
            value = field[c, r + HALO, :, :LANES]
            out[c, r] = value
            if r < halo:
                low[c, r] = value
            if r >= rows - halo:
                high[c, r - rows + halo] = value


def last_up_kernel(own, left, right, g0, f0, v0, g1, f1, out, wide, u, w, field, other, scratch):
    climb(own, left, right, g0, f0, v0, g1, f1, wide, u, w, field, other)
    blocks, _, rows, _ = out.shape
    depth = NZ // blocks
    for c in range(C):
        for r in range(rows):
            scratch[c, pl.ds(r, NZ, stride=rows), :] = field[c, r + HALO, :, :LANES]
    for c in range(C):
        for z in range(NZ):
            out[z // depth, c * depth + z % depth] = scratch[c, z * rows : (z + 1) * rows]


def join_kernel(taken, out):
    for b in range(taken.shape[0]):
        out[:, :, b * LANES : (b + 1) * LANES] = taken[b]


def call(kernel, outs, scratch, *args, scalars=0):
    shape = lambda s: jax.ShapeDtypeStruct(s, jnp.float32)
    specs = [pl.BlockSpec(memory_space=pltpu.SMEM)] * scalars + [pl.BlockSpec(memory_space=pltpu.VMEM)] * (len(args) - scalars)
    out = pl.pallas_call(
        kernel,
        out_shape=[shape(s) for s in outs],
        in_specs=specs,
        out_specs=[pl.BlockSpec(memory_space=pltpu.VMEM)] * len(outs),
        scratch_shapes=[pltpu.VMEM(s, jnp.float32) for s in scratch],
        compiler_params=PARAMS,
        name=kernel.__name__,
    )(*args)
    return out


def onward(values, axis, distance, closed=False):
    count = lax.axis_size(axis)
    pairs = [(i, (i + distance) % count) for i in range(count) if closed or 0 <= i + distance < count]
    return lax.ppermute(values, axis, pairs)


def shards(right_side, density):
    blocks = lax.axis_size("gz")
    depth, rows, columns = density.shape
    position = jnp.stack([lax.axis_index("gx"), lax.axis_index("gz"), lax.axis_size("gx"), blocks]).astype(jnp.int32)
    W, R0, R1 = 2 * LANES, rows + 2 * HALO, rows // 2

    (sent,) = call(pack_kernel, [(blocks, (C + 1) * depth, rows, W)], [], right_side.reshape(C * depth, rows, columns), density)
    taken = lax.all_to_all(sent, "gz", 0, 0)
    own, low, high = call(
        unpack_kernel,
        [(C + 1, rows, NZ, W), (C + 1, HALO, NZ, W), (C + 1, HALO, NZ, W)],
        [(C + 1, 2, NZ * rows, LANES)],
        taken,
    )
    fine, mid = (C, R0, NZ, W), (C, R1 + 4, NZ, LANES)
    g0, d0, f0, v0, g1, d1, f1, v1, packed = call(
        first_down_kernel,
        [fine, fine[1:], fine[1:], fine, mid, (R1 + 6, NZ, LANES), (R1 + 6, NZ, LANES), mid, (C + 1, NZ, LANES)],
        [fine, mid],
        position,
        own,
        onward(high, "gx", 1),
        onward(low, "gx", -1),
        scalars=1,
    )

    def coarse(packed, v1):
        near = jnp.stack([onward(packed, "gx", 1, True), packed, onward(packed, "gx", -1, True)])
        nine = jnp.concatenate([onward(near, "gx", 3, True), near, onward(near, "gx", -3, True)])
        two, three = (C, 18, NZ, LANES), (C, 9, NZ, LANES)
        (out,) = call(
            coarse_kernel,
            [(C, R1, NZ, LANES)],
            [two, two[1:], two[1:], three, three[1:], three[1:], two, two, three, three],
            position,
            nine,
            v1,
            scalars=1,
        )
        return out, onward(out[:, 1:], "gx", 1), onward(out[:, :-1], "gx", -1)

    middle = (C, R1 + 6, NZ, LANES)
    reach = HALO + 1
    field, low, high = call(
        first_up_kernel,
        [(C, rows, NZ, LANES), (C, reach, NZ, LANES), (C, reach, NZ, LANES)],
        [middle, middle, middle, fine, fine],
        *coarse(packed, v1),
        g0,
        f0,
        v0,
        g1,
        f1,
    )
    left, right = onward(high, "gx", 1), onward(low, "gx", -1)
    half = (rows + 2 * reach) // 2
    to_left, to_right = call(side_kernel, [(C, half, NZ, LANES)] * 2, [], field, left, right)
    v0, g1, v1, packed = call(
        second_down_kernel,
        [fine, mid, mid, (C + 1, NZ, LANES)],
        [(C, rows + 2 * reach, NZ, W), fine, mid],
        field,
        left,
        right,
        onward(to_left, "gz", -1),
        onward(to_right, "gz", 1),
        g0,
        d0,
        f0,
        d1,
        f1,
    )
    (sent,) = call(
        last_up_kernel,
        [(blocks, C * depth, rows, LANES)],
        [middle, middle, middle, fine, fine, (C, NZ * rows, LANES)],
        *coarse(packed, v1),
        g0,
        f0,
        v0,
        g1,
        f1,
    )
    (out,) = call(join_kernel, [(C * depth, rows, columns)], [], lax.all_to_all(sent, "gz", 0, 0))
    return out.reshape(right_side.shape)


def solution(mesh):
    return jax.shard_map(
        shards,
        mesh=mesh,
        in_specs=(P(None, "gz", "gx", None), P("gz", "gx", None)),
        out_specs=P(None, "gz", "gx", None),
        check_vma=False,
    )
```

time: 633 us -> 207 us (0.33)
  the two profiles are of different devices: /device:TPU:256 before, /device:TPU:198 now
where the time goes in v1:
time: 207 us; the launch traced here: 206 us
  starting transfers between devices  74.6 us (36%)
  blocking collectives  46.2 us (22%)
  waiting for transfers between devices  43.4 us (21%)
  Pallas kernels  39.5 us (19%)
    ppermute x18, starting transfers between devices, onward(): return lax.ppermute(values, axis, pairs)  74.6 us
    ppermute x18, waiting for transfers between devices, onward(): return lax.ppermute(values, axis, pairs)  43.4 us
    pallas_call x10, Pallas kernels, call(): pl.pallas_call(kernel, out_shape=[shape(s) for s in outs], in_specs=specs...  39.5 us
    all_to_all x1, blocking collectives, shards(): taken = lax.all_to_all(sent, 'gz', 0, 0)  30 us
    all_to_all x1, blocking collectives, shards(): lax.all_to_all(sent, 'gz', 0, 0)  16.2 us
  transfers between devices with their start and end apart: 18, of which 16 were waited for; matrix products, arithmetic and copies ran while one was open for 0% of the time, Pallas kernels for 0%

profile of v1, /device:TPU:198, one launch (start us, length us, event | category | flops | bytes accessed | tf_op | source)
XLA Modules:
  0.0 206.0 jit_solution(16614613440725924534)
XLA Ops:
  0.0 0.0 copy-start
  0.0 1.0 copy-done
  1.0 0.0 copy-start.1
  1.0 0.9 copy-done.1
  1.9 0.1 pack_kernel.1
  1.9 30.0 %all_to_all.10.taken = f32[8,12,8,256]{3,2,1,0:T(8,128)S(1)} all-to-all(f32[8,12,8,256]{3,2,1,0:T(8,128)S(1)} %pack_kernel.1), channel_id=1, replica_groups=mesh['gx'=64,'gz'=8] {'gz'}, dimensions={0} | all-to-all | bytes 1572864 | tf_op jit(solution)/shard_map/all_to_all | solution.py:374
  31.9 0.2 unpack_kernel.1
  32.2 1.9 collective-permute-start
  34.1 3.6 %collective-permute-start.1 = (f32[4,6,24,256]{3,2,1,0:T(8,128)S(1)}, f32[4,6,24,256]{3,2,1,0:T(8,128)S(1)}, u32[]{:S(2)}, u32[]{:S(2)}) collective-permute-start(f32[4,6,24,256]{3,2,1,0:T(8,128)S(1)} %get-tuple-element.28), channel_id=1, source_target_pairs={{8,0},{16,8},{24,16},{32,24},{40,32},{48,40},{56,48},{64,56},{72,6... | collective-permute-start | bytes 1769480 | tf_op jit(solution)/shard_map/ppermute | solution.py:364
  37.7 0.1 pad_add_fusion.position
  37.8 5.5 %collective-permute-done.left = f32[4,6,24,256]{3,2,1,0:T(8,128)S(1)} collective-permute-done((f32[4,6,24,256]{3,2,1,0:T(8,128)S(1)}, f32[4,6,24,256]{3,2,1,0:T(8,128)S(1)}, u32[]{:S(2)}, u32[]{:S(2)}) %collective-permute-start) | collective-permute-done | bytes 589856 | tf_op jit(solution)/shard_map/ppermute | solution.py:364
  43.4 1.8 collective-permute-done.1.right
  45.1 8.2 %first_down_kernel.1 = (f32[3,20,24,256]{3,2,1,0:T(8,128)S(1)}, f32[20,24,256]{2,1,0:T(8,128)S(1)}, f32[20,24,256]{2,1,0:T(8,128)S(1)}, f32[3,20,24,256]{3,2,1,0...) custom-call(s32[4]{0:T(128)S(1)} %pad_add_fusion.position, ...), custom_call_target="tpu_custom_call" | custom-call | tf_op jit(solution)/shard_map/first_down_kernel/pallas_call | solution.py:349
  53.3 3.8 %collective-permute-start.3 = (f32[4,24,128]{2,1,0:T(8,128)S(1)}, f32[4,24,128]{2,1,0:T(8,128)S(1)}, u32[]{:S(2)}, u32[]{:S(2)}) collective-permute-start(f32[4,24,128]{2,1,0:T(8,128)S(1)} %get-tuple-element.29), channel_id=1, source_target_pairs={{0,504},{8,0},{16,8},{24,16},{32,24},{40,32},{48,40},{56,48},{64,5... | collective-permute-start | bytes 147464 | tf_op jit(solution)/shard_map/ppermute | solution.py:364
  57.1 7.1 %collective-permute-start.2 = (f32[4,24,128]{2,1,0:T(8,128)S(1)}, f32[4,24,128]{2,1,0:T(8,128)S(1)}, u32[]{:S(2)}, u32[]{:S(2)}) collective-permute-start(f32[4,24,128]{2,1,0:T(8,128)S(1)} %get-tuple-element.29), channel_id=1, source_target_pairs={{0,8},{8,16},{16,24},{24,32},{32,40},{40,48},{48,56},{56,64},{64,7... | collective-permute-start | bytes 147464 | tf_op jit(solution)/shard_map/ppermute | solution.py:364
  64.2 0.0 collective-permute-done.3
  64.3 0.8 collective-permute-done.2
  65.1 6.8 %collective-permute-start.4 = (f32[3,4,24,128]{3,2,1,0:T(8,128)S(1)}, f32[3,4,24,128]{3,2,1,0:T(8,128)S(1)}, u32[]{:S(2)}, u32[]{:S(2)}) collective-permute-start(f32[3,4,24,128]{3,2,1,0:T(8,128)S(1)} %pad_maximum_fusion), channel_id=1, source_target_pairs={{0,24},{8,32},{16,40},{24,48},{32,56},{40,64},{48,72},{56,80},{64,... | collective-permute-start | bytes 442376 | tf_op jit(solution)/shard_map/ppermute | solution.py:364
  71.9 1.9 collective-permute-start.5
  73.9 2.1 collective-permute-done.4
  76.0 6.4 %collective-permute-done.5 = f32[3,4,24,128]{3,2,1,0:T(8,128)S(1)} collective-permute-done((f32[3,4,24,128]{3,2,1,0:T(8,128)S(1)}, f32[3,4,24,128]{3,2,1,0:T(8,128)S(1)}, u32[]{:S(2)}, u32[]{:S(2)}) %collective-permute-start.5) | collective-permute-done | bytes 147488 | tf_op jit(solution)/shard_map/ppermute | solution.py:364
  82.4 7.0 %coarse_kernel.2.own = f32[3,4,24,128]{3,2,1,0:T(8,128)S(1)} custom-call(s32[4]{0:T(128)S(1)} %pad_add_fusion.position, f32[9,4,24,128]{3,2,1,0:T(8,128)S(1)} %constant_dynamic-update-slice_fusion.blocks, f32[3,8,24,128]{3,2,1,0:T(8,128)S(1)} %get-tuple-element.30.v1), custom_call_target="tpu_custom_call" | custom-call | tf_op jit(solution)/shard_map/coarse_kernel/pallas_call | solution.py:349
  89.4 8.1 %collective-permute-start.7 = (f32[3,3,24,128]{3,2,1,0:T(8,128)S(1)}, f32[3,3,24,128]{3,2,1,0:T(8,128)S(1)}, u32[]{:S(2)}, u32[]{:S(2)}) collective-permute-start(f32[3,3,24,128]{3,2,1,0:T(8,128)S(1)} %get-tuple-element.49), channel_id=1, source_target_pairs={{8,0},{16,8},{24,16},{32,24},{40,32},{48,40},{56,48},{64,56},{72,6... | collective-permute-start | bytes 331784 | tf_op jit(solution)/shard_map/ppermute | solution.py:364
  97.5 1.9 collective-permute-start.6
  99.4 0.4 collective-permute-done.7.right
  99.8 3.8 %collective-permute-done.6.left = f32[3,3,24,128]{3,2,1,0:T(8,128)S(1)} collective-permute-done((f32[3,3,24,128]{3,2,1,0:T(8,128)S(1)}, f32[3,3,24,128]{3,2,1,0:T(8,128)S(1)}, u32[]{:S(2)}, u32[]{:S(2)}) %collective-permute-start.6) | collective-permute-done | bytes 110624 | tf_op jit(solution)/shard_map/ppermute | solution.py:364
  103.6 4.1 %first_up_kernel.1 = (f32[3,8,24,128]{3,2,1,0:T(8,128)S(1)}, f32[3,7,24,128]{3,2,1,0:T(8,128)S(1)}, f32[3,7,24,128]{3,2,1,0:T(8,128)S(1)}) custom-call(f32[3,4,24,128]{3,2,1,0:T(8,128)S(1)} %coarse_kernel.2.own, f32[3,3,24,128]{3,2,1,0:T(8,128)S(1)} %collective-permute-done.6.left, f32[3,3,24,128]{3,2,1,0:T(8,128)S(1)} %collective-permute-done.7.right, ...), custom_call_target="tpu_custom_call" | custom-call | tf_op jit(solution)/shard_map/first_up_kernel/pallas_call | solution.py:349
  107.7 1.9 collective-permute-start.8
  109.6 3.6 %collective-permute-start.9 = (f32[3,7,24,128]{3,2,1,0:T(8,128)S(1)}, f32[3,7,24,128]{3,2,1,0:T(8,128)S(1)}, u32[]{:S(2)}, u32[]{:S(2)}) collective-permute-start(f32[3,7,24,128]{3,2,1,0:T(8,128)S(1)} %get-tuple-element.38), channel_id=1, source_target_pairs={{8,0},{16,8},{24,16},{32,24},{40,32},{48,40},{56,48},{64,56},{72,6... | collective-permute-start | bytes 774152 | tf_op jit(solution)/shard_map/ppermute | solution.py:364
  113.3 2.1 %collective-permute-done.8.left = f32[3,7,24,128]{3,2,1,0:T(8,128)S(1)} collective-permute-done((f32[3,7,24,128]{3,2,1,0:T(8,128)S(1)}, f32[3,7,24,128]{3,2,1,0:T(8,128)S(1)}, u32[]{:S(2)}, u32[]{:S(2)}) %collective-permute-start.8) | collective-permute-done | bytes 258080 | tf_op jit(solution)/shard_map/ppermute | solution.py:364
  115.3 1.8 collective-permute-done.9.right
  117.1 0.2 side_kernel.1
  117.3 1.3 collective-permute-start.10
  118.6 4.6 %collective-permute-start.11 = (f32[3,11,24,128]{3,2,1,0:T(8,128)S(1)}, f32[3,11,24,128]{3,2,1,0:T(8,128)S(1)}, u32[]{:S(2)}, u32[]{:S(2)}) collective-permute-start(f32[3,11,24,128]{3,2,1,0:T(8,128)S(1)} %get-tuple-element.40), channel_id=1, source_target_pairs={{0,1},{1,2},{2,3},{3,4},{4,5},{5,6},{6,7},{8,9},{9,10},{10,11},{11... | collective-permute-start | bytes 1216520 | tf_op jit(solution)/shard_map/ppermute | solution.py:364
  123.1 3.9 %collective-permute-done.10.after = f32[3,11,24,128]{3,2,1,0:T(8,128)S(1)} collective-permute-done((f32[3,11,24,128]{3,2,1,0:T(8,128)S(1)}, f32[3,11,24,128]{3,2,1,0:T(8,128)S(1)}, u32[]{:S(2)}, u32[]{:S(2)}) %collective-permute-start.10) | collective-permute-done | bytes 405536 | tf_op jit(solution)/shard_map/ppermute | solution.py:364
  127.1 1.5 collective-permute-done.11.before
  128.5 8.0 %second_down_kernel.1 = (f32[3,20,24,256]{3,2,1,0:T(8,128)S(1)}, f32[3,8,24,128]{3,2,1,0:T(8,128)S(1)}, f32[3,8,24,128]{3,2,1,0:T(8,128)S(1)}, f32[4,24,128]{2,1,0:T(8,128)S(1)}) custom-call(f32[3,8,24,128]{3,2,1,0:T(8,128)S(1)} %get-tuple-element.36.own, f32[3,7,24,128]{3,2,1,0:T(8,128)S(1)} %collective-permute-done.8.left, ...), custom_call_target="tpu_custom_call" | custom-call | tf_op jit(solution)/shard_map/second_down_kernel/pallas_call | solution.py:349
  136.5 4.0 %collective-permute-start.13 = (f32[4,24,128]{2,1,0:T(8,128)S(1)}, f32[4,24,128]{2,1,0:T(8,128)S(1)}, u32[]{:S(2)}, u32[]{:S(2)}) collective-permute-start(f32[4,24,128]{2,1,0:T(8,128)S(1)} %get-tuple-element.43), channel_id=1, source_target_pairs={{0,504},{8,0},{16,8},{24,16},{32,24},{40,32},{48,40},{56,48},{64,5... | collective-permute-start | bytes 147464 | tf_op jit(solution)/shard_map/ppermute | solution.py:364
  140.5 5.1 %collective-permute-start.12 = (f32[4,24,128]{2,1,0:T(8,128)S(1)}, f32[4,24,128]{2,1,0:T(8,128)S(1)}, u32[]{:S(2)}, u32[]{:S(2)}) collective-permute-start(f32[4,24,128]{2,1,0:T(8,128)S(1)} %get-tuple-element.43), channel_id=1, source_target_pairs={{0,8},{8,16},{16,24},{24,32},{32,40},{40,48},{48,56},{56,64},{64,7... | collective-permute-start | bytes 147464 | tf_op jit(solution)/shard_map/ppermute | solution.py:364
  145.7 0.0 collective-permute-done.13
  145.7 0.8 collective-permute-done.12
  146.5 6.8 %collective-permute-start.14 = (f32[3,4,24,128]{3,2,1,0:T(8,128)S(1)}, f32[3,4,24,128]{3,2,1,0:T(8,128)S(1)}, u32[]{:S(2)}, u32[]{:S(2)}) collective-permute-start(f32[3,4,24,128]{3,2,1,0:T(8,128)S(1)} %pad_maximum_fusion.1), channel_id=1, source_target_pairs={{0,24},{8,32},{16,40},{24,48},{32,56},{40,64},{48,72},{56,80},{64,... | collective-permute-start | bytes 442376 | tf_op jit(solution)/shard_map/ppermute | solution.py:364
  153.4 1.9 collective-permute-start.15
  155.3 2.1 collective-permute-done.14
  157.4 6.4 %collective-permute-done.15 = f32[3,4,24,128]{3,2,1,0:T(8,128)S(1)} collective-permute-done((f32[3,4,24,128]{3,2,1,0:T(8,128)S(1)}, f32[3,4,24,128]{3,2,1,0:T(8,128)S(1)}, u32[]{:S(2)}, u32[]{:S(2)}) %collective-permute-start.15) | collective-permute-done | bytes 147488 | tf_op jit(solution)/shard_map/ppermute | solution.py:364
  163.8 7.0 %coarse_kernel.3.own = f32[3,4,24,128]{3,2,1,0:T(8,128)S(1)} custom-call(s32[4]{0:T(128)S(1)} %pad_add_fusion.position, f32[9,4,24,128]{3,2,1,0:T(8,128)S(1)} %constant_dynamic-update-slice_fusion.5.blocks, f32[3,8,24,128]{3,2,1,0:T(8,128)S(1)} %get-tuple-element.44.v1), custom_call_target="tpu_custom_call" | custom-call | tf_op jit(solution)/shard_map/coarse_kernel/pallas_call | solution.py:349
  170.8 8.1 %collective-permute-start.17 = (f32[3,3,24,128]{3,2,1,0:T(8,128)S(1)}, f32[3,3,24,128]{3,2,1,0:T(8,128)S(1)}, u32[]{:S(2)}, u32[]{:S(2)}) collective-permute-start(f32[3,3,24,128]{3,2,1,0:T(8,128)S(1)} %get-tuple-element.47), channel_id=1, source_target_pairs={{8,0},{16,8},{24,16},{32,24},{40,32},{48,40},{56,48},{64,56},{72,6... | collective-permute-start | bytes 331784 | tf_op jit(solution)/shard_map/ppermute | solution.py:364
  178.9 1.9 collective-permute-start.16
  180.9 0.4 collective-permute-done.17.right
  181.2 3.8 %collective-permute-done.16.left = f32[3,3,24,128]{3,2,1,0:T(8,128)S(1)} collective-permute-done((f32[3,3,24,128]{3,2,1,0:T(8,128)S(1)}, f32[3,3,24,128]{3,2,1,0:T(8,128)S(1)}, u32[]{:S(2)}, u32[]{:S(2)}) %collective-permute-start.16) | collective-permute-done | bytes 110624 | tf_op jit(solution)/shard_map/ppermute | solution.py:364
  185.0 4.1 %last_up_kernel.1 = f32[8,9,8,128]{3,2,1,0:T(8,128)S(1)} custom-call(f32[3,4,24,128]{3,2,1,0:T(8,128)S(1)} %coarse_kernel.3.own, f32[3,3,24,128]{3,2,1,0:T(8,128)S(1)} %collective-permute-done.16.left, f32[3,3,24,128]{3,2,1,0:T(8,128)S(1)} %collective-permute-done.17.right, f32[3,20,24,256]{3,2,1,0:T(8,128)S(1)} %get-tuple-element.31.g0, ...), custom_call_target="tpu_custom_call" | custom-call | tf_op jit(solution)/shard_map/last_up_kernel/pallas_call | solution.py:349
  189.1 16.2 %all_to_all.11.taken = f32[8,9,8,128]{3,2,1,0:T(8,128)S(1)} all-to-all(f32[8,9,8,128]{3,2,1,0:T(8,128)S(1)} %last_up_kernel.1), channel_id=1, replica_groups=mesh['gx'=64,'gz'=8] {'gz'}, dimensions={0} | all-to-all | bytes 589824 | tf_op jit(solution)/shard_map/all_to_all | solution.py:450
  205.3 0.7 join_kernel.1
  (14 shorter events, 0.1 us)
Async XLA Ops:
  0.0 1.0 copy-start
  1.0 0.9 copy-start.1
  32.2 11.2 %collective-permute-start = (f32[4,6,24,256]{3,2,1,0:T(8,128)S(1)}, f32[4,6,24,256]{3,2,1,0:T(8,128)S(1)}, u32[]{:S(2)}, u32[]{:S(2)}) collective-permute-start(f32[4,6,24,256]{3,2,1,0:T(8,128)S(1)} %get-tuple-element.27), channel_id=1, source_target_pairs={{0,8},{8,16},{16,24},{24,32},{32,40},{40,48},{48,56},{56,64},{64,7... | collective-permute-start | bytes 1769480 | tf_op jit(solution)/shard_map/ppermute | solution.py:364
  34.1 11.0 %collective-permute-start.1 = (f32[4,6,24,256]{3,2,1,0:T(8,128)S(1)}, f32[4,6,24,256]{3,2,1,0:T(8,128)S(1)}, u32[]{:S(2)}, u32[]{:S(2)}) collective-permute-start(f32[4,6,24,256]{3,2,1,0:T(8,128)S(1)} %get-tuple-element.28), channel_id=1, source_target_pairs={{8,0},{16,8},{24,16},{32,24},{40,32},{48,40},{56,48},{64,56},{72,6... | collective-permute-start | bytes 1769480 | tf_op jit(solution)/shard_map/ppermute | solution.py:364
  53.3 10.9 %collective-permute-start.3 = (f32[4,24,128]{2,1,0:T(8,128)S(1)}, f32[4,24,128]{2,1,0:T(8,128)S(1)}, u32[]{:S(2)}, u32[]{:S(2)}) collective-permute-start(f32[4,24,128]{2,1,0:T(8,128)S(1)} %get-tuple-element.29), channel_id=1, source_target_pairs={{0,504},{8,0},{16,8},{24,16},{32,24},{40,32},{48,40},{56,48},{64,5... | collective-permute-start | bytes 147464 | tf_op jit(solution)/shard_map/ppermute | solution.py:364
  57.1 8.0 %collective-permute-start.2 = (f32[4,24,128]{2,1,0:T(8,128)S(1)}, f32[4,24,128]{2,1,0:T(8,128)S(1)}, u32[]{:S(2)}, u32[]{:S(2)}) collective-permute-start(f32[4,24,128]{2,1,0:T(8,128)S(1)} %get-tuple-element.29), channel_id=1, source_target_pairs={{0,8},{8,16},{16,24},{24,32},{32,40},{40,48},{48,56},{56,64},{64,7... | collective-permute-start | bytes 147464 | tf_op jit(solution)/shard_map/ppermute | solution.py:364
  65.1 10.8 %collective-permute-start.4 = (f32[3,4,24,128]{3,2,1,0:T(8,128)S(1)}, f32[3,4,24,128]{3,2,1,0:T(8,128)S(1)}, u32[]{:S(2)}, u32[]{:S(2)}) collective-permute-start(f32[3,4,24,128]{3,2,1,0:T(8,128)S(1)} %pad_maximum_fusion), channel_id=1, source_target_pairs={{0,24},{8,32},{16,40},{24,48},{32,56},{40,64},{48,72},{56,80},{64,... | collective-permute-start | bytes 442376 | tf_op jit(solution)/shard_map/ppermute | solution.py:364
  71.9 10.4 %collective-permute-start.5 = (f32[3,4,24,128]{3,2,1,0:T(8,128)S(1)}, f32[3,4,24,128]{3,2,1,0:T(8,128)S(1)}, u32[]{:S(2)}, u32[]{:S(2)}) collective-permute-start(f32[3,4,24,128]{3,2,1,0:T(8,128)S(1)} %pad_maximum_fusion), channel_id=1, source_target_pairs={{0,488},{8,496},{16,504},{24,0},{32,8},{40,16},{48,24},{56,32},{64... | collective-permute-start | bytes 442376 | tf_op jit(solution)/shard_map/ppermute | solution.py:364
  89.4 10.4 %collective-permute-start.7 = (f32[3,3,24,128]{3,2,1,0:T(8,128)S(1)}, f32[3,3,24,128]{3,2,1,0:T(8,128)S(1)}, u32[]{:S(2)}, u32[]{:S(2)}) collective-permute-start(f32[3,3,24,128]{3,2,1,0:T(8,128)S(1)} %get-tuple-element.49), channel_id=1, source_target_pairs={{8,0},{16,8},{24,16},{32,24},{40,32},{48,40},{56,48},{64,56},{72,6... | collective-permute-start | bytes 331784 | tf_op jit(solution)/shard_map/ppermute | solution.py:364
  97.5 6.1 %collective-permute-start.6 = (f32[3,3,24,128]{3,2,1,0:T(8,128)S(1)}, f32[3,3,24,128]{3,2,1,0:T(8,128)S(1)}, u32[]{:S(2)}, u32[]{:S(2)}) collective-permute-start(f32[3,3,24,128]{3,2,1,0:T(8,128)S(1)} %get-tuple-element.50), channel_id=1, source_target_pairs={{0,8},{8,16},{16,24},{24,32},{32,40},{40,48},{48,56},{56,64},{64,7... | collective-permute-start | bytes 331784 | tf_op jit(solution)/shard_map/ppermute | solution.py:364
  107.7 7.6 %collective-permute-start.8 = (f32[3,7,24,128]{3,2,1,0:T(8,128)S(1)}, f32[3,7,24,128]{3,2,1,0:T(8,128)S(1)}, u32[]{:S(2)}, u32[]{:S(2)}) collective-permute-start(f32[3,7,24,128]{3,2,1,0:T(8,128)S(1)} %get-tuple-element.37), channel_id=1, source_target_pairs={{0,8},{8,16},{16,24},{24,32},{32,40},{40,48},{48,56},{56,64},{64,7... | collective-permute-start | bytes 774152 | tf_op jit(solution)/shard_map/ppermute | solution.py:364
  109.6 7.5 %collective-permute-start.9 = (f32[3,7,24,128]{3,2,1,0:T(8,128)S(1)}, f32[3,7,24,128]{3,2,1,0:T(8,128)S(1)}, u32[]{:S(2)}, u32[]{:S(2)}) collective-permute-start(f32[3,7,24,128]{3,2,1,0:T(8,128)S(1)} %get-tuple-element.38), channel_id=1, source_target_pairs={{8,0},{16,8},{24,16},{32,24},{40,32},{48,40},{56,48},{64,56},{72,6... | collective-permute-start | bytes 774152 | tf_op jit(solution)/shard_map/ppermute | solution.py:364
  117.3 9.8 %collective-permute-start.10 = (f32[3,11,24,128]{3,2,1,0:T(8,128)S(1)}, f32[3,11,24,128]{3,2,1,0:T(8,128)S(1)}, u32[]{:S(2)}, u32[]{:S(2)}) collective-permute-start(f32[3,11,24,128]{3,2,1,0:T(8,128)S(1)} %get-tuple-element.39), channel_id=1, source_target_pairs={{1,0},{2,1},{3,2},{4,3},{5,4},{6,5},{7,6},{9,8},{10,9},{11,10},{12... | collective-permute-start | bytes 1216520 | tf_op jit(solution)/shard_map/ppermute | solution.py:364
  118.6 10.0 %collective-permute-start.11 = (f32[3,11,24,128]{3,2,1,0:T(8,128)S(1)}, f32[3,11,24,128]{3,2,1,0:T(8,128)S(1)}, u32[]{:S(2)}, u32[]{:S(2)}) collective-permute-start(f32[3,11,24,128]{3,2,1,0:T(8,128)S(1)} %get-tuple-element.40), channel_id=1, source_target_pairs={{0,1},{1,2},{2,3},{3,4},{4,5},{5,6},{6,7},{8,9},{9,10},{10,11},{11... | collective-permute-start | bytes 1216520 | tf_op jit(solution)/shard_map/ppermute | solution.py:364
  136.5 9.1 %collective-permute-start.13 = (f32[4,24,128]{2,1,0:T(8,128)S(1)}, f32[4,24,128]{2,1,0:T(8,128)S(1)}, u32[]{:S(2)}, u32[]{:S(2)}) collective-permute-start(f32[4,24,128]{2,1,0:T(8,128)S(1)} %get-tuple-element.43), channel_id=1, source_target_pairs={{0,504},{8,0},{16,8},{24,16},{32,24},{40,32},{48,40},{56,48},{64,5... | collective-permute-start | bytes 147464 | tf_op jit(solution)/shard_map/ppermute | solution.py:364
  140.5 6.0 %collective-permute-start.12 = (f32[4,24,128]{2,1,0:T(8,128)S(1)}, f32[4,24,128]{2,1,0:T(8,128)S(1)}, u32[]{:S(2)}, u32[]{:S(2)}) collective-permute-start(f32[4,24,128]{2,1,0:T(8,128)S(1)} %get-tuple-element.43), channel_id=1, source_target_pairs={{0,8},{8,16},{16,24},{24,32},{32,40},{40,48},{48,56},{56,64},{64,7... | collective-permute-start | bytes 147464 | tf_op jit(solution)/shard_map/ppermute | solution.py:364
  146.5 10.8 %collective-permute-start.14 = (f32[3,4,24,128]{3,2,1,0:T(8,128)S(1)}, f32[3,4,24,128]{3,2,1,0:T(8,128)S(1)}, u32[]{:S(2)}, u32[]{:S(2)}) collective-permute-start(f32[3,4,24,128]{3,2,1,0:T(8,128)S(1)} %pad_maximum_fusion.1), channel_id=1, source_target_pairs={{0,24},{8,32},{16,40},{24,48},{32,56},{40,64},{48,72},{56,80},{64,... | collective-permute-start | bytes 442376 | tf_op jit(solution)/shard_map/ppermute | solution.py:364
  153.4 10.4 %collective-permute-start.15 = (f32[3,4,24,128]{3,2,1,0:T(8,128)S(1)}, f32[3,4,24,128]{3,2,1,0:T(8,128)S(1)}, u32[]{:S(2)}, u32[]{:S(2)}) collective-permute-start(f32[3,4,24,128]{3,2,1,0:T(8,128)S(1)} %pad_maximum_fusion.1), channel_id=1, source_target_pairs={{0,488},{8,496},{16,504},{24,0},{32,8},{40,16},{48,24},{56,32},{64... | collective-permute-start | bytes 442376 | tf_op jit(solution)/shard_map/ppermute | solution.py:364
  170.8 10.4 %collective-permute-start.17 = (f32[3,3,24,128]{3,2,1,0:T(8,128)S(1)}, f32[3,3,24,128]{3,2,1,0:T(8,128)S(1)}, u32[]{:S(2)}, u32[]{:S(2)}) collective-permute-start(f32[3,3,24,128]{3,2,1,0:T(8,128)S(1)} %get-tuple-element.47), channel_id=1, source_target_pairs={{8,0},{16,8},{24,16},{32,24},{40,32},{48,40},{56,48},{64,56},{72,6... | collective-permute-start | bytes 331784 | tf_op jit(solution)/shard_map/ppermute | solution.py:364
  178.9 6.1 %collective-permute-start.16 = (f32[3,3,24,128]{3,2,1,0:T(8,128)S(1)}, f32[3,3,24,128]{3,2,1,0:T(8,128)S(1)}, u32[]{:S(2)}, u32[]{:S(2)}) collective-permute-start(f32[3,3,24,128]{3,2,1,0:T(8,128)S(1)} %get-tuple-element.48), channel_id=1, source_target_pairs={{0,8},{8,16},{16,24},{24,32},{32,40},{40,48},{48,56},{56,64},{64,7... | collective-permute-start | bytes 331784 | tf_op jit(solution)/shard_map/ppermute | solution.py:364

commit v2 on v1

--- a/solution.py
+++ b/solution.py
@@ -12,6 +12,7 @@
 NZ = 24
 HALO = 6
 LANES = 128
+UNROLL = (2, 4, 8, 8)
 PARAMS = pltpu.CompilerParams(vmem_limit_bytes=28 << 20)
 
 
@@ -57,12 +58,19 @@
     return mid, coupling_of(level) * lateral + depth_coupling * vertical
 
 
-def each_row(low, high, body):
+def each_row(low, high, body, unroll):
+    steps = (high - low) // unroll
+
     def step(n, carry):
-        body(Row(n, low))
+        for k in range(unroll):
+            body(Row(unroll * n, low + k))
         return carry
 
-    lax.fori_loop(0, high - low, step, 0)
+    if steps > 1:
+        lax.fori_loop(0, steps, step, 0)
+        low += steps * unroll
+    for r in range(low, high):
+        body(Row(0, r))
 
 
 def sweep(target, field, source, factor, level, low, high):
@@ -72,16 +80,7 @@
             mid, around = neighbours(field, c, r, level)
             target[0][c, index(target, r)] = (1.0 - relaxation) * mid + f * (row(source, c, r) + around)
 
-    each_row(low, high, body)
-
-
-def first_sweep(target, source, factor, low, high):
-    def body(r):
-        f = shared(factor, r)
-        for c in range(C):
-            target[0][c, index(target, r)] = f * row(source, c, r)
-
-    each_row(low, high, body)
+    each_row(low, high, body, UNROLL[level])
 
 
 def lane_index():
@@ -118,33 +117,47 @@
                 total = residual if total is None else total + residual
             target[0][c, index(target, q)] = 0.25 * pair_sum(total, period)
 
-    each_row(low, high, body)
-
-
-def coarse_density(target, density, period, low, high):
-    def body(q):
-        total = shared(density, q.double()) + shared(density, q.double() + 1)
-        target[0][index(target, q)] = 0.25 * pair_sum(total, period)
-
-    each_row(low, high, body)
-
-
-def factors(target, density, level, period, rows, position, low, high):
+    each_row(low, high, body, max(1, UNROLL[level] // 2))
+
+
+def from_zero(target, source, density, factor, level, period, rows, position, low, high, finer=None, reach=0):
     i, j, count_x, count_y = position[0], position[1], position[2], position[3]
-    width = target[0].shape[-1]
+    width = factor[0].shape[-1]
     lane = lax.broadcasted_iota(jnp.int32, (NZ, width), 1) % period
     inside_y = ((lane < 3 * period // 4) | (j > 0)) & ((lane < period // 2) | (lane >= 3 * period // 4) | (j < count_y - 1))
 
     def body(r):
+        if finer is None:
+            own = shared(density, r)
+        else:
+            own = 0.25 * pair_sum(shared(finer, r.double()) + shared(finer, r.double() + 1), 2 * period)
+            density[0][index(density, r)] = own
         at = i * rows + r.base
         inside = inside_y & ((at >= -r.shift) & (at < count_x * rows - r.shift))
-        target[0][index(target, r)] = jnp.where(inside, relaxation / (shared(density, r) + base_of(level)), 0.0)
-
-    each_row(low, high, body)
+        f = jnp.where(inside, relaxation / (own + base_of(level)), 0.0)
+        factor[0][index(factor, r)] = f
+        return f
+
+    def whole(r):
+        f = body(r)
+        for c in range(C):
+            target[0][c, index(target, r)] = f * row(source, c, r)
+
+    for r in [*range(low - reach, low), *range(high, high + reach)]:
+        body(Row(0, r))
+    each_row(low, high, whole, UNROLL[level])
+
+
+def first_sweep(target, source, factor, level, low, high):
+    def body(r):
+        f = shared(factor, r)
+        for c in range(C):
+            target[0][c, index(target, r)] = f * row(source, c, r)
+
+    each_row(low, high, body, UNROLL[level])
 
 
 def level_one_down(g1, v1, scratch, d1, f1, packed):
-    first_sweep(scratch, g1, f1, -2, 6)
     sweep(v1, scratch, g1, f1, 1, -1, 5)
     lane = lane_index()
     for c in range(C + 1):
@@ -206,12 +219,10 @@
                 else:
                     d0[at + r] = piece[c, r]
     g, d, f, a, b = (g0, -HALO), (d0, -HALO), (f0, -HALO), (field, -HALO), (v0, -HALO)
-    factors(f, d, 0, 2 * LANES, rows, position, -HALO, rows + HALO)
-    coarse_density((d1, -3), d, 2 * LANES, -3, rows // 2 + 3)
-    factors((f1, -3), (d1, -3), 1, LANES, rows // 2, position, -3, rows // 2 + 3)
-    first_sweep(a, g, f, -6, rows + 6)
+    from_zero(a, g, d, f, 0, 2 * LANES, rows, position, -HALO, rows + HALO)
     sweep(b, a, g, f, 0, -5, rows + 5)
     coarse_source((g1, -2), b, g, d, 0, 2 * LANES, -2, rows // 2 + 2)
+    from_zero((field1, -2), (g1, -2), (d1, -3), (f1, -3), 1, LANES, rows // 2, position, -2, rows // 2 + 2, d, 1)
     level_one_down((g1, -2), (v1, -2), (field1, -2), (d1, -3), (f1, -3), packed)
 
 
@@ -248,31 +259,37 @@
     sweep(a, (wide, -halo), g, f, 0, -6, rows + 6)
     sweep(b, a, g, f, 0, -5, rows + 5)
     coarse_source((g1, -2), b, g, d, 0, 2 * LANES, -2, rows // 2 + 2)
+    first_sweep((field1, -2), (g1, -2), (f1, -3), 1, -2, rows // 2 + 2)
     level_one_down((g1, -2), (v1, -2), (field1, -2), (d1, -3), (f1, -3), packed)
 
 
-def coarse_kernel(position, blocks, v1, out, g2, d2, f2, g3, d3, f3, a, b, a3, b3):
-    lane = lane_index()
-    count = blocks.shape[0]
+def coarse_kernel(position, left, near, right, end, v1, out, g2, d2, f2, g3, d3, f3, a, b, a3, b3):
+    lane = lane_index()
+    side = near.shape[0]
+    count = 3 * side
     reach = count // 2 * 2
-    for n in range(count):
+
+    def place(n, block):
         for c in range(C + 1):
-            both = blocks[n, c]
+            both = block[c]
             other = pltpu.roll(both, LANES // 2, 1)
             for q, value in ((0, jnp.where(lane < LANES // 2, both, other)), (1, jnp.where(lane < LANES // 2, other, both))):
                 if c < C:
                     g2[c, 2 * n + q] = value
                 else:
                     d2[2 * n + q] = value
+
+    for at, blocks in ((0, left), (side, near), (2 * side, right)):
+        for n in range(side):
+            place(at + n, blocks.at[n])
+    pl.when(position[0] == side - 1)(lambda: place(count // 2 - side + 1, end))
+    pl.when(position[0] == position[2] - side)(lambda: place(count // 2 + side - 1, end))
     g, d, f, u, w = (g2, -reach), (d2, -reach), (f2, -reach), (a, -reach), (b, -reach)
     h, e, k, s, t = (g3, -reach // 2), (d3, -reach // 2), (f3, -reach // 2), (a3, -reach // 2), (b3, -reach // 2)
-    factors(f, d, 2, LANES // 2, 2, position, -8, 10)
-    coarse_density(e, d, LANES // 2, -3, 4)
-    factors(k, e, 3, LANES // 4, 1, position, -3, 4)
-    first_sweep(u, g, f, -8, 10)
+    from_zero(u, g, d, f, 2, LANES // 2, 2, position, -8, 10)
     sweep(w, u, g, f, 2, -7, 9)
     coarse_source(h, w, g, d, 2, LANES // 2, -3, 4)
-    first_sweep(s, h, k, -3, 4)
+    from_zero(s, h, e, k, 3, LANES // 4, 1, position, -3, 4, d)
     sweep(t, s, h, k, 3, -2, 3)
     sweep(s, t, h, k, 3, -1, 2)
 
@@ -282,7 +299,7 @@
             for r in (q.double(), q.double() + 1):
                 b[c, index(w, r)] = row(w, c, r) + fine
 
-    each_row(-1, 2, correct)
+    each_row(-1, 2, correct, 3)
     sweep(u, w, g, f, 2, -1, 3)
     sweep(w, u, g, f, 2, 0, 2)
     for c in range(C):
@@ -307,7 +324,7 @@
             for r in (q.double(), q.double() + 1):
                 field[c, index((field, -HALO), r)] = row((v0, -HALO), c, r) + fine
 
-    each_row(-1, rows1 + 1, correct)
+    each_row(-1, rows1 + 1, correct, 2)
     rows = 2 * rows1
     sweep((emit, -HALO), (field, -HALO), (g0, -HALO), (f0, -HALO), 0, -1, rows + 1)
     sweep((field, -HALO), (emit, -HALO), (g0, -HALO), (f0, -HALO), 0, 0, rows)
@@ -358,9 +375,9 @@
     return out
 
 
-def onward(values, axis, distance, closed=False):
+def onward(values, axis, distance):
     count = lax.axis_size(axis)
-    pairs = [(i, (i + distance) % count) for i in range(count) if closed or 0 <= i + distance < count]
+    pairs = [(i, i + distance) for i in range(count) if 0 <= i + distance < count]
     return lax.ppermute(values, axis, pairs)
 
 
@@ -391,15 +408,19 @@
     )
 
     def coarse(packed, v1):
-        near = jnp.stack([onward(packed, "gx", 1, True), packed, onward(packed, "gx", -1, True)])
-        nine = jnp.concatenate([onward(near, "gx", 3, True), near, onward(near, "gx", -3, True)])
+        near = jnp.stack([onward(packed, "gx", 1), packed, onward(packed, "gx", -1)])
+        last = lax.axis_size("gx") - 1
+        end = lax.ppermute(packed, "gx", [(0, 2), (last, last - 2)])
         two, three = (C, 18, NZ, LANES), (C, 9, NZ, LANES)
         (out,) = call(
             coarse_kernel,
             [(C, R1, NZ, LANES)],
             [two, two[1:], two[1:], three, three[1:], three[1:], two, two, three, three],
             position,
-            nine,
+            onward(near, "gx", 3),
+            near,
+            onward(near, "gx", -3),
+            end,
             v1,
             scalars=1,
         )

time: 207 us -> 195 us (0.942)
  the two profiles are of different devices: /device:TPU:198 before, /device:TPU:256 now
where the time goes in v2:
time: 195 us; the launch traced here: 194 us
  starting transfers between devices  61.7 us (32%)
  waiting for transfers between devices  55.5 us (28%)
  blocking collectives  46.2 us (24%)
  Pallas kernels  28.1 us (14%)
    ppermute x18, starting transfers between devices, onward(): return lax.ppermute(values, axis, pairs)  60.4 us
    ppermute x18, waiting for transfers between devices, onward(): return lax.ppermute(values, axis, pairs)  55.5 us
    all_to_all x1, blocking collectives, shards(): taken = lax.all_to_all(sent, 'gz', 0, 0)  30 us
    pallas_call x10, Pallas kernels, call(): pl.pallas_call(kernel, out_shape=[shape(s) for s in outs], in_specs=specs...  28.1 us
    all_to_all x1, blocking collectives, shards(): lax.all_to_all(sent, 'gz', 0, 0)  16.2 us
  transfers between devices with their start and end apart: 20, of which 14 were waited for; matrix products, arithmetic and copies ran while one was open for 0% of the time, Pallas kernels for 0%

profile of v2, /device:TPU:256, one launch (start us, length us, event | category | flops | bytes accessed | tf_op | source)
XLA Modules:
  0.0 193.8 jit_solution(6073324513598449955)
XLA Ops:
  0.0 0.0 copy-start
  0.0 1.0 copy-done
  1.0 0.0 copy-start.1
  1.0 0.9 copy-done.1
  1.9 0.1 pack_kernel.1
  1.9 30.0 %all_to_all.10.taken = f32[8,12,8,256]{3,2,1,0:T(8,128)S(1)} all-to-all(f32[8,12,8,256]{3,2,1,0:T(8,128)S(1)} %pack_kernel.1), channel_id=1, replica_groups=mesh['gx'=64,'gz'=8] {'gz'}, dimensions={0} | all-to-all | bytes 1572864 | tf_op jit(solution)/shard_map/all_to_all | solution.py:391
  31.9 0.2 unpack_kernel.1
  32.2 1.9 collective-permute-start
  34.1 7.0 %collective-permute-start.1 = (f32[4,6,24,256]{3,2,1,0:T(8,128)S(1)}, f32[4,6,24,256]{3,2,1,0:T(8,128)S(1)}, u32[]{:S(2)}, u32[]{:S(2)}) collective-permute-start(f32[4,6,24,256]{3,2,1,0:T(8,128)S(1)} %get-tuple-element.28), channel_id=1, source_target_pairs={{8,0},{16,8},{24,16},{32,24},{40,32},{48,40},{56,48},{64,56},{72,6... | collective-permute-start | bytes 1769480 | tf_op jit(solution)/shard_map/ppermute | solution.py:381
  41.1 0.1 pad_add_fusion.position
  41.1 5.5 %collective-permute-done.left = f32[4,6,24,256]{3,2,1,0:T(8,128)S(1)} collective-permute-done((f32[4,6,24,256]{3,2,1,0:T(8,128)S(1)}, f32[4,6,24,256]{3,2,1,0:T(8,128)S(1)}, u32[]{:S(2)}, u32[]{:S(2)}) %collective-permute-start) | collective-permute-done | bytes 589856 | tf_op jit(solution)/shard_map/ppermute | solution.py:381
  46.7 1.8 collective-permute-done.1.right
  48.4 5.9 %first_down_kernel.1 = (f32[3,20,24,256]{3,2,1,0:T(8,128)S(1)}, f32[20,24,256]{2,1,0:T(8,128)S(1)}, f32[20,24,256]{2,1,0:T(8,128)S(1)}, f32[3,20,24,256]{3,2,1,0...) custom-call(s32[4]{0:T(128)S(1)} %pad_add_fusion.position, ...), custom_call_target="tpu_custom_call" | custom-call | tf_op jit(solution)/shard_map/first_down_kernel/pallas_call | solution.py:366
  54.3 7.1 %collective-permute-start.3 = (f32[4,24,128]{2,1,0:T(8,128)S(1)}, f32[4,24,128]{2,1,0:T(8,128)S(1)}, u32[]{:S(2)}, u32[]{:S(2)}) collective-permute-start(f32[4,24,128]{2,1,0:T(8,128)S(1)} %get-tuple-element.29), channel_id=1, source_target_pairs={{8,0},{16,8},{24,16},{32,24},{40,32},{48,40},{56,48},{64,56},{72,6... | collective-permute-start | bytes 147464 | tf_op jit(solution)/shard_map/ppermute | solution.py:381
  61.4 1.9 collective-permute-start.2
  63.4 0.0 collective-permute-done.3
  63.4 6.8 %collective-permute-done.2 = f32[4,24,128]{2,1,0:T(8,128)S(1)} collective-permute-done((f32[4,24,128]{2,1,0:T(8,128)S(1)}, f32[4,24,128]{2,1,0:T(8,128)S(1)}, u32[]{:S(2)}, u32[]{:S(2)}) %collective-permute-start.2) | collective-permute-done | bytes 49184 | tf_op jit(solution)/shard_map/ppermute | solution.py:381
  70.2 1.9 collective-permute-start.5
  72.1 3.6 %collective-permute-start.4 = (f32[3,4,24,128]{3,2,1,0:T(8,128)S(1)}, f32[3,4,24,128]{3,2,1,0:T(8,128)S(1)}, u32[]{:S(2)}, u32[]{:S(2)}) collective-permute-start(f32[3,4,24,128]{3,2,1,0:T(8,128)S(1)} %pad_maximum_fusion.near), channel_id=1, source_target_pairs={{0,24},{8,32},{16,40},{24,48},{32,56},{40,64},{48,72},{56,80},{64,... | collective-permute-start | bytes 442376 | tf_op jit(solution)/shard_map/ppermute | solution.py:381
  75.8 0.7 collective-permute-start.6
  76.4 0.0 collective-permute-done.6.end
  76.5 0.2 collective-permute-done.5.right
  76.7 5.5 %collective-permute-done.4.left = f32[3,4,24,128]{3,2,1,0:T(8,128)S(1)} collective-permute-done((f32[3,4,24,128]{3,2,1,0:T(8,128)S(1)}, f32[3,4,24,128]{3,2,1,0:T(8,128)S(1)}, u32[]{:S(2)}, u32[]{:S(2)}) %collective-permute-start.4) | collective-permute-done | bytes 147488 | tf_op jit(solution)/shard_map/ppermute | solution.py:381
  82.2 4.9 %coarse_kernel.2.own = f32[3,4,24,128]{3,2,1,0:T(8,128)S(1)} custom-call(s32[4]{0:T(128)S(1)} %pad_add_fusion.position, f32[3,4,24,128]{3,2,1,0:T(8,128)S(1)} %collective-permute-done.4.left, f32[3,4,24,128]{3,2,1,0:T(8,128)S(1)} %pad_maximum_fusion.near, f32[3,4,24,128]{3,2,1,0:T(8,128)S(1)} %collective-permute-done.5.right, ...), custom_call_target="tpu_custom_call" | custom-call | tf_op jit(solution)/shard_map/coarse_kernel/pallas_call | solution.py:366
  87.2 1.9 collective-permute-start.8
  89.1 2.4 %collective-permute-start.7 = (f32[3,3,24,128]{3,2,1,0:T(8,128)S(1)}, f32[3,3,24,128]{3,2,1,0:T(8,128)S(1)}, u32[]{:S(2)}, u32[]{:S(2)}) collective-permute-start(f32[3,3,24,128]{3,2,1,0:T(8,128)S(1)} %get-tuple-element.50), channel_id=1, source_target_pairs={{0,8},{8,16},{16,24},{24,32},{32,40},{40,48},{48,56},{56,64},{64,7... | collective-permute-start | bytes 331784 | tf_op jit(solution)/shard_map/ppermute | solution.py:381
  91.5 0.0 collective-permute-done.8.right
  91.5 7.0 %collective-permute-done.7.left = f32[3,3,24,128]{3,2,1,0:T(8,128)S(1)} collective-permute-done((f32[3,3,24,128]{3,2,1,0:T(8,128)S(1)}, f32[3,3,24,128]{3,2,1,0:T(8,128)S(1)}, u32[]{:S(2)}, u32[]{:S(2)}) %collective-permute-start.7) | collective-permute-done | bytes 110624 | tf_op jit(solution)/shard_map/ppermute | solution.py:381
  98.5 2.5 %first_up_kernel.1 = (f32[3,8,24,128]{3,2,1,0:T(8,128)S(1)}, f32[3,7,24,128]{3,2,1,0:T(8,128)S(1)}, f32[3,7,24,128]{3,2,1,0:T(8,128)S(1)}) custom-call(f32[3,4,24,128]{3,2,1,0:T(8,128)S(1)} %coarse_kernel.2.own, f32[3,3,24,128]{3,2,1,0:T(8,128)S(1)} %collective-permute-done.7.left, f32[3,3,24,128]{3,2,1,0:T(8,128)S(1)} %collective-permute-done.8.right, ...), custom_call_target="tpu_custom_call" | custom-call | tf_op jit(solution)/shard_map/first_up_kernel/pallas_call | solution.py:366
  100.9 1.9 collective-permute-start.9
  102.9 7.0 %collective-permute-start.10 = (f32[3,7,24,128]{3,2,1,0:T(8,128)S(1)}, f32[3,7,24,128]{3,2,1,0:T(8,128)S(1)}, u32[]{:S(2)}, u32[]{:S(2)}) collective-permute-start(f32[3,7,24,128]{3,2,1,0:T(8,128)S(1)} %get-tuple-element.38), channel_id=1, source_target_pairs={{8,0},{16,8},{24,16},{32,24},{40,32},{48,40},{56,48},{64,56},{72,6... | collective-permute-start | bytes 774152 | tf_op jit(solution)/shard_map/ppermute | solution.py:381
  109.8 2.1 %collective-permute-done.9.left = f32[3,7,24,128]{3,2,1,0:T(8,128)S(1)} collective-permute-done((f32[3,7,24,128]{3,2,1,0:T(8,128)S(1)}, f32[3,7,24,128]{3,2,1,0:T(8,128)S(1)}, u32[]{:S(2)}, u32[]{:S(2)}) %collective-permute-start.9) | collective-permute-done | bytes 258080 | tf_op jit(solution)/shard_map/ppermute | solution.py:381
  111.9 1.8 collective-permute-done.10.right
  113.7 0.2 side_kernel.1
  113.8 1.3 collective-permute-start.11
  115.1 4.6 %collective-permute-start.12 = (f32[3,11,24,128]{3,2,1,0:T(8,128)S(1)}, f32[3,11,24,128]{3,2,1,0:T(8,128)S(1)}, u32[]{:S(2)}, u32[]{:S(2)}) collective-permute-start(f32[3,11,24,128]{3,2,1,0:T(8,128)S(1)} %get-tuple-element.40), channel_id=1, source_target_pairs={{0,1},{1,2},{2,3},{3,4},{4,5},{5,6},{6,7},{8,9},{9,10},{10,11},{11... | collective-permute-start | bytes 1216520 | tf_op jit(solution)/shard_map/ppermute | solution.py:381
  119.7 3.9 %collective-permute-done.11.after = f32[3,11,24,128]{3,2,1,0:T(8,128)S(1)} collective-permute-done((f32[3,11,24,128]{3,2,1,0:T(8,128)S(1)}, f32[3,11,24,128]{3,2,1,0:T(8,128)S(1)}, u32[]{:S(2)}, u32[]{:S(2)}) %collective-permute-start.11) | collective-permute-done | bytes 405536 | tf_op jit(solution)/shard_map/ppermute | solution.py:381
  123.6 1.5 collective-permute-done.12.before
  125.1 6.3 %second_down_kernel.1 = (f32[3,20,24,256]{3,2,1,0:T(8,128)S(1)}, f32[3,8,24,128]{3,2,1,0:T(8,128)S(1)}, f32[3,8,24,128]{3,2,1,0:T(8,128)S(1)}, f32[4,24,128]{2,1,0:T(8,128)S(1)}) custom-call(f32[3,8,24,128]{3,2,1,0:T(8,128)S(1)} %get-tuple-element.36.own, f32[3,7,24,128]{3,2,1,0:T(8,128)S(1)} %collective-permute-done.9.left, ...), custom_call_target="tpu_custom_call" | custom-call | tf_op jit(solution)/shard_map/second_down_kernel/pallas_call | solution.py:366
  131.4 6.0 %collective-permute-start.14 = (f32[4,24,128]{2,1,0:T(8,128)S(1)}, f32[4,24,128]{2,1,0:T(8,128)S(1)}, u32[]{:S(2)}, u32[]{:S(2)}) collective-permute-start(f32[4,24,128]{2,1,0:T(8,128)S(1)} %get-tuple-element.43), channel_id=1, source_target_pairs={{8,0},{16,8},{24,16},{32,24},{40,32},{48,40},{56,48},{64,56},{72,6... | collective-permute-start | bytes 147464 | tf_op jit(solution)/shard_map/ppermute | solution.py:381
  137.4 1.9 collective-permute-start.13
  139.3 0.0 collective-permute-done.14
  139.3 6.8 %collective-permute-done.13 = f32[4,24,128]{2,1,0:T(8,128)S(1)} collective-permute-done((f32[4,24,128]{2,1,0:T(8,128)S(1)}, f32[4,24,128]{2,1,0:T(8,128)S(1)}, u32[]{:S(2)}, u32[]{:S(2)}) %collective-permute-start.13) | collective-permute-done | bytes 49184 | tf_op jit(solution)/shard_map/ppermute | solution.py:381
  146.1 1.9 collective-permute-start.16
  148.1 3.6 %collective-permute-start.15 = (f32[3,4,24,128]{3,2,1,0:T(8,128)S(1)}, f32[3,4,24,128]{3,2,1,0:T(8,128)S(1)}, u32[]{:S(2)}, u32[]{:S(2)}) collective-permute-start(f32[3,4,24,128]{3,2,1,0:T(8,128)S(1)} %pad_maximum_fusion.1.near), channel_id=1, source_target_pairs={{0,24},{8,32},{16,40},{24,48},{32,56},{40,64},{48,72},{56,80},{64,... | collective-permute-start | bytes 442376 | tf_op jit(solution)/shard_map/ppermute | solution.py:381
  151.7 0.7 collective-permute-start.17
  152.4 0.0 collective-permute-done.17.end
  152.4 0.2 collective-permute-done.16.right
  152.6 5.5 %collective-permute-done.15.left = f32[3,4,24,128]{3,2,1,0:T(8,128)S(1)} collective-permute-done((f32[3,4,24,128]{3,2,1,0:T(8,128)S(1)}, f32[3,4,24,128]{3,2,1,0:T(8,128)S(1)}, u32[]{:S(2)}, u32[]{:S(2)}) %collective-permute-start.15) | collective-permute-done | bytes 147488 | tf_op jit(solution)/shard_map/ppermute | solution.py:381
  158.1 4.9 %coarse_kernel.3.own = f32[3,4,24,128]{3,2,1,0:T(8,128)S(1)} custom-call(s32[4]{0:T(128)S(1)} %pad_add_fusion.position, f32[3,4,24,128]{3,2,1,0:T(8,128)S(1)} %collective-permute-done.15.left, f32[3,4,24,128]{3,2,1,0:T(8,128)S(1)} %pad_maximum_fusion.1.near, f32[3,4,24,128]{3,2,1,0:T(8,128)S(1)} %collective-permute-done.16.right, ...), custom_call_target="tpu_custom_call" | custom-call | tf_op jit(solution)/shard_map/coarse_kernel/pallas_call | solution.py:366
  163.1 1.9 collective-permute-start.19
  165.0 2.4 %collective-permute-start.18 = (f32[3,3,24,128]{3,2,1,0:T(8,128)S(1)}, f32[3,3,24,128]{3,2,1,0:T(8,128)S(1)}, u32[]{:S(2)}, u32[]{:S(2)}) collective-permute-start(f32[3,3,24,128]{3,2,1,0:T(8,128)S(1)} %get-tuple-element.48), channel_id=1, source_target_pairs={{0,8},{8,16},{16,24},{24,32},{32,40},{40,48},{48,56},{56,64},{64,7... | collective-permute-start | bytes 331784 | tf_op jit(solution)/shard_map/ppermute | solution.py:381
  167.5 0.0 collective-permute-done.19.right
  167.5 7.0 %collective-permute-done.18.left = f32[3,3,24,128]{3,2,1,0:T(8,128)S(1)} collective-permute-done((f32[3,3,24,128]{3,2,1,0:T(8,128)S(1)}, f32[3,3,24,128]{3,2,1,0:T(8,128)S(1)}, u32[]{:S(2)}, u32[]{:S(2)}) %collective-permute-start.18) | collective-permute-done | bytes 110624 | tf_op jit(solution)/shard_map/ppermute | solution.py:381
  174.4 2.5 %last_up_kernel.1 = f32[8,9,8,128]{3,2,1,0:T(8,128)S(1)} custom-call(f32[3,4,24,128]{3,2,1,0:T(8,128)S(1)} %coarse_kernel.3.own, f32[3,3,24,128]{3,2,1,0:T(8,128)S(1)} %collective-permute-done.18.left, f32[3,3,24,128]{3,2,1,0:T(8,128)S(1)} %collective-permute-done.19.right, f32[3,20,24,256]{3,2,1,0:T(8,128)S(1)} %get-tuple-element.31.g0, ...), custom_call_target="tpu_custom_call" | custom-call | tf_op jit(solution)/shard_map/last_up_kernel/pallas_call | solution.py:366
  176.9 16.2 %all_to_all.11.taken = f32[8,9,8,128]{3,2,1,0:T(8,128)S(1)} all-to-all(f32[8,9,8,128]{3,2,1,0:T(8,128)S(1)} %last_up_kernel.1), channel_id=1, replica_groups=mesh['gx'=64,'gz'=8] {'gz'}, dimensions={0} | all-to-all | bytes 589824 | tf_op jit(solution)/shard_map/all_to_all | solution.py:471
  193.1 0.7 join_kernel.1
  (4 shorter events, 0.1 us)
Async XLA Ops:
  0.0 1.0 copy-start
  1.0 0.9 copy-start.1
  32.2 14.5 %collective-permute-start = (f32[4,6,24,256]{3,2,1,0:T(8,128)S(1)}, f32[4,6,24,256]{3,2,1,0:T(8,128)S(1)}, u32[]{:S(2)}, u32[]{:S(2)}) collective-permute-start(f32[4,6,24,256]{3,2,1,0:T(8,128)S(1)} %get-tuple-element.27), channel_id=1, source_target_pairs={{0,8},{8,16},{16,24},{24,32},{32,40},{40,48},{48,56},{56,64},{64,7... | collective-permute-start | bytes 1769480 | tf_op jit(solution)/shard_map/ppermute | solution.py:381
  34.1 14.3 %collective-permute-start.1 = (f32[4,6,24,256]{3,2,1,0:T(8,128)S(1)}, f32[4,6,24,256]{3,2,1,0:T(8,128)S(1)}, u32[]{:S(2)}, u32[]{:S(2)}) collective-permute-start(f32[4,6,24,256]{3,2,1,0:T(8,128)S(1)} %get-tuple-element.28), channel_id=1, source_target_pairs={{8,0},{16,8},{24,16},{32,24},{40,32},{48,40},{56,48},{64,56},{72,6... | collective-permute-start | bytes 1769480 | tf_op jit(solution)/shard_map/ppermute | solution.py:381
  54.3 9.1 %collective-permute-start.3 = (f32[4,24,128]{2,1,0:T(8,128)S(1)}, f32[4,24,128]{2,1,0:T(8,128)S(1)}, u32[]{:S(2)}, u32[]{:S(2)}) collective-permute-start(f32[4,24,128]{2,1,0:T(8,128)S(1)} %get-tuple-element.29), channel_id=1, source_target_pairs={{8,0},{16,8},{24,16},{32,24},{40,32},{48,40},{56,48},{64,56},{72,6... | collective-permute-start | bytes 147464 | tf_op jit(solution)/shard_map/ppermute | solution.py:381
  61.4 8.7 %collective-permute-start.2 = (f32[4,24,128]{2,1,0:T(8,128)S(1)}, f32[4,24,128]{2,1,0:T(8,128)S(1)}, u32[]{:S(2)}, u32[]{:S(2)}) collective-permute-start(f32[4,24,128]{2,1,0:T(8,128)S(1)} %get-tuple-element.29), channel_id=1, source_target_pairs={{0,8},{8,16},{16,24},{24,32},{32,40},{40,48},{48,56},{56,64},{64,7... | collective-permute-start | bytes 147464 | tf_op jit(solution)/shard_map/ppermute | solution.py:381
  70.2 6.5 %collective-permute-start.5 = (f32[3,4,24,128]{3,2,1,0:T(8,128)S(1)}, f32[3,4,24,128]{3,2,1,0:T(8,128)S(1)}, u32[]{:S(2)}, u32[]{:S(2)}) collective-permute-start(f32[3,4,24,128]{3,2,1,0:T(8,128)S(1)} %pad_maximum_fusion.near), channel_id=1, source_target_pairs={{24,0},{32,8},{40,16},{48,24},{56,32},{64,40},{72,48},{80,56},{88,... | collective-permute-start | bytes 442376 | tf_op jit(solution)/shard_map/ppermute | solution.py:381
  72.1 10.1 %collective-permute-start.4 = (f32[3,4,24,128]{3,2,1,0:T(8,128)S(1)}, f32[3,4,24,128]{3,2,1,0:T(8,128)S(1)}, u32[]{:S(2)}, u32[]{:S(2)}) collective-permute-start(f32[3,4,24,128]{3,2,1,0:T(8,128)S(1)} %pad_maximum_fusion.near), channel_id=1, source_target_pairs={{0,24},{8,32},{16,40},{24,48},{32,56},{40,64},{48,72},{56,80},{64,... | collective-permute-start | bytes 442376 | tf_op jit(solution)/shard_map/ppermute | solution.py:381
  75.8 0.7 collective-permute-start.6
  87.2 4.3 %collective-permute-start.8 = (f32[3,3,24,128]{3,2,1,0:T(8,128)S(1)}, f32[3,3,24,128]{3,2,1,0:T(8,128)S(1)}, u32[]{:S(2)}, u32[]{:S(2)}) collective-permute-start(f32[3,3,24,128]{3,2,1,0:T(8,128)S(1)} %get-tuple-element.49), channel_id=1, source_target_pairs={{8,0},{16,8},{24,16},{32,24},{40,32},{48,40},{56,48},{64,56},{72,6... | collective-permute-start | bytes 331784 | tf_op jit(solution)/shard_map/ppermute | solution.py:381
  89.1 9.4 %collective-permute-start.7 = (f32[3,3,24,128]{3,2,1,0:T(8,128)S(1)}, f32[3,3,24,128]{3,2,1,0:T(8,128)S(1)}, u32[]{:S(2)}, u32[]{:S(2)}) collective-permute-start(f32[3,3,24,128]{3,2,1,0:T(8,128)S(1)} %get-tuple-element.50), channel_id=1, source_target_pairs={{0,8},{8,16},{16,24},{24,32},{32,40},{40,48},{48,56},{56,64},{64,7... | collective-permute-start | bytes 331784 | tf_op jit(solution)/shard_map/ppermute | solution.py:381
  100.9 11.0 %collective-permute-start.9 = (f32[3,7,24,128]{3,2,1,0:T(8,128)S(1)}, f32[3,7,24,128]{3,2,1,0:T(8,128)S(1)}, u32[]{:S(2)}, u32[]{:S(2)}) collective-permute-start(f32[3,7,24,128]{3,2,1,0:T(8,128)S(1)} %get-tuple-element.37), channel_id=1, source_target_pairs={{0,8},{8,16},{16,24},{24,32},{32,40},{40,48},{48,56},{56,64},{64,7... | collective-permute-start | bytes 774152 | tf_op jit(solution)/shard_map/ppermute | solution.py:381
  102.9 10.8 %collective-permute-start.10 = (f32[3,7,24,128]{3,2,1,0:T(8,128)S(1)}, f32[3,7,24,128]{3,2,1,0:T(8,128)S(1)}, u32[]{:S(2)}, u32[]{:S(2)}) collective-permute-start(f32[3,7,24,128]{3,2,1,0:T(8,128)S(1)} %get-tuple-element.38), channel_id=1, source_target_pairs={{8,0},{16,8},{24,16},{32,24},{40,32},{48,40},{56,48},{64,56},{72,6... | collective-permute-start | bytes 774152 | tf_op jit(solution)/shard_map/ppermute | solution.py:381
  113.8 9.8 %collective-permute-start.11 = (f32[3,11,24,128]{3,2,1,0:T(8,128)S(1)}, f32[3,11,24,128]{3,2,1,0:T(8,128)S(1)}, u32[]{:S(2)}, u32[]{:S(2)}) collective-permute-start(f32[3,11,24,128]{3,2,1,0:T(8,128)S(1)} %get-tuple-element.39), channel_id=1, source_target_pairs={{1,0},{2,1},{3,2},{4,3},{5,4},{6,5},{7,6},{9,8},{10,9},{11,10},{12... | collective-permute-start | bytes 1216520 | tf_op jit(solution)/shard_map/ppermute | solution.py:381
  115.1 10.0 %collective-permute-start.12 = (f32[3,11,24,128]{3,2,1,0:T(8,128)S(1)}, f32[3,11,24,128]{3,2,1,0:T(8,128)S(1)}, u32[]{:S(2)}, u32[]{:S(2)}) collective-permute-start(f32[3,11,24,128]{3,2,1,0:T(8,128)S(1)} %get-tuple-element.40), channel_id=1, source_target_pairs={{0,1},{1,2},{2,3},{3,4},{4,5},{5,6},{6,7},{8,9},{9,10},{10,11},{11... | collective-permute-start | bytes 1216520 | tf_op jit(solution)/shard_map/ppermute | solution.py:381
  131.4 7.9 %collective-permute-start.14 = (f32[4,24,128]{2,1,0:T(8,128)S(1)}, f32[4,24,128]{2,1,0:T(8,128)S(1)}, u32[]{:S(2)}, u32[]{:S(2)}) collective-permute-start(f32[4,24,128]{2,1,0:T(8,128)S(1)} %get-tuple-element.43), channel_id=1, source_target_pairs={{8,0},{16,8},{24,16},{32,24},{40,32},{48,40},{56,48},{64,56},{72,6... | collective-permute-start | bytes 147464 | tf_op jit(solution)/shard_map/ppermute | solution.py:381
  137.4 8.7 %collective-permute-start.13 = (f32[4,24,128]{2,1,0:T(8,128)S(1)}, f32[4,24,128]{2,1,0:T(8,128)S(1)}, u32[]{:S(2)}, u32[]{:S(2)}) collective-permute-start(f32[4,24,128]{2,1,0:T(8,128)S(1)} %get-tuple-element.43), channel_id=1, source_target_pairs={{0,8},{8,16},{16,24},{24,32},{32,40},{40,48},{48,56},{56,64},{64,7... | collective-permute-start | bytes 147464 | tf_op jit(solution)/shard_map/ppermute | solution.py:381
  146.1 6.5 %collective-permute-start.16 = (f32[3,4,24,128]{3,2,1,0:T(8,128)S(1)}, f32[3,4,24,128]{3,2,1,0:T(8,128)S(1)}, u32[]{:S(2)}, u32[]{:S(2)}) collective-permute-start(f32[3,4,24,128]{3,2,1,0:T(8,128)S(1)} %pad_maximum_fusion.1.near), channel_id=1, source_target_pairs={{24,0},{32,8},{40,16},{48,24},{56,32},{64,40},{72,48},{80,56},{88,... | collective-permute-start | bytes 442376 | tf_op jit(solution)/shard_map/ppermute | solution.py:381
  148.1 10.1 %collective-permute-start.15 = (f32[3,4,24,128]{3,2,1,0:T(8,128)S(1)}, f32[3,4,24,128]{3,2,1,0:T(8,128)S(1)}, u32[]{:S(2)}, u32[]{:S(2)}) collective-permute-start(f32[3,4,24,128]{3,2,1,0:T(8,128)S(1)} %pad_maximum_fusion.1.near), channel_id=1, source_target_pairs={{0,24},{8,32},{16,40},{24,48},{32,56},{40,64},{48,72},{56,80},{64,... | collective-permute-start | bytes 442376 | tf_op jit(solution)/shard_map/ppermute | solution.py:381
  151.7 0.7 collective-permute-start.17
  163.1 4.3 %collective-permute-start.19 = (f32[3,3,24,128]{3,2,1,0:T(8,128)S(1)}, f32[3,3,24,128]{3,2,1,0:T(8,128)S(1)}, u32[]{:S(2)}, u32[]{:S(2)}) collective-permute-start(f32[3,3,24,128]{3,2,1,0:T(8,128)S(1)} %get-tuple-element.47), channel_id=1, source_target_pairs={{8,0},{16,8},{24,16},{32,24},{40,32},{48,40},{56,48},{64,56},{72,6... | collective-permute-start | bytes 331784 | tf_op jit(solution)/shard_map/ppermute | solution.py:381
  165.0 9.4 %collective-permute-start.18 = (f32[3,3,24,128]{3,2,1,0:T(8,128)S(1)}, f32[3,3,24,128]{3,2,1,0:T(8,128)S(1)}, u32[]{:S(2)}, u32[]{:S(2)}) collective-permute-start(f32[3,3,24,128]{3,2,1,0:T(8,128)S(1)} %get-tuple-element.48), channel_id=1, source_target_pairs={{0,8},{8,16},{16,24},{24,32},{32,40},{40,48},{48,56},{56,64},{64,7... | collective-permute-start | bytes 331784 | tf_op jit(solution)/shard_map/ppermute | solution.py:381

commit v3 on v2

--- a/solution.py
+++ b/solution.py
@@ -175,6 +175,22 @@
         packed[c] = jnp.where(lane < LANES // 2, pair[0], pair[1])
 
 
+def rows_to_send(position, own, first, second):
+    odd, spare = position[4], own.shape[1] - first.shape[1]
+    for c in range(own.shape[0]):
+        for r in range(first.shape[1]):
+            first[c, r] = own[c, (1 - odd) * spare + r]
+            second[c, r] = own[c, odd * spare + r]
+
+
+def with_halo(position, own, first, second, store):
+    odd, rows, halo = position[4], own.shape[1], first.shape[1]
+    for c in range(own.shape[0]):
+        for piece, at in ((first, (1 - odd) * (halo + rows)), (own, halo), (second, odd * (halo + rows))):
+            for r in range(piece.shape[1]):
+                store(c, at + r, piece[c, r])
+
+
 def pack_kernel(source, density, out):
     blocks = out.shape[0]
     for ref, at, n in ((source, 0, source.shape[0]), (density, source.shape[0], density.shape[0])):
@@ -188,7 +204,7 @@
                 out[b, at + m, :, LANES:] = jnp.where(lane < LANES // 2, after, before)
 
 
-def unpack_kernel(taken, own, low, high, scratch):
+def unpack_kernel(position, taken, own, first, second, scratch):
     blocks, _, rows, _ = taken.shape
     depth = NZ // blocks
     for c in range(C + 1):
@@ -203,21 +219,19 @@
                 part = scratch[c, h, pl.ds(r, NZ, stride=rows), :]
                 lanes = slice(h * LANES, (h + 1) * LANES)
                 own[c, r, :, lanes] = part
-                if r < HALO:
-                    low[c, r, :, lanes] = part
-                if r >= rows - HALO:
-                    high[c, r - rows + HALO, :, lanes] = part
-
-
-def first_down_kernel(position, own, left, right, g0, d0, f0, v0, g1, d1, f1, v1, packed, field, field1):
+    rows_to_send(position, own, first, second)
+
+
+def first_down_kernel(position, own, first, second, g0, d0, f0, v0, g1, d1, f1, v1, packed, field, field1):
     rows = own.shape[1]
-    for c in range(C + 1):
-        for piece, at, n in ((left, 0, HALO), (own, HALO, rows), (right, HALO + rows, HALO)):
-            for r in range(n):
-                if c < C:
-                    g0[c, at + r] = piece[c, r]
-                else:
-                    d0[at + r] = piece[c, r]
+
+    def store(c, at, value):
+        if c < C:
+            g0[c, at] = value
+        else:
+            d0[at] = value
+
+    with_halo(position, own, first, second, store)
     g, d, f, a, b = (g0, -HALO), (d0, -HALO), (f0, -HALO), (field, -HALO), (v0, -HALO)
     from_zero(a, g, d, f, 0, 2 * LANES, rows, position, -HALO, rows + HALO)
     sweep(b, a, g, f, 0, -5, rows + 5)
@@ -226,35 +240,32 @@
     level_one_down((g1, -2), (v1, -2), (field1, -2), (d1, -3), (f1, -3), packed)
 
 
-def side_kernel(own, left, right, to_left, to_right):
-    rows, halo = own.shape[1], left.shape[1]
-    half = (rows + 2 * halo) // 2
-    lane = lane_index()
-
-    def at(c, r):
-        if r < halo:
-            return left[c, r]
-        return own[c, r - halo] if r < halo + rows else right[c, r - halo - rows]
-
+def side_kernel(position, own, first, second, tall, to_first, to_second):
+    half = tall.shape[1] // 2
+    low = (lane_index() < LANES // 2) == (position[5] == 1)
+
+    def store(c, at, value):
+        tall[c, at] = value
+
+    with_halo(position, own, first, second, store)
     for c in range(C):
         for r in range(half):
-            one, two = at(c, r), pltpu.roll(at(c, r + half), LANES // 2, 1)
-            to_left[c, r] = jnp.where(lane < LANES // 2, one, two)
-            to_right[c, r] = jnp.where(lane < LANES // 2, two, one)
-
-
-def second_down_kernel(own, left, right, after, before, g0, d0, f0, d1, f1, v0, g1, v1, packed, wide, field, field1):
-    rows, halo = own.shape[1], left.shape[1]
-    half = (rows + 2 * halo) // 2
-    lane = lane_index()
+            one, two = tall[c, r], pltpu.roll(tall[c, r + half], LANES // 2, 1)
+            to_first[c, r] = jnp.where(low, one, two)
+            to_second[c, r] = jnp.where(low, two, one)
+
+
+def second_down_kernel(position, tall, first, second, g0, d0, f0, d1, f1, v0, g1, v1, packed, wide, field, field1):
+    half = tall.shape[1] // 2
+    halo = half - v0.shape[1] // 2 + HALO
+    rows = 2 * (half - halo)
+    low = (lane_index() < LANES // 2) == (position[5] == 0)
     for c in range(C):
-        for piece, at, n in ((left, 0, halo), (own, halo, rows), (right, halo + rows, halo)):
-            for r in range(n):
-                wide[c, at + r, :, :LANES] = piece[c, r]
+        for r in range(2 * half):
+            wide[c, r, :, :LANES] = tall[c, r]
         for r in range(half):
-            wide[c, r, :, LANES:] = jnp.where(lane < LANES // 2, after[c, r], before[c, r])
-            two = jnp.where(lane < LANES // 2, before[c, r], after[c, r])
-            wide[c, r + half, :, LANES:] = pltpu.roll(two, LANES // 2, 1)
+            wide[c, r, :, LANES:] = jnp.where(low, first[c, r], second[c, r])
+            wide[c, r + half, :, LANES:] = pltpu.roll(jnp.where(low, second[c, r], first[c, r]), LANES // 2, 1)
     g, d, f, a, b = (g0, -HALO), (d0, -HALO), (f0, -HALO), (field, -HALO), (v0, -HALO)
     sweep(a, (wide, -halo), g, f, 0, -6, rows + 6)
     sweep(b, a, g, f, 0, -5, rows + 5)
@@ -263,13 +274,12 @@
     level_one_down((g1, -2), (v1, -2), (field1, -2), (d1, -3), (f1, -3), packed)
 
 
-def coarse_kernel(position, left, near, right, end, v1, out, g2, d2, f2, g3, d3, f3, a, b, a3, b3):
+def coarse_kernel(position, pair, near1, near2, far1, far2, v1, out, first, second, g2, d2, f2, g3, d3, f3, a, b, a3, b3):
     lane = lane_index()
-    side = near.shape[0]
-    count = 3 * side
-    reach = count // 2 * 2
-
-    def place(n, block):
+    reach = 10
+    odd, step = position[4], 1 - 2 * position[6]
+
+    def place(block, n):
         for c in range(C + 1):
             both = block[c]
             other = pltpu.roll(both, LANES // 2, 1)
@@ -279,11 +289,9 @@
                 else:
                     d2[2 * n + q] = value
 
-    for at, blocks in ((0, left), (side, near), (2 * side, right)):
-        for n in range(side):
-            place(at + n, blocks.at[n])
-    pl.when(position[0] == side - 1)(lambda: place(count // 2 - side + 1, end))
-    pl.when(position[0] == position[2] - side)(lambda: place(count // 2 + side - 1, end))
+    for blocks, away in ((pair, 0), (near1, step), (near2, -step), (far1, 2 * step), (far2, -2 * step)):
+        for core in range(2):
+            place(blocks.at[core], 2 * away + (reach // 2 + core - odd))
     g, d, f, u, w = (g2, -reach), (d2, -reach), (f2, -reach), (a, -reach), (b, -reach)
     h, e, k, s, t = (g3, -reach // 2), (d3, -reach // 2), (f3, -reach // 2), (a3, -reach // 2), (b3, -reach // 2)
     from_zero(u, g, d, f, 2, LANES // 2, 2, position, -8, 10)
@@ -307,14 +315,16 @@
             fine = spread(row(w, c, q), LANES)
             for r in (2 * q, 2 * q + 1):
                 out[c, r] = v1[c, r + 2] + fine
-
-
-def climb(own, left, right, g0, f0, v0, g1, f1, wide, u, w, field, emit):
-    rows1, halo = own.shape[1], left.shape[1]
-    for c in range(C):
-        for piece, at, n in ((left, 0, halo), (own, halo, rows1), (right, halo + rows1, halo)):
-            for r in range(n):
-                wide[c, at + r] = piece[c, r]
+    rows_to_send(position, out, first, second)
+
+
+def climb(position, own, first, second, g0, f0, v0, g1, f1, wide, u, w, field, emit):
+    rows1, halo = own.shape[1], first.shape[1]
+
+    def store(c, at, value):
+        wide[c, at] = value
+
+    with_halo(position, own, first, second, store)
     sweep((u, -3), (wide, -halo), (g1, -2), (f1, -3), 1, -2, rows1 + 2)
     sweep((w, -3), (u, -3), (g1, -2), (f1, -3), 1, -1, rows1 + 1)
 
@@ -330,21 +340,16 @@
     sweep((field, -HALO), (emit, -HALO), (g0, -HALO), (f0, -HALO), 0, 0, rows)
 
 
-def first_up_kernel(own, left, right, g0, f0, v0, g1, f1, out, low, high, wide, u, w, field, other):
-    climb(own, left, right, g0, f0, v0, g1, f1, wide, u, w, field, other)
-    rows, halo = out.shape[1], low.shape[1]
+def first_up_kernel(position, own, left, right, g0, f0, v0, g1, f1, out, first, second, wide, u, w, field, other):
+    climb(position, own, left, right, g0, f0, v0, g1, f1, wide, u, w, field, other)
     for c in range(C):
-        for r in range(rows):
-            value = field[c, r + HALO, :, :LANES]
-            out[c, r] = value
-            if r < halo:
-                low[c, r] = value
-            if r >= rows - halo:
-                high[c, r - rows + halo] = value
-
-
-def last_up_kernel(own, left, right, g0, f0, v0, g1, f1, out, wide, u, w, field, other, scratch):
-    climb(own, left, right, g0, f0, v0, g1, f1, wide, u, w, field, other)
+        for r in range(out.shape[1]):
+            out[c, r] = field[c, r + HALO, :, :LANES]
+    rows_to_send(position, out, first, second)
+
+
+def last_up_kernel(position, own, left, right, g0, f0, v0, g1, f1, out, wide, u, w, field, other, scratch):
+    climb(position, own, left, right, g0, f0, v0, g1, f1, wide, u, w, field, other)
     blocks, _, rows, _ = out.shape
     depth = NZ // blocks
     for c in range(C):
@@ -375,25 +380,32 @@
     return out
 
 
-def onward(values, axis, distance):
-    count = lax.axis_size(axis)
-    pairs = [(i, i + distance) for i in range(count) if 0 <= i + distance < count]
+def swap(values, axis, first, unit=1):
+    count, pairs = lax.axis_size(axis), []
+    for i in range(count):
+        group = i // unit
+        other = group ^ 1 if first else ((group - 1) ^ 1) + 1
+        if 0 <= other < count // unit:
+            pairs.append((i, other * unit + i % unit))
     return lax.ppermute(values, axis, pairs)
 
 
 def shards(right_side, density):
     blocks = lax.axis_size("gz")
     depth, rows, columns = density.shape
-    position = jnp.stack([lax.axis_index("gx"), lax.axis_index("gz"), lax.axis_size("gx"), blocks]).astype(jnp.int32)
+    i, j = lax.axis_index("gx"), lax.axis_index("gz")
+    position = jnp.stack([i, j, lax.axis_size("gx"), blocks, i % 2, j % 2, i // 2 % 2]).astype(jnp.int32)
     W, R0, R1 = 2 * LANES, rows + 2 * HALO, rows // 2
 
     (sent,) = call(pack_kernel, [(blocks, (C + 1) * depth, rows, W)], [], right_side.reshape(C * depth, rows, columns), density)
     taken = lax.all_to_all(sent, "gz", 0, 0)
-    own, low, high = call(
+    own, first, second = call(
         unpack_kernel,
         [(C + 1, rows, NZ, W), (C + 1, HALO, NZ, W), (C + 1, HALO, NZ, W)],
         [(C + 1, 2, NZ * rows, LANES)],
+        position,
         taken,
+        scalars=1,
     )
     fine, mid = (C, R0, NZ, W), (C, R1 + 4, NZ, LANES)
     g0, d0, f0, v0, g1, d1, f1, v1, packed = call(
@@ -402,71 +414,83 @@
         [fine, mid],
         position,
         own,
-        onward(high, "gx", 1),
-        onward(low, "gx", -1),
+        swap(first, "gx", True),
+        swap(second, "gx", False),
         scalars=1,
     )
 
     def coarse(packed, v1):
-        near = jnp.stack([onward(packed, "gx", 1), packed, onward(packed, "gx", -1)])
-        last = lax.axis_size("gx") - 1
-        end = lax.ppermute(packed, "gx", [(0, 2), (last, last - 2)])
-        two, three = (C, 18, NZ, LANES), (C, 9, NZ, LANES)
-        (out,) = call(
+        partner = swap(packed, "gx", True)
+        pair = jnp.where(i % 2 == 0, jnp.stack([packed, partner]), jnp.stack([partner, packed]))
+        near = [swap(pair, "gx", first, 2) for first in (True, False)]
+        far = [swap(near[1], "gx", True, 2), swap(near[0], "gx", False, 2)]
+        two, three = (C, 22, NZ, LANES), (C, 11, NZ, LANES)
+        out, first, second = call(
             coarse_kernel,
-            [(C, R1, NZ, LANES)],
+            [(C, R1, NZ, LANES)] + [(C, R1 - 1, NZ, LANES)] * 2,
             [two, two[1:], two[1:], three, three[1:], three[1:], two, two, three, three],
             position,
-            onward(near, "gx", 3),
-            near,
-            onward(near, "gx", -3),
-            end,
+            pair,
+            *near,
+            *far,
             v1,
             scalars=1,
         )
-        return out, onward(out[:, 1:], "gx", 1), onward(out[:, :-1], "gx", -1)
+        return out, swap(first, "gx", True), swap(second, "gx", False)
 
     middle = (C, R1 + 6, NZ, LANES)
     reach = HALO + 1
-    field, low, high = call(
+    field, first, second = call(
         first_up_kernel,
         [(C, rows, NZ, LANES), (C, reach, NZ, LANES), (C, reach, NZ, LANES)],
         [middle, middle, middle, fine, fine],
+        position,
         *coarse(packed, v1),
         g0,
         f0,
         v0,
         g1,
         f1,
-    )
-    left, right = onward(high, "gx", 1), onward(low, "gx", -1)
+        scalars=1,
+    )
     half = (rows + 2 * reach) // 2
-    to_left, to_right = call(side_kernel, [(C, half, NZ, LANES)] * 2, [], field, left, right)
+    tall, first, second = call(
+        side_kernel,
+        [(C, 2 * half, NZ, LANES)] + [(C, half, NZ, LANES)] * 2,
+        [],
+        position,
+        field,
+        swap(first, "gx", True),
+        swap(second, "gx", False),
+        scalars=1,
+    )
     v0, g1, v1, packed = call(
         second_down_kernel,
         [fine, mid, mid, (C + 1, NZ, LANES)],
-        [(C, rows + 2 * reach, NZ, W), fine, mid],
-        field,
-        left,
-        right,
-        onward(to_left, "gz", -1),
-        onward(to_right, "gz", 1),
+        [(C, 2 * half, NZ, W), fine, mid],
+        position,
+        tall,
+        swap(first, "gz", True),
+        swap(second, "gz", False),
         g0,
         d0,
         f0,
         d1,
         f1,
+        scalars=1,
     )
     (sent,) = call(
         last_up_kernel,
         [(blocks, C * depth, rows, LANES)],
         [middle, middle, middle, fine, fine, (C, NZ * rows, LANES)],
+        position,
         *coarse(packed, v1),
         g0,
         f0,
         v0,
         g1,
         f1,
+        scalars=1,
     )
     (out,) = call(join_kernel, [(C * depth, rows, columns)], [], lax.all_to_all(sent, "gz", 0, 0))
     return out.reshape(right_side.shape)

time: 195 us -> 201 us (1.031)
  the two profiles are of different devices: /device:TPU:256 before, /device:TPU:198 now
where the time goes in v3:
time: 201 us; the launch traced here: 197 us
  waiting for transfers between devices  71.9 us (36%)
  starting transfers between devices  67.9 us (34%)
  Pallas kernels  31.6 us (16%)
  blocking collectives  17.2 us (9%)
  local copies, waits for them, and re-layouts  8.27 us (4%)
    ppermute x20, starting transfers between devices, swap(): return lax.ppermute(values, axis, pairs)  60.8 us
    ppermute x20, waiting for transfers between devices, swap(): return lax.ppermute(values, axis, pairs)  48.8 us
    pallas_call x10, Pallas kernels, call(): pl.pallas_call(kernel, out_shape=[shape(s) for s in outs], in_specs=specs...  31.6 us
    all_to_all x1, waiting for transfers between devices, shards(): taken = lax.all_to_all(sent, 'gz', 0, 0)  23 us
    all_to_all x1, blocking collectives, shards(): lax.all_to_all(sent, 'gz', 0, 0)  17.2 us
    unnamed x26, local copies, waits for them, and re-layouts  8.19 us
    all_to_all x1, starting transfers between devices, shards(): taken = lax.all_to_all(sent, 'gz', 0, 0)  7.1 us
  transfers between devices with their start and end apart: 21, of which 12 were waited for; matrix products, arithmetic and copies ran while one was open for 0% of the time, Pallas kernels for 0%

profile of v3, /device:TPU:198, one launch (start us, length us, event | category | flops | bytes accessed | tf_op | source)
XLA Modules:
  0.0 197.2 jit_solution(7444082702336957723)
XLA Ops:
  0.0 1.0 copy-done.7
  1.0 0.9 copy-done.12
  1.9 0.9 pack_kernel.1
  2.8 7.1 %all-to-all-start = ((f32[8,12,8,256]{3,2,1,0:T(8,128)}), f32[8,12,8,256]{3,2,1,0:T(8,128)S(1)}, u32[]{:S(2)}, u32[]{:S(2)}) async-start(f32[8,12,8,256]{3,2,1,0:T(8,128)} %pack_kernel.1), calls=%async_computation | async-start | bytes 1572864 | tf_op jit(solution)/shard_map/all_to_all | solution.py:401
  9.9 0.1 stack.51.position
  10.0 23.0 %all-to-all-done.taken = f32[8,12,8,256]{3,2,1,0:T(8,128)S(1)} async-done(((f32[8,12,8,256]{3,2,1,0:T(8,128)}), f32[8,12,8,256]{3,2,1,0:T(8,128)S(1)}, u32[]{:S(2)}, u32[]{:S(2)}) %all-to-all-start) | async-done | bytes 786464 | tf_op jit(solution)/shard_map/all_to_all | solution.py:401
  33.0 0.8 unpack_kernel.1
  33.8 1.9 collective-permute-start
  35.8 2.8 %collective-permute-start.1 = (f32[4,6,24,256]{3,2,1,0:T(8,128)S(1)}, f32[4,6,24,256]{3,2,1,0:T(8,128)S(1)}, u32[]{:S(2)}, u32[]{:S(2)}) collective-permute-start(f32[4,6,24,256]{3,2,1,0:T(8,128)S(1)} %get-tuple-element.35), channel_id=1, source_target_pairs={{8,16},{16,8},{24,32},{32,24},{40,48},{48,40},{56,64},{64,56},{72,... | collective-permute-start | bytes 1769480 | tf_op jit(solution)/shard_map/ppermute | solution.py:390
  38.6 0.0 collective-permute-done.first
  38.6 8.3 %collective-permute-done.1.second = f32[4,6,24,256]{3,2,1,0:T(8,128)S(1)} collective-permute-done((f32[4,6,24,256]{3,2,1,0:T(8,128)S(1)}, f32[4,6,24,256]{3,2,1,0:T(8,128)S(1)}, u32[]{:S(2)}, u32[]{:S(2)}) %collective-permute-start.1) | collective-permute-done | bytes 589856 | tf_op jit(solution)/shard_map/ppermute | solution.py:390
  47.0 5.8 %first_down_kernel.1 = (f32[3,20,24,256]{3,2,1,0:T(8,128)S(1)}, f32[20,24,256]{2,1,0:T(8,128)S(1)}, f32[20,24,256]{2,1,0:T(8,128)S(1)}, f32[3,20,24,256]{3,2,1,0...) custom-call(s32[7]{0:T(128)S(1)} %stack.51.position, ...), custom_call_target="tpu_custom_call" | custom-call | tf_op jit(solution)/shard_map/first_down_kernel/pallas_call | solution.py:371
  52.7 0.6 copy-done
  53.4 0.8 copy-done.3
  54.2 0.7 copy-done.5
  54.9 0.7 copy-done.8
  55.6 0.6 copy-done.10
  56.2 5.7 %collective-permute-start.2 = (f32[4,24,128]{2,1,0:T(8,128)S(1)}, f32[4,24,128]{2,1,0:T(8,128)S(1)}, u32[]{:S(2)}, u32[]{:S(2)}) collective-permute-start(f32[4,24,128]{2,1,0:T(8,128)S(1)} %get-tuple-element.36), channel_id=1, source_target_pairs={{0,8},{8,0},{16,24},{24,16},{32,40},{40,32},{48,56},{56,48},{64,72... | collective-permute-start | bytes 147464 | tf_op jit(solution)/shard_map/ppermute | solution.py:390
  62.0 0.9 collective-permute-done.2
  62.8 5.3 %collective-permute-start.4 = (f32[2,4,24,128]{3,2,1,0:T(8,128)S(1)}, f32[2,4,24,128]{3,2,1,0:T(8,128)S(1)}, u32[]{:S(2)}, u32[]{:S(2)}) collective-permute-start(f32[2,4,24,128]{3,2,1,0:T(8,128)S(1)} %maximum_select_fusion.pair), channel_id=1, source_target_pairs={{16,32},{24,40},{32,16},{40,24},{48,64},{56,72},{64,48},{72,56},{8... | collective-permute-start | bytes 294920 | tf_op jit(solution)/shard_map/ppermute | solution.py:390
  68.1 1.9 collective-permute-start.3
  70.0 3.1 %collective-permute-done.4.near2 = f32[2,4,24,128]{3,2,1,0:T(8,128)S(1)} collective-permute-done((f32[2,4,24,128]{3,2,1,0:T(8,128)S(1)}, f32[2,4,24,128]{3,2,1,0:T(8,128)S(1)}, u32[]{:S(2)}, u32[]{:S(2)}) %collective-permute-start.4) | collective-permute-done | bytes 98336 | tf_op jit(solution)/shard_map/ppermute | solution.py:390
  73.1 1.9 collective-permute-start.5
  75.0 0.0 collective-permute-done.3.near1
  75.0 5.1 %collective-permute-start.6 = (f32[2,4,24,128]{3,2,1,0:T(8,128)S(1)}, f32[2,4,24,128]{3,2,1,0:T(8,128)S(1)}, u32[]{:S(2)}, u32[]{:S(2)}) collective-permute-start(f32[2,4,24,128]{3,2,1,0:T(8,128)S(1)} %collective-permute-done.3.near1), channel_id=1, source_target_pairs={{16,32},{24,40},{32,16},{40,24},{48,64},{56,72},{64,48},{72,56},{8... | collective-permute-start | bytes 294920 | tf_op jit(solution)/shard_map/ppermute | solution.py:390
  80.1 0.0 collective-permute-done.5.far1
  80.1 4.7 %collective-permute-done.6.far2 = f32[2,4,24,128]{3,2,1,0:T(8,128)S(1)} collective-permute-done((f32[2,4,24,128]{3,2,1,0:T(8,128)S(1)}, f32[2,4,24,128]{3,2,1,0:T(8,128)S(1)}, u32[]{:S(2)}, u32[]{:S(2)}) %collective-permute-start.6) | collective-permute-done | bytes 98336 | tf_op jit(solution)/shard_map/ppermute | solution.py:390
  84.9 1.0 copy-done.9
  85.8 5.0 %coarse_kernel.2 = (f32[3,4,24,128]{3,2,1,0:T(8,128)S(1)}, f32[3,3,24,128]{3,2,1,0:T(8,128)S(1)}, f32[3,3,24,128]{3,2,1,0:T(8,128)S(1)}) custom-call(s32[7]{0:T(128)S(1)} %stack.51.position, f32[2,4,24,128]{3,2,1,0:T(8,128)S(1)} %maximum_select_fusion.pair, f32[2,4,24,128]{3,2,1,0:T(8,128)S(1)} %collective-permute-done.3.near1, ...), custom_call_target="tpu_custom_call" | custom-call | tf_op jit(solution)/shard_map/coarse_kernel/pallas_call | solution.py:371
  90.8 1.9 collective-permute-start.7
  92.7 1.9 collective-permute-start.8
  94.6 0.0 collective-permute-done.7.left
  94.7 4.1 %collective-permute-done.8.right = f32[3,3,24,128]{3,2,1,0:T(8,128)S(1)} collective-permute-done((f32[3,3,24,128]{3,2,1,0:T(8,128)S(1)}, f32[3,3,24,128]{3,2,1,0:T(8,128)S(1)}, u32[]{:S(2)}, u32[]{:S(2)}) %collective-permute-start.8) | collective-permute-done | bytes 110624 | tf_op jit(solution)/shard_map/ppermute | solution.py:390
  98.8 0.9 copy-done.1
  99.7 1.0 copy-done.6
  100.7 3.0 %first_up_kernel.1 = (f32[3,8,24,128]{3,2,1,0:T(8,128)S(1)}, f32[3,7,24,128]{3,2,1,0:T(8,128)S(1)}, f32[3,7,24,128]{3,2,1,0:T(8,128)S(1)}) custom-call(s32[7]{0:T(128)S(1)} %stack.51.position, f32[3,4,24,128]{3,2,1,0:T(8,128)S(1)} %get-tuple-element.38.own, f32[3,3,24,128]{3,2,1,0:T(8,128)S(1)} %collective-permute-done.7.left, ...), custom_call_target="tpu_custom_call" | custom-call | tf_op jit(solution)/shard_map/first_up_kernel/pallas_call | solution.py:371
  103.6 5.7 %collective-permute-start.9 = (f32[3,7,24,128]{3,2,1,0:T(8,128)S(1)}, f32[3,7,24,128]{3,2,1,0:T(8,128)S(1)}, u32[]{:S(2)}, u32[]{:S(2)}) collective-permute-start(f32[3,7,24,128]{3,2,1,0:T(8,128)S(1)} %get-tuple-element.47), channel_id=1, source_target_pairs={{0,8},{8,0},{16,24},{24,16},{32,40},{40,32},{48,56},{56,48},{64,72... | collective-permute-start | bytes 774152 | tf_op jit(solution)/shard_map/ppermute | solution.py:390
  109.4 1.9 collective-permute-start.10
  111.3 0.0 collective-permute-done.9.first
  111.3 5.7 %collective-permute-done.10.second = f32[3,7,24,128]{3,2,1,0:T(8,128)S(1)} collective-permute-done((f32[3,7,24,128]{3,2,1,0:T(8,128)S(1)}, f32[3,7,24,128]{3,2,1,0:T(8,128)S(1)}, u32[]{:S(2)}, u32[]{:S(2)}) %collective-permute-start.10) | collective-permute-done | bytes 258080 | tf_op jit(solution)/shard_map/ppermute | solution.py:390
  117.0 0.8 side_kernel.1
  117.8 2.5 %collective-permute-start.11 = (f32[3,11,24,128]{3,2,1,0:T(8,128)S(1)}, f32[3,11,24,128]{3,2,1,0:T(8,128)S(1)}, u32[]{:S(2)}, u32[]{:S(2)}) collective-permute-start(f32[3,11,24,128]{3,2,1,0:T(8,128)S(1)} %get-tuple-element.50), channel_id=1, source_target_pairs={{0,1},{1,0},{2,3},{3,2},{4,5},{5,4},{6,7},{7,6},{8,9},{9,8},{10,11... | collective-permute-start | bytes 1216520 | tf_op jit(solution)/shard_map/ppermute | solution.py:390
  120.3 0.7 collective-permute-start.12
  121.0 8.5 %collective-permute-done.11.first = f32[3,11,24,128]{3,2,1,0:T(8,128)S(1)} collective-permute-done((f32[3,11,24,128]{3,2,1,0:T(8,128)S(1)}, f32[3,11,24,128]{3,2,1,0:T(8,128)S(1)}, u32[]{:S(2)}, u32[]{:S(2)}) %collective-permute-start.11) | collective-permute-done | bytes 405536 | tf_op jit(solution)/shard_map/ppermute | solution.py:390
  129.5 0.0 collective-permute-done.12.second
  129.5 6.7 %second_down_kernel.1 = (f32[3,20,24,256]{3,2,1,0:T(8,128)S(1)}, f32[3,8,24,128]{3,2,1,0:T(8,128)S(1)}, f32[3,8,24,128]{3,2,1,0:T(8,128)S(1)}, f32[4,24,128]{2,1,0:T(8,128)S(1)}) custom-call(s32[7]{0:T(128)S(1)} %stack.51.position, f32[3,22,24,128]{3,2,1,0:T(8,128)S(1)} %get-tuple-element.49.tall, f32[3,11,24,128]{3,2,1,0:T(8,128)S(1)} %collective-permute-done.11.first, ...), custom_call_target="tpu_custom_call" | custom-call | tf_op jit(solution)/shard_map/second_down_kernel/pallas_call | solution.py:371
  136.2 4.2 %collective-permute-start.13 = (f32[4,24,128]{2,1,0:T(8,128)S(1)}, f32[4,24,128]{2,1,0:T(8,128)S(1)}, u32[]{:S(2)}, u32[]{:S(2)}) collective-permute-start(f32[4,24,128]{2,1,0:T(8,128)S(1)} %get-tuple-element.54), channel_id=1, source_target_pairs={{0,8},{8,0},{16,24},{24,16},{32,40},{40,32},{48,56},{56,48},{64,72... | collective-permute-start | bytes 147464 | tf_op jit(solution)/shard_map/ppermute | solution.py:390
  140.4 0.9 collective-permute-done.13
  141.3 4.9 %collective-permute-start.15 = (f32[2,4,24,128]{3,2,1,0:T(8,128)S(1)}, f32[2,4,24,128]{3,2,1,0:T(8,128)S(1)}, u32[]{:S(2)}, u32[]{:S(2)}) collective-permute-start(f32[2,4,24,128]{3,2,1,0:T(8,128)S(1)} %maximum_select_fusion.1.pair), channel_id=1, source_target_pairs={{16,32},{24,40},{32,16},{40,24},{48,64},{56,72},{64,48},{72,56},{8... | collective-permute-start | bytes 294920 | tf_op jit(solution)/shard_map/ppermute | solution.py:390
  146.2 1.9 collective-permute-start.14
  148.2 3.4 %collective-permute-done.15.near2 = f32[2,4,24,128]{3,2,1,0:T(8,128)S(1)} collective-permute-done((f32[2,4,24,128]{3,2,1,0:T(8,128)S(1)}, f32[2,4,24,128]{3,2,1,0:T(8,128)S(1)}, u32[]{:S(2)}, u32[]{:S(2)}) %collective-permute-start.15) | collective-permute-done | bytes 98336 | tf_op jit(solution)/shard_map/ppermute | solution.py:390
  151.5 1.9 collective-permute-start.16
  153.4 0.0 collective-permute-done.14.near1
  153.5 4.8 %collective-permute-start.17 = (f32[2,4,24,128]{3,2,1,0:T(8,128)S(1)}, f32[2,4,24,128]{3,2,1,0:T(8,128)S(1)}, u32[]{:S(2)}, u32[]{:S(2)}) collective-permute-start(f32[2,4,24,128]{3,2,1,0:T(8,128)S(1)} %collective-permute-done.14.near1), channel_id=1, source_target_pairs={{16,32},{24,40},{32,16},{40,24},{48,64},{56,72},{64,48},{72,56},{8... | collective-permute-start | bytes 294920 | tf_op jit(solution)/shard_map/ppermute | solution.py:390
  158.2 0.0 collective-permute-done.16.far1
  158.2 5.1 %collective-permute-done.17.far2 = f32[2,4,24,128]{3,2,1,0:T(8,128)S(1)} collective-permute-done((f32[2,4,24,128]{3,2,1,0:T(8,128)S(1)}, f32[2,4,24,128]{3,2,1,0:T(8,128)S(1)}, u32[]{:S(2)}, u32[]{:S(2)}) %collective-permute-start.17) | collective-permute-done | bytes 98336 | tf_op jit(solution)/shard_map/ppermute | solution.py:390
  163.3 5.0 %coarse_kernel.3 = (f32[3,4,24,128]{3,2,1,0:T(8,128)S(1)}, f32[3,3,24,128]{3,2,1,0:T(8,128)S(1)}, f32[3,3,24,128]{3,2,1,0:T(8,128)S(1)}) custom-call(s32[7]{0:T(128)S(1)} %stack.51.position, f32[2,4,24,128]{3,2,1,0:T(8,128)S(1)} %maximum_select_fusion.1.pair, f32[2,4,24,128]{3,2,1,0:T(8,128)S(1)} %collective-permute-done.14.near1, ...), custom_call_target="tpu_custom_call" | custom-call | tf_op jit(solution)/shard_map/coarse_kernel/pallas_call | solution.py:371
  168.3 1.9 collective-permute-start.18
  170.2 1.9 collective-permute-start.19
  172.1 0.0 collective-permute-done.18.left
  172.1 4.1 %collective-permute-done.19.right = f32[3,3,24,128]{3,2,1,0:T(8,128)S(1)} collective-permute-done((f32[3,3,24,128]{3,2,1,0:T(8,128)S(1)}, f32[3,3,24,128]{3,2,1,0:T(8,128)S(1)}, u32[]{:S(2)}, u32[]{:S(2)}) %collective-permute-start.19) | collective-permute-done | bytes 110624 | tf_op jit(solution)/shard_map/ppermute | solution.py:390
  176.3 3.0 %last_up_kernel.1 = f32[8,9,8,128]{3,2,1,0:T(8,128)S(1)} custom-call(s32[7]{0:T(128)S(1)} %stack.51.position, f32[3,4,24,128]{3,2,1,0:T(8,128)S(1)} %get-tuple-element.56.own, f32[3,3,24,128]{3,2,1,0:T(8,128)S(1)} %collective-permute-done.18.left, f32[3,3,24,128]{3,2,1,0:T(8,128)S(1)} %collective-permute-done.19.right, ...), custom_call_target="tpu_custom_call" | custom-call | tf_op jit(solution)/shard_map/last_up_kernel/pallas_call | solution.py:371
  179.2 17.2 %all_to_all.10.taken = f32[8,9,8,128]{3,2,1,0:T(8,128)S(1)} all-to-all(f32[8,9,8,128]{3,2,1,0:T(8,128)S(1)} %last_up_kernel.1), channel_id=1, replica_groups=mesh['gx'=64,'gz'=8] {'gz'}, dimensions={0} | all-to-all | bytes 589824 | tf_op jit(solution)/shard_map/all_to_all | solution.py:495
  196.5 0.7 join_kernel.1
  (18 shorter events, 0.0 us)
Async XLA Ops:
  0.0 1.0 copy-start.7
  1.0 0.9 copy-start.12
  2.8 30.2 %all-to-all-start = ((f32[8,12,8,256]{3,2,1,0:T(8,128)}), f32[8,12,8,256]{3,2,1,0:T(8,128)S(1)}, u32[]{:S(2)}, u32[]{:S(2)}) async-start(f32[8,12,8,256]{3,2,1,0:T(8,128)} %pack_kernel.1), calls=%async_computation | async-start | bytes 1572864 | tf_op jit(solution)/shard_map/all_to_all | solution.py:401
  33.8 4.8 %collective-permute-start = (f32[4,6,24,256]{3,2,1,0:T(8,128)S(1)}, f32[4,6,24,256]{3,2,1,0:T(8,128)S(1)}, u32[]{:S(2)}, u32[]{:S(2)}) collective-permute-start(f32[4,6,24,256]{3,2,1,0:T(8,128)S(1)} %get-tuple-element.34), channel_id=1, source_target_pairs={{0,8},{8,0},{16,24},{24,16},{32,40},{40,32},{48,56},{56,48},{64,72... | collective-permute-start | bytes 1769480 | tf_op jit(solution)/shard_map/ppermute | solution.py:390
  35.8 11.2 %collective-permute-start.1 = (f32[4,6,24,256]{3,2,1,0:T(8,128)S(1)}, f32[4,6,24,256]{3,2,1,0:T(8,128)S(1)}, u32[]{:S(2)}, u32[]{:S(2)}) collective-permute-start(f32[4,6,24,256]{3,2,1,0:T(8,128)S(1)} %get-tuple-element.35), channel_id=1, source_target_pairs={{8,16},{16,8},{24,32},{32,24},{40,48},{48,40},{56,64},{64,56},{72,... | collective-permute-start | bytes 1769480 | tf_op jit(solution)/shard_map/ppermute | solution.py:390
  52.7 0.6 copy-start
  53.4 0.8 copy-start.3
  54.2 0.7 copy-start.5
  54.9 0.7 copy-start.8
  55.6 0.7 copy-start.10
  56.2 6.6 %collective-permute-start.2 = (f32[4,24,128]{2,1,0:T(8,128)S(1)}, f32[4,24,128]{2,1,0:T(8,128)S(1)}, u32[]{:S(2)}, u32[]{:S(2)}) collective-permute-start(f32[4,24,128]{2,1,0:T(8,128)S(1)} %get-tuple-element.36), channel_id=1, source_target_pairs={{0,8},{8,0},{16,24},{24,16},{32,40},{40,32},{48,56},{56,48},{64,72... | collective-permute-start | bytes 147464 | tf_op jit(solution)/shard_map/ppermute | solution.py:390
  62.8 10.3 %collective-permute-start.4 = (f32[2,4,24,128]{3,2,1,0:T(8,128)S(1)}, f32[2,4,24,128]{3,2,1,0:T(8,128)S(1)}, u32[]{:S(2)}, u32[]{:S(2)}) collective-permute-start(f32[2,4,24,128]{3,2,1,0:T(8,128)S(1)} %maximum_select_fusion.pair), channel_id=1, source_target_pairs={{16,32},{24,40},{32,16},{40,24},{48,64},{56,72},{64,48},{72,56},{8... | collective-permute-start | bytes 294920 | tf_op jit(solution)/shard_map/ppermute | solution.py:390
  68.1 6.9 %collective-permute-start.3 = (f32[2,4,24,128]{3,2,1,0:T(8,128)S(1)}, f32[2,4,24,128]{3,2,1,0:T(8,128)S(1)}, u32[]{:S(2)}, u32[]{:S(2)}) collective-permute-start(f32[2,4,24,128]{3,2,1,0:T(8,128)S(1)} %maximum_select_fusion.pair), channel_id=1, source_target_pairs={{0,16},{8,24},{16,0},{24,8},{32,48},{40,56},{48,32},{56,40},{64,80... | collective-permute-start | bytes 294920 | tf_op jit(solution)/shard_map/ppermute | solution.py:390
  73.1 7.0 %collective-permute-start.5 = (f32[2,4,24,128]{3,2,1,0:T(8,128)S(1)}, f32[2,4,24,128]{3,2,1,0:T(8,128)S(1)}, u32[]{:S(2)}, u32[]{:S(2)}) collective-permute-start(f32[2,4,24,128]{3,2,1,0:T(8,128)S(1)} %collective-permute-done.4.near2), channel_id=1, source_target_pairs={{0,16},{8,24},{16,0},{24,8},{32,48},{40,56},{48,32},{56,40},{64,80... | collective-permute-start | bytes 294920 | tf_op jit(solution)/shard_map/ppermute | solution.py:390
  75.0 9.8 %collective-permute-start.6 = (f32[2,4,24,128]{3,2,1,0:T(8,128)S(1)}, f32[2,4,24,128]{3,2,1,0:T(8,128)S(1)}, u32[]{:S(2)}, u32[]{:S(2)}) collective-permute-start(f32[2,4,24,128]{3,2,1,0:T(8,128)S(1)} %collective-permute-done.3.near1), channel_id=1, source_target_pairs={{16,32},{24,40},{32,16},{40,24},{48,64},{56,72},{64,48},{72,56},{8... | collective-permute-start | bytes 294920 | tf_op jit(solution)/shard_map/ppermute | solution.py:390
  84.9 1.0 copy-start.9
  90.8 3.9 %collective-permute-start.7 = (f32[3,3,24,128]{3,2,1,0:T(8,128)S(1)}, f32[3,3,24,128]{3,2,1,0:T(8,128)S(1)}, u32[]{:S(2)}, u32[]{:S(2)}) collective-permute-start(f32[3,3,24,128]{3,2,1,0:T(8,128)S(1)} %get-tuple-element.39), channel_id=1, source_target_pairs={{0,8},{8,0},{16,24},{24,16},{32,40},{40,32},{48,56},{56,48},{64,72... | collective-permute-start | bytes 331784 | tf_op jit(solution)/shard_map/ppermute | solution.py:390
  92.7 6.1 %collective-permute-start.8 = (f32[3,3,24,128]{3,2,1,0:T(8,128)S(1)}, f32[3,3,24,128]{3,2,1,0:T(8,128)S(1)}, u32[]{:S(2)}, u32[]{:S(2)}) collective-permute-start(f32[3,3,24,128]{3,2,1,0:T(8,128)S(1)} %get-tuple-element.40), channel_id=1, source_target_pairs={{8,16},{16,8},{24,32},{32,24},{40,48},{48,40},{56,64},{64,56},{72,... | collective-permute-start | bytes 331784 | tf_op jit(solution)/shard_map/ppermute | solution.py:390
  98.8 0.9 copy-start.1
  99.7 1.0 copy-start.6
  100.6 28.9 %copy-start.2 = (f32[10,24,128]{2,1,0:T(8,128)S(1)}, f32[10,24,128]{2,1,0:T(8,128)}, u32[]{:S(2)}) copy-start(f32[10,24,128]{2,1,0:T(8,128)} %copy-done) | copy-start | bytes 368644
  100.6 28.9 %copy-start.4 = (f32[20,24,256]{2,1,0:T(8,128)S(1)}, f32[20,24,256]{2,1,0:T(8,128)}, u32[]{:S(2)}) copy-start(f32[20,24,256]{2,1,0:T(8,128)} %copy-done.3) | copy-start | bytes 1474564
  100.6 28.9 %copy-start.11 = (f32[10,24,128]{2,1,0:T(8,128)S(1)}, f32[10,24,128]{2,1,0:T(8,128)}, u32[]{:S(2)}) copy-start(f32[10,24,128]{2,1,0:T(8,128)} %copy-done.10) | copy-start | bytes 368644
  103.6 7.7 %collective-permute-start.9 = (f32[3,7,24,128]{3,2,1,0:T(8,128)S(1)}, f32[3,7,24,128]{3,2,1,0:T(8,128)S(1)}, u32[]{:S(2)}, u32[]{:S(2)}) collective-permute-start(f32[3,7,24,128]{3,2,1,0:T(8,128)S(1)} %get-tuple-element.47), channel_id=1, source_target_pairs={{0,8},{8,0},{16,24},{24,16},{32,40},{40,32},{48,56},{56,48},{64,72... | collective-permute-start | bytes 774152 | tf_op jit(solution)/shard_map/ppermute | solution.py:390
  109.4 7.6 %collective-permute-start.10 = (f32[3,7,24,128]{3,2,1,0:T(8,128)S(1)}, f32[3,7,24,128]{3,2,1,0:T(8,128)S(1)}, u32[]{:S(2)}, u32[]{:S(2)}) collective-permute-start(f32[3,7,24,128]{3,2,1,0:T(8,128)S(1)} %get-tuple-element.48), channel_id=1, source_target_pairs={{8,16},{16,8},{24,32},{32,24},{40,48},{48,40},{56,64},{64,56},{72,... | collective-permute-start | bytes 774152 | tf_op jit(solution)/shard_map/ppermute | solution.py:390
  117.8 11.7 %collective-permute-start.11 = (f32[3,11,24,128]{3,2,1,0:T(8,128)S(1)}, f32[3,11,24,128]{3,2,1,0:T(8,128)S(1)}, u32[]{:S(2)}, u32[]{:S(2)}) collective-permute-start(f32[3,11,24,128]{3,2,1,0:T(8,128)S(1)} %get-tuple-element.50), channel_id=1, source_target_pairs={{0,1},{1,0},{2,3},{3,2},{4,5},{5,4},{6,7},{7,6},{8,9},{9,8},{10,11... | collective-permute-start | bytes 1216520 | tf_op jit(solution)/shard_map/ppermute | solution.py:390
  120.3 9.2 %collective-permute-start.12 = (f32[3,11,24,128]{3,2,1,0:T(8,128)S(1)}, f32[3,11,24,128]{3,2,1,0:T(8,128)S(1)}, u32[]{:S(2)}, u32[]{:S(2)}) collective-permute-start(f32[3,11,24,128]{3,2,1,0:T(8,128)S(1)} %get-tuple-element.51), channel_id=1, source_target_pairs={{1,2},{2,1},{3,4},{4,3},{5,6},{6,5},{9,10},{10,9},{11,12},{12,11},... | collective-permute-start | bytes 1216520 | tf_op jit(solution)/shard_map/ppermute | solution.py:390
  136.2 5.0 %collective-permute-start.13 = (f32[4,24,128]{2,1,0:T(8,128)S(1)}, f32[4,24,128]{2,1,0:T(8,128)S(1)}, u32[]{:S(2)}, u32[]{:S(2)}) collective-permute-start(f32[4,24,128]{2,1,0:T(8,128)S(1)} %get-tuple-element.54), channel_id=1, source_target_pairs={{0,8},{8,0},{16,24},{24,16},{32,40},{40,32},{48,56},{56,48},{64,72... | collective-permute-start | bytes 147464 | tf_op jit(solution)/shard_map/ppermute | solution.py:390
  141.3 10.3 %collective-permute-start.15 = (f32[2,4,24,128]{3,2,1,0:T(8,128)S(1)}, f32[2,4,24,128]{3,2,1,0:T(8,128)S(1)}, u32[]{:S(2)}, u32[]{:S(2)}) collective-permute-start(f32[2,4,24,128]{3,2,1,0:T(8,128)S(1)} %maximum_select_fusion.1.pair), channel_id=1, source_target_pairs={{16,32},{24,40},{32,16},{40,24},{48,64},{56,72},{64,48},{72,56},{8... | collective-permute-start | bytes 294920 | tf_op jit(solution)/shard_map/ppermute | solution.py:390
  146.2 7.2 %collective-permute-start.14 = (f32[2,4,24,128]{3,2,1,0:T(8,128)S(1)}, f32[2,4,24,128]{3,2,1,0:T(8,128)S(1)}, u32[]{:S(2)}, u32[]{:S(2)}) collective-permute-start(f32[2,4,24,128]{3,2,1,0:T(8,128)S(1)} %maximum_select_fusion.1.pair), channel_id=1, source_target_pairs={{0,16},{8,24},{16,0},{24,8},{32,48},{40,56},{48,32},{56,40},{64,80... | collective-permute-start | bytes 294920 | tf_op jit(solution)/shard_map/ppermute | solution.py:390
  151.5 6.7 %collective-permute-start.16 = (f32[2,4,24,128]{3,2,1,0:T(8,128)S(1)}, f32[2,4,24,128]{3,2,1,0:T(8,128)S(1)}, u32[]{:S(2)}, u32[]{:S(2)}) collective-permute-start(f32[2,4,24,128]{3,2,1,0:T(8,128)S(1)} %collective-permute-done.15.near2), channel_id=1, source_target_pairs={{0,16},{8,24},{16,0},{24,8},{32,48},{40,56},{48,32},{56,40},{64,80... | collective-permute-start | bytes 294920 | tf_op jit(solution)/shard_map/ppermute | solution.py:390
  153.5 9.8 %collective-permute-start.17 = (f32[2,4,24,128]{3,2,1,0:T(8,128)S(1)}, f32[2,4,24,128]{3,2,1,0:T(8,128)S(1)}, u32[]{:S(2)}, u32[]{:S(2)}) collective-permute-start(f32[2,4,24,128]{3,2,1,0:T(8,128)S(1)} %collective-permute-done.14.near1), channel_id=1, source_target_pairs={{16,32},{24,40},{32,16},{40,24},{48,64},{56,72},{64,48},{72,56},{8... | collective-permute-start | bytes 294920 | tf_op jit(solution)/shard_map/ppermute | solution.py:390
  168.3 3.9 %collective-permute-start.18 = (f32[3,3,24,128]{3,2,1,0:T(8,128)S(1)}, f32[3,3,24,128]{3,2,1,0:T(8,128)S(1)}, u32[]{:S(2)}, u32[]{:S(2)}) collective-permute-start(f32[3,3,24,128]{3,2,1,0:T(8,128)S(1)} %get-tuple-element.57), channel_id=1, source_target_pairs={{0,8},{8,0},{16,24},{24,16},{32,40},{40,32},{48,56},{56,48},{64,72... | collective-permute-start | bytes 331784 | tf_op jit(solution)/shard_map/ppermute | solution.py:390
  170.2 6.1 %collective-permute-start.19 = (f32[3,3,24,128]{3,2,1,0:T(8,128)S(1)}, f32[3,3,24,128]{3,2,1,0:T(8,128)S(1)}, u32[]{:S(2)}, u32[]{:S(2)}) collective-permute-start(f32[3,3,24,128]{3,2,1,0:T(8,128)S(1)} %get-tuple-element.58), channel_id=1, source_target_pairs={{8,16},{16,8},{24,32},{32,24},{40,48},{48,40},{56,64},{64,56},{72,... | collective-permute-start | bytes 331784 | tf_op jit(solution)/shard_map/ppermute | solution.py:390

commit v4 on v3

--- a/solution.py
+++ b/solution.py
@@ -13,7 +13,7 @@
 HALO = 6
 LANES = 128
 UNROLL = (2, 4, 8, 8)
-PARAMS = pltpu.CompilerParams(vmem_limit_bytes=28 << 20)
+PARAMS = pltpu.CompilerParams(vmem_limit_bytes=12 << 20)
 
 
 def coupling_of(level):
@@ -120,8 +120,8 @@
     each_row(low, high, body, max(1, UNROLL[level] // 2))
 
 
-def from_zero(target, source, density, factor, level, period, rows, position, low, high, finer=None, reach=0):
-    i, j, count_x, count_y = position[0], position[1], position[2], position[3]
+def from_zero(target, source, density, factor, level, period, rows, position, low, high, finer=None, reach=0, group=1):
+    i, j, count_x, count_y = position[0] // group, position[1], position[2] // group, position[3]
     width = factor[0].shape[-1]
     lane = lax.broadcasted_iota(jnp.int32, (NZ, width), 1) % period
     inside_y = ((lane < 3 * period // 4) | (j > 0)) & ((lane < period // 2) | (lane >= 3 * period // 4) | (j < count_y - 1))
@@ -157,7 +157,7 @@
     each_row(low, high, body, UNROLL[level])
 
 
-def level_one_down(g1, v1, scratch, d1, f1, packed):
+def level_one_down(position, g1, v1, scratch, d1, f1, packed, edge):
     sweep(v1, scratch, g1, f1, 1, -1, 5)
     lane = lane_index()
     for c in range(C + 1):
@@ -173,6 +173,10 @@
                 total = part if total is None else total + part
             pair.append(0.25 * pair_sum(total, LANES))
         packed[c] = jnp.where(lane < LANES // 2, pair[0], pair[1])
+    count = edge.shape[0] // C
+    for c in range(C):
+        for r in range(count):
+            edge[c * count + r] = v1[0][c, (1 - position[4]) + (r - v1[1])]
 
 
 def rows_to_send(position, own, first, second):
@@ -222,7 +226,7 @@
     rows_to_send(position, own, first, second)
 
 
-def first_down_kernel(position, own, first, second, g0, d0, f0, v0, g1, d1, f1, v1, packed, field, field1):
+def first_down_kernel(position, own, first, second, g0, d0, f0, v0, g1, d1, f1, v1, packed, edge, field, field1):
     rows = own.shape[1]
 
     def store(c, at, value):
@@ -237,7 +241,7 @@
     sweep(b, a, g, f, 0, -5, rows + 5)
     coarse_source((g1, -2), b, g, d, 0, 2 * LANES, -2, rows // 2 + 2)
     from_zero((field1, -2), (g1, -2), (d1, -3), (f1, -3), 1, LANES, rows // 2, position, -2, rows // 2 + 2, d, 1)
-    level_one_down((g1, -2), (v1, -2), (field1, -2), (d1, -3), (f1, -3), packed)
+    level_one_down(position, (g1, -2), (v1, -2), (field1, -2), (d1, -3), (f1, -3), packed, edge)
 
 
 def side_kernel(position, own, first, second, tall, to_first, to_second):
@@ -255,7 +259,7 @@
             to_second[c, r] = jnp.where(low, two, one)
 
 
-def second_down_kernel(position, tall, first, second, g0, d0, f0, d1, f1, v0, g1, v1, packed, wide, field, field1):
+def second_down_kernel(position, tall, first, second, g0, d0, f0, d1, f1, v0, g1, v1, packed, edge, wide, field, field1):
     half = tall.shape[1] // 2
     halo = half - v0.shape[1] // 2 + HALO
     rows = 2 * (half - halo)
@@ -271,35 +275,34 @@
     sweep(b, a, g, f, 0, -5, rows + 5)
     coarse_source((g1, -2), b, g, d, 0, 2 * LANES, -2, rows // 2 + 2)
     first_sweep((field1, -2), (g1, -2), (f1, -3), 1, -2, rows // 2 + 2)
-    level_one_down((g1, -2), (v1, -2), (field1, -2), (d1, -3), (f1, -3), packed)
-
-
-def coarse_kernel(position, pair, near1, near2, far1, far2, v1, out, first, second, g2, d2, f2, g3, d3, f3, a, b, a3, b3):
+    level_one_down(position, (g1, -2), (v1, -2), (field1, -2), (d1, -3), (f1, -3), packed, edge)
+
+
+def coarse_kernel(position, mine, other, v1, out, first, second, g2, d2, f2, g3, d3, f3, a, b, a3, b3):
     lane = lane_index()
-    reach = 10
     odd, step = position[4], 1 - 2 * position[6]
-
-    def place(block, n):
-        for c in range(C + 1):
-            both = block[c]
-            other = pltpu.roll(both, LANES // 2, 1)
-            for q, value in ((0, jnp.where(lane < LANES // 2, both, other)), (1, jnp.where(lane < LANES // 2, other, both))):
-                if c < C:
-                    g2[c, 2 * n + q] = value
-                else:
-                    d2[2 * n + q] = value
-
-    for blocks, away in ((pair, 0), (near1, step), (near2, -step), (far1, 2 * step), (far2, -2 * step)):
-        for core in range(2):
-            place(blocks.at[core], 2 * away + (reach // 2 + core - odd))
+    count, reach = first.shape[1], 8
+    units = C + 1
+
+    for ref, core in ((mine, odd), (other, 1 - odd)):
+        for n, away in enumerate((0, step, -step, 2 * step, -2 * step)):
+            at = 4 * away + (2 * core + reach)
+            for c in range(units):
+                both = ref[n * units + c]
+                twin = pltpu.roll(both, LANES // 2, 1)
+                for q, value in ((0, jnp.where(lane < LANES // 2, both, twin)), (1, jnp.where(lane < LANES // 2, twin, both))):
+                    if c < C:
+                        g2[c, at + q] = value
+                    else:
+                        d2[at + q] = value
     g, d, f, u, w = (g2, -reach), (d2, -reach), (f2, -reach), (a, -reach), (b, -reach)
     h, e, k, s, t = (g3, -reach // 2), (d3, -reach // 2), (f3, -reach // 2), (a3, -reach // 2), (b3, -reach // 2)
-    from_zero(u, g, d, f, 2, LANES // 2, 2, position, -8, 10)
-    sweep(w, u, g, f, 2, -7, 9)
-    coarse_source(h, w, g, d, 2, LANES // 2, -3, 4)
-    from_zero(s, h, e, k, 3, LANES // 4, 1, position, -3, 4, d)
-    sweep(t, s, h, k, 3, -2, 3)
-    sweep(s, t, h, k, 3, -1, 2)
+    from_zero(u, g, d, f, 2, LANES // 2, 4, position, -8, 12, group=2)
+    sweep(w, u, g, f, 2, -7, 11)
+    coarse_source(h, w, g, d, 2, LANES // 2, -3, 5)
+    from_zero(s, h, e, k, 3, LANES // 4, 2, position, -3, 5, d, group=2)
+    sweep(t, s, h, k, 3, -2, 4)
+    sweep(s, t, h, k, 3, -1, 3)
 
     def correct(q):
         for c in range(C):
@@ -307,15 +310,19 @@
             for r in (q.double(), q.double() + 1):
                 b[c, index(w, r)] = row(w, c, r) + fine
 
-    each_row(-1, 2, correct, 3)
-    sweep(u, w, g, f, 2, -1, 3)
-    sweep(w, u, g, f, 2, 0, 2)
+    each_row(-1, 3, correct, 4)
+    sweep(u, w, g, f, 2, -1, 5)
+    sweep(w, u, g, f, 2, 0, 4)
     for c in range(C):
         for q in (0, 1):
-            fine = spread(row(w, c, q), LANES)
+            fine = spread(b[c, 2 * odd + (q + reach)], LANES)
             for r in (2 * q, 2 * q + 1):
                 out[c, r] = v1[c, r + 2] + fine
-    rows_to_send(position, out, first, second)
+        for r, q in enumerate((0, odd, 1)):
+            fine = spread(b[c, 2 * (1 - odd) + (reach + q)], LANES)
+            first[c, r] = other[5 * units + c * count + r] + fine
+        for r in range(count):
+            second[c, r] = out[c, odd * (out.shape[1] - count) + r]
 
 
 def climb(position, own, first, second, g0, f0, v0, g1, f1, wide, u, w, field, emit):
@@ -408,9 +415,10 @@
         scalars=1,
     )
     fine, mid = (C, R0, NZ, W), (C, R1 + 4, NZ, LANES)
-    g0, d0, f0, v0, g1, d1, f1, v1, packed = call(
+    sends = [(C + 1, NZ, LANES), (C * (R1 - 1), NZ, LANES)]
+    g0, d0, f0, v0, g1, d1, f1, *down = call(
         first_down_kernel,
-        [fine, fine[1:], fine[1:], fine, mid, (R1 + 6, NZ, LANES), (R1 + 6, NZ, LANES), mid, (C + 1, NZ, LANES)],
+        [fine, fine[1:], fine[1:], fine, mid, (R1 + 6, NZ, LANES), (R1 + 6, NZ, LANES), mid, *sends],
         [fine, mid],
         position,
         own,
@@ -419,24 +427,22 @@
         scalars=1,
     )
 
-    def coarse(packed, v1):
-        partner = swap(packed, "gx", True)
-        pair = jnp.where(i % 2 == 0, jnp.stack([packed, partner]), jnp.stack([partner, packed]))
-        near = [swap(pair, "gx", first, 2) for first in (True, False)]
+    def coarse(v1, packed, edge):
+        near = [swap(packed, "gx", first, 2) for first in (True, False)]
         far = [swap(near[1], "gx", True, 2), swap(near[0], "gx", False, 2)]
-        two, three = (C, 22, NZ, LANES), (C, 11, NZ, LANES)
+        mine = jnp.concatenate([packed, *near, *far, edge])
+        two, three = (C, 20, NZ, LANES), (C, 10, NZ, LANES)
         out, first, second = call(
             coarse_kernel,
             [(C, R1, NZ, LANES)] + [(C, R1 - 1, NZ, LANES)] * 2,
             [two, two[1:], two[1:], three, three[1:], three[1:], two, two, three, three],
             position,
-            pair,
-            *near,
-            *far,
+            mine,
+            swap(mine, "gx", True),
             v1,
             scalars=1,
         )
-        return out, swap(first, "gx", True), swap(second, "gx", False)
+        return out, first, swap(second, "gx", False)
 
     middle = (C, R1 + 6, NZ, LANES)
     reach = HALO + 1
@@ -445,7 +451,7 @@
         [(C, rows, NZ, LANES), (C, reach, NZ, LANES), (C, reach, NZ, LANES)],
         [middle, middle, middle, fine, fine],
         position,
-        *coarse(packed, v1),
+        *coarse(*down),
         g0,
         f0,
         v0,
@@ -464,9 +470,9 @@
         swap(second, "gx", False),
         scalars=1,
     )
-    v0, g1, v1, packed = call(
+    v0, g1, *down = call(
         second_down_kernel,
-        [fine, mid, mid, (C + 1, NZ, LANES)],
+        [fine, mid, mid, *sends],
         [(C, 2 * half, NZ, W), fine, mid],
         position,
         tall,
@@ -484,7 +490,7 @@
         [(blocks, C * depth, rows, LANES)],
         [middle, middle, middle, fine, fine, (C, NZ * rows, LANES)],
         position,
-        *coarse(packed, v1),
+        *coarse(*down),
         g0,
         f0,
         v0,

time: 201 us -> 185 us (0.920)
  waiting for transfers between devices: 71.9 us -> 65.6 us
  local copies, waits for them, and re-layouts: 8.27 us -> 2.01 us
  Pallas kernels: 31.6 us -> 28.5 us
    unnamed x26 -> x14, local copies, waits for them, and re-layouts: 8.19 us -> 1.91 us
    ppermute x20 -> x18, waiting for transfers between devices: 48.8 us -> 42.6 us  [swap(): return lax.ppermute(values, axis, pairs)]
    pallas_call x10, Pallas kernels: 31.6 us -> 28.5 us  [call(): pl.pallas_call(kernel, out_shape=[shape(s) for s in outs], in_specs=specs...]
    ppermute x20 -> x18, starting transfers between devices: 60.8 us -> 60.9 us  [swap(): return lax.ppermute(values, axis, pairs)]
  transfers between devices with their start and end apart: 21 -> 19, of which waited for: 12 -> 14; matrix products, arithmetic and copies ran while one was open for 0% -> 0% of each run, Pallas kernels for 0% -> 0%
where the time goes in v4:
time: 185 us; the launch traced here: 182 us
  starting transfers between devices  68 us (37%)
  waiting for transfers between devices  65.6 us (35%)
  Pallas kernels  28.5 us (15%)
  blocking collectives  17.5 us (9%)
  local copies, waits for them, and re-layouts  2.01 us (1%)
    ppermute x18, starting transfers between devices, swap(): return lax.ppermute(values, axis, pairs)  60.9 us
    ppermute x18, waiting for transfers between devices, swap(): return lax.ppermute(values, axis, pairs)  42.6 us
    pallas_call x10, Pallas kernels, call(): pl.pallas_call(kernel, out_shape=[shape(s) for s in outs], in_specs=specs...  28.5 us
    all_to_all x1, waiting for transfers between devices, shards(): taken = lax.all_to_all(sent, 'gz', 0, 0)  23 us
    all_to_all x1, blocking collectives, shards(): lax.all_to_all(sent, 'gz', 0, 0)  17.5 us
    all_to_all x1, starting transfers between devices, shards(): taken = lax.all_to_all(sent, 'gz', 0, 0)  7.1 us
  transfers between devices with their start and end apart: 19, of which 14 were waited for; matrix products, arithmetic and copies ran while one was open for 0% of the time, Pallas kernels for 0%

profile of v4, /device:TPU:198, one launch (start us, length us, event | category | flops | bytes accessed | tf_op | source)
XLA Modules:
  0.0 182.0 jit_solution(9708387845837155250)
XLA Ops:
  0.0 0.0 copy-start
  0.0 1.0 copy-done
  1.0 0.0 copy-start.1
  1.0 0.9 copy-done.1
  1.9 0.9 pack_kernel.1
  2.8 7.1 %all-to-all-start = ((f32[8,12,8,256]{3,2,1,0:T(8,128)}), f32[8,12,8,256]{3,2,1,0:T(8,128)S(1)}, u32[]{:S(2)}, u32[]{:S(2)}) async-start(f32[8,12,8,256]{3,2,1,0:T(8,128)} %pack_kernel.1), calls=%async_computation | async-start | bytes 1572864 | tf_op jit(solution)/shard_map/all_to_all | solution.py:408
  9.9 0.1 stack.23.position
  10.0 23.0 %all-to-all-done.taken = f32[8,12,8,256]{3,2,1,0:T(8,128)S(1)} async-done(((f32[8,12,8,256]{3,2,1,0:T(8,128)}), f32[8,12,8,256]{3,2,1,0:T(8,128)S(1)}, u32[]{:S(2)}, u32[]{:S(2)}) %all-to-all-start) | async-done | bytes 786464 | tf_op jit(solution)/shard_map/all_to_all | solution.py:408
  33.0 0.8 unpack_kernel.1
  33.8 1.9 %collective-permute-start = (f32[4,6,24,256]{3,2,1,0:T(8,128)S(1)}, f32[4,6,24,256]{3,2,1,0:T(8,128)S(1)}, u32[]{:S(2)}, u32[]{:S(2)}) collective-permute-start(f32[4,6,24,256]{3,2,1,0:T(8,128)S(1)} %get-tuple-element.36), channel_id=1, source_target_pairs={{0,8},{8,0},{16,24},{24,16},{32,40},{40,32},{48,56},{56,48},{64,72... | collective-permute-start | bytes 1769480 | tf_op jit(solution)/shard_map/ppermute | solution.py:397
  35.8 2.8 %collective-permute-start.1 = (f32[4,6,24,256]{3,2,1,0:T(8,128)S(1)}, f32[4,6,24,256]{3,2,1,0:T(8,128)S(1)}, u32[]{:S(2)}, u32[]{:S(2)}) collective-permute-start(f32[4,6,24,256]{3,2,1,0:T(8,128)S(1)} %get-tuple-element.37), channel_id=1, source_target_pairs={{8,16},{16,8},{24,32},{32,24},{40,48},{48,40},{56,64},{64,56},{72,... | collective-permute-start | bytes 1769480 | tf_op jit(solution)/shard_map/ppermute | solution.py:397
  38.6 0.0 collective-permute-done.first
  38.6 8.3 %collective-permute-done.1.second = f32[4,6,24,256]{3,2,1,0:T(8,128)S(1)} collective-permute-done((f32[4,6,24,256]{3,2,1,0:T(8,128)S(1)}, f32[4,6,24,256]{3,2,1,0:T(8,128)S(1)}, u32[]{:S(2)}, u32[]{:S(2)}) %collective-permute-start.1) | collective-permute-done | bytes 589856 | tf_op jit(solution)/shard_map/ppermute | solution.py:397
  47.0 5.8 %first_down_kernel.1 = (f32[3,20,24,256]{3,2,1,0:T(8,128)S(1)}, f32[20,24,256]{2,1,0:T(8,128)S(1)}, f32[20,24,256]{2,1,0:T(8,128)S(1)}, f32[3,20,24,256]{3,2,1,0...) custom-call(s32[7]{0:T(128)S(1)} %stack.23.position, ...), custom_call_target="tpu_custom_call" | custom-call | tf_op jit(solution)/shard_map/first_down_kernel/pallas_call | solution.py:378
  52.7 8.7 %collective-permute-start.3 = (f32[4,24,128]{2,1,0:T(8,128)S(1)}, f32[4,24,128]{2,1,0:T(8,128)S(1)}, u32[]{:S(2)}, u32[]{:S(2)}) collective-permute-start(f32[4,24,128]{2,1,0:T(8,128)S(1)} %get-tuple-element.38), channel_id=1, source_target_pairs={{16,32},{24,40},{32,16},{40,24},{48,64},{56,72},{64,48},{72,56},{8... | collective-permute-start | bytes 147464 | tf_op jit(solution)/shard_map/ppermute | solution.py:397
  61.5 1.9 %collective-permute-start.2 = (f32[4,24,128]{2,1,0:T(8,128)S(1)}, f32[4,24,128]{2,1,0:T(8,128)S(1)}, u32[]{:S(2)}, u32[]{:S(2)}) collective-permute-start(f32[4,24,128]{2,1,0:T(8,128)S(1)} %get-tuple-element.38), channel_id=1, source_target_pairs={{0,16},{8,24},{16,0},{24,8},{32,48},{40,56},{48,32},{56,40},{64,80... | collective-permute-start | bytes 147464 | tf_op jit(solution)/shard_map/ppermute | solution.py:397
  63.4 0.1 collective-permute-done.3
  63.5 3.8 %collective-permute-start.4 = (f32[4,24,128]{2,1,0:T(8,128)S(1)}, f32[4,24,128]{2,1,0:T(8,128)S(1)}, u32[]{:S(2)}, u32[]{:S(2)}) collective-permute-start(f32[4,24,128]{2,1,0:T(8,128)S(1)} %collective-permute-done.3), channel_id=1, source_target_pairs={{0,16},{8,24},{16,0},{24,8},{32,48},{40,56},{48,32},{56,40},{64,80... | collective-permute-start | bytes 147464 | tf_op jit(solution)/shard_map/ppermute | solution.py:397
  67.4 0.1 collective-permute-done.2
  67.5 5.2 %collective-permute-start.5 = (f32[4,24,128]{2,1,0:T(8,128)S(1)}, f32[4,24,128]{2,1,0:T(8,128)S(1)}, u32[]{:S(2)}, u32[]{:S(2)}) collective-permute-start(f32[4,24,128]{2,1,0:T(8,128)S(1)} %collective-permute-done.2), channel_id=1, source_target_pairs={{16,32},{24,40},{32,16},{40,24},{48,64},{56,72},{64,48},{72,56},{8... | collective-permute-start | bytes 147464 | tf_op jit(solution)/shard_map/ppermute | solution.py:397
  72.7 0.0 collective-permute-done.4
  72.8 4.0 %collective-permute-done.5 = f32[4,24,128]{2,1,0:T(8,128)S(1)} collective-permute-done((f32[4,24,128]{2,1,0:T(8,128)S(1)}, f32[4,24,128]{2,1,0:T(8,128)S(1)}, u32[]{:S(2)}, u32[]{:S(2)}) %collective-permute-start.5) | collective-permute-done | bytes 49184 | tf_op jit(solution)/shard_map/ppermute | solution.py:397
  76.8 1.9 %collective-permute-start.6 = (f32[29,24,128]{2,1,0:T(8,128)S(1)}, f32[29,24,128]{2,1,0:T(8,128)S(1)}, u32[]{:S(2)}, u32[]{:S(2)}) collective-permute-start(f32[29,24,128]{2,1,0:T(8,128)S(1)} %constant_dynamic-update-slice_fusion.mine), channel_id=1, source_target_pairs={{0,8},{8,0},{16,24},{24,16},{32,40},{40,32},{48,56},{56,48},{64,72... | collective-permute-start | bytes 1069064 | tf_op jit(solution)/shard_map/ppermute | solution.py:397
  78.7 1.6 collective-permute-done.6.other
  80.3 3.4 %coarse_kernel.2 = (f32[3,4,24,128]{3,2,1,0:T(8,128)S(1)}, f32[3,3,24,128]{3,2,1,0:T(8,128)S(1)}, f32[3,3,24,128]{3,2,1,0:T(8,128)S(1)}) custom-call(s32[7]{0:T(128)S(1)} %stack.23.position, f32[29,24,128]{2,1,0:T(8,128)S(1)} %constant_dynamic-update-slice_fusion.mine, f32[29,24,128]{2,1,0:T(8,128)S(1)} %collective-permute-done.6.other, ...), custom_call_target="tpu_custom_call" | custom-call | tf_op jit(solution)/shard_map/coarse_kernel/pallas_call | solution.py:378
  83.8 1.9 %collective-permute-start.7 = (f32[3,3,24,128]{3,2,1,0:T(8,128)S(1)}, f32[3,3,24,128]{3,2,1,0:T(8,128)S(1)}, u32[]{:S(2)}, u32[]{:S(2)}) collective-permute-start(f32[3,3,24,128]{3,2,1,0:T(8,128)S(1)} %get-tuple-element.43), channel_id=1, source_target_pairs={{8,16},{16,8},{24,32},{32,24},{40,48},{48,40},{56,64},{64,56},{72,... | collective-permute-start | bytes 331784 | tf_op jit(solution)/shard_map/ppermute | solution.py:397
  85.7 4.1 %collective-permute-done.7.right = f32[3,3,24,128]{3,2,1,0:T(8,128)S(1)} collective-permute-done((f32[3,3,24,128]{3,2,1,0:T(8,128)S(1)}, f32[3,3,24,128]{3,2,1,0:T(8,128)S(1)}, u32[]{:S(2)}, u32[]{:S(2)}) %collective-permute-start.7) | collective-permute-done | bytes 110624 | tf_op jit(solution)/shard_map/ppermute | solution.py:397
  89.8 3.0 %first_up_kernel.1 = (f32[3,8,24,128]{3,2,1,0:T(8,128)S(1)}, f32[3,7,24,128]{3,2,1,0:T(8,128)S(1)}, f32[3,7,24,128]{3,2,1,0:T(8,128)S(1)}) custom-call(s32[7]{0:T(128)S(1)} %stack.23.position, f32[3,4,24,128]{3,2,1,0:T(8,128)S(1)} %get-tuple-element.41.own, f32[3,3,24,128]{3,2,1,0:T(8,128)S(1)} %get-tuple-element.42.left, ...), custom_call_target="tpu_custom_call" | custom-call | tf_op jit(solution)/shard_map/first_up_kernel/pallas_call | solution.py:378
  92.8 5.4 %collective-permute-start.8 = (f32[3,7,24,128]{3,2,1,0:T(8,128)S(1)}, f32[3,7,24,128]{3,2,1,0:T(8,128)S(1)}, u32[]{:S(2)}, u32[]{:S(2)}) collective-permute-start(f32[3,7,24,128]{3,2,1,0:T(8,128)S(1)} %get-tuple-element.50), channel_id=1, source_target_pairs={{0,8},{8,0},{16,24},{24,16},{32,40},{40,32},{48,56},{56,48},{64,72... | collective-permute-start | bytes 774152 | tf_op jit(solution)/shard_map/ppermute | solution.py:397
  98.2 1.9 %collective-permute-start.9 = (f32[3,7,24,128]{3,2,1,0:T(8,128)S(1)}, f32[3,7,24,128]{3,2,1,0:T(8,128)S(1)}, u32[]{:S(2)}, u32[]{:S(2)}) collective-permute-start(f32[3,7,24,128]{3,2,1,0:T(8,128)S(1)} %get-tuple-element.51), channel_id=1, source_target_pairs={{8,16},{16,8},{24,32},{32,24},{40,48},{48,40},{56,64},{64,56},{72,... | collective-permute-start | bytes 774152 | tf_op jit(solution)/shard_map/ppermute | solution.py:397
  100.1 0.0 collective-permute-done.8.first
  100.1 5.7 %collective-permute-done.9.second = f32[3,7,24,128]{3,2,1,0:T(8,128)S(1)} collective-permute-done((f32[3,7,24,128]{3,2,1,0:T(8,128)S(1)}, f32[3,7,24,128]{3,2,1,0:T(8,128)S(1)}, u32[]{:S(2)}, u32[]{:S(2)}) %collective-permute-start.9) | collective-permute-done | bytes 258080 | tf_op jit(solution)/shard_map/ppermute | solution.py:397
  105.8 0.8 side_kernel.1
  106.6 2.5 %collective-permute-start.10 = (f32[3,11,24,128]{3,2,1,0:T(8,128)S(1)}, f32[3,11,24,128]{3,2,1,0:T(8,128)S(1)}, u32[]{:S(2)}, u32[]{:S(2)}) collective-permute-start(f32[3,11,24,128]{3,2,1,0:T(8,128)S(1)} %get-tuple-element.53), channel_id=1, source_target_pairs={{0,1},{1,0},{2,3},{3,2},{4,5},{5,4},{6,7},{7,6},{8,9},{9,8},{10,11... | collective-permute-start | bytes 1216520 | tf_op jit(solution)/shard_map/ppermute | solution.py:397
  109.1 0.7 collective-permute-start.11
  109.8 8.5 %collective-permute-done.10.first = f32[3,11,24,128]{3,2,1,0:T(8,128)S(1)} collective-permute-done((f32[3,11,24,128]{3,2,1,0:T(8,128)S(1)}, f32[3,11,24,128]{3,2,1,0:T(8,128)S(1)}, u32[]{:S(2)}, u32[]{:S(2)}) %collective-permute-start.10) | collective-permute-done | bytes 405536 | tf_op jit(solution)/shard_map/ppermute | solution.py:397
  118.3 0.0 collective-permute-done.11.second
  118.3 6.7 %second_down_kernel.1 = (f32[3,20,24,256]{3,2,1,0:T(8,128)S(1)}, f32[3,8,24,128]{3,2,1,0:T(8,128)S(1)}, f32[3,8,24,128]{3,2,1,0:T(8,128)S(1)}, f32[4,24,128]{2,1,0:T(8,128)S(1)}, f32[9,24,128]{2,1,0:T(8,128)S(1)}) custom-call(s32[7]{0:T(128)S(1)} %stack.23.position, f32[3,22,24,128]{3,2,1,0:T(8,128)S(1)} %get-tuple-element.52.tall, ...), custom_call_target="tpu_custom_call" | custom-call | tf_op jit(solution)/shard_map/second_down_kernel/pallas_call | solution.py:378
  125.0 7.4 %collective-permute-start.13 = (f32[4,24,128]{2,1,0:T(8,128)S(1)}, f32[4,24,128]{2,1,0:T(8,128)S(1)}, u32[]{:S(2)}, u32[]{:S(2)}) collective-permute-start(f32[4,24,128]{2,1,0:T(8,128)S(1)} %get-tuple-element.57), channel_id=1, source_target_pairs={{16,32},{24,40},{32,16},{40,24},{48,64},{56,72},{64,48},{72,56},{8... | collective-permute-start | bytes 147464 | tf_op jit(solution)/shard_map/ppermute | solution.py:397
  132.4 1.9 %collective-permute-start.12 = (f32[4,24,128]{2,1,0:T(8,128)S(1)}, f32[4,24,128]{2,1,0:T(8,128)S(1)}, u32[]{:S(2)}, u32[]{:S(2)}) collective-permute-start(f32[4,24,128]{2,1,0:T(8,128)S(1)} %get-tuple-element.57), channel_id=1, source_target_pairs={{0,16},{8,24},{16,0},{24,8},{32,48},{40,56},{48,32},{56,40},{64,80... | collective-permute-start | bytes 147464 | tf_op jit(solution)/shard_map/ppermute | solution.py:397
  134.3 0.1 collective-permute-done.13
  134.5 3.8 %collective-permute-start.14 = (f32[4,24,128]{2,1,0:T(8,128)S(1)}, f32[4,24,128]{2,1,0:T(8,128)S(1)}, u32[]{:S(2)}, u32[]{:S(2)}) collective-permute-start(f32[4,24,128]{2,1,0:T(8,128)S(1)} %collective-permute-done.13), channel_id=1, source_target_pairs={{0,16},{8,24},{16,0},{24,8},{32,48},{40,56},{48,32},{56,40},{64,80... | collective-permute-start | bytes 147464 | tf_op jit(solution)/shard_map/ppermute | solution.py:397
  138.3 0.1 collective-permute-done.12
  138.4 5.2 %collective-permute-start.15 = (f32[4,24,128]{2,1,0:T(8,128)S(1)}, f32[4,24,128]{2,1,0:T(8,128)S(1)}, u32[]{:S(2)}, u32[]{:S(2)}) collective-permute-start(f32[4,24,128]{2,1,0:T(8,128)S(1)} %collective-permute-done.12), channel_id=1, source_target_pairs={{16,32},{24,40},{32,16},{40,24},{48,64},{56,72},{64,48},{72,56},{8... | collective-permute-start | bytes 147464 | tf_op jit(solution)/shard_map/ppermute | solution.py:397
  143.7 0.0 collective-permute-done.14
  143.7 4.0 %collective-permute-done.15 = f32[4,24,128]{2,1,0:T(8,128)S(1)} collective-permute-done((f32[4,24,128]{2,1,0:T(8,128)S(1)}, f32[4,24,128]{2,1,0:T(8,128)S(1)}, u32[]{:S(2)}, u32[]{:S(2)}) %collective-permute-start.15) | collective-permute-done | bytes 49184 | tf_op jit(solution)/shard_map/ppermute | solution.py:397
  147.7 1.9 %collective-permute-start.16 = (f32[29,24,128]{2,1,0:T(8,128)S(1)}, f32[29,24,128]{2,1,0:T(8,128)S(1)}, u32[]{:S(2)}, u32[]{:S(2)}) collective-permute-start(f32[29,24,128]{2,1,0:T(8,128)S(1)} %constant_dynamic-update-slice_fusion.6.mine), channel_id=1, source_target_pairs={{0,8},{8,0},{16,24},{24,16},{32,40},{40,32},{48,56},{56,48},{64,72... | collective-permute-start | bytes 1069064 | tf_op jit(solution)/shard_map/ppermute | solution.py:397
  149.6 1.6 collective-permute-done.16.other
  151.3 3.4 %coarse_kernel.3 = (f32[3,4,24,128]{3,2,1,0:T(8,128)S(1)}, f32[3,3,24,128]{3,2,1,0:T(8,128)S(1)}, f32[3,3,24,128]{3,2,1,0:T(8,128)S(1)}) custom-call(s32[7]{0:T(128)S(1)} %stack.23.position, f32[29,24,128]{2,1,0:T(8,128)S(1)} %constant_dynamic-update-slice_fusion.6.mine, f32[29,24,128]{2,1,0:T(8,128)S(1)} %collective-permute-done.16.other, ...), custom_call_target="tpu_custom_call" | custom-call | tf_op jit(solution)/shard_map/coarse_kernel/pallas_call | solution.py:378
  154.7 1.9 %collective-permute-start.17 = (f32[3,3,24,128]{3,2,1,0:T(8,128)S(1)}, f32[3,3,24,128]{3,2,1,0:T(8,128)S(1)}, u32[]{:S(2)}, u32[]{:S(2)}) collective-permute-start(f32[3,3,24,128]{3,2,1,0:T(8,128)S(1)} %get-tuple-element.62), channel_id=1, source_target_pairs={{8,16},{16,8},{24,32},{32,24},{40,48},{48,40},{56,64},{64,56},{72,... | collective-permute-start | bytes 331784 | tf_op jit(solution)/shard_map/ppermute | solution.py:397
  156.6 4.1 %collective-permute-done.17.right = f32[3,3,24,128]{3,2,1,0:T(8,128)S(1)} collective-permute-done((f32[3,3,24,128]{3,2,1,0:T(8,128)S(1)}, f32[3,3,24,128]{3,2,1,0:T(8,128)S(1)}, u32[]{:S(2)}, u32[]{:S(2)}) %collective-permute-start.17) | collective-permute-done | bytes 110624 | tf_op jit(solution)/shard_map/ppermute | solution.py:397
  160.8 3.0 %last_up_kernel.1 = f32[8,9,8,128]{3,2,1,0:T(8,128)S(1)} custom-call(s32[7]{0:T(128)S(1)} %stack.23.position, f32[3,4,24,128]{3,2,1,0:T(8,128)S(1)} %get-tuple-element.60.own, f32[3,3,24,128]{3,2,1,0:T(8,128)S(1)} %get-tuple-element.61.left, f32[3,3,24,128]{3,2,1,0:T(8,128)S(1)} %collective-permute-done.17.right, ...), custom_call_target="tpu_custom_call" | custom-call | tf_op jit(solution)/shard_map/last_up_kernel/pallas_call | solution.py:378
  163.7 17.5 %all_to_all.10.taken = f32[8,9,8,128]{3,2,1,0:T(8,128)S(1)} all-to-all(f32[8,9,8,128]{3,2,1,0:T(8,128)S(1)} %last_up_kernel.1), channel_id=1, replica_groups=mesh['gx'=64,'gz'=8] {'gz'}, dimensions={0} | all-to-all | bytes 589824 | tf_op jit(solution)/shard_map/all_to_all | solution.py:501
  181.3 0.7 join_kernel.1
  (12 shorter events, 0.1 us)
Async XLA Ops:
  0.0 1.0 copy-start
  1.0 0.9 copy-start.1
  2.8 30.2 %all-to-all-start = ((f32[8,12,8,256]{3,2,1,0:T(8,128)}), f32[8,12,8,256]{3,2,1,0:T(8,128)S(1)}, u32[]{:S(2)}, u32[]{:S(2)}) async-start(f32[8,12,8,256]{3,2,1,0:T(8,128)} %pack_kernel.1), calls=%async_computation | async-start | bytes 1572864 | tf_op jit(solution)/shard_map/all_to_all | solution.py:408
  33.8 4.8 %collective-permute-start = (f32[4,6,24,256]{3,2,1,0:T(8,128)S(1)}, f32[4,6,24,256]{3,2,1,0:T(8,128)S(1)}, u32[]{:S(2)}, u32[]{:S(2)}) collective-permute-start(f32[4,6,24,256]{3,2,1,0:T(8,128)S(1)} %get-tuple-element.36), channel_id=1, source_target_pairs={{0,8},{8,0},{16,24},{24,16},{32,40},{40,32},{48,56},{56,48},{64,72... | collective-permute-start | bytes 1769480 | tf_op jit(solution)/shard_map/ppermute | solution.py:397
  35.8 11.2 %collective-permute-start.1 = (f32[4,6,24,256]{3,2,1,0:T(8,128)S(1)}, f32[4,6,24,256]{3,2,1,0:T(8,128)S(1)}, u32[]{:S(2)}, u32[]{:S(2)}) collective-permute-start(f32[4,6,24,256]{3,2,1,0:T(8,128)S(1)} %get-tuple-element.37), channel_id=1, source_target_pairs={{8,16},{16,8},{24,32},{32,24},{40,48},{48,40},{56,64},{64,56},{72,... | collective-permute-start | bytes 1769480 | tf_op jit(solution)/shard_map/ppermute | solution.py:397
  52.7 10.8 %collective-permute-start.3 = (f32[4,24,128]{2,1,0:T(8,128)S(1)}, f32[4,24,128]{2,1,0:T(8,128)S(1)}, u32[]{:S(2)}, u32[]{:S(2)}) collective-permute-start(f32[4,24,128]{2,1,0:T(8,128)S(1)} %get-tuple-element.38), channel_id=1, source_target_pairs={{16,32},{24,40},{32,16},{40,24},{48,64},{56,72},{64,48},{72,56},{8... | collective-permute-start | bytes 147464 | tf_op jit(solution)/shard_map/ppermute | solution.py:397
  61.5 6.0 %collective-permute-start.2 = (f32[4,24,128]{2,1,0:T(8,128)S(1)}, f32[4,24,128]{2,1,0:T(8,128)S(1)}, u32[]{:S(2)}, u32[]{:S(2)}) collective-permute-start(f32[4,24,128]{2,1,0:T(8,128)S(1)} %get-tuple-element.38), channel_id=1, source_target_pairs={{0,16},{8,24},{16,0},{24,8},{32,48},{40,56},{48,32},{56,40},{64,80... | collective-permute-start | bytes 147464 | tf_op jit(solution)/shard_map/ppermute | solution.py:397
  63.5 9.2 %collective-permute-start.4 = (f32[4,24,128]{2,1,0:T(8,128)S(1)}, f32[4,24,128]{2,1,0:T(8,128)S(1)}, u32[]{:S(2)}, u32[]{:S(2)}) collective-permute-start(f32[4,24,128]{2,1,0:T(8,128)S(1)} %collective-permute-done.3), channel_id=1, source_target_pairs={{0,16},{8,24},{16,0},{24,8},{32,48},{40,56},{48,32},{56,40},{64,80... | collective-permute-start | bytes 147464 | tf_op jit(solution)/shard_map/ppermute | solution.py:397
  67.5 9.3 %collective-permute-start.5 = (f32[4,24,128]{2,1,0:T(8,128)S(1)}, f32[4,24,128]{2,1,0:T(8,128)S(1)}, u32[]{:S(2)}, u32[]{:S(2)}) collective-permute-start(f32[4,24,128]{2,1,0:T(8,128)S(1)} %collective-permute-done.2), channel_id=1, source_target_pairs={{16,32},{24,40},{32,16},{40,24},{48,64},{56,72},{64,48},{72,56},{8... | collective-permute-start | bytes 147464 | tf_op jit(solution)/shard_map/ppermute | solution.py:397
  76.8 3.6 %collective-permute-start.6 = (f32[29,24,128]{2,1,0:T(8,128)S(1)}, f32[29,24,128]{2,1,0:T(8,128)S(1)}, u32[]{:S(2)}, u32[]{:S(2)}) collective-permute-start(f32[29,24,128]{2,1,0:T(8,128)S(1)} %constant_dynamic-update-slice_fusion.mine), channel_id=1, source_target_pairs={{0,8},{8,0},{16,24},{24,16},{32,40},{40,32},{48,56},{56,48},{64,72... | collective-permute-start | bytes 1069064 | tf_op jit(solution)/shard_map/ppermute | solution.py:397
  83.8 6.1 %collective-permute-start.7 = (f32[3,3,24,128]{3,2,1,0:T(8,128)S(1)}, f32[3,3,24,128]{3,2,1,0:T(8,128)S(1)}, u32[]{:S(2)}, u32[]{:S(2)}) collective-permute-start(f32[3,3,24,128]{3,2,1,0:T(8,128)S(1)} %get-tuple-element.43), channel_id=1, source_target_pairs={{8,16},{16,8},{24,32},{32,24},{40,48},{48,40},{56,64},{64,56},{72,... | collective-permute-start | bytes 331784 | tf_op jit(solution)/shard_map/ppermute | solution.py:397
  92.8 7.3 %collective-permute-start.8 = (f32[3,7,24,128]{3,2,1,0:T(8,128)S(1)}, f32[3,7,24,128]{3,2,1,0:T(8,128)S(1)}, u32[]{:S(2)}, u32[]{:S(2)}) collective-permute-start(f32[3,7,24,128]{3,2,1,0:T(8,128)S(1)} %get-tuple-element.50), channel_id=1, source_target_pairs={{0,8},{8,0},{16,24},{24,16},{32,40},{40,32},{48,56},{56,48},{64,72... | collective-permute-start | bytes 774152 | tf_op jit(solution)/shard_map/ppermute | solution.py:397
  98.2 7.6 %collective-permute-start.9 = (f32[3,7,24,128]{3,2,1,0:T(8,128)S(1)}, f32[3,7,24,128]{3,2,1,0:T(8,128)S(1)}, u32[]{:S(2)}, u32[]{:S(2)}) collective-permute-start(f32[3,7,24,128]{3,2,1,0:T(8,128)S(1)} %get-tuple-element.51), channel_id=1, source_target_pairs={{8,16},{16,8},{24,32},{32,24},{40,48},{48,40},{56,64},{64,56},{72,... | collective-permute-start | bytes 774152 | tf_op jit(solution)/shard_map/ppermute | solution.py:397
  106.6 11.7 %collective-permute-start.10 = (f32[3,11,24,128]{3,2,1,0:T(8,128)S(1)}, f32[3,11,24,128]{3,2,1,0:T(8,128)S(1)}, u32[]{:S(2)}, u32[]{:S(2)}) collective-permute-start(f32[3,11,24,128]{3,2,1,0:T(8,128)S(1)} %get-tuple-element.53), channel_id=1, source_target_pairs={{0,1},{1,0},{2,3},{3,2},{4,5},{5,4},{6,7},{7,6},{8,9},{9,8},{10,11... | collective-permute-start | bytes 1216520 | tf_op jit(solution)/shard_map/ppermute | solution.py:397
  109.1 9.2 %collective-permute-start.11 = (f32[3,11,24,128]{3,2,1,0:T(8,128)S(1)}, f32[3,11,24,128]{3,2,1,0:T(8,128)S(1)}, u32[]{:S(2)}, u32[]{:S(2)}) collective-permute-start(f32[3,11,24,128]{3,2,1,0:T(8,128)S(1)} %get-tuple-element.54), channel_id=1, source_target_pairs={{1,2},{2,1},{3,4},{4,3},{5,6},{6,5},{9,10},{10,9},{11,12},{12,11},... | collective-permute-start | bytes 1216520 | tf_op jit(solution)/shard_map/ppermute | solution.py:397
  125.0 9.4 %collective-permute-start.13 = (f32[4,24,128]{2,1,0:T(8,128)S(1)}, f32[4,24,128]{2,1,0:T(8,128)S(1)}, u32[]{:S(2)}, u32[]{:S(2)}) collective-permute-start(f32[4,24,128]{2,1,0:T(8,128)S(1)} %get-tuple-element.57), channel_id=1, source_target_pairs={{16,32},{24,40},{32,16},{40,24},{48,64},{56,72},{64,48},{72,56},{8... | collective-permute-start | bytes 147464 | tf_op jit(solution)/shard_map/ppermute | solution.py:397
  132.4 6.0 %collective-permute-start.12 = (f32[4,24,128]{2,1,0:T(8,128)S(1)}, f32[4,24,128]{2,1,0:T(8,128)S(1)}, u32[]{:S(2)}, u32[]{:S(2)}) collective-permute-start(f32[4,24,128]{2,1,0:T(8,128)S(1)} %get-tuple-element.57), channel_id=1, source_target_pairs={{0,16},{8,24},{16,0},{24,8},{32,48},{40,56},{48,32},{56,40},{64,80... | collective-permute-start | bytes 147464 | tf_op jit(solution)/shard_map/ppermute | solution.py:397
  134.5 9.2 %collective-permute-start.14 = (f32[4,24,128]{2,1,0:T(8,128)S(1)}, f32[4,24,128]{2,1,0:T(8,128)S(1)}, u32[]{:S(2)}, u32[]{:S(2)}) collective-permute-start(f32[4,24,128]{2,1,0:T(8,128)S(1)} %collective-permute-done.13), channel_id=1, source_target_pairs={{0,16},{8,24},{16,0},{24,8},{32,48},{40,56},{48,32},{56,40},{64,80... | collective-permute-start | bytes 147464 | tf_op jit(solution)/shard_map/ppermute | solution.py:397
  138.4 9.3 %collective-permute-start.15 = (f32[4,24,128]{2,1,0:T(8,128)S(1)}, f32[4,24,128]{2,1,0:T(8,128)S(1)}, u32[]{:S(2)}, u32[]{:S(2)}) collective-permute-start(f32[4,24,128]{2,1,0:T(8,128)S(1)} %collective-permute-done.12), channel_id=1, source_target_pairs={{16,32},{24,40},{32,16},{40,24},{48,64},{56,72},{64,48},{72,56},{8... | collective-permute-start | bytes 147464 | tf_op jit(solution)/shard_map/ppermute | solution.py:397
  147.7 3.6 %collective-permute-start.16 = (f32[29,24,128]{2,1,0:T(8,128)S(1)}, f32[29,24,128]{2,1,0:T(8,128)S(1)}, u32[]{:S(2)}, u32[]{:S(2)}) collective-permute-start(f32[29,24,128]{2,1,0:T(8,128)S(1)} %constant_dynamic-update-slice_fusion.6.mine), channel_id=1, source_target_pairs={{0,8},{8,0},{16,24},{24,16},{32,40},{40,32},{48,56},{56,48},{64,72... | collective-permute-start | bytes 1069064 | tf_op jit(solution)/shard_map/ppermute | solution.py:397
  154.7 6.1 %collective-permute-start.17 = (f32[3,3,24,128]{3,2,1,0:T(8,128)S(1)}, f32[3,3,24,128]{3,2,1,0:T(8,128)S(1)}, u32[]{:S(2)}, u32[]{:S(2)}) collective-permute-start(f32[3,3,24,128]{3,2,1,0:T(8,128)S(1)} %get-tuple-element.62), channel_id=1, source_target_pairs={{8,16},{16,8},{24,32},{32,24},{40,48},{48,40},{56,64},{64,56},{72,... | collective-permute-start | bytes 331784 | tf_op jit(solution)/shard_map/ppermute | solution.py:397

commit v5 on v4

--- a/solution.py
+++ b/solution.py
@@ -12,7 +12,7 @@
 NZ = 24
 HALO = 6
 LANES = 128
-UNROLL = (2, 4, 8, 8)
+UNROLL = (3, 8, 10, 10)
 PARAMS = pltpu.CompilerParams(vmem_limit_bytes=12 << 20)
 
 
@@ -117,7 +117,7 @@
                 total = residual if total is None else total + residual
             target[0][c, index(target, q)] = 0.25 * pair_sum(total, period)
 
-    each_row(low, high, body, max(1, UNROLL[level] // 2))
+    each_row(low, high, body, (UNROLL[level] + 1) // 2)
 
 
 def from_zero(target, source, density, factor, level, period, rows, position, low, high, finer=None, reach=0, group=1):
@@ -179,23 +179,39 @@
             edge[c * count + r] = v1[0][c, (1 - position[4]) + (r - v1[1])]
 
 
+def by_parity(position, body):
+    for odd in range(2):
+        pl.when(position[4] == odd)(lambda odd=odd: body(odd))
+
+
 def rows_to_send(position, own, first, second):
-    odd, spare = position[4], own.shape[1] - first.shape[1]
+    spare = own.shape[1] - first.shape[1]
+
+    def body(odd):
+        for c in range(own.shape[0]):
+            for r in range(first.shape[1]):
+                first[c, r] = own[c, (1 - odd) * spare + r]
+                second[c, r] = own[c, odd * spare + r]
+
+    by_parity(position, body)
+
+
+def with_halo(position, own, first, second, store):
+    rows, halo = own.shape[1], first.shape[1]
+
+    def body(odd):
+        for c in range(own.shape[0]):
+            for piece, at in ((first, (1 - odd) * (halo + rows)), (second, odd * (halo + rows))):
+                for r in range(halo):
+                    store(c, at + r, piece[c, r])
+
     for c in range(own.shape[0]):
-        for r in range(first.shape[1]):
-            first[c, r] = own[c, (1 - odd) * spare + r]
-            second[c, r] = own[c, odd * spare + r]
-
-
-def with_halo(position, own, first, second, store):
-    odd, rows, halo = position[4], own.shape[1], first.shape[1]
-    for c in range(own.shape[0]):
-        for piece, at in ((first, (1 - odd) * (halo + rows)), (own, halo), (second, odd * (halo + rows))):
-            for r in range(piece.shape[1]):
-                store(c, at + r, piece[c, r])
-
-
-def pack_kernel(source, density, out):
+        for r in range(rows):
+            store(c, halo + r, own[c, r])
+    by_parity(position, body)
+
+
+def pack_kernel(position, source, density, out):
     blocks = out.shape[0]
     for ref, at, n in ((source, 0, source.shape[0]), (density, source.shape[0], density.shape[0])):
         for m in range(n):
@@ -226,7 +242,7 @@
     rows_to_send(position, own, first, second)
 
 
-def first_down_kernel(position, own, first, second, g0, d0, f0, v0, g1, d1, f1, v1, packed, edge, field, field1):
+def first_down_kernel(position, own, second, first, g0, d0, f0, v0, g1, d1, f1, v1, packed, edge, field, field1):
     rows = own.shape[1]
 
     def store(c, at, value):
@@ -244,7 +260,7 @@
     level_one_down(position, (g1, -2), (v1, -2), (field1, -2), (d1, -3), (f1, -3), packed, edge)
 
 
-def side_kernel(position, own, first, second, tall, to_first, to_second):
+def side_kernel(position, own, second, first, tall, to_first, to_second):
     half = tall.shape[1] // 2
     low = (lane_index() < LANES // 2) == (position[5] == 1)
 
@@ -404,7 +420,7 @@
     position = jnp.stack([i, j, lax.axis_size("gx"), blocks, i % 2, j % 2, i // 2 % 2]).astype(jnp.int32)
     W, R0, R1 = 2 * LANES, rows + 2 * HALO, rows // 2
 
-    (sent,) = call(pack_kernel, [(blocks, (C + 1) * depth, rows, W)], [], right_side.reshape(C * depth, rows, columns), density)
+    (sent,) = call(pack_kernel, [(blocks, (C + 1) * depth, rows, W)], [], position, right_side.reshape(C * depth, rows, columns), density, scalars=1)
     taken = lax.all_to_all(sent, "gz", 0, 0)
     own, first, second = call(
         unpack_kernel,
@@ -422,8 +438,8 @@
         [fine, mid],
         position,
         own,
+        swap(second, "gx", False),
         swap(first, "gx", True),
-        swap(second, "gx", False),
         scalars=1,
     )
 
@@ -466,8 +482,8 @@
         [],
         position,
         field,
+        swap(second, "gx", False),
         swap(first, "gx", True),
-        swap(second, "gx", False),
         scalars=1,
     )
     v0, g1, *down = call(

time: 185 us -> 184 us (level)
  blocking collectives: 17.5 us -> 48 us
  waiting for transfers between devices: 65.6 us -> 36.1 us
  starting transfers between devices: 68 us -> 62.8 us
  Pallas kernels: 28.5 us -> 31.9 us
    all_to_all x0 -> x1, blocking collectives: none -> 30 us  [shards(): taken = lax.all_to_all(sent, 'gz', 0, 0)]
    all_to_all x1 -> x0, waiting for transfers between devices: 23 us -> none  [shards(): taken = lax.all_to_all(sent, 'gz', 0, 0)]
    all_to_all x1 -> x0, starting transfers between devices: 7.1 us -> none  [shards(): taken = lax.all_to_all(sent, 'gz', 0, 0)]
    ppermute x18, waiting for transfers between devices: 42.6 us -> 36.1 us  [swap(): return lax.ppermute(values, axis, pairs)]
    pallas_call x10, Pallas kernels: 28.5 us -> 31.9 us  [call(): pl.pallas_call(kernel, out_shape=[shape(s) for s in outs], in_specs=specs...]
  transfers between devices with their start and end apart: 19 -> 18, of which waited for: 14 -> 13; matrix products, arithmetic and copies ran while one was open for 0% -> 0% of each run, Pallas kernels for 0% -> 0%
where the time goes in v5:
time: 184 us; the launch traced here: 181 us
  starting transfers between devices  62.8 us (34%)
  blocking collectives  48 us (26%)
  waiting for transfers between devices  36.1 us (20%)
  Pallas kernels  31.9 us (17%)
  local copies, waits for them, and re-layouts  2.01 us (1%)
    ppermute x18, starting transfers between devices, swap(): return lax.ppermute(values, axis, pairs)  62.8 us
    ppermute x18, waiting for transfers between devices, swap(): return lax.ppermute(values, axis, pairs)  36.1 us
    pallas_call x10, Pallas kernels, call(): pl.pallas_call(kernel, out_shape=[shape(s) for s in outs], in_specs=specs...  31.9 us
    all_to_all x1, blocking collectives, shards(): taken = lax.all_to_all(sent, 'gz', 0, 0)  30 us
    all_to_all x1, blocking collectives, shards(): lax.all_to_all(sent, 'gz', 0, 0)  17.9 us
  transfers between devices with their start and end apart: 18, of which 13 were waited for; matrix products, arithmetic and copies ran while one was open for 0% of the time, Pallas kernels for 0%

profile of v5, /device:TPU:198, one launch (start us, length us, event | category | flops | bytes accessed | tf_op | source)
XLA Modules:
  0.0 181.0 jit_solution(17175821807999900808)
XLA Ops:
  0.0 0.1 stack.23.position
  0.1 0.0 copy-start
  0.1 1.0 copy-done
  1.0 0.0 copy-start.1
  1.1 0.9 copy-done.1
  1.9 0.6 pack_kernel.1
  2.5 30.0 %all_to_all.10.taken = f32[8,12,8,256]{3,2,1,0:T(8,128)S(1)} all-to-all(f32[8,12,8,256]{3,2,1,0:T(8,128)S(1)} %pack_kernel.1), channel_id=1, replica_groups=mesh['gx'=64,'gz'=8] {'gz'}, dimensions={0} | all-to-all | bytes 1572864 | tf_op jit(solution)/shard_map/all_to_all | solution.py:424
  32.6 0.8 unpack_kernel.1
  33.4 1.9 %collective-permute-start = (f32[4,6,24,256]{3,2,1,0:T(8,128)S(1)}, f32[4,6,24,256]{3,2,1,0:T(8,128)S(1)}, u32[]{:S(2)}, u32[]{:S(2)}) collective-permute-start(f32[4,6,24,256]{3,2,1,0:T(8,128)S(1)} %get-tuple-element.36), channel_id=1, source_target_pairs={{8,16},{16,8},{24,32},{32,24},{40,48},{48,40},{56,64},{64,56},{72,... | collective-permute-start | bytes 1769480 | tf_op jit(solution)/shard_map/ppermute | solution.py:413
  35.3 5.5 %collective-permute-start.1 = (f32[4,6,24,256]{3,2,1,0:T(8,128)S(1)}, f32[4,6,24,256]{3,2,1,0:T(8,128)S(1)}, u32[]{:S(2)}, u32[]{:S(2)}) collective-permute-start(f32[4,6,24,256]{3,2,1,0:T(8,128)S(1)} %get-tuple-element.37), channel_id=1, source_target_pairs={{0,8},{8,0},{16,24},{24,16},{32,40},{40,32},{48,56},{56,48},{64,72... | collective-permute-start | bytes 1769480 | tf_op jit(solution)/shard_map/ppermute | solution.py:413
  40.8 3.8 %collective-permute-done.second = f32[4,6,24,256]{3,2,1,0:T(8,128)S(1)} collective-permute-done((f32[4,6,24,256]{3,2,1,0:T(8,128)S(1)}, f32[4,6,24,256]{3,2,1,0:T(8,128)S(1)}, u32[]{:S(2)}, u32[]{:S(2)}) %collective-permute-start) | collective-permute-done | bytes 589856 | tf_op jit(solution)/shard_map/ppermute | solution.py:413
  44.6 0.0 collective-permute-done.1.first
  44.6 5.6 %first_down_kernel.1 = (f32[3,20,24,256]{3,2,1,0:T(8,128)S(1)}, f32[20,24,256]{2,1,0:T(8,128)S(1)}, f32[20,24,256]{2,1,0:T(8,128)S(1)}, f32[3,20,24,256]{3,2,1,0...) custom-call(s32[7]{0:T(128)S(1)} %stack.23.position, ...), custom_call_target="tpu_custom_call" | custom-call | tf_op jit(solution)/shard_map/first_down_kernel/pallas_call | solution.py:394
  50.2 8.7 %collective-permute-start.3 = (f32[4,24,128]{2,1,0:T(8,128)S(1)}, f32[4,24,128]{2,1,0:T(8,128)S(1)}, u32[]{:S(2)}, u32[]{:S(2)}) collective-permute-start(f32[4,24,128]{2,1,0:T(8,128)S(1)} %get-tuple-element.38), channel_id=1, source_target_pairs={{16,32},{24,40},{32,16},{40,24},{48,64},{56,72},{64,48},{72,56},{8... | collective-permute-start | bytes 147464 | tf_op jit(solution)/shard_map/ppermute | solution.py:413
  58.9 1.9 %collective-permute-start.2 = (f32[4,24,128]{2,1,0:T(8,128)S(1)}, f32[4,24,128]{2,1,0:T(8,128)S(1)}, u32[]{:S(2)}, u32[]{:S(2)}) collective-permute-start(f32[4,24,128]{2,1,0:T(8,128)S(1)} %get-tuple-element.38), channel_id=1, source_target_pairs={{0,16},{8,24},{16,0},{24,8},{32,48},{40,56},{48,32},{56,40},{64,80... | collective-permute-start | bytes 147464 | tf_op jit(solution)/shard_map/ppermute | solution.py:413
  60.8 0.1 collective-permute-done.3
  60.9 3.8 %collective-permute-start.4 = (f32[4,24,128]{2,1,0:T(8,128)S(1)}, f32[4,24,128]{2,1,0:T(8,128)S(1)}, u32[]{:S(2)}, u32[]{:S(2)}) collective-permute-start(f32[4,24,128]{2,1,0:T(8,128)S(1)} %collective-permute-done.3), channel_id=1, source_target_pairs={{0,16},{8,24},{16,0},{24,8},{32,48},{40,56},{48,32},{56,40},{64,80... | collective-permute-start | bytes 147464 | tf_op jit(solution)/shard_map/ppermute | solution.py:413
  64.8 0.3 collective-permute-done.2
  65.1 5.0 %collective-permute-start.5 = (f32[4,24,128]{2,1,0:T(8,128)S(1)}, f32[4,24,128]{2,1,0:T(8,128)S(1)}, u32[]{:S(2)}, u32[]{:S(2)}) collective-permute-start(f32[4,24,128]{2,1,0:T(8,128)S(1)} %collective-permute-done.2), channel_id=1, source_target_pairs={{16,32},{24,40},{32,16},{40,24},{48,64},{56,72},{64,48},{72,56},{8... | collective-permute-start | bytes 147464 | tf_op jit(solution)/shard_map/ppermute | solution.py:413
  70.2 0.0 collective-permute-done.4
  70.2 4.2 %collective-permute-done.5 = f32[4,24,128]{2,1,0:T(8,128)S(1)} collective-permute-done((f32[4,24,128]{2,1,0:T(8,128)S(1)}, f32[4,24,128]{2,1,0:T(8,128)S(1)}, u32[]{:S(2)}, u32[]{:S(2)}) %collective-permute-start.5) | collective-permute-done | bytes 49184 | tf_op jit(solution)/shard_map/ppermute | solution.py:413
  74.4 1.9 %collective-permute-start.6 = (f32[29,24,128]{2,1,0:T(8,128)S(1)}, f32[29,24,128]{2,1,0:T(8,128)S(1)}, u32[]{:S(2)}, u32[]{:S(2)}) collective-permute-start(f32[29,24,128]{2,1,0:T(8,128)S(1)} %constant_dynamic-update-slice_fusion.mine), channel_id=1, source_target_pairs={{0,8},{8,0},{16,24},{24,16},{32,40},{40,32},{48,56},{56,48},{64,72... | collective-permute-start | bytes 1069064 | tf_op jit(solution)/shard_map/ppermute | solution.py:413
  76.3 1.6 collective-permute-done.6.other
  78.0 6.1 %coarse_kernel.2 = (f32[3,4,24,128]{3,2,1,0:T(8,128)S(1)}, f32[3,3,24,128]{3,2,1,0:T(8,128)S(1)}, f32[3,3,24,128]{3,2,1,0:T(8,128)S(1)}) custom-call(s32[7]{0:T(128)S(1)} %stack.23.position, f32[29,24,128]{2,1,0:T(8,128)S(1)} %constant_dynamic-update-slice_fusion.mine, f32[29,24,128]{2,1,0:T(8,128)S(1)} %collective-permute-done.6.other, ...), custom_call_target="tpu_custom_call" | custom-call | tf_op jit(solution)/shard_map/coarse_kernel/pallas_call | solution.py:394
  84.0 1.9 %collective-permute-start.7 = (f32[3,3,24,128]{3,2,1,0:T(8,128)S(1)}, f32[3,3,24,128]{3,2,1,0:T(8,128)S(1)}, u32[]{:S(2)}, u32[]{:S(2)}) collective-permute-start(f32[3,3,24,128]{3,2,1,0:T(8,128)S(1)} %get-tuple-element.43), channel_id=1, source_target_pairs={{8,16},{16,8},{24,32},{32,24},{40,48},{48,40},{56,64},{64,56},{72,... | collective-permute-start | bytes 331784 | tf_op jit(solution)/shard_map/ppermute | solution.py:413
  86.0 4.1 %collective-permute-done.7.right = f32[3,3,24,128]{3,2,1,0:T(8,128)S(1)} collective-permute-done((f32[3,3,24,128]{3,2,1,0:T(8,128)S(1)}, f32[3,3,24,128]{3,2,1,0:T(8,128)S(1)}, u32[]{:S(2)}, u32[]{:S(2)}) %collective-permute-start.7) | collective-permute-done | bytes 110624 | tf_op jit(solution)/shard_map/ppermute | solution.py:413
  90.1 2.6 %first_up_kernel.1 = (f32[3,8,24,128]{3,2,1,0:T(8,128)S(1)}, f32[3,7,24,128]{3,2,1,0:T(8,128)S(1)}, f32[3,7,24,128]{3,2,1,0:T(8,128)S(1)}) custom-call(s32[7]{0:T(128)S(1)} %stack.23.position, f32[3,4,24,128]{3,2,1,0:T(8,128)S(1)} %get-tuple-element.41.own, f32[3,3,24,128]{3,2,1,0:T(8,128)S(1)} %get-tuple-element.42.left, ...), custom_call_target="tpu_custom_call" | custom-call | tf_op jit(solution)/shard_map/first_up_kernel/pallas_call | solution.py:394
  92.8 1.9 %collective-permute-start.8 = (f32[3,7,24,128]{3,2,1,0:T(8,128)S(1)}, f32[3,7,24,128]{3,2,1,0:T(8,128)S(1)}, u32[]{:S(2)}, u32[]{:S(2)}) collective-permute-start(f32[3,7,24,128]{3,2,1,0:T(8,128)S(1)} %get-tuple-element.50), channel_id=1, source_target_pairs={{8,16},{16,8},{24,32},{32,24},{40,48},{48,40},{56,64},{64,56},{72,... | collective-permute-start | bytes 774152 | tf_op jit(solution)/shard_map/ppermute | solution.py:413
  94.7 8.5 %collective-permute-start.9 = (f32[3,7,24,128]{3,2,1,0:T(8,128)S(1)}, f32[3,7,24,128]{3,2,1,0:T(8,128)S(1)}, u32[]{:S(2)}, u32[]{:S(2)}) collective-permute-start(f32[3,7,24,128]{3,2,1,0:T(8,128)S(1)} %get-tuple-element.51), channel_id=1, source_target_pairs={{0,8},{8,0},{16,24},{24,16},{32,40},{40,32},{48,56},{56,48},{64,72... | collective-permute-start | bytes 774152 | tf_op jit(solution)/shard_map/ppermute | solution.py:413
  103.2 0.0 collective-permute-done.8.second
  103.2 1.1 collective-permute-done.9.first
  104.3 0.8 side_kernel.1
  105.1 2.5 %collective-permute-start.10 = (f32[3,11,24,128]{3,2,1,0:T(8,128)S(1)}, f32[3,11,24,128]{3,2,1,0:T(8,128)S(1)}, u32[]{:S(2)}, u32[]{:S(2)}) collective-permute-start(f32[3,11,24,128]{3,2,1,0:T(8,128)S(1)} %get-tuple-element.53), channel_id=1, source_target_pairs={{0,1},{1,0},{2,3},{3,2},{4,5},{5,4},{6,7},{7,6},{8,9},{9,8},{10,11... | collective-permute-start | bytes 1216520 | tf_op jit(solution)/shard_map/ppermute | solution.py:413
  107.5 0.7 collective-permute-start.11
  108.2 9.0 %collective-permute-done.10.first = f32[3,11,24,128]{3,2,1,0:T(8,128)S(1)} collective-permute-done((f32[3,11,24,128]{3,2,1,0:T(8,128)S(1)}, f32[3,11,24,128]{3,2,1,0:T(8,128)S(1)}, u32[]{:S(2)}, u32[]{:S(2)}) %collective-permute-start.10) | collective-permute-done | bytes 405536 | tf_op jit(solution)/shard_map/ppermute | solution.py:413
  117.2 0.0 collective-permute-done.11.second
  117.2 6.0 %second_down_kernel.1 = (f32[3,20,24,256]{3,2,1,0:T(8,128)S(1)}, f32[3,8,24,128]{3,2,1,0:T(8,128)S(1)}, f32[3,8,24,128]{3,2,1,0:T(8,128)S(1)}, f32[4,24,128]{2,1,0:T(8,128)S(1)}, f32[9,24,128]{2,1,0:T(8,128)S(1)}) custom-call(s32[7]{0:T(128)S(1)} %stack.23.position, f32[3,22,24,128]{3,2,1,0:T(8,128)S(1)} %get-tuple-element.52.tall, ...), custom_call_target="tpu_custom_call" | custom-call | tf_op jit(solution)/shard_map/second_down_kernel/pallas_call | solution.py:394
  123.2 5.4 %collective-permute-start.13 = (f32[4,24,128]{2,1,0:T(8,128)S(1)}, f32[4,24,128]{2,1,0:T(8,128)S(1)}, u32[]{:S(2)}, u32[]{:S(2)}) collective-permute-start(f32[4,24,128]{2,1,0:T(8,128)S(1)} %get-tuple-element.57), channel_id=1, source_target_pairs={{16,32},{24,40},{32,16},{40,24},{48,64},{56,72},{64,48},{72,56},{8... | collective-permute-start | bytes 147464 | tf_op jit(solution)/shard_map/ppermute | solution.py:413
  128.7 1.9 %collective-permute-start.12 = (f32[4,24,128]{2,1,0:T(8,128)S(1)}, f32[4,24,128]{2,1,0:T(8,128)S(1)}, u32[]{:S(2)}, u32[]{:S(2)}) collective-permute-start(f32[4,24,128]{2,1,0:T(8,128)S(1)} %get-tuple-element.57), channel_id=1, source_target_pairs={{0,16},{8,24},{16,0},{24,8},{32,48},{40,56},{48,32},{56,40},{64,80... | collective-permute-start | bytes 147464 | tf_op jit(solution)/shard_map/ppermute | solution.py:413
  130.6 1.9 %collective-permute-done.13 = f32[4,24,128]{2,1,0:T(8,128)S(1)} collective-permute-done((f32[4,24,128]{2,1,0:T(8,128)S(1)}, f32[4,24,128]{2,1,0:T(8,128)S(1)}, u32[]{:S(2)}, u32[]{:S(2)}) %collective-permute-start.13) | collective-permute-done | bytes 49184 | tf_op jit(solution)/shard_map/ppermute | solution.py:413
  132.5 2.0 %collective-permute-start.14 = (f32[4,24,128]{2,1,0:T(8,128)S(1)}, f32[4,24,128]{2,1,0:T(8,128)S(1)}, u32[]{:S(2)}, u32[]{:S(2)}) collective-permute-start(f32[4,24,128]{2,1,0:T(8,128)S(1)} %collective-permute-done.13), channel_id=1, source_target_pairs={{0,16},{8,24},{16,0},{24,8},{32,48},{40,56},{48,32},{56,40},{64,80... | collective-permute-start | bytes 147464 | tf_op jit(solution)/shard_map/ppermute | solution.py:413
  134.5 0.1 collective-permute-done.12
  134.6 5.2 %collective-permute-start.15 = (f32[4,24,128]{2,1,0:T(8,128)S(1)}, f32[4,24,128]{2,1,0:T(8,128)S(1)}, u32[]{:S(2)}, u32[]{:S(2)}) collective-permute-start(f32[4,24,128]{2,1,0:T(8,128)S(1)} %collective-permute-done.12), channel_id=1, source_target_pairs={{16,32},{24,40},{32,16},{40,24},{48,64},{56,72},{64,48},{72,56},{8... | collective-permute-start | bytes 147464 | tf_op jit(solution)/shard_map/ppermute | solution.py:413
  139.9 0.0 collective-permute-done.14
  139.9 4.0 %collective-permute-done.15 = f32[4,24,128]{2,1,0:T(8,128)S(1)} collective-permute-done((f32[4,24,128]{2,1,0:T(8,128)S(1)}, f32[4,24,128]{2,1,0:T(8,128)S(1)}, u32[]{:S(2)}, u32[]{:S(2)}) %collective-permute-start.15) | collective-permute-done | bytes 49184 | tf_op jit(solution)/shard_map/ppermute | solution.py:413
  144.0 1.9 %collective-permute-start.16 = (f32[29,24,128]{2,1,0:T(8,128)S(1)}, f32[29,24,128]{2,1,0:T(8,128)S(1)}, u32[]{:S(2)}, u32[]{:S(2)}) collective-permute-start(f32[29,24,128]{2,1,0:T(8,128)S(1)} %constant_dynamic-update-slice_fusion.6.mine), channel_id=1, source_target_pairs={{0,8},{8,0},{16,24},{24,16},{32,40},{40,32},{48,56},{56,48},{64,72... | collective-permute-start | bytes 1069064 | tf_op jit(solution)/shard_map/ppermute | solution.py:413
  145.9 1.6 collective-permute-done.16.other
  147.5 6.1 %coarse_kernel.3 = (f32[3,4,24,128]{3,2,1,0:T(8,128)S(1)}, f32[3,3,24,128]{3,2,1,0:T(8,128)S(1)}, f32[3,3,24,128]{3,2,1,0:T(8,128)S(1)}) custom-call(s32[7]{0:T(128)S(1)} %stack.23.position, f32[29,24,128]{2,1,0:T(8,128)S(1)} %constant_dynamic-update-slice_fusion.6.mine, f32[29,24,128]{2,1,0:T(8,128)S(1)} %collective-permute-done.16.other, ...), custom_call_target="tpu_custom_call" | custom-call | tf_op jit(solution)/shard_map/coarse_kernel/pallas_call | solution.py:394
  153.6 1.9 %collective-permute-start.17 = (f32[3,3,24,128]{3,2,1,0:T(8,128)S(1)}, f32[3,3,24,128]{3,2,1,0:T(8,128)S(1)}, u32[]{:S(2)}, u32[]{:S(2)}) collective-permute-start(f32[3,3,24,128]{3,2,1,0:T(8,128)S(1)} %get-tuple-element.62), channel_id=1, source_target_pairs={{8,16},{16,8},{24,32},{32,24},{40,48},{48,40},{56,64},{64,56},{72,... | collective-permute-start | bytes 331784 | tf_op jit(solution)/shard_map/ppermute | solution.py:413
  155.6 4.1 %collective-permute-done.17.right = f32[3,3,24,128]{3,2,1,0:T(8,128)S(1)} collective-permute-done((f32[3,3,24,128]{3,2,1,0:T(8,128)S(1)}, f32[3,3,24,128]{3,2,1,0:T(8,128)S(1)}, u32[]{:S(2)}, u32[]{:S(2)}) %collective-permute-start.17) | collective-permute-done | bytes 110624 | tf_op jit(solution)/shard_map/ppermute | solution.py:413
  159.7 2.6 %last_up_kernel.1 = f32[8,9,8,128]{3,2,1,0:T(8,128)S(1)} custom-call(s32[7]{0:T(128)S(1)} %stack.23.position, f32[3,4,24,128]{3,2,1,0:T(8,128)S(1)} %get-tuple-element.60.own, f32[3,3,24,128]{3,2,1,0:T(8,128)S(1)} %get-tuple-element.61.left, f32[3,3,24,128]{3,2,1,0:T(8,128)S(1)} %collective-permute-done.17.right, ...), custom_call_target="tpu_custom_call" | custom-call | tf_op jit(solution)/shard_map/last_up_kernel/pallas_call | solution.py:394
  162.3 17.9 %all_to_all.11.taken = f32[8,9,8,128]{3,2,1,0:T(8,128)S(1)} all-to-all(f32[8,9,8,128]{3,2,1,0:T(8,128)S(1)} %last_up_kernel.1), channel_id=1, replica_groups=mesh['gx'=64,'gz'=8] {'gz'}, dimensions={0} | all-to-all | bytes 589824 | tf_op jit(solution)/shard_map/all_to_all | solution.py:517
  180.3 0.7 join_kernel.1
  (12 shorter events, 0.1 us)
Async XLA Ops:
  0.1 1.0 copy-start
  1.0 0.9 copy-start.1
  33.4 11.2 %collective-permute-start = (f32[4,6,24,256]{3,2,1,0:T(8,128)S(1)}, f32[4,6,24,256]{3,2,1,0:T(8,128)S(1)}, u32[]{:S(2)}, u32[]{:S(2)}) collective-permute-start(f32[4,6,24,256]{3,2,1,0:T(8,128)S(1)} %get-tuple-element.36), channel_id=1, source_target_pairs={{8,16},{16,8},{24,32},{32,24},{40,48},{48,40},{56,64},{64,56},{72,... | collective-permute-start | bytes 1769480 | tf_op jit(solution)/shard_map/ppermute | solution.py:413
  35.3 9.3 %collective-permute-start.1 = (f32[4,6,24,256]{3,2,1,0:T(8,128)S(1)}, f32[4,6,24,256]{3,2,1,0:T(8,128)S(1)}, u32[]{:S(2)}, u32[]{:S(2)}) collective-permute-start(f32[4,6,24,256]{3,2,1,0:T(8,128)S(1)} %get-tuple-element.37), channel_id=1, source_target_pairs={{0,8},{8,0},{16,24},{24,16},{32,40},{40,32},{48,56},{56,48},{64,72... | collective-permute-start | bytes 1769480 | tf_op jit(solution)/shard_map/ppermute | solution.py:413
  50.2 10.8 %collective-permute-start.3 = (f32[4,24,128]{2,1,0:T(8,128)S(1)}, f32[4,24,128]{2,1,0:T(8,128)S(1)}, u32[]{:S(2)}, u32[]{:S(2)}) collective-permute-start(f32[4,24,128]{2,1,0:T(8,128)S(1)} %get-tuple-element.38), channel_id=1, source_target_pairs={{16,32},{24,40},{32,16},{40,24},{48,64},{56,72},{64,48},{72,56},{8... | collective-permute-start | bytes 147464 | tf_op jit(solution)/shard_map/ppermute | solution.py:413
  58.9 6.2 %collective-permute-start.2 = (f32[4,24,128]{2,1,0:T(8,128)S(1)}, f32[4,24,128]{2,1,0:T(8,128)S(1)}, u32[]{:S(2)}, u32[]{:S(2)}) collective-permute-start(f32[4,24,128]{2,1,0:T(8,128)S(1)} %get-tuple-element.38), channel_id=1, source_target_pairs={{0,16},{8,24},{16,0},{24,8},{32,48},{40,56},{48,32},{56,40},{64,80... | collective-permute-start | bytes 147464 | tf_op jit(solution)/shard_map/ppermute | solution.py:413
  60.9 9.2 %collective-permute-start.4 = (f32[4,24,128]{2,1,0:T(8,128)S(1)}, f32[4,24,128]{2,1,0:T(8,128)S(1)}, u32[]{:S(2)}, u32[]{:S(2)}) collective-permute-start(f32[4,24,128]{2,1,0:T(8,128)S(1)} %collective-permute-done.3), channel_id=1, source_target_pairs={{0,16},{8,24},{16,0},{24,8},{32,48},{40,56},{48,32},{56,40},{64,80... | collective-permute-start | bytes 147464 | tf_op jit(solution)/shard_map/ppermute | solution.py:413
  65.1 9.3 %collective-permute-start.5 = (f32[4,24,128]{2,1,0:T(8,128)S(1)}, f32[4,24,128]{2,1,0:T(8,128)S(1)}, u32[]{:S(2)}, u32[]{:S(2)}) collective-permute-start(f32[4,24,128]{2,1,0:T(8,128)S(1)} %collective-permute-done.2), channel_id=1, source_target_pairs={{16,32},{24,40},{32,16},{40,24},{48,64},{56,72},{64,48},{72,56},{8... | collective-permute-start | bytes 147464 | tf_op jit(solution)/shard_map/ppermute | solution.py:413
  74.4 3.6 %collective-permute-start.6 = (f32[29,24,128]{2,1,0:T(8,128)S(1)}, f32[29,24,128]{2,1,0:T(8,128)S(1)}, u32[]{:S(2)}, u32[]{:S(2)}) collective-permute-start(f32[29,24,128]{2,1,0:T(8,128)S(1)} %constant_dynamic-update-slice_fusion.mine), channel_id=1, source_target_pairs={{0,8},{8,0},{16,24},{24,16},{32,40},{40,32},{48,56},{56,48},{64,72... | collective-permute-start | bytes 1069064 | tf_op jit(solution)/shard_map/ppermute | solution.py:413
  84.0 6.1 %collective-permute-start.7 = (f32[3,3,24,128]{3,2,1,0:T(8,128)S(1)}, f32[3,3,24,128]{3,2,1,0:T(8,128)S(1)}, u32[]{:S(2)}, u32[]{:S(2)}) collective-permute-start(f32[3,3,24,128]{3,2,1,0:T(8,128)S(1)} %get-tuple-element.43), channel_id=1, source_target_pairs={{8,16},{16,8},{24,32},{32,24},{40,48},{48,40},{56,64},{64,56},{72,... | collective-permute-start | bytes 331784 | tf_op jit(solution)/shard_map/ppermute | solution.py:413
  92.8 10.4 %collective-permute-start.8 = (f32[3,7,24,128]{3,2,1,0:T(8,128)S(1)}, f32[3,7,24,128]{3,2,1,0:T(8,128)S(1)}, u32[]{:S(2)}, u32[]{:S(2)}) collective-permute-start(f32[3,7,24,128]{3,2,1,0:T(8,128)S(1)} %get-tuple-element.50), channel_id=1, source_target_pairs={{8,16},{16,8},{24,32},{32,24},{40,48},{48,40},{56,64},{64,56},{72,... | collective-permute-start | bytes 774152 | tf_op jit(solution)/shard_map/ppermute | solution.py:413
  94.7 9.6 %collective-permute-start.9 = (f32[3,7,24,128]{3,2,1,0:T(8,128)S(1)}, f32[3,7,24,128]{3,2,1,0:T(8,128)S(1)}, u32[]{:S(2)}, u32[]{:S(2)}) collective-permute-start(f32[3,7,24,128]{3,2,1,0:T(8,128)S(1)} %get-tuple-element.51), channel_id=1, source_target_pairs={{0,8},{8,0},{16,24},{24,16},{32,40},{40,32},{48,56},{56,48},{64,72... | collective-permute-start | bytes 774152 | tf_op jit(solution)/shard_map/ppermute | solution.py:413
  105.1 12.2 %collective-permute-start.10 = (f32[3,11,24,128]{3,2,1,0:T(8,128)S(1)}, f32[3,11,24,128]{3,2,1,0:T(8,128)S(1)}, u32[]{:S(2)}, u32[]{:S(2)}) collective-permute-start(f32[3,11,24,128]{3,2,1,0:T(8,128)S(1)} %get-tuple-element.53), channel_id=1, source_target_pairs={{0,1},{1,0},{2,3},{3,2},{4,5},{5,4},{6,7},{7,6},{8,9},{9,8},{10,11... | collective-permute-start | bytes 1216520 | tf_op jit(solution)/shard_map/ppermute | solution.py:413
  107.5 9.7 %collective-permute-start.11 = (f32[3,11,24,128]{3,2,1,0:T(8,128)S(1)}, f32[3,11,24,128]{3,2,1,0:T(8,128)S(1)}, u32[]{:S(2)}, u32[]{:S(2)}) collective-permute-start(f32[3,11,24,128]{3,2,1,0:T(8,128)S(1)} %get-tuple-element.54), channel_id=1, source_target_pairs={{1,2},{2,1},{3,4},{4,3},{5,6},{6,5},{9,10},{10,9},{11,12},{12,11},... | collective-permute-start | bytes 1216520 | tf_op jit(solution)/shard_map/ppermute | solution.py:413
  123.2 9.3 %collective-permute-start.13 = (f32[4,24,128]{2,1,0:T(8,128)S(1)}, f32[4,24,128]{2,1,0:T(8,128)S(1)}, u32[]{:S(2)}, u32[]{:S(2)}) collective-permute-start(f32[4,24,128]{2,1,0:T(8,128)S(1)} %get-tuple-element.57), channel_id=1, source_target_pairs={{16,32},{24,40},{32,16},{40,24},{48,64},{56,72},{64,48},{72,56},{8... | collective-permute-start | bytes 147464 | tf_op jit(solution)/shard_map/ppermute | solution.py:413
  128.7 6.0 %collective-permute-start.12 = (f32[4,24,128]{2,1,0:T(8,128)S(1)}, f32[4,24,128]{2,1,0:T(8,128)S(1)}, u32[]{:S(2)}, u32[]{:S(2)}) collective-permute-start(f32[4,24,128]{2,1,0:T(8,128)S(1)} %get-tuple-element.57), channel_id=1, source_target_pairs={{0,16},{8,24},{16,0},{24,8},{32,48},{40,56},{48,32},{56,40},{64,80... | collective-permute-start | bytes 147464 | tf_op jit(solution)/shard_map/ppermute | solution.py:413
  132.5 7.4 %collective-permute-start.14 = (f32[4,24,128]{2,1,0:T(8,128)S(1)}, f32[4,24,128]{2,1,0:T(8,128)S(1)}, u32[]{:S(2)}, u32[]{:S(2)}) collective-permute-start(f32[4,24,128]{2,1,0:T(8,128)S(1)} %collective-permute-done.13), channel_id=1, source_target_pairs={{0,16},{8,24},{16,0},{24,8},{32,48},{40,56},{48,32},{56,40},{64,80... | collective-permute-start | bytes 147464 | tf_op jit(solution)/shard_map/ppermute | solution.py:413
  134.6 9.3 %collective-permute-start.15 = (f32[4,24,128]{2,1,0:T(8,128)S(1)}, f32[4,24,128]{2,1,0:T(8,128)S(1)}, u32[]{:S(2)}, u32[]{:S(2)}) collective-permute-start(f32[4,24,128]{2,1,0:T(8,128)S(1)} %collective-permute-done.12), channel_id=1, source_target_pairs={{16,32},{24,40},{32,16},{40,24},{48,64},{56,72},{64,48},{72,56},{8... | collective-permute-start | bytes 147464 | tf_op jit(solution)/shard_map/ppermute | solution.py:413
  144.0 3.6 %collective-permute-start.16 = (f32[29,24,128]{2,1,0:T(8,128)S(1)}, f32[29,24,128]{2,1,0:T(8,128)S(1)}, u32[]{:S(2)}, u32[]{:S(2)}) collective-permute-start(f32[29,24,128]{2,1,0:T(8,128)S(1)} %constant_dynamic-update-slice_fusion.6.mine), channel_id=1, source_target_pairs={{0,8},{8,0},{16,24},{24,16},{32,40},{40,32},{48,56},{56,48},{64,72... | collective-permute-start | bytes 1069064 | tf_op jit(solution)/shard_map/ppermute | solution.py:413
  153.6 6.1 %collective-permute-start.17 = (f32[3,3,24,128]{3,2,1,0:T(8,128)S(1)}, f32[3,3,24,128]{3,2,1,0:T(8,128)S(1)}, u32[]{:S(2)}, u32[]{:S(2)}) collective-permute-start(f32[3,3,24,128]{3,2,1,0:T(8,128)S(1)} %get-tuple-element.62), channel_id=1, source_target_pairs={{8,16},{16,8},{24,32},{32,24},{40,48},{48,40},{56,64},{64,56},{72,... | collective-permute-start | bytes 331784 | tf_op jit(solution)/shard_map/ppermute | solution.py:413

commit v6 on v5

--- a/solution.py
+++ b/solution.py
@@ -12,7 +12,7 @@
 NZ = 24
 HALO = 6
 LANES = 128
-UNROLL = (3, 8, 10, 10)
+UNROLL = (3, 4, 8, 8)
 PARAMS = pltpu.CompilerParams(vmem_limit_bytes=12 << 20)
 
 
@@ -117,7 +117,7 @@
                 total = residual if total is None else total + residual
             target[0][c, index(target, q)] = 0.25 * pair_sum(total, period)
 
-    each_row(low, high, body, (UNROLL[level] + 1) // 2)
+    each_row(low, high, body, max(1, UNROLL[level] // 2))
 
 
 def from_zero(target, source, density, factor, level, period, rows, position, low, high, finer=None, reach=0, group=1):
@@ -179,6 +179,11 @@
             edge[c * count + r] = v1[0][c, (1 - position[4]) + (r - v1[1])]
 
 
+def own_position():
+    i, j = lax.axis_index("gx"), lax.axis_index("gz")
+    return i, j, lax.axis_size("gx"), lax.axis_size("gz"), i % 2, j % 2, i // 2 % 2
+
+
 def by_parity(position, body):
     for odd in range(2):
         pl.when(position[4] == odd)(lambda odd=odd: body(odd))
@@ -211,7 +216,7 @@
     by_parity(position, body)
 
 
-def pack_kernel(position, source, density, out):
+def pack_kernel(source, density, out):
     blocks = out.shape[0]
     for ref, at, n in ((source, 0, source.shape[0]), (density, source.shape[0], density.shape[0])):
         for m in range(n):
@@ -224,7 +229,8 @@
                 out[b, at + m, :, LANES:] = jnp.where(lane < LANES // 2, after, before)
 
 
-def unpack_kernel(position, taken, own, first, second, scratch):
+def unpack_kernel(taken, own, first, second, scratch):
+    position = own_position()
     blocks, _, rows, _ = taken.shape
     depth = NZ // blocks
     for c in range(C + 1):
@@ -242,7 +248,8 @@
     rows_to_send(position, own, first, second)
 
 
-def first_down_kernel(position, own, second, first, g0, d0, f0, v0, g1, d1, f1, v1, packed, edge, field, field1):
+def first_down_kernel(own, second, first, g0, d0, f0, v0, g1, d1, f1, v1, packed, edge, field, field1):
+    position = own_position()
     rows = own.shape[1]
 
     def store(c, at, value):
@@ -260,7 +267,8 @@
     level_one_down(position, (g1, -2), (v1, -2), (field1, -2), (d1, -3), (f1, -3), packed, edge)
 
 
-def side_kernel(position, own, second, first, tall, to_first, to_second):
+def side_kernel(own, second, first, tall, to_first, to_second):
+    position = own_position()
     half = tall.shape[1] // 2
     low = (lane_index() < LANES // 2) == (position[5] == 1)
 
@@ -275,7 +283,8 @@
             to_second[c, r] = jnp.where(low, two, one)
 
 
-def second_down_kernel(position, tall, first, second, g0, d0, f0, d1, f1, v0, g1, v1, packed, edge, wide, field, field1):
+def second_down_kernel(tall, first, second, g0, d0, f0, d1, f1, v0, g1, v1, packed, edge, wide, field, field1):
+    position = own_position()
     half = tall.shape[1] // 2
     halo = half - v0.shape[1] // 2 + HALO
     rows = 2 * (half - halo)
@@ -294,7 +303,8 @@
     level_one_down(position, (g1, -2), (v1, -2), (field1, -2), (d1, -3), (f1, -3), packed, edge)
 
 
-def coarse_kernel(position, mine, other, v1, out, first, second, g2, d2, f2, g3, d3, f3, a, b, a3, b3):
+def coarse_kernel(mine, other, v1, out, first, second, g2, d2, f2, g3, d3, f3, a, b, a3, b3):
+    position = own_position()
     lane = lane_index()
     odd, step = position[4], 1 - 2 * position[6]
     count, reach = first.shape[1], 8
@@ -363,7 +373,8 @@
     sweep((field, -HALO), (emit, -HALO), (g0, -HALO), (f0, -HALO), 0, 0, rows)
 
 
-def first_up_kernel(position, own, left, right, g0, f0, v0, g1, f1, out, first, second, wide, u, w, field, other):
+def first_up_kernel(own, left, right, g0, f0, v0, g1, f1, out, first, second, wide, u, w, field, other):
+    position = own_position()
     climb(position, own, left, right, g0, f0, v0, g1, f1, wide, u, w, field, other)
     for c in range(C):
         for r in range(out.shape[1]):
@@ -371,7 +382,8 @@
     rows_to_send(position, out, first, second)
 
 
-def last_up_kernel(position, own, left, right, g0, f0, v0, g1, f1, out, wide, u, w, field, other, scratch):
+def last_up_kernel(own, left, right, g0, f0, v0, g1, f1, out, wide, u, w, field, other, scratch):
+    position = own_position()
     climb(position, own, left, right, g0, f0, v0, g1, f1, wide, u, w, field, other)
     blocks, _, rows, _ = out.shape
     depth = NZ // blocks
@@ -388,13 +400,12 @@
         out[:, :, b * LANES : (b + 1) * LANES] = taken[b]
 
 
-def call(kernel, outs, scratch, *args, scalars=0):
+def call(kernel, outs, scratch, *args):
     shape = lambda s: jax.ShapeDtypeStruct(s, jnp.float32)
-    specs = [pl.BlockSpec(memory_space=pltpu.SMEM)] * scalars + [pl.BlockSpec(memory_space=pltpu.VMEM)] * (len(args) - scalars)
     out = pl.pallas_call(
         kernel,
         out_shape=[shape(s) for s in outs],
-        in_specs=specs,
+        in_specs=[pl.BlockSpec(memory_space=pltpu.VMEM)] * len(args),
         out_specs=[pl.BlockSpec(memory_space=pltpu.VMEM)] * len(outs),
         scratch_shapes=[pltpu.VMEM(s, jnp.float32) for s in scratch],
         compiler_params=PARAMS,
@@ -416,19 +427,15 @@
 def shards(right_side, density):
     blocks = lax.axis_size("gz")
     depth, rows, columns = density.shape
-    i, j = lax.axis_index("gx"), lax.axis_index("gz")
-    position = jnp.stack([i, j, lax.axis_size("gx"), blocks, i % 2, j % 2, i // 2 % 2]).astype(jnp.int32)
     W, R0, R1 = 2 * LANES, rows + 2 * HALO, rows // 2
 
-    (sent,) = call(pack_kernel, [(blocks, (C + 1) * depth, rows, W)], [], position, right_side.reshape(C * depth, rows, columns), density, scalars=1)
+    (sent,) = call(pack_kernel, [(blocks, (C + 1) * depth, rows, W)], [], right_side.reshape(C * depth, rows, columns), density)
     taken = lax.all_to_all(sent, "gz", 0, 0)
     own, first, second = call(
         unpack_kernel,
         [(C + 1, rows, NZ, W), (C + 1, HALO, NZ, W), (C + 1, HALO, NZ, W)],
         [(C + 1, 2, NZ * rows, LANES)],
-        position,
         taken,
-        scalars=1,
     )
     fine, mid = (C, R0, NZ, W), (C, R1 + 4, NZ, LANES)
     sends = [(C + 1, NZ, LANES), (C * (R1 - 1), NZ, LANES)]
@@ -436,11 +443,9 @@
         first_down_kernel,
         [fine, fine[1:], fine[1:], fine, mid, (R1 + 6, NZ, LANES), (R1 + 6, NZ, LANES), mid, *sends],
         [fine, mid],
-        position,
         own,
         swap(second, "gx", False),
         swap(first, "gx", True),
-        scalars=1,
     )
 
     def coarse(v1, packed, edge):
@@ -452,11 +457,9 @@
             coarse_kernel,
             [(C, R1, NZ, LANES)] + [(C, R1 - 1, NZ, LANES)] * 2,
             [two, two[1:], two[1:], three, three[1:], three[1:], two, two, three, three],
-            position,
-            mine,
+                mine,
             swap(mine, "gx", True),
             v1,
-            scalars=1,
         )
         return out, first, swap(second, "gx", False)
 
@@ -466,31 +469,26 @@
         first_up_kernel,
         [(C, rows, NZ, LANES), (C, reach, NZ, LANES), (C, reach, NZ, LANES)],
         [middle, middle, middle, fine, fine],
-        position,
         *coarse(*down),
         g0,
         f0,
         v0,
         g1,
         f1,
-        scalars=1,
     )
     half = (rows + 2 * reach) // 2
     tall, first, second = call(
         side_kernel,
         [(C, 2 * half, NZ, LANES)] + [(C, half, NZ, LANES)] * 2,
         [],
-        position,
         field,
         swap(second, "gx", False),
         swap(first, "gx", True),
-        scalars=1,
     )
     v0, g1, *down = call(
         second_down_kernel,
         [fine, mid, mid, *sends],
         [(C, 2 * half, NZ, W), fine, mid],
-        position,
         tall,
         swap(first, "gz", True),
         swap(second, "gz", False),
@@ -499,20 +497,17 @@
         f0,
         d1,
         f1,
-        scalars=1,
     )
     (sent,) = call(
         last_up_kernel,
         [(blocks, C * depth, rows, LANES)],
         [middle, middle, middle, fine, fine, (C, NZ * rows, LANES)],
-        position,
         *coarse(*down),
         g0,
         f0,
         v0,
         g1,
         f1,
-        scalars=1,
     )
     (out,) = call(join_kernel, [(C * depth, rows, columns)], [], lax.all_to_all(sent, "gz", 0, 0))
     return out.reshape(right_side.shape)

time: 184 us -> 174 us (0.946)
  Pallas kernels: 31.9 us -> 22.4 us
    pallas_call x10, Pallas kernels: 31.9 us -> 22.4 us  [call(): pl.pallas_call(kernel, out_shape=[shape(s) for s in outs], in_specs=[pl.B...]
where the time goes in v6:
time: 174 us; the launch traced here: 171 us
  starting transfers between devices  62.8 us (36%)
  blocking collectives  48 us (28%)
  waiting for transfers between devices  36.1 us (21%)
  Pallas kernels  22.4 us (13%)
  local copies, waits for them, and re-layouts  1.93 us (1%)
    ppermute x18, starting transfers between devices, swap(): return lax.ppermute(values, axis, pairs)  62.8 us
    ppermute x18, waiting for transfers between devices, swap(): return lax.ppermute(values, axis, pairs)  36.1 us
    all_to_all x1, blocking collectives, shards(): taken = lax.all_to_all(sent, 'gz', 0, 0)  30 us
    pallas_call x10, Pallas kernels, call(): pl.pallas_call(kernel, out_shape=[shape(s) for s in outs], in_specs=[pl.B...  22.4 us
    all_to_all x1, blocking collectives, shards(): lax.all_to_all(sent, 'gz', 0, 0)  17.9 us
  transfers between devices with their start and end apart: 18, of which 13 were waited for; matrix products, arithmetic and copies ran while one was open for 0% of the time, Pallas kernels for 0%

profile of v6, /device:TPU:198, one launch (start us, length us, event | category | flops | bytes accessed | tf_op | source)
XLA Modules:
  0.0 171.4 jit_solution(14012768444559178210)
XLA Ops:
  0.0 0.0 copy-start
  0.0 1.0 copy-done
  1.0 0.0 copy-start.1
  1.0 0.9 copy-done.1
  1.9 0.1 pack_kernel.1
  1.9 30.0 %all_to_all.10.taken = f32[8,12,8,256]{3,2,1,0:T(8,128)S(1)} all-to-all(f32[8,12,8,256]{3,2,1,0:T(8,128)S(1)} %pack_kernel.1), channel_id=1, replica_groups=mesh['gx'=64,'gz'=8] {'gz'}, dimensions={0} | all-to-all | bytes 1572864 | tf_op jit(solution)/shard_map/all_to_all | solution.py:433
  31.9 0.3 unpack_kernel.1
  32.2 1.9 %collective-permute-start = (f32[4,6,24,256]{3,2,1,0:T(8,128)S(1)}, f32[4,6,24,256]{3,2,1,0:T(8,128)S(1)}, u32[]{:S(2)}, u32[]{:S(2)}) collective-permute-start(f32[4,6,24,256]{3,2,1,0:T(8,128)S(1)} %get-tuple-element.36), channel_id=1, source_target_pairs={{8,16},{16,8},{24,32},{32,24},{40,48},{48,40},{56,64},{64,56},{72,... | collective-permute-start | bytes 1769480 | tf_op jit(solution)/shard_map/ppermute | solution.py:424
  34.1 5.5 %collective-permute-start.1 = (f32[4,6,24,256]{3,2,1,0:T(8,128)S(1)}, f32[4,6,24,256]{3,2,1,0:T(8,128)S(1)}, u32[]{:S(2)}, u32[]{:S(2)}) collective-permute-start(f32[4,6,24,256]{3,2,1,0:T(8,128)S(1)} %get-tuple-element.37), channel_id=1, source_target_pairs={{0,8},{8,0},{16,24},{24,16},{32,40},{40,32},{48,56},{56,48},{64,72... | collective-permute-start | bytes 1769480 | tf_op jit(solution)/shard_map/ppermute | solution.py:424
  39.6 3.8 %collective-permute-done.second = f32[4,6,24,256]{3,2,1,0:T(8,128)S(1)} collective-permute-done((f32[4,6,24,256]{3,2,1,0:T(8,128)S(1)}, f32[4,6,24,256]{3,2,1,0:T(8,128)S(1)}, u32[]{:S(2)}, u32[]{:S(2)}) %collective-permute-start) | collective-permute-done | bytes 589856 | tf_op jit(solution)/shard_map/ppermute | solution.py:424
  43.4 0.0 collective-permute-done.1.first
  43.4 5.0 %first_down_kernel.1 = (f32[3,20,24,256]{3,2,1,0:T(8,128)S(1)}, f32[20,24,256]{2,1,0:T(8,128)S(1)}, f32[20,24,256]{2,1,0:T(8,128)S(1)}, f32[3,20,24,256]{3,2,1,0...) custom-call(f32[4,8,24,256]{3,2,1,0:T(8,128)S(1)} %get-tuple-element, ...), custom_call_target="tpu_custom_call" | custom-call | tf_op jit(solution)/shard_map/first_down_kernel/pallas_call | solution.py:405
  48.4 8.7 %collective-permute-start.3 = (f32[4,24,128]{2,1,0:T(8,128)S(1)}, f32[4,24,128]{2,1,0:T(8,128)S(1)}, u32[]{:S(2)}, u32[]{:S(2)}) collective-permute-start(f32[4,24,128]{2,1,0:T(8,128)S(1)} %get-tuple-element.38), channel_id=1, source_target_pairs={{16,32},{24,40},{32,16},{40,24},{48,64},{56,72},{64,48},{72,56},{8... | collective-permute-start | bytes 147464 | tf_op jit(solution)/shard_map/ppermute | solution.py:424
  57.2 1.9 %collective-permute-start.2 = (f32[4,24,128]{2,1,0:T(8,128)S(1)}, f32[4,24,128]{2,1,0:T(8,128)S(1)}, u32[]{:S(2)}, u32[]{:S(2)}) collective-permute-start(f32[4,24,128]{2,1,0:T(8,128)S(1)} %get-tuple-element.38), channel_id=1, source_target_pairs={{0,16},{8,24},{16,0},{24,8},{32,48},{40,56},{48,32},{56,40},{64,80... | collective-permute-start | bytes 147464 | tf_op jit(solution)/shard_map/ppermute | solution.py:424
  59.1 0.1 collective-permute-done.3
  59.2 3.8 %collective-permute-start.4 = (f32[4,24,128]{2,1,0:T(8,128)S(1)}, f32[4,24,128]{2,1,0:T(8,128)S(1)}, u32[]{:S(2)}, u32[]{:S(2)}) collective-permute-start(f32[4,24,128]{2,1,0:T(8,128)S(1)} %collective-permute-done.3), channel_id=1, source_target_pairs={{0,16},{8,24},{16,0},{24,8},{32,48},{40,56},{48,32},{56,40},{64,80... | collective-permute-start | bytes 147464 | tf_op jit(solution)/shard_map/ppermute | solution.py:424
  63.1 0.3 collective-permute-done.2
  63.4 5.0 %collective-permute-start.5 = (f32[4,24,128]{2,1,0:T(8,128)S(1)}, f32[4,24,128]{2,1,0:T(8,128)S(1)}, u32[]{:S(2)}, u32[]{:S(2)}) collective-permute-start(f32[4,24,128]{2,1,0:T(8,128)S(1)} %collective-permute-done.2), channel_id=1, source_target_pairs={{16,32},{24,40},{32,16},{40,24},{48,64},{56,72},{64,48},{72,56},{8... | collective-permute-start | bytes 147464 | tf_op jit(solution)/shard_map/ppermute | solution.py:424
  68.4 0.0 collective-permute-done.4
  68.5 4.2 %collective-permute-done.5 = f32[4,24,128]{2,1,0:T(8,128)S(1)} collective-permute-done((f32[4,24,128]{2,1,0:T(8,128)S(1)}, f32[4,24,128]{2,1,0:T(8,128)S(1)}, u32[]{:S(2)}, u32[]{:S(2)}) %collective-permute-start.5) | collective-permute-done | bytes 49184 | tf_op jit(solution)/shard_map/ppermute | solution.py:424
  72.7 1.9 %collective-permute-start.6 = (f32[29,24,128]{2,1,0:T(8,128)S(1)}, f32[29,24,128]{2,1,0:T(8,128)S(1)}, u32[]{:S(2)}, u32[]{:S(2)}) collective-permute-start(f32[29,24,128]{2,1,0:T(8,128)S(1)} %constant_dynamic-update-slice_fusion.mine), channel_id=1, source_target_pairs={{0,8},{8,0},{16,24},{24,16},{32,40},{40,32},{48,56},{56,48},{64,72... | collective-permute-start | bytes 1069064 | tf_op jit(solution)/shard_map/ppermute | solution.py:424
  74.6 1.6 collective-permute-done.6.other
  76.2 2.9 %coarse_kernel.2 = (f32[3,4,24,128]{3,2,1,0:T(8,128)S(1)}, f32[3,3,24,128]{3,2,1,0:T(8,128)S(1)}, f32[3,3,24,128]{3,2,1,0:T(8,128)S(1)}) custom-call(f32[29,24,128]{2,1,0:T(8,128)S(1)} %constant_dynamic-update-slice_fusion.mine, f32[29,24,128]{2,1,0:T(8,128)S(1)} %collective-permute-done.6.other, f32[3,8,24,128]{3,2,1,0:T(8,128)S(1)} %get-tuple-element.40.v1), custom_call_target="tpu_custom_call" | custom-call | tf_op jit(solution)/shard_map/coarse_kernel/pallas_call | solution.py:405
  79.1 1.9 %collective-permute-start.7 = (f32[3,3,24,128]{3,2,1,0:T(8,128)S(1)}, f32[3,3,24,128]{3,2,1,0:T(8,128)S(1)}, u32[]{:S(2)}, u32[]{:S(2)}) collective-permute-start(f32[3,3,24,128]{3,2,1,0:T(8,128)S(1)} %get-tuple-element.43), channel_id=1, source_target_pairs={{8,16},{16,8},{24,32},{32,24},{40,48},{48,40},{56,64},{64,56},{72,... | collective-permute-start | bytes 331784 | tf_op jit(solution)/shard_map/ppermute | solution.py:424
  81.1 4.1 %collective-permute-done.7.right = f32[3,3,24,128]{3,2,1,0:T(8,128)S(1)} collective-permute-done((f32[3,3,24,128]{3,2,1,0:T(8,128)S(1)}, f32[3,3,24,128]{3,2,1,0:T(8,128)S(1)}, u32[]{:S(2)}, u32[]{:S(2)}) %collective-permute-start.7) | collective-permute-done | bytes 110624 | tf_op jit(solution)/shard_map/ppermute | solution.py:424
  85.2 2.3 %first_up_kernel.1 = (f32[3,8,24,128]{3,2,1,0:T(8,128)S(1)}, f32[3,7,24,128]{3,2,1,0:T(8,128)S(1)}, f32[3,7,24,128]{3,2,1,0:T(8,128)S(1)}) custom-call(f32[3,4,24,128]{3,2,1,0:T(8,128)S(1)} %get-tuple-element.41.own, f32[3,3,24,128]{3,2,1,0:T(8,128)S(1)} %get-tuple-element.42.left, f32[3,3,24,128]{3,2,1,0:T(8,128)S(1)} %collective-permute-done.7.right, ...), custom_call_target="tpu_custom_call" | custom-call | tf_op jit(solution)/shard_map/first_up_kernel/pallas_call | solution.py:405
  87.5 1.9 %collective-permute-start.8 = (f32[3,7,24,128]{3,2,1,0:T(8,128)S(1)}, f32[3,7,24,128]{3,2,1,0:T(8,128)S(1)}, u32[]{:S(2)}, u32[]{:S(2)}) collective-permute-start(f32[3,7,24,128]{3,2,1,0:T(8,128)S(1)} %get-tuple-element.50), channel_id=1, source_target_pairs={{8,16},{16,8},{24,32},{32,24},{40,48},{48,40},{56,64},{64,56},{72,... | collective-permute-start | bytes 774152 | tf_op jit(solution)/shard_map/ppermute | solution.py:424
  89.4 8.5 %collective-permute-start.9 = (f32[3,7,24,128]{3,2,1,0:T(8,128)S(1)}, f32[3,7,24,128]{3,2,1,0:T(8,128)S(1)}, u32[]{:S(2)}, u32[]{:S(2)}) collective-permute-start(f32[3,7,24,128]{3,2,1,0:T(8,128)S(1)} %get-tuple-element.51), channel_id=1, source_target_pairs={{0,8},{8,0},{16,24},{24,16},{32,40},{40,32},{48,56},{56,48},{64,72... | collective-permute-start | bytes 774152 | tf_op jit(solution)/shard_map/ppermute | solution.py:424
  97.9 0.0 collective-permute-done.8.second
  97.9 1.1 collective-permute-done.9.first
  99.0 0.2 side_kernel.1
  99.2 2.5 %collective-permute-start.10 = (f32[3,11,24,128]{3,2,1,0:T(8,128)S(1)}, f32[3,11,24,128]{3,2,1,0:T(8,128)S(1)}, u32[]{:S(2)}, u32[]{:S(2)}) collective-permute-start(f32[3,11,24,128]{3,2,1,0:T(8,128)S(1)} %get-tuple-element.53), channel_id=1, source_target_pairs={{0,1},{1,0},{2,3},{3,2},{4,5},{5,4},{6,7},{7,6},{8,9},{9,8},{10,11... | collective-permute-start | bytes 1216520 | tf_op jit(solution)/shard_map/ppermute | solution.py:424
  101.7 0.7 collective-permute-start.11
  102.4 9.0 %collective-permute-done.10.first = f32[3,11,24,128]{3,2,1,0:T(8,128)S(1)} collective-permute-done((f32[3,11,24,128]{3,2,1,0:T(8,128)S(1)}, f32[3,11,24,128]{3,2,1,0:T(8,128)S(1)}, u32[]{:S(2)}, u32[]{:S(2)}) %collective-permute-start.10) | collective-permute-done | bytes 405536 | tf_op jit(solution)/shard_map/ppermute | solution.py:424
  111.4 0.0 collective-permute-done.11.second
  111.4 5.8 %second_down_kernel.1 = (f32[3,20,24,256]{3,2,1,0:T(8,128)S(1)}, f32[3,8,24,128]{3,2,1,0:T(8,128)S(1)}, f32[3,8,24,128]{3,2,1,0:T(8,128)S(1)}, f32[4,24,128]{2,1,0:T(8,128)S(1)}, f32[9,24,128]{2,1,0:T(8,128)S(1)}) custom-call(f32[3,22,24,128]{3,2,1,0:T(8,128)S(1)} %get-tuple-element.52.tall, f32[3,11,24,128]{3,2,1,0:T(8,128)S(1)} %collective-permute-done.10.first, ...), custom_call_target="tpu_custom_call" | custom-call | tf_op jit(solution)/shard_map/second_down_kernel/pallas_call | solution.py:405
  117.2 5.4 %collective-permute-start.13 = (f32[4,24,128]{2,1,0:T(8,128)S(1)}, f32[4,24,128]{2,1,0:T(8,128)S(1)}, u32[]{:S(2)}, u32[]{:S(2)}) collective-permute-start(f32[4,24,128]{2,1,0:T(8,128)S(1)} %get-tuple-element.57), channel_id=1, source_target_pairs={{16,32},{24,40},{32,16},{40,24},{48,64},{56,72},{64,48},{72,56},{8... | collective-permute-start | bytes 147464 | tf_op jit(solution)/shard_map/ppermute | solution.py:424
  122.6 1.9 %collective-permute-start.12 = (f32[4,24,128]{2,1,0:T(8,128)S(1)}, f32[4,24,128]{2,1,0:T(8,128)S(1)}, u32[]{:S(2)}, u32[]{:S(2)}) collective-permute-start(f32[4,24,128]{2,1,0:T(8,128)S(1)} %get-tuple-element.57), channel_id=1, source_target_pairs={{0,16},{8,24},{16,0},{24,8},{32,48},{40,56},{48,32},{56,40},{64,80... | collective-permute-start | bytes 147464 | tf_op jit(solution)/shard_map/ppermute | solution.py:424
  124.6 1.9 %collective-permute-done.13 = f32[4,24,128]{2,1,0:T(8,128)S(1)} collective-permute-done((f32[4,24,128]{2,1,0:T(8,128)S(1)}, f32[4,24,128]{2,1,0:T(8,128)S(1)}, u32[]{:S(2)}, u32[]{:S(2)}) %collective-permute-start.13) | collective-permute-done | bytes 49184 | tf_op jit(solution)/shard_map/ppermute | solution.py:424
  126.5 2.0 %collective-permute-start.14 = (f32[4,24,128]{2,1,0:T(8,128)S(1)}, f32[4,24,128]{2,1,0:T(8,128)S(1)}, u32[]{:S(2)}, u32[]{:S(2)}) collective-permute-start(f32[4,24,128]{2,1,0:T(8,128)S(1)} %collective-permute-done.13), channel_id=1, source_target_pairs={{0,16},{8,24},{16,0},{24,8},{32,48},{40,56},{48,32},{56,40},{64,80... | collective-permute-start | bytes 147464 | tf_op jit(solution)/shard_map/ppermute | solution.py:424
  128.5 0.1 collective-permute-done.12
  128.6 5.2 %collective-permute-start.15 = (f32[4,24,128]{2,1,0:T(8,128)S(1)}, f32[4,24,128]{2,1,0:T(8,128)S(1)}, u32[]{:S(2)}, u32[]{:S(2)}) collective-permute-start(f32[4,24,128]{2,1,0:T(8,128)S(1)} %collective-permute-done.12), channel_id=1, source_target_pairs={{16,32},{24,40},{32,16},{40,24},{48,64},{56,72},{64,48},{72,56},{8... | collective-permute-start | bytes 147464 | tf_op jit(solution)/shard_map/ppermute | solution.py:424
  133.9 0.0 collective-permute-done.14
  133.9 4.0 %collective-permute-done.15 = f32[4,24,128]{2,1,0:T(8,128)S(1)} collective-permute-done((f32[4,24,128]{2,1,0:T(8,128)S(1)}, f32[4,24,128]{2,1,0:T(8,128)S(1)}, u32[]{:S(2)}, u32[]{:S(2)}) %collective-permute-start.15) | collective-permute-done | bytes 49184 | tf_op jit(solution)/shard_map/ppermute | solution.py:424
  138.0 1.9 %collective-permute-start.16 = (f32[29,24,128]{2,1,0:T(8,128)S(1)}, f32[29,24,128]{2,1,0:T(8,128)S(1)}, u32[]{:S(2)}, u32[]{:S(2)}) collective-permute-start(f32[29,24,128]{2,1,0:T(8,128)S(1)} %constant_dynamic-update-slice_fusion.6.mine), channel_id=1, source_target_pairs={{0,8},{8,0},{16,24},{24,16},{32,40},{40,32},{48,56},{56,48},{64,72... | collective-permute-start | bytes 1069064 | tf_op jit(solution)/shard_map/ppermute | solution.py:424
  139.9 1.6 collective-permute-done.16.other
  141.5 2.9 %coarse_kernel.3 = (f32[3,4,24,128]{3,2,1,0:T(8,128)S(1)}, f32[3,3,24,128]{3,2,1,0:T(8,128)S(1)}, f32[3,3,24,128]{3,2,1,0:T(8,128)S(1)}) custom-call(f32[29,24,128]{2,1,0:T(8,128)S(1)} %constant_dynamic-update-slice_fusion.6.mine, f32[29,24,128]{2,1,0:T(8,128)S(1)} %collective-permute-done.16.other, f32[3,8,24,128]{3,2,1,0:T(8,128)S(1)} %get-tuple-element.59.v1), custom_call_target="tpu_custom_call" | custom-call | tf_op jit(solution)/shard_map/coarse_kernel/pallas_call | solution.py:405
  144.4 1.9 %collective-permute-start.17 = (f32[3,3,24,128]{3,2,1,0:T(8,128)S(1)}, f32[3,3,24,128]{3,2,1,0:T(8,128)S(1)}, u32[]{:S(2)}, u32[]{:S(2)}) collective-permute-start(f32[3,3,24,128]{3,2,1,0:T(8,128)S(1)} %get-tuple-element.62), channel_id=1, source_target_pairs={{8,16},{16,8},{24,32},{32,24},{40,48},{48,40},{56,64},{64,56},{72,... | collective-permute-start | bytes 331784 | tf_op jit(solution)/shard_map/ppermute | solution.py:424
  146.3 4.1 %collective-permute-done.17.right = f32[3,3,24,128]{3,2,1,0:T(8,128)S(1)} collective-permute-done((f32[3,3,24,128]{3,2,1,0:T(8,128)S(1)}, f32[3,3,24,128]{3,2,1,0:T(8,128)S(1)}, u32[]{:S(2)}, u32[]{:S(2)}) %collective-permute-start.17) | collective-permute-done | bytes 110624 | tf_op jit(solution)/shard_map/ppermute | solution.py:424
  150.5 2.3 %last_up_kernel.1 = f32[8,9,8,128]{3,2,1,0:T(8,128)S(1)} custom-call(f32[3,4,24,128]{3,2,1,0:T(8,128)S(1)} %get-tuple-element.60.own, f32[3,3,24,128]{3,2,1,0:T(8,128)S(1)} %get-tuple-element.61.left, f32[3,3,24,128]{3,2,1,0:T(8,128)S(1)} %collective-permute-done.17.right, f32[3,20,24,256]{3,2,1,0:T(8,128)S(1)} %get-tuple-element.44.g0, ...), custom_call_target="tpu_custom_call" | custom-call | tf_op jit(solution)/shard_map/last_up_kernel/pallas_call | solution.py:405
  152.7 17.9 %all_to_all.11.taken = f32[8,9,8,128]{3,2,1,0:T(8,128)S(1)} all-to-all(f32[8,9,8,128]{3,2,1,0:T(8,128)S(1)} %last_up_kernel.1), channel_id=1, replica_groups=mesh['gx'=64,'gz'=8] {'gz'}, dimensions={0} | all-to-all | bytes 589824 | tf_op jit(solution)/shard_map/all_to_all | solution.py:512
  170.7 0.7 join_kernel.1
  (12 shorter events, 0.1 us)
Async XLA Ops:
  0.0 1.0 copy-start
  1.0 0.9 copy-start.1
  32.2 11.2 %collective-permute-start = (f32[4,6,24,256]{3,2,1,0:T(8,128)S(1)}, f32[4,6,24,256]{3,2,1,0:T(8,128)S(1)}, u32[]{:S(2)}, u32[]{:S(2)}) collective-permute-start(f32[4,6,24,256]{3,2,1,0:T(8,128)S(1)} %get-tuple-element.36), channel_id=1, source_target_pairs={{8,16},{16,8},{24,32},{32,24},{40,48},{48,40},{56,64},{64,56},{72,... | collective-permute-start | bytes 1769480 | tf_op jit(solution)/shard_map/ppermute | solution.py:424
  34.1 9.3 %collective-permute-start.1 = (f32[4,6,24,256]{3,2,1,0:T(8,128)S(1)}, f32[4,6,24,256]{3,2,1,0:T(8,128)S(1)}, u32[]{:S(2)}, u32[]{:S(2)}) collective-permute-start(f32[4,6,24,256]{3,2,1,0:T(8,128)S(1)} %get-tuple-element.37), channel_id=1, source_target_pairs={{0,8},{8,0},{16,24},{24,16},{32,40},{40,32},{48,56},{56,48},{64,72... | collective-permute-start | bytes 1769480 | tf_op jit(solution)/shard_map/ppermute | solution.py:424
  48.4 10.8 %collective-permute-start.3 = (f32[4,24,128]{2,1,0:T(8,128)S(1)}, f32[4,24,128]{2,1,0:T(8,128)S(1)}, u32[]{:S(2)}, u32[]{:S(2)}) collective-permute-start(f32[4,24,128]{2,1,0:T(8,128)S(1)} %get-tuple-element.38), channel_id=1, source_target_pairs={{16,32},{24,40},{32,16},{40,24},{48,64},{56,72},{64,48},{72,56},{8... | collective-permute-start | bytes 147464 | tf_op jit(solution)/shard_map/ppermute | solution.py:424
  57.2 6.2 %collective-permute-start.2 = (f32[4,24,128]{2,1,0:T(8,128)S(1)}, f32[4,24,128]{2,1,0:T(8,128)S(1)}, u32[]{:S(2)}, u32[]{:S(2)}) collective-permute-start(f32[4,24,128]{2,1,0:T(8,128)S(1)} %get-tuple-element.38), channel_id=1, source_target_pairs={{0,16},{8,24},{16,0},{24,8},{32,48},{40,56},{48,32},{56,40},{64,80... | collective-permute-start | bytes 147464 | tf_op jit(solution)/shard_map/ppermute | solution.py:424
  59.2 9.2 %collective-permute-start.4 = (f32[4,24,128]{2,1,0:T(8,128)S(1)}, f32[4,24,128]{2,1,0:T(8,128)S(1)}, u32[]{:S(2)}, u32[]{:S(2)}) collective-permute-start(f32[4,24,128]{2,1,0:T(8,128)S(1)} %collective-permute-done.3), channel_id=1, source_target_pairs={{0,16},{8,24},{16,0},{24,8},{32,48},{40,56},{48,32},{56,40},{64,80... | collective-permute-start | bytes 147464 | tf_op jit(solution)/shard_map/ppermute | solution.py:424
  63.4 9.3 %collective-permute-start.5 = (f32[4,24,128]{2,1,0:T(8,128)S(1)}, f32[4,24,128]{2,1,0:T(8,128)S(1)}, u32[]{:S(2)}, u32[]{:S(2)}) collective-permute-start(f32[4,24,128]{2,1,0:T(8,128)S(1)} %collective-permute-done.2), channel_id=1, source_target_pairs={{16,32},{24,40},{32,16},{40,24},{48,64},{56,72},{64,48},{72,56},{8... | collective-permute-start | bytes 147464 | tf_op jit(solution)/shard_map/ppermute | solution.py:424
  72.7 3.6 %collective-permute-start.6 = (f32[29,24,128]{2,1,0:T(8,128)S(1)}, f32[29,24,128]{2,1,0:T(8,128)S(1)}, u32[]{:S(2)}, u32[]{:S(2)}) collective-permute-start(f32[29,24,128]{2,1,0:T(8,128)S(1)} %constant_dynamic-update-slice_fusion.mine), channel_id=1, source_target_pairs={{0,8},{8,0},{16,24},{24,16},{32,40},{40,32},{48,56},{56,48},{64,72... | collective-permute-start | bytes 1069064 | tf_op jit(solution)/shard_map/ppermute | solution.py:424
  79.1 6.1 %collective-permute-start.7 = (f32[3,3,24,128]{3,2,1,0:T(8,128)S(1)}, f32[3,3,24,128]{3,2,1,0:T(8,128)S(1)}, u32[]{:S(2)}, u32[]{:S(2)}) collective-permute-start(f32[3,3,24,128]{3,2,1,0:T(8,128)S(1)} %get-tuple-element.43), channel_id=1, source_target_pairs={{8,16},{16,8},{24,32},{32,24},{40,48},{48,40},{56,64},{64,56},{72,... | collective-permute-start | bytes 331784 | tf_op jit(solution)/shard_map/ppermute | solution.py:424
  87.5 10.4 %collective-permute-start.8 = (f32[3,7,24,128]{3,2,1,0:T(8,128)S(1)}, f32[3,7,24,128]{3,2,1,0:T(8,128)S(1)}, u32[]{:S(2)}, u32[]{:S(2)}) collective-permute-start(f32[3,7,24,128]{3,2,1,0:T(8,128)S(1)} %get-tuple-element.50), channel_id=1, source_target_pairs={{8,16},{16,8},{24,32},{32,24},{40,48},{48,40},{56,64},{64,56},{72,... | collective-permute-start | bytes 774152 | tf_op jit(solution)/shard_map/ppermute | solution.py:424
  89.4 9.6 %collective-permute-start.9 = (f32[3,7,24,128]{3,2,1,0:T(8,128)S(1)}, f32[3,7,24,128]{3,2,1,0:T(8,128)S(1)}, u32[]{:S(2)}, u32[]{:S(2)}) collective-permute-start(f32[3,7,24,128]{3,2,1,0:T(8,128)S(1)} %get-tuple-element.51), channel_id=1, source_target_pairs={{0,8},{8,0},{16,24},{24,16},{32,40},{40,32},{48,56},{56,48},{64,72... | collective-permute-start | bytes 774152 | tf_op jit(solution)/shard_map/ppermute | solution.py:424
  99.2 12.2 %collective-permute-start.10 = (f32[3,11,24,128]{3,2,1,0:T(8,128)S(1)}, f32[3,11,24,128]{3,2,1,0:T(8,128)S(1)}, u32[]{:S(2)}, u32[]{:S(2)}) collective-permute-start(f32[3,11,24,128]{3,2,1,0:T(8,128)S(1)} %get-tuple-element.53), channel_id=1, source_target_pairs={{0,1},{1,0},{2,3},{3,2},{4,5},{5,4},{6,7},{7,6},{8,9},{9,8},{10,11... | collective-permute-start | bytes 1216520 | tf_op jit(solution)/shard_map/ppermute | solution.py:424
  101.7 9.7 %collective-permute-start.11 = (f32[3,11,24,128]{3,2,1,0:T(8,128)S(1)}, f32[3,11,24,128]{3,2,1,0:T(8,128)S(1)}, u32[]{:S(2)}, u32[]{:S(2)}) collective-permute-start(f32[3,11,24,128]{3,2,1,0:T(8,128)S(1)} %get-tuple-element.54), channel_id=1, source_target_pairs={{1,2},{2,1},{3,4},{4,3},{5,6},{6,5},{9,10},{10,9},{11,12},{12,11},... | collective-permute-start | bytes 1216520 | tf_op jit(solution)/shard_map/ppermute | solution.py:424
  117.2 9.3 %collective-permute-start.13 = (f32[4,24,128]{2,1,0:T(8,128)S(1)}, f32[4,24,128]{2,1,0:T(8,128)S(1)}, u32[]{:S(2)}, u32[]{:S(2)}) collective-permute-start(f32[4,24,128]{2,1,0:T(8,128)S(1)} %get-tuple-element.57), channel_id=1, source_target_pairs={{16,32},{24,40},{32,16},{40,24},{48,64},{56,72},{64,48},{72,56},{8... | collective-permute-start | bytes 147464 | tf_op jit(solution)/shard_map/ppermute | solution.py:424
  122.6 6.0 %collective-permute-start.12 = (f32[4,24,128]{2,1,0:T(8,128)S(1)}, f32[4,24,128]{2,1,0:T(8,128)S(1)}, u32[]{:S(2)}, u32[]{:S(2)}) collective-permute-start(f32[4,24,128]{2,1,0:T(8,128)S(1)} %get-tuple-element.57), channel_id=1, source_target_pairs={{0,16},{8,24},{16,0},{24,8},{32,48},{40,56},{48,32},{56,40},{64,80... | collective-permute-start | bytes 147464 | tf_op jit(solution)/shard_map/ppermute | solution.py:424
  126.5 7.4 %collective-permute-start.14 = (f32[4,24,128]{2,1,0:T(8,128)S(1)}, f32[4,24,128]{2,1,0:T(8,128)S(1)}, u32[]{:S(2)}, u32[]{:S(2)}) collective-permute-start(f32[4,24,128]{2,1,0:T(8,128)S(1)} %collective-permute-done.13), channel_id=1, source_target_pairs={{0,16},{8,24},{16,0},{24,8},{32,48},{40,56},{48,32},{56,40},{64,80... | collective-permute-start | bytes 147464 | tf_op jit(solution)/shard_map/ppermute | solution.py:424
  128.6 9.3 %collective-permute-start.15 = (f32[4,24,128]{2,1,0:T(8,128)S(1)}, f32[4,24,128]{2,1,0:T(8,128)S(1)}, u32[]{:S(2)}, u32[]{:S(2)}) collective-permute-start(f32[4,24,128]{2,1,0:T(8,128)S(1)} %collective-permute-done.12), channel_id=1, source_target_pairs={{16,32},{24,40},{32,16},{40,24},{48,64},{56,72},{64,48},{72,56},{8... | collective-permute-start | bytes 147464 | tf_op jit(solution)/shard_map/ppermute | solution.py:424
  138.0 3.6 %collective-permute-start.16 = (f32[29,24,128]{2,1,0:T(8,128)S(1)}, f32[29,24,128]{2,1,0:T(8,128)S(1)}, u32[]{:S(2)}, u32[]{:S(2)}) collective-permute-start(f32[29,24,128]{2,1,0:T(8,128)S(1)} %constant_dynamic-update-slice_fusion.6.mine), channel_id=1, source_target_pairs={{0,8},{8,0},{16,24},{24,16},{32,40},{40,32},{48,56},{56,48},{64,72... | collective-permute-start | bytes 1069064 | tf_op jit(solution)/shard_map/ppermute | solution.py:424
  144.4 6.1 %collective-permute-start.17 = (f32[3,3,24,128]{3,2,1,0:T(8,128)S(1)}, f32[3,3,24,128]{3,2,1,0:T(8,128)S(1)}, u32[]{:S(2)}, u32[]{:S(2)}) collective-permute-start(f32[3,3,24,128]{3,2,1,0:T(8,128)S(1)} %get-tuple-element.62), channel_id=1, source_target_pairs={{8,16},{16,8},{24,32},{32,24},{40,48},{48,40},{56,64},{64,56},{72,... | collective-permute-start | bytes 331784 | tf_op jit(solution)/shard_map/ppermute | solution.py:424

commit v7 on v6

--- a/solution.py
+++ b/solution.py
@@ -216,36 +216,69 @@
     by_parity(position, body)
 
 
+def squeeze(parts):
+    lane = lax.broadcasted_iota(jnp.int32, parts[0].shape, 1)
+    last = parts[3]
+    spare = [pltpu.roll(last, 48, 1), pltpu.roll(last, 80, 1), jnp.where(lane < 64, pltpu.roll(last, 16, 1), pltpu.roll(last, 112, 1))]
+    return [jnp.where((lane < 48) | (lane >= 80), parts[t], spare[t]) for t in range(3)]
+
+
+def unsqueeze(tiles):
+    lane = lax.broadcasted_iota(jnp.int32, tiles[0].shape, 1)
+    low = jnp.where(lane < 32, pltpu.roll(tiles[0], 80, 1), pltpu.roll(tiles[2], 112, 1))
+    high = jnp.where(lane < 96, pltpu.roll(tiles[2], 16, 1), pltpu.roll(tiles[1], 48, 1))
+    return [*tiles, jnp.where(lane < 48, low, jnp.where(lane < 80, 1.0, high))]
+
+
 def pack_kernel(source, density, out):
-    blocks = out.shape[0]
-    for ref, at, n in ((source, 0, source.shape[0]), (density, source.shape[0], density.shape[0])):
-        for m in range(n):
-            for b in range(blocks):
-                out[b, at + m, :, :LANES] = ref[m, :, b * LANES : (b + 1) * LANES]
-                zero = jnp.zeros((ref.shape[1], LANES), jnp.float32)
-                after = ref[m, :, (b + 1) * LANES : (b + 2) * LANES] if b + 1 < blocks else zero
-                before = ref[m, :, (b - 1) * LANES : b * LANES] if b else zero
-                lane = lax.broadcasted_iota(jnp.int32, zero.shape, 1)
-                out[b, at + m, :, LANES:] = jnp.where(lane < LANES // 2, after, before)
+    blocks, n = out.shape[0], source.shape[0]
+    count = n + density.shape[0]
+
+    def block(m, b):
+        ref, at = (source, m) if m < n else (density, m - n)
+        return ref[at, :, b * LANES : (b + 1) * LANES]
+
+    zero = jnp.zeros((out.shape[2], LANES), jnp.float32)
+    lane = lax.broadcasted_iota(jnp.int32, zero.shape, 1)
+    for k in range(count // 4):
+        for b in range(blocks):
+            halos = []
+            for m in range(4 * k, 4 * k + 4):
+                out[b, m] = block(m, b)
+                after = block(m, b + 1) if b + 1 < blocks else zero
+                before = block(m, b - 1) if b else zero
+                halos.append(jnp.where(lane < LANES // 2, after, before))
+            for t, tile in enumerate(squeeze(halos)):
+                out[b, count + 3 * k + t] = tile
 
 
 def unpack_kernel(taken, own, first, second, scratch):
     position = own_position()
     blocks, _, rows, _ = taken.shape
     depth = NZ // blocks
-    for c in range(C + 1):
-        for b in range(blocks):
-            for z in range(depth):
-                at = (b * depth + z) * rows
-                for h in range(2):
-                    scratch[c, h, at : at + rows] = taken[b, c * depth + z, :, h * LANES : (h + 1) * LANES]
+    count = (C + 1) * depth
+    for b in range(blocks):
+        for k in range(count // 4):
+            halos = unsqueeze([taken[b, count + 3 * k + t] for t in range(3)])
+            for m in range(4 * k, 4 * k + 4):
+                at = (b * depth + m % depth) * rows
+                scratch[m // depth, 0, at : at + rows] = taken[b, m]
+                scratch[m // depth, 1, at : at + rows] = halos[m - 4 * k]
     for c in range(C + 1):
         for r in range(rows):
             for h in range(2):
-                part = scratch[c, h, pl.ds(r, NZ, stride=rows), :]
-                lanes = slice(h * LANES, (h + 1) * LANES)
-                own[c, r, :, lanes] = part
-    rows_to_send(position, own, first, second)
+                own[c, r, :, h * LANES : (h + 1) * LANES] = scratch[c, h, pl.ds(r, NZ, stride=rows), :]
+    spare = rows - HALO
+
+    def send(odd):
+        for target, start in ((first, (1 - odd) * spare), (second, odd * spare)):
+            for r in range(HALO):
+                for c in range(C + 1):
+                    target[c, r] = own[c, start + r, :, :LANES]
+                for t, tile in enumerate(squeeze([own[c, start + r, :, LANES:] for c in range(C + 1)])):
+                    target[C + 1 + t, r] = tile
+
+    by_parity(position, send)
 
 
 def first_down_kernel(own, second, first, g0, d0, f0, v0, g1, d1, f1, v1, packed, edge, field, field1):
@@ -258,7 +291,18 @@
         else:
             d0[at] = value
 
-    with_halo(position, own, first, second, store)
+    for c in range(C + 1):
+        for r in range(rows):
+            store(c, HALO + r, own[c, r])
+
+    def receive(odd):
+        for piece, at in ((first, (1 - odd) * (HALO + rows)), (second, odd * (HALO + rows))):
+            for r in range(HALO):
+                halos = unsqueeze([piece[C + 1 + t, r] for t in range(3)])
+                for c in range(C + 1):
+                    store(c, at + r, jnp.concatenate([piece[c, r], halos[c]], axis=1))
+
+    by_parity(position, receive)
     g, d, f, a, b = (g0, -HALO), (d0, -HALO), (f0, -HALO), (field, -HALO), (v0, -HALO)
     from_zero(a, g, d, f, 0, 2 * LANES, rows, position, -HALO, rows + HALO)
     sweep(b, a, g, f, 0, -5, rows + 5)
@@ -429,11 +473,18 @@
     depth, rows, columns = density.shape
     W, R0, R1 = 2 * LANES, rows + 2 * HALO, rows // 2
 
-    (sent,) = call(pack_kernel, [(blocks, (C + 1) * depth, rows, W)], [], right_side.reshape(C * depth, rows, columns), density)
+    count = (C + 1) * depth
+    (sent,) = call(
+        pack_kernel,
+        [(blocks, count + 3 * (count // 4), rows, LANES)],
+        [],
+        right_side.reshape(C * depth, rows, columns),
+        density,
+    )
     taken = lax.all_to_all(sent, "gz", 0, 0)
     own, first, second = call(
         unpack_kernel,
-        [(C + 1, rows, NZ, W), (C + 1, HALO, NZ, W), (C + 1, HALO, NZ, W)],
+        [(C + 1, rows, NZ, W)] + [(C + 4, HALO, NZ, LANES)] * 2,
         [(C + 1, 2, NZ * rows, LANES)],
         taken,
     )

time: 174 us -> 172 us (0.989)
  blocking collectives: 48 us -> 45.9 us
    all_to_all x1, blocking collectives: 30 us -> 27.9 us  [shards(): taken = lax.all_to_all(sent, 'gz', 0, 0)]
where the time goes in v7:
time: 172 us; the launch traced here: 169 us
  starting transfers between devices  62.8 us (37%)
  blocking collectives  45.9 us (27%)
  waiting for transfers between devices  35.3 us (21%)
  Pallas kernels  22.9 us (13%)
  local copies, waits for them, and re-layouts  1.93 us (1%)
    ppermute x18, starting transfers between devices, swap(): return lax.ppermute(values, axis, pairs)  62.8 us
    ppermute x18, waiting for transfers between devices, swap(): return lax.ppermute(values, axis, pairs)  35.3 us
    all_to_all x1, blocking collectives, shards(): taken = lax.all_to_all(sent, 'gz', 0, 0)  27.9 us
    pallas_call x10, Pallas kernels, call(): pl.pallas_call(kernel, out_shape=[shape(s) for s in outs], in_specs=[pl.B...  22.9 us
    all_to_all x1, blocking collectives, shards(): lax.all_to_all(sent, 'gz', 0, 0)  17.9 us
  transfers between devices with their start and end apart: 18, of which 13 were waited for; matrix products, arithmetic and copies ran while one was open for 0% of the time, Pallas kernels for 0%

profile of v7, /device:TPU:198, one launch (start us, length us, event | category | flops | bytes accessed | tf_op | source)
XLA Modules:
  0.0 169.0 jit_solution(10250319812170350342)
XLA Ops:
  0.0 0.0 copy-start
  0.0 1.0 copy-done
  1.0 0.0 copy-start.1
  1.0 0.9 copy-done.1
  1.9 0.2 pack_kernel.1
  2.0 27.9 %all_to_all.10.taken = f32[8,21,8,128]{3,2,1,0:T(8,128)S(1)} all-to-all(f32[8,21,8,128]{3,2,1,0:T(8,128)S(1)} %pack_kernel.1), channel_id=1, replica_groups=mesh['gx'=64,'gz'=8] {'gz'}, dimensions={0} | all-to-all | bytes 1376256 | tf_op jit(solution)/shard_map/all_to_all | solution.py:484
  29.9 0.5 unpack_kernel.1
  30.4 1.9 %collective-permute-start = (f32[7,6,24,128]{3,2,1,0:T(8,128)S(1)}, f32[7,6,24,128]{3,2,1,0:T(8,128)S(1)}, u32[]{:S(2)}, u32[]{:S(2)}) collective-permute-start(f32[7,6,24,128]{3,2,1,0:T(8,128)S(1)} %get-tuple-element.36), channel_id=1, source_target_pairs={{8,16},{16,8},{24,32},{32,24},{40,48},{48,40},{56,64},{64,56},{72,... | collective-permute-start | bytes 1548296 | tf_op jit(solution)/shard_map/ppermute | solution.py:468
  32.3 5.5 %collective-permute-start.1 = (f32[7,6,24,128]{3,2,1,0:T(8,128)S(1)}, f32[7,6,24,128]{3,2,1,0:T(8,128)S(1)}, u32[]{:S(2)}, u32[]{:S(2)}) collective-permute-start(f32[7,6,24,128]{3,2,1,0:T(8,128)S(1)} %get-tuple-element.37), channel_id=1, source_target_pairs={{0,8},{8,0},{16,24},{24,16},{32,40},{40,32},{48,56},{56,48},{64,72... | collective-permute-start | bytes 1548296 | tf_op jit(solution)/shard_map/ppermute | solution.py:468
  37.9 3.0 %collective-permute-done.second = f32[7,6,24,128]{3,2,1,0:T(8,128)S(1)} collective-permute-done((f32[7,6,24,128]{3,2,1,0:T(8,128)S(1)}, f32[7,6,24,128]{3,2,1,0:T(8,128)S(1)}, u32[]{:S(2)}, u32[]{:S(2)}) %collective-permute-start) | collective-permute-done | bytes 516128 | tf_op jit(solution)/shard_map/ppermute | solution.py:468
  40.8 0.0 collective-permute-done.1.first
  40.8 5.2 %first_down_kernel.1 = (f32[3,20,24,256]{3,2,1,0:T(8,128)S(1)}, f32[20,24,256]{2,1,0:T(8,128)S(1)}, f32[20,24,256]{2,1,0:T(8,128)S(1)}, f32[3,20,24,256]{3,2,1,0...) custom-call(f32[4,8,24,256]{3,2,1,0:T(8,128)S(1)} %get-tuple-element, ...), custom_call_target="tpu_custom_call" | custom-call | tf_op jit(solution)/shard_map/first_down_kernel/pallas_call | solution.py:449
  46.0 8.7 %collective-permute-start.3 = (f32[4,24,128]{2,1,0:T(8,128)S(1)}, f32[4,24,128]{2,1,0:T(8,128)S(1)}, u32[]{:S(2)}, u32[]{:S(2)}) collective-permute-start(f32[4,24,128]{2,1,0:T(8,128)S(1)} %get-tuple-element.38), channel_id=1, source_target_pairs={{16,32},{24,40},{32,16},{40,24},{48,64},{56,72},{64,48},{72,56},{8... | collective-permute-start | bytes 147464 | tf_op jit(solution)/shard_map/ppermute | solution.py:468
  54.8 1.9 %collective-permute-start.2 = (f32[4,24,128]{2,1,0:T(8,128)S(1)}, f32[4,24,128]{2,1,0:T(8,128)S(1)}, u32[]{:S(2)}, u32[]{:S(2)}) collective-permute-start(f32[4,24,128]{2,1,0:T(8,128)S(1)} %get-tuple-element.38), channel_id=1, source_target_pairs={{0,16},{8,24},{16,0},{24,8},{32,48},{40,56},{48,32},{56,40},{64,80... | collective-permute-start | bytes 147464 | tf_op jit(solution)/shard_map/ppermute | solution.py:468
  56.7 0.1 collective-permute-done.3
  56.8 3.8 %collective-permute-start.4 = (f32[4,24,128]{2,1,0:T(8,128)S(1)}, f32[4,24,128]{2,1,0:T(8,128)S(1)}, u32[]{:S(2)}, u32[]{:S(2)}) collective-permute-start(f32[4,24,128]{2,1,0:T(8,128)S(1)} %collective-permute-done.3), channel_id=1, source_target_pairs={{0,16},{8,24},{16,0},{24,8},{32,48},{40,56},{48,32},{56,40},{64,80... | collective-permute-start | bytes 147464 | tf_op jit(solution)/shard_map/ppermute | solution.py:468
  60.6 0.3 collective-permute-done.2
  61.0 5.0 %collective-permute-start.5 = (f32[4,24,128]{2,1,0:T(8,128)S(1)}, f32[4,24,128]{2,1,0:T(8,128)S(1)}, u32[]{:S(2)}, u32[]{:S(2)}) collective-permute-start(f32[4,24,128]{2,1,0:T(8,128)S(1)} %collective-permute-done.2), channel_id=1, source_target_pairs={{16,32},{24,40},{32,16},{40,24},{48,64},{56,72},{64,48},{72,56},{8... | collective-permute-start | bytes 147464 | tf_op jit(solution)/shard_map/ppermute | solution.py:468
  66.0 0.0 collective-permute-done.4
  66.0 4.2 %collective-permute-done.5 = f32[4,24,128]{2,1,0:T(8,128)S(1)} collective-permute-done((f32[4,24,128]{2,1,0:T(8,128)S(1)}, f32[4,24,128]{2,1,0:T(8,128)S(1)}, u32[]{:S(2)}, u32[]{:S(2)}) %collective-permute-start.5) | collective-permute-done | bytes 49184 | tf_op jit(solution)/shard_map/ppermute | solution.py:468
  70.3 1.9 %collective-permute-start.6 = (f32[29,24,128]{2,1,0:T(8,128)S(1)}, f32[29,24,128]{2,1,0:T(8,128)S(1)}, u32[]{:S(2)}, u32[]{:S(2)}) collective-permute-start(f32[29,24,128]{2,1,0:T(8,128)S(1)} %constant_dynamic-update-slice_fusion.mine), channel_id=1, source_target_pairs={{0,8},{8,0},{16,24},{24,16},{32,40},{40,32},{48,56},{56,48},{64,72... | collective-permute-start | bytes 1069064 | tf_op jit(solution)/shard_map/ppermute | solution.py:468
  72.2 1.6 collective-permute-done.6.other
  73.8 2.9 %coarse_kernel.2 = (f32[3,4,24,128]{3,2,1,0:T(8,128)S(1)}, f32[3,3,24,128]{3,2,1,0:T(8,128)S(1)}, f32[3,3,24,128]{3,2,1,0:T(8,128)S(1)}) custom-call(f32[29,24,128]{2,1,0:T(8,128)S(1)} %constant_dynamic-update-slice_fusion.mine, f32[29,24,128]{2,1,0:T(8,128)S(1)} %collective-permute-done.6.other, f32[3,8,24,128]{3,2,1,0:T(8,128)S(1)} %get-tuple-element.40.v1), custom_call_target="tpu_custom_call" | custom-call | tf_op jit(solution)/shard_map/coarse_kernel/pallas_call | solution.py:449
  76.7 1.9 %collective-permute-start.7 = (f32[3,3,24,128]{3,2,1,0:T(8,128)S(1)}, f32[3,3,24,128]{3,2,1,0:T(8,128)S(1)}, u32[]{:S(2)}, u32[]{:S(2)}) collective-permute-start(f32[3,3,24,128]{3,2,1,0:T(8,128)S(1)} %get-tuple-element.43), channel_id=1, source_target_pairs={{8,16},{16,8},{24,32},{32,24},{40,48},{48,40},{56,64},{64,56},{72,... | collective-permute-start | bytes 331784 | tf_op jit(solution)/shard_map/ppermute | solution.py:468
  78.6 4.1 %collective-permute-done.7.right = f32[3,3,24,128]{3,2,1,0:T(8,128)S(1)} collective-permute-done((f32[3,3,24,128]{3,2,1,0:T(8,128)S(1)}, f32[3,3,24,128]{3,2,1,0:T(8,128)S(1)}, u32[]{:S(2)}, u32[]{:S(2)}) %collective-permute-start.7) | collective-permute-done | bytes 110624 | tf_op jit(solution)/shard_map/ppermute | solution.py:468
  82.8 2.3 %first_up_kernel.1 = (f32[3,8,24,128]{3,2,1,0:T(8,128)S(1)}, f32[3,7,24,128]{3,2,1,0:T(8,128)S(1)}, f32[3,7,24,128]{3,2,1,0:T(8,128)S(1)}) custom-call(f32[3,4,24,128]{3,2,1,0:T(8,128)S(1)} %get-tuple-element.41.own, f32[3,3,24,128]{3,2,1,0:T(8,128)S(1)} %get-tuple-element.42.left, f32[3,3,24,128]{3,2,1,0:T(8,128)S(1)} %collective-permute-done.7.right, ...), custom_call_target="tpu_custom_call" | custom-call | tf_op jit(solution)/shard_map/first_up_kernel/pallas_call | solution.py:449
  85.0 1.9 %collective-permute-start.8 = (f32[3,7,24,128]{3,2,1,0:T(8,128)S(1)}, f32[3,7,24,128]{3,2,1,0:T(8,128)S(1)}, u32[]{:S(2)}, u32[]{:S(2)}) collective-permute-start(f32[3,7,24,128]{3,2,1,0:T(8,128)S(1)} %get-tuple-element.50), channel_id=1, source_target_pairs={{8,16},{16,8},{24,32},{32,24},{40,48},{48,40},{56,64},{64,56},{72,... | collective-permute-start | bytes 774152 | tf_op jit(solution)/shard_map/ppermute | solution.py:468
  87.0 8.5 %collective-permute-start.9 = (f32[3,7,24,128]{3,2,1,0:T(8,128)S(1)}, f32[3,7,24,128]{3,2,1,0:T(8,128)S(1)}, u32[]{:S(2)}, u32[]{:S(2)}) collective-permute-start(f32[3,7,24,128]{3,2,1,0:T(8,128)S(1)} %get-tuple-element.51), channel_id=1, source_target_pairs={{0,8},{8,0},{16,24},{24,16},{32,40},{40,32},{48,56},{56,48},{64,72... | collective-permute-start | bytes 774152 | tf_op jit(solution)/shard_map/ppermute | solution.py:468
  95.5 0.0 collective-permute-done.8.second
  95.5 1.1 collective-permute-done.9.first
  96.6 0.2 side_kernel.1
  96.8 2.5 %collective-permute-start.10 = (f32[3,11,24,128]{3,2,1,0:T(8,128)S(1)}, f32[3,11,24,128]{3,2,1,0:T(8,128)S(1)}, u32[]{:S(2)}, u32[]{:S(2)}) collective-permute-start(f32[3,11,24,128]{3,2,1,0:T(8,128)S(1)} %get-tuple-element.53), channel_id=1, source_target_pairs={{0,1},{1,0},{2,3},{3,2},{4,5},{5,4},{6,7},{7,6},{8,9},{9,8},{10,11... | collective-permute-start | bytes 1216520 | tf_op jit(solution)/shard_map/ppermute | solution.py:468
  99.3 0.7 collective-permute-start.11
  100.0 9.0 %collective-permute-done.10.first = f32[3,11,24,128]{3,2,1,0:T(8,128)S(1)} collective-permute-done((f32[3,11,24,128]{3,2,1,0:T(8,128)S(1)}, f32[3,11,24,128]{3,2,1,0:T(8,128)S(1)}, u32[]{:S(2)}, u32[]{:S(2)}) %collective-permute-start.10) | collective-permute-done | bytes 405536 | tf_op jit(solution)/shard_map/ppermute | solution.py:468
  109.0 0.0 collective-permute-done.11.second
  109.0 5.8 %second_down_kernel.1 = (f32[3,20,24,256]{3,2,1,0:T(8,128)S(1)}, f32[3,8,24,128]{3,2,1,0:T(8,128)S(1)}, f32[3,8,24,128]{3,2,1,0:T(8,128)S(1)}, f32[4,24,128]{2,1,0:T(8,128)S(1)}, f32[9,24,128]{2,1,0:T(8,128)S(1)}) custom-call(f32[3,22,24,128]{3,2,1,0:T(8,128)S(1)} %get-tuple-element.52.tall, f32[3,11,24,128]{3,2,1,0:T(8,128)S(1)} %collective-permute-done.10.first, ...), custom_call_target="tpu_custom_call" | custom-call | tf_op jit(solution)/shard_map/second_down_kernel/pallas_call | solution.py:449
  114.8 5.4 %collective-permute-start.13 = (f32[4,24,128]{2,1,0:T(8,128)S(1)}, f32[4,24,128]{2,1,0:T(8,128)S(1)}, u32[]{:S(2)}, u32[]{:S(2)}) collective-permute-start(f32[4,24,128]{2,1,0:T(8,128)S(1)} %get-tuple-element.57), channel_id=1, source_target_pairs={{16,32},{24,40},{32,16},{40,24},{48,64},{56,72},{64,48},{72,56},{8... | collective-permute-start | bytes 147464 | tf_op jit(solution)/shard_map/ppermute | solution.py:468
  120.2 1.9 %collective-permute-start.12 = (f32[4,24,128]{2,1,0:T(8,128)S(1)}, f32[4,24,128]{2,1,0:T(8,128)S(1)}, u32[]{:S(2)}, u32[]{:S(2)}) collective-permute-start(f32[4,24,128]{2,1,0:T(8,128)S(1)} %get-tuple-element.57), channel_id=1, source_target_pairs={{0,16},{8,24},{16,0},{24,8},{32,48},{40,56},{48,32},{56,40},{64,80... | collective-permute-start | bytes 147464 | tf_op jit(solution)/shard_map/ppermute | solution.py:468
  122.2 1.9 %collective-permute-done.13 = f32[4,24,128]{2,1,0:T(8,128)S(1)} collective-permute-done((f32[4,24,128]{2,1,0:T(8,128)S(1)}, f32[4,24,128]{2,1,0:T(8,128)S(1)}, u32[]{:S(2)}, u32[]{:S(2)}) %collective-permute-start.13) | collective-permute-done | bytes 49184 | tf_op jit(solution)/shard_map/ppermute | solution.py:468
  124.1 2.0 %collective-permute-start.14 = (f32[4,24,128]{2,1,0:T(8,128)S(1)}, f32[4,24,128]{2,1,0:T(8,128)S(1)}, u32[]{:S(2)}, u32[]{:S(2)}) collective-permute-start(f32[4,24,128]{2,1,0:T(8,128)S(1)} %collective-permute-done.13), channel_id=1, source_target_pairs={{0,16},{8,24},{16,0},{24,8},{32,48},{40,56},{48,32},{56,40},{64,80... | collective-permute-start | bytes 147464 | tf_op jit(solution)/shard_map/ppermute | solution.py:468
  126.1 0.1 collective-permute-done.12
  126.2 5.2 %collective-permute-start.15 = (f32[4,24,128]{2,1,0:T(8,128)S(1)}, f32[4,24,128]{2,1,0:T(8,128)S(1)}, u32[]{:S(2)}, u32[]{:S(2)}) collective-permute-start(f32[4,24,128]{2,1,0:T(8,128)S(1)} %collective-permute-done.12), channel_id=1, source_target_pairs={{16,32},{24,40},{32,16},{40,24},{48,64},{56,72},{64,48},{72,56},{8... | collective-permute-start | bytes 147464 | tf_op jit(solution)/shard_map/ppermute | solution.py:468
  131.5 0.0 collective-permute-done.14
  131.5 4.0 %collective-permute-done.15 = f32[4,24,128]{2,1,0:T(8,128)S(1)} collective-permute-done((f32[4,24,128]{2,1,0:T(8,128)S(1)}, f32[4,24,128]{2,1,0:T(8,128)S(1)}, u32[]{:S(2)}, u32[]{:S(2)}) %collective-permute-start.15) | collective-permute-done | bytes 49184 | tf_op jit(solution)/shard_map/ppermute | solution.py:468
  135.5 1.9 %collective-permute-start.16 = (f32[29,24,128]{2,1,0:T(8,128)S(1)}, f32[29,24,128]{2,1,0:T(8,128)S(1)}, u32[]{:S(2)}, u32[]{:S(2)}) collective-permute-start(f32[29,24,128]{2,1,0:T(8,128)S(1)} %constant_dynamic-update-slice_fusion.6.mine), channel_id=1, source_target_pairs={{0,8},{8,0},{16,24},{24,16},{32,40},{40,32},{48,56},{56,48},{64,72... | collective-permute-start | bytes 1069064 | tf_op jit(solution)/shard_map/ppermute | solution.py:468
  137.5 1.6 collective-permute-done.16.other
  139.1 2.9 %coarse_kernel.3 = (f32[3,4,24,128]{3,2,1,0:T(8,128)S(1)}, f32[3,3,24,128]{3,2,1,0:T(8,128)S(1)}, f32[3,3,24,128]{3,2,1,0:T(8,128)S(1)}) custom-call(f32[29,24,128]{2,1,0:T(8,128)S(1)} %constant_dynamic-update-slice_fusion.6.mine, f32[29,24,128]{2,1,0:T(8,128)S(1)} %collective-permute-done.16.other, f32[3,8,24,128]{3,2,1,0:T(8,128)S(1)} %get-tuple-element.59.v1), custom_call_target="tpu_custom_call" | custom-call | tf_op jit(solution)/shard_map/coarse_kernel/pallas_call | solution.py:449
  142.0 1.9 %collective-permute-start.17 = (f32[3,3,24,128]{3,2,1,0:T(8,128)S(1)}, f32[3,3,24,128]{3,2,1,0:T(8,128)S(1)}, u32[]{:S(2)}, u32[]{:S(2)}) collective-permute-start(f32[3,3,24,128]{3,2,1,0:T(8,128)S(1)} %get-tuple-element.62), channel_id=1, source_target_pairs={{8,16},{16,8},{24,32},{32,24},{40,48},{48,40},{56,64},{64,56},{72,... | collective-permute-start | bytes 331784 | tf_op jit(solution)/shard_map/ppermute | solution.py:468
  143.9 4.1 %collective-permute-done.17.right = f32[3,3,24,128]{3,2,1,0:T(8,128)S(1)} collective-permute-done((f32[3,3,24,128]{3,2,1,0:T(8,128)S(1)}, f32[3,3,24,128]{3,2,1,0:T(8,128)S(1)}, u32[]{:S(2)}, u32[]{:S(2)}) %collective-permute-start.17) | collective-permute-done | bytes 110624 | tf_op jit(solution)/shard_map/ppermute | solution.py:468
  148.1 2.3 %last_up_kernel.1 = f32[8,9,8,128]{3,2,1,0:T(8,128)S(1)} custom-call(f32[3,4,24,128]{3,2,1,0:T(8,128)S(1)} %get-tuple-element.60.own, f32[3,3,24,128]{3,2,1,0:T(8,128)S(1)} %get-tuple-element.61.left, f32[3,3,24,128]{3,2,1,0:T(8,128)S(1)} %collective-permute-done.17.right, f32[3,20,24,256]{3,2,1,0:T(8,128)S(1)} %get-tuple-element.44.g0, ...), custom_call_target="tpu_custom_call" | custom-call | tf_op jit(solution)/shard_map/last_up_kernel/pallas_call | solution.py:449
  150.3 17.9 %all_to_all.11.taken = f32[8,9,8,128]{3,2,1,0:T(8,128)S(1)} all-to-all(f32[8,9,8,128]{3,2,1,0:T(8,128)S(1)} %last_up_kernel.1), channel_id=1, replica_groups=mesh['gx'=64,'gz'=8] {'gz'}, dimensions={0} | all-to-all | bytes 589824 | tf_op jit(solution)/shard_map/all_to_all | solution.py:563
  168.3 0.7 join_kernel.1
  (12 shorter events, 0.1 us)
Async XLA Ops:
  0.0 1.0 copy-start
  1.0 0.9 copy-start.1
  30.4 10.4 %collective-permute-start = (f32[7,6,24,128]{3,2,1,0:T(8,128)S(1)}, f32[7,6,24,128]{3,2,1,0:T(8,128)S(1)}, u32[]{:S(2)}, u32[]{:S(2)}) collective-permute-start(f32[7,6,24,128]{3,2,1,0:T(8,128)S(1)} %get-tuple-element.36), channel_id=1, source_target_pairs={{8,16},{16,8},{24,32},{32,24},{40,48},{48,40},{56,64},{64,56},{72,... | collective-permute-start | bytes 1548296 | tf_op jit(solution)/shard_map/ppermute | solution.py:468
  32.3 8.5 %collective-permute-start.1 = (f32[7,6,24,128]{3,2,1,0:T(8,128)S(1)}, f32[7,6,24,128]{3,2,1,0:T(8,128)S(1)}, u32[]{:S(2)}, u32[]{:S(2)}) collective-permute-start(f32[7,6,24,128]{3,2,1,0:T(8,128)S(1)} %get-tuple-element.37), channel_id=1, source_target_pairs={{0,8},{8,0},{16,24},{24,16},{32,40},{40,32},{48,56},{56,48},{64,72... | collective-permute-start | bytes 1548296 | tf_op jit(solution)/shard_map/ppermute | solution.py:468
  46.0 10.8 %collective-permute-start.3 = (f32[4,24,128]{2,1,0:T(8,128)S(1)}, f32[4,24,128]{2,1,0:T(8,128)S(1)}, u32[]{:S(2)}, u32[]{:S(2)}) collective-permute-start(f32[4,24,128]{2,1,0:T(8,128)S(1)} %get-tuple-element.38), channel_id=1, source_target_pairs={{16,32},{24,40},{32,16},{40,24},{48,64},{56,72},{64,48},{72,56},{8... | collective-permute-start | bytes 147464 | tf_op jit(solution)/shard_map/ppermute | solution.py:468
  54.8 6.2 %collective-permute-start.2 = (f32[4,24,128]{2,1,0:T(8,128)S(1)}, f32[4,24,128]{2,1,0:T(8,128)S(1)}, u32[]{:S(2)}, u32[]{:S(2)}) collective-permute-start(f32[4,24,128]{2,1,0:T(8,128)S(1)} %get-tuple-element.38), channel_id=1, source_target_pairs={{0,16},{8,24},{16,0},{24,8},{32,48},{40,56},{48,32},{56,40},{64,80... | collective-permute-start | bytes 147464 | tf_op jit(solution)/shard_map/ppermute | solution.py:468
  56.8 9.2 %collective-permute-start.4 = (f32[4,24,128]{2,1,0:T(8,128)S(1)}, f32[4,24,128]{2,1,0:T(8,128)S(1)}, u32[]{:S(2)}, u32[]{:S(2)}) collective-permute-start(f32[4,24,128]{2,1,0:T(8,128)S(1)} %collective-permute-done.3), channel_id=1, source_target_pairs={{0,16},{8,24},{16,0},{24,8},{32,48},{40,56},{48,32},{56,40},{64,80... | collective-permute-start | bytes 147464 | tf_op jit(solution)/shard_map/ppermute | solution.py:468
  61.0 9.3 %collective-permute-start.5 = (f32[4,24,128]{2,1,0:T(8,128)S(1)}, f32[4,24,128]{2,1,0:T(8,128)S(1)}, u32[]{:S(2)}, u32[]{:S(2)}) collective-permute-start(f32[4,24,128]{2,1,0:T(8,128)S(1)} %collective-permute-done.2), channel_id=1, source_target_pairs={{16,32},{24,40},{32,16},{40,24},{48,64},{56,72},{64,48},{72,56},{8... | collective-permute-start | bytes 147464 | tf_op jit(solution)/shard_map/ppermute | solution.py:468
  70.3 3.6 %collective-permute-start.6 = (f32[29,24,128]{2,1,0:T(8,128)S(1)}, f32[29,24,128]{2,1,0:T(8,128)S(1)}, u32[]{:S(2)}, u32[]{:S(2)}) collective-permute-start(f32[29,24,128]{2,1,0:T(8,128)S(1)} %constant_dynamic-update-slice_fusion.mine), channel_id=1, source_target_pairs={{0,8},{8,0},{16,24},{24,16},{32,40},{40,32},{48,56},{56,48},{64,72... | collective-permute-start | bytes 1069064 | tf_op jit(solution)/shard_map/ppermute | solution.py:468
  76.7 6.1 %collective-permute-start.7 = (f32[3,3,24,128]{3,2,1,0:T(8,128)S(1)}, f32[3,3,24,128]{3,2,1,0:T(8,128)S(1)}, u32[]{:S(2)}, u32[]{:S(2)}) collective-permute-start(f32[3,3,24,128]{3,2,1,0:T(8,128)S(1)} %get-tuple-element.43), channel_id=1, source_target_pairs={{8,16},{16,8},{24,32},{32,24},{40,48},{48,40},{56,64},{64,56},{72,... | collective-permute-start | bytes 331784 | tf_op jit(solution)/shard_map/ppermute | solution.py:468
  85.0 10.4 %collective-permute-start.8 = (f32[3,7,24,128]{3,2,1,0:T(8,128)S(1)}, f32[3,7,24,128]{3,2,1,0:T(8,128)S(1)}, u32[]{:S(2)}, u32[]{:S(2)}) collective-permute-start(f32[3,7,24,128]{3,2,1,0:T(8,128)S(1)} %get-tuple-element.50), channel_id=1, source_target_pairs={{8,16},{16,8},{24,32},{32,24},{40,48},{48,40},{56,64},{64,56},{72,... | collective-permute-start | bytes 774152 | tf_op jit(solution)/shard_map/ppermute | solution.py:468
  87.0 9.6 %collective-permute-start.9 = (f32[3,7,24,128]{3,2,1,0:T(8,128)S(1)}, f32[3,7,24,128]{3,2,1,0:T(8,128)S(1)}, u32[]{:S(2)}, u32[]{:S(2)}) collective-permute-start(f32[3,7,24,128]{3,2,1,0:T(8,128)S(1)} %get-tuple-element.51), channel_id=1, source_target_pairs={{0,8},{8,0},{16,24},{24,16},{32,40},{40,32},{48,56},{56,48},{64,72... | collective-permute-start | bytes 774152 | tf_op jit(solution)/shard_map/ppermute | solution.py:468
  96.8 12.2 %collective-permute-start.10 = (f32[3,11,24,128]{3,2,1,0:T(8,128)S(1)}, f32[3,11,24,128]{3,2,1,0:T(8,128)S(1)}, u32[]{:S(2)}, u32[]{:S(2)}) collective-permute-start(f32[3,11,24,128]{3,2,1,0:T(8,128)S(1)} %get-tuple-element.53), channel_id=1, source_target_pairs={{0,1},{1,0},{2,3},{3,2},{4,5},{5,4},{6,7},{7,6},{8,9},{9,8},{10,11... | collective-permute-start | bytes 1216520 | tf_op jit(solution)/shard_map/ppermute | solution.py:468
  99.3 9.7 %collective-permute-start.11 = (f32[3,11,24,128]{3,2,1,0:T(8,128)S(1)}, f32[3,11,24,128]{3,2,1,0:T(8,128)S(1)}, u32[]{:S(2)}, u32[]{:S(2)}) collective-permute-start(f32[3,11,24,128]{3,2,1,0:T(8,128)S(1)} %get-tuple-element.54), channel_id=1, source_target_pairs={{1,2},{2,1},{3,4},{4,3},{5,6},{6,5},{9,10},{10,9},{11,12},{12,11},... | collective-permute-start | bytes 1216520 | tf_op jit(solution)/shard_map/ppermute | solution.py:468
  114.8 9.3 %collective-permute-start.13 = (f32[4,24,128]{2,1,0:T(8,128)S(1)}, f32[4,24,128]{2,1,0:T(8,128)S(1)}, u32[]{:S(2)}, u32[]{:S(2)}) collective-permute-start(f32[4,24,128]{2,1,0:T(8,128)S(1)} %get-tuple-element.57), channel_id=1, source_target_pairs={{16,32},{24,40},{32,16},{40,24},{48,64},{56,72},{64,48},{72,56},{8... | collective-permute-start | bytes 147464 | tf_op jit(solution)/shard_map/ppermute | solution.py:468
  120.2 6.0 %collective-permute-start.12 = (f32[4,24,128]{2,1,0:T(8,128)S(1)}, f32[4,24,128]{2,1,0:T(8,128)S(1)}, u32[]{:S(2)}, u32[]{:S(2)}) collective-permute-start(f32[4,24,128]{2,1,0:T(8,128)S(1)} %get-tuple-element.57), channel_id=1, source_target_pairs={{0,16},{8,24},{16,0},{24,8},{32,48},{40,56},{48,32},{56,40},{64,80... | collective-permute-start | bytes 147464 | tf_op jit(solution)/shard_map/ppermute | solution.py:468
  124.1 7.4 %collective-permute-start.14 = (f32[4,24,128]{2,1,0:T(8,128)S(1)}, f32[4,24,128]{2,1,0:T(8,128)S(1)}, u32[]{:S(2)}, u32[]{:S(2)}) collective-permute-start(f32[4,24,128]{2,1,0:T(8,128)S(1)} %collective-permute-done.13), channel_id=1, source_target_pairs={{0,16},{8,24},{16,0},{24,8},{32,48},{40,56},{48,32},{56,40},{64,80... | collective-permute-start | bytes 147464 | tf_op jit(solution)/shard_map/ppermute | solution.py:468
  126.2 9.3 %collective-permute-start.15 = (f32[4,24,128]{2,1,0:T(8,128)S(1)}, f32[4,24,128]{2,1,0:T(8,128)S(1)}, u32[]{:S(2)}, u32[]{:S(2)}) collective-permute-start(f32[4,24,128]{2,1,0:T(8,128)S(1)} %collective-permute-done.12), channel_id=1, source_target_pairs={{16,32},{24,40},{32,16},{40,24},{48,64},{56,72},{64,48},{72,56},{8... | collective-permute-start | bytes 147464 | tf_op jit(solution)/shard_map/ppermute | solution.py:468
  135.5 3.6 %collective-permute-start.16 = (f32[29,24,128]{2,1,0:T(8,128)S(1)}, f32[29,24,128]{2,1,0:T(8,128)S(1)}, u32[]{:S(2)}, u32[]{:S(2)}) collective-permute-start(f32[29,24,128]{2,1,0:T(8,128)S(1)} %constant_dynamic-update-slice_fusion.6.mine), channel_id=1, source_target_pairs={{0,8},{8,0},{16,24},{24,16},{32,40},{40,32},{48,56},{56,48},{64,72... | collective-permute-start | bytes 1069064 | tf_op jit(solution)/shard_map/ppermute | solution.py:468
  142.0 6.1 %collective-permute-start.17 = (f32[3,3,24,128]{3,2,1,0:T(8,128)S(1)}, f32[3,3,24,128]{3,2,1,0:T(8,128)S(1)}, u32[]{:S(2)}, u32[]{:S(2)}) collective-permute-start(f32[3,3,24,128]{3,2,1,0:T(8,128)S(1)} %get-tuple-element.62), channel_id=1, source_target_pairs={{8,16},{16,8},{24,32},{32,24},{40,48},{48,40},{56,64},{64,56},{72,... | collective-permute-start | bytes 331784 | tf_op jit(solution)/shard_map/ppermute | solution.py:468

commit v8 on v7

--- a/solution.py
+++ b/solution.py
@@ -12,7 +12,9 @@
 NZ = 24
 HALO = 6
 LANES = 128
-UNROLL = (3, 4, 8, 8)
+UNROLL = (18, 8, 18, 8)
+SOURCE = (2, 1, 4, 4)
+CLIMB = (10, 8)
 PARAMS = pltpu.CompilerParams(vmem_limit_bytes=12 << 20)
 
 
@@ -73,14 +75,14 @@
         body(Row(0, r))
 
 
-def sweep(target, field, source, factor, level, low, high):
+def sweep(target, field, source, factor, level, low, high, unroll=None):
     def body(r):
         f = shared(factor, r)
         for c in range(C):
             mid, around = neighbours(field, c, r, level)
             target[0][c, index(target, r)] = (1.0 - relaxation) * mid + f * (row(source, c, r) + around)
 
-    each_row(low, high, body, UNROLL[level])
+    each_row(low, high, body, unroll or UNROLL[level])
 
 
 def lane_index():
@@ -117,7 +119,7 @@
                 total = residual if total is None else total + residual
             target[0][c, index(target, q)] = 0.25 * pair_sum(total, period)
 
-    each_row(low, high, body, max(1, UNROLL[level] // 2))
+    each_row(low, high, body, SOURCE[level])
 
 
 def from_zero(target, source, density, factor, level, period, rows, position, low, high, finer=None, reach=0, group=1):
@@ -402,8 +404,8 @@
         wide[c, at] = value
 
     with_halo(position, own, first, second, store)
-    sweep((u, -3), (wide, -halo), (g1, -2), (f1, -3), 1, -2, rows1 + 2)
-    sweep((w, -3), (u, -3), (g1, -2), (f1, -3), 1, -1, rows1 + 1)
+    sweep((u, -3), (wide, -halo), (g1, -2), (f1, -3), 1, -2, rows1 + 2, CLIMB[1])
+    sweep((w, -3), (u, -3), (g1, -2), (f1, -3), 1, -1, rows1 + 1, CLIMB[1])
 
     def correct(q):
         for c in range(C):
@@ -411,10 +413,10 @@
             for r in (q.double(), q.double() + 1):
                 field[c, index((field, -HALO), r)] = row((v0, -HALO), c, r) + fine
 
-    each_row(-1, rows1 + 1, correct, 2)
+    each_row(-1, rows1 + 1, correct, CLIMB[1])
     rows = 2 * rows1
-    sweep((emit, -HALO), (field, -HALO), (g0, -HALO), (f0, -HALO), 0, -1, rows + 1)
-    sweep((field, -HALO), (emit, -HALO), (g0, -HALO), (f0, -HALO), 0, 0, rows)
+    sweep((emit, -HALO), (field, -HALO), (g0, -HALO), (f0, -HALO), 0, -1, rows + 1, CLIMB[0])
+    sweep((field, -HALO), (emit, -HALO), (g0, -HALO), (f0, -HALO), 0, 0, rows, CLIMB[0])
 
 
 def first_up_kernel(own, left, right, g0, f0, v0, g1, f1, out, first, second, wide, u, w, field, other):

time: 172 us -> 168 us (0.977)
  Pallas kernels: 22.9 us -> 19.2 us
    pallas_call x10, Pallas kernels: 22.9 us -> 19.2 us  [call(): pl.pallas_call(kernel, out_shape=[shape(s) for s in outs], in_specs=[pl.B...]
where the time goes in v8:
time: 168 us; the launch traced here: 165 us
  starting transfers between devices  63 us (38%)
  blocking collectives  45.9 us (27%)
  waiting for transfers between devices  35.1 us (21%)
  Pallas kernels  19.2 us (11%)
  local copies, waits for them, and re-layouts  1.93 us (1%)
    ppermute x18, starting transfers between devices, swap(): return lax.ppermute(values, axis, pairs)  63 us
    ppermute x18, waiting for transfers between devices, swap(): return lax.ppermute(values, axis, pairs)  35.1 us
    all_to_all x1, blocking collectives, shards(): taken = lax.all_to_all(sent, 'gz', 0, 0)  27.9 us
    pallas_call x10, Pallas kernels, call(): pl.pallas_call(kernel, out_shape=[shape(s) for s in outs], in_specs=[pl.B...  19.2 us
    all_to_all x1, blocking collectives, shards(): lax.all_to_all(sent, 'gz', 0, 0)  17.9 us
  transfers between devices with their start and end apart: 18, of which 13 were waited for; matrix products, arithmetic and copies ran while one was open for 0% of the time, Pallas kernels for 0%

profile of v8, /device:TPU:198, one launch (start us, length us, event | category | flops | bytes accessed | tf_op | source)
XLA Modules:
  0.0 165.4 jit_solution(7849484077478153299)
XLA Ops:
  0.0 0.0 copy-start
  0.0 1.0 copy-done
  1.0 0.0 copy-start.1
  1.0 0.9 copy-done.1
  1.9 0.2 pack_kernel.1
  2.0 27.9 %all_to_all.10.taken = f32[8,21,8,128]{3,2,1,0:T(8,128)S(1)} all-to-all(f32[8,21,8,128]{3,2,1,0:T(8,128)S(1)} %pack_kernel.1), channel_id=1, replica_groups=mesh['gx'=64,'gz'=8] {'gz'}, dimensions={0} | all-to-all | bytes 1376256 | tf_op jit(solution)/shard_map/all_to_all | solution.py:486
  29.9 0.5 unpack_kernel.1
  30.4 1.9 %collective-permute-start = (f32[7,6,24,128]{3,2,1,0:T(8,128)S(1)}, f32[7,6,24,128]{3,2,1,0:T(8,128)S(1)}, u32[]{:S(2)}, u32[]{:S(2)}) collective-permute-start(f32[7,6,24,128]{3,2,1,0:T(8,128)S(1)} %get-tuple-element.36), channel_id=1, source_target_pairs={{8,16},{16,8},{24,32},{32,24},{40,48},{48,40},{56,64},{64,56},{72,... | collective-permute-start | bytes 1548296 | tf_op jit(solution)/shard_map/ppermute | solution.py:470
  32.3 5.5 %collective-permute-start.1 = (f32[7,6,24,128]{3,2,1,0:T(8,128)S(1)}, f32[7,6,24,128]{3,2,1,0:T(8,128)S(1)}, u32[]{:S(2)}, u32[]{:S(2)}) collective-permute-start(f32[7,6,24,128]{3,2,1,0:T(8,128)S(1)} %get-tuple-element.37), channel_id=1, source_target_pairs={{0,8},{8,0},{16,24},{24,16},{32,40},{40,32},{48,56},{56,48},{64,72... | collective-permute-start | bytes 1548296 | tf_op jit(solution)/shard_map/ppermute | solution.py:470
  37.9 3.0 %collective-permute-done.second = f32[7,6,24,128]{3,2,1,0:T(8,128)S(1)} collective-permute-done((f32[7,6,24,128]{3,2,1,0:T(8,128)S(1)}, f32[7,6,24,128]{3,2,1,0:T(8,128)S(1)}, u32[]{:S(2)}, u32[]{:S(2)}) %collective-permute-start) | collective-permute-done | bytes 516128 | tf_op jit(solution)/shard_map/ppermute | solution.py:470
  40.8 0.0 collective-permute-done.1.first
  40.8 4.7 %first_down_kernel.1 = (f32[3,20,24,256]{3,2,1,0:T(8,128)S(1)}, f32[20,24,256]{2,1,0:T(8,128)S(1)}, f32[20,24,256]{2,1,0:T(8,128)S(1)}, f32[3,20,24,256]{3,2,1,0...) custom-call(f32[4,8,24,256]{3,2,1,0:T(8,128)S(1)} %get-tuple-element, ...), custom_call_target="tpu_custom_call" | custom-call | tf_op jit(solution)/shard_map/first_down_kernel/pallas_call | solution.py:451
  45.5 8.7 %collective-permute-start.3 = (f32[4,24,128]{2,1,0:T(8,128)S(1)}, f32[4,24,128]{2,1,0:T(8,128)S(1)}, u32[]{:S(2)}, u32[]{:S(2)}) collective-permute-start(f32[4,24,128]{2,1,0:T(8,128)S(1)} %get-tuple-element.38), channel_id=1, source_target_pairs={{16,32},{24,40},{32,16},{40,24},{48,64},{56,72},{64,48},{72,56},{8... | collective-permute-start | bytes 147464 | tf_op jit(solution)/shard_map/ppermute | solution.py:470
  54.2 1.9 %collective-permute-start.2 = (f32[4,24,128]{2,1,0:T(8,128)S(1)}, f32[4,24,128]{2,1,0:T(8,128)S(1)}, u32[]{:S(2)}, u32[]{:S(2)}) collective-permute-start(f32[4,24,128]{2,1,0:T(8,128)S(1)} %get-tuple-element.38), channel_id=1, source_target_pairs={{0,16},{8,24},{16,0},{24,8},{32,48},{40,56},{48,32},{56,40},{64,80... | collective-permute-start | bytes 147464 | tf_op jit(solution)/shard_map/ppermute | solution.py:470
  56.2 0.1 collective-permute-done.3
  56.3 3.8 %collective-permute-start.4 = (f32[4,24,128]{2,1,0:T(8,128)S(1)}, f32[4,24,128]{2,1,0:T(8,128)S(1)}, u32[]{:S(2)}, u32[]{:S(2)}) collective-permute-start(f32[4,24,128]{2,1,0:T(8,128)S(1)} %collective-permute-done.3), channel_id=1, source_target_pairs={{0,16},{8,24},{16,0},{24,8},{32,48},{40,56},{48,32},{56,40},{64,80... | collective-permute-start | bytes 147464 | tf_op jit(solution)/shard_map/ppermute | solution.py:470
  60.1 0.3 collective-permute-done.2
  60.4 5.0 %collective-permute-start.5 = (f32[4,24,128]{2,1,0:T(8,128)S(1)}, f32[4,24,128]{2,1,0:T(8,128)S(1)}, u32[]{:S(2)}, u32[]{:S(2)}) collective-permute-start(f32[4,24,128]{2,1,0:T(8,128)S(1)} %collective-permute-done.2), channel_id=1, source_target_pairs={{16,32},{24,40},{32,16},{40,24},{48,64},{56,72},{64,48},{72,56},{8... | collective-permute-start | bytes 147464 | tf_op jit(solution)/shard_map/ppermute | solution.py:470
  65.5 0.0 collective-permute-done.4
  65.5 4.2 %collective-permute-done.5 = f32[4,24,128]{2,1,0:T(8,128)S(1)} collective-permute-done((f32[4,24,128]{2,1,0:T(8,128)S(1)}, f32[4,24,128]{2,1,0:T(8,128)S(1)}, u32[]{:S(2)}, u32[]{:S(2)}) %collective-permute-start.5) | collective-permute-done | bytes 49184 | tf_op jit(solution)/shard_map/ppermute | solution.py:470
  69.7 1.9 %collective-permute-start.6 = (f32[29,24,128]{2,1,0:T(8,128)S(1)}, f32[29,24,128]{2,1,0:T(8,128)S(1)}, u32[]{:S(2)}, u32[]{:S(2)}) collective-permute-start(f32[29,24,128]{2,1,0:T(8,128)S(1)} %constant_dynamic-update-slice_fusion.mine), channel_id=1, source_target_pairs={{0,8},{8,0},{16,24},{24,16},{32,40},{40,32},{48,56},{56,48},{64,72... | collective-permute-start | bytes 1069064 | tf_op jit(solution)/shard_map/ppermute | solution.py:470
  71.7 1.6 collective-permute-done.6.other
  73.3 2.6 %coarse_kernel.2 = (f32[3,4,24,128]{3,2,1,0:T(8,128)S(1)}, f32[3,3,24,128]{3,2,1,0:T(8,128)S(1)}, f32[3,3,24,128]{3,2,1,0:T(8,128)S(1)}) custom-call(f32[29,24,128]{2,1,0:T(8,128)S(1)} %constant_dynamic-update-slice_fusion.mine, f32[29,24,128]{2,1,0:T(8,128)S(1)} %collective-permute-done.6.other, f32[3,8,24,128]{3,2,1,0:T(8,128)S(1)} %get-tuple-element.40.v1), custom_call_target="tpu_custom_call" | custom-call | tf_op jit(solution)/shard_map/coarse_kernel/pallas_call | solution.py:451
  75.9 1.9 %collective-permute-start.7 = (f32[3,3,24,128]{3,2,1,0:T(8,128)S(1)}, f32[3,3,24,128]{3,2,1,0:T(8,128)S(1)}, u32[]{:S(2)}, u32[]{:S(2)}) collective-permute-start(f32[3,3,24,128]{3,2,1,0:T(8,128)S(1)} %get-tuple-element.43), channel_id=1, source_target_pairs={{8,16},{16,8},{24,32},{32,24},{40,48},{48,40},{56,64},{64,56},{72,... | collective-permute-start | bytes 331784 | tf_op jit(solution)/shard_map/ppermute | solution.py:470
  77.9 4.1 %collective-permute-done.7.right = f32[3,3,24,128]{3,2,1,0:T(8,128)S(1)} collective-permute-done((f32[3,3,24,128]{3,2,1,0:T(8,128)S(1)}, f32[3,3,24,128]{3,2,1,0:T(8,128)S(1)}, u32[]{:S(2)}, u32[]{:S(2)}) %collective-permute-start.7) | collective-permute-done | bytes 110624 | tf_op jit(solution)/shard_map/ppermute | solution.py:470
  82.0 1.4 first_up_kernel.1
  83.5 1.9 %collective-permute-start.8 = (f32[3,7,24,128]{3,2,1,0:T(8,128)S(1)}, f32[3,7,24,128]{3,2,1,0:T(8,128)S(1)}, u32[]{:S(2)}, u32[]{:S(2)}) collective-permute-start(f32[3,7,24,128]{3,2,1,0:T(8,128)S(1)} %get-tuple-element.50), channel_id=1, source_target_pairs={{8,16},{16,8},{24,32},{32,24},{40,48},{48,40},{56,64},{64,56},{72,... | collective-permute-start | bytes 774152 | tf_op jit(solution)/shard_map/ppermute | solution.py:470
  85.4 8.5 %collective-permute-start.9 = (f32[3,7,24,128]{3,2,1,0:T(8,128)S(1)}, f32[3,7,24,128]{3,2,1,0:T(8,128)S(1)}, u32[]{:S(2)}, u32[]{:S(2)}) collective-permute-start(f32[3,7,24,128]{3,2,1,0:T(8,128)S(1)} %get-tuple-element.51), channel_id=1, source_target_pairs={{0,8},{8,0},{16,24},{24,16},{32,40},{40,32},{48,56},{56,48},{64,72... | collective-permute-start | bytes 774152 | tf_op jit(solution)/shard_map/ppermute | solution.py:470
  93.9 0.0 collective-permute-done.8.second
  93.9 1.1 collective-permute-done.9.first
  95.0 0.2 side_kernel.1
  95.2 2.5 %collective-permute-start.10 = (f32[3,11,24,128]{3,2,1,0:T(8,128)S(1)}, f32[3,11,24,128]{3,2,1,0:T(8,128)S(1)}, u32[]{:S(2)}, u32[]{:S(2)}) collective-permute-start(f32[3,11,24,128]{3,2,1,0:T(8,128)S(1)} %get-tuple-element.53), channel_id=1, source_target_pairs={{0,1},{1,0},{2,3},{3,2},{4,5},{5,4},{6,7},{7,6},{8,9},{9,8},{10,11... | collective-permute-start | bytes 1216520 | tf_op jit(solution)/shard_map/ppermute | solution.py:470
  97.7 0.7 collective-permute-start.11
  98.4 9.0 %collective-permute-done.10.first = f32[3,11,24,128]{3,2,1,0:T(8,128)S(1)} collective-permute-done((f32[3,11,24,128]{3,2,1,0:T(8,128)S(1)}, f32[3,11,24,128]{3,2,1,0:T(8,128)S(1)}, u32[]{:S(2)}, u32[]{:S(2)}) %collective-permute-start.10) | collective-permute-done | bytes 405536 | tf_op jit(solution)/shard_map/ppermute | solution.py:470
  107.4 0.0 collective-permute-done.11.second
  107.4 4.8 %second_down_kernel.1 = (f32[3,20,24,256]{3,2,1,0:T(8,128)S(1)}, f32[3,8,24,128]{3,2,1,0:T(8,128)S(1)}, f32[3,8,24,128]{3,2,1,0:T(8,128)S(1)}, f32[4,24,128]{2,1,0:T(8,128)S(1)}, f32[9,24,128]{2,1,0:T(8,128)S(1)}) custom-call(f32[3,22,24,128]{3,2,1,0:T(8,128)S(1)} %get-tuple-element.52.tall, f32[3,11,24,128]{3,2,1,0:T(8,128)S(1)} %collective-permute-done.10.first, ...), custom_call_target="tpu_custom_call" | custom-call | tf_op jit(solution)/shard_map/second_down_kernel/pallas_call | solution.py:451
  112.2 5.5 %collective-permute-start.13 = (f32[4,24,128]{2,1,0:T(8,128)S(1)}, f32[4,24,128]{2,1,0:T(8,128)S(1)}, u32[]{:S(2)}, u32[]{:S(2)}) collective-permute-start(f32[4,24,128]{2,1,0:T(8,128)S(1)} %get-tuple-element.57), channel_id=1, source_target_pairs={{16,32},{24,40},{32,16},{40,24},{48,64},{56,72},{64,48},{72,56},{8... | collective-permute-start | bytes 147464 | tf_op jit(solution)/shard_map/ppermute | solution.py:470
  117.6 1.9 %collective-permute-start.12 = (f32[4,24,128]{2,1,0:T(8,128)S(1)}, f32[4,24,128]{2,1,0:T(8,128)S(1)}, u32[]{:S(2)}, u32[]{:S(2)}) collective-permute-start(f32[4,24,128]{2,1,0:T(8,128)S(1)} %get-tuple-element.57), channel_id=1, source_target_pairs={{0,16},{8,24},{16,0},{24,8},{32,48},{40,56},{48,32},{56,40},{64,80... | collective-permute-start | bytes 147464 | tf_op jit(solution)/shard_map/ppermute | solution.py:470
  119.6 1.9 %collective-permute-done.13 = f32[4,24,128]{2,1,0:T(8,128)S(1)} collective-permute-done((f32[4,24,128]{2,1,0:T(8,128)S(1)}, f32[4,24,128]{2,1,0:T(8,128)S(1)}, u32[]{:S(2)}, u32[]{:S(2)}) %collective-permute-start.13) | collective-permute-done | bytes 49184 | tf_op jit(solution)/shard_map/ppermute | solution.py:470
  121.5 2.0 %collective-permute-start.14 = (f32[4,24,128]{2,1,0:T(8,128)S(1)}, f32[4,24,128]{2,1,0:T(8,128)S(1)}, u32[]{:S(2)}, u32[]{:S(2)}) collective-permute-start(f32[4,24,128]{2,1,0:T(8,128)S(1)} %collective-permute-done.13), channel_id=1, source_target_pairs={{0,16},{8,24},{16,0},{24,8},{32,48},{40,56},{48,32},{56,40},{64,80... | collective-permute-start | bytes 147464 | tf_op jit(solution)/shard_map/ppermute | solution.py:470
  123.5 0.1 collective-permute-done.12
  123.6 5.2 %collective-permute-start.15 = (f32[4,24,128]{2,1,0:T(8,128)S(1)}, f32[4,24,128]{2,1,0:T(8,128)S(1)}, u32[]{:S(2)}, u32[]{:S(2)}) collective-permute-start(f32[4,24,128]{2,1,0:T(8,128)S(1)} %collective-permute-done.12), channel_id=1, source_target_pairs={{16,32},{24,40},{32,16},{40,24},{48,64},{56,72},{64,48},{72,56},{8... | collective-permute-start | bytes 147464 | tf_op jit(solution)/shard_map/ppermute | solution.py:470
  128.9 0.0 collective-permute-done.14
  128.9 4.0 %collective-permute-done.15 = f32[4,24,128]{2,1,0:T(8,128)S(1)} collective-permute-done((f32[4,24,128]{2,1,0:T(8,128)S(1)}, f32[4,24,128]{2,1,0:T(8,128)S(1)}, u32[]{:S(2)}, u32[]{:S(2)}) %collective-permute-start.15) | collective-permute-done | bytes 49184 | tf_op jit(solution)/shard_map/ppermute | solution.py:470
  132.9 2.1 %collective-permute-start.16 = (f32[29,24,128]{2,1,0:T(8,128)S(1)}, f32[29,24,128]{2,1,0:T(8,128)S(1)}, u32[]{:S(2)}, u32[]{:S(2)}) collective-permute-start(f32[29,24,128]{2,1,0:T(8,128)S(1)} %constant_dynamic-update-slice_fusion.6.mine), channel_id=1, source_target_pairs={{0,8},{8,0},{16,24},{24,16},{32,40},{40,32},{48,56},{56,48},{64,72... | collective-permute-start | bytes 1069064 | tf_op jit(solution)/shard_map/ppermute | solution.py:470
  135.1 1.5 collective-permute-done.16.other
  136.5 2.6 %coarse_kernel.3 = (f32[3,4,24,128]{3,2,1,0:T(8,128)S(1)}, f32[3,3,24,128]{3,2,1,0:T(8,128)S(1)}, f32[3,3,24,128]{3,2,1,0:T(8,128)S(1)}) custom-call(f32[29,24,128]{2,1,0:T(8,128)S(1)} %constant_dynamic-update-slice_fusion.6.mine, f32[29,24,128]{2,1,0:T(8,128)S(1)} %collective-permute-done.16.other, f32[3,8,24,128]{3,2,1,0:T(8,128)S(1)} %get-tuple-element.59.v1), custom_call_target="tpu_custom_call" | custom-call | tf_op jit(solution)/shard_map/coarse_kernel/pallas_call | solution.py:451
  139.2 1.9 %collective-permute-start.17 = (f32[3,3,24,128]{3,2,1,0:T(8,128)S(1)}, f32[3,3,24,128]{3,2,1,0:T(8,128)S(1)}, u32[]{:S(2)}, u32[]{:S(2)}) collective-permute-start(f32[3,3,24,128]{3,2,1,0:T(8,128)S(1)} %get-tuple-element.62), channel_id=1, source_target_pairs={{8,16},{16,8},{24,32},{32,24},{40,48},{48,40},{56,64},{64,56},{72,... | collective-permute-start | bytes 331784 | tf_op jit(solution)/shard_map/ppermute | solution.py:470
  141.1 4.1 %collective-permute-done.17.right = f32[3,3,24,128]{3,2,1,0:T(8,128)S(1)} collective-permute-done((f32[3,3,24,128]{3,2,1,0:T(8,128)S(1)}, f32[3,3,24,128]{3,2,1,0:T(8,128)S(1)}, u32[]{:S(2)}, u32[]{:S(2)}) %collective-permute-start.17) | collective-permute-done | bytes 110624 | tf_op jit(solution)/shard_map/ppermute | solution.py:470
  145.2 1.5 last_up_kernel.1
  146.7 17.9 %all_to_all.11.taken = f32[8,9,8,128]{3,2,1,0:T(8,128)S(1)} all-to-all(f32[8,9,8,128]{3,2,1,0:T(8,128)S(1)} %last_up_kernel.1), channel_id=1, replica_groups=mesh['gx'=64,'gz'=8] {'gz'}, dimensions={0} | all-to-all | bytes 589824 | tf_op jit(solution)/shard_map/all_to_all | solution.py:565
  164.6 0.7 join_kernel.1
  (12 shorter events, 0.1 us)
Async XLA Ops:
  0.0 1.0 copy-start
  1.0 0.9 copy-start.1
  30.4 10.4 %collective-permute-start = (f32[7,6,24,128]{3,2,1,0:T(8,128)S(1)}, f32[7,6,24,128]{3,2,1,0:T(8,128)S(1)}, u32[]{:S(2)}, u32[]{:S(2)}) collective-permute-start(f32[7,6,24,128]{3,2,1,0:T(8,128)S(1)} %get-tuple-element.36), channel_id=1, source_target_pairs={{8,16},{16,8},{24,32},{32,24},{40,48},{48,40},{56,64},{64,56},{72,... | collective-permute-start | bytes 1548296 | tf_op jit(solution)/shard_map/ppermute | solution.py:470
  32.3 8.5 %collective-permute-start.1 = (f32[7,6,24,128]{3,2,1,0:T(8,128)S(1)}, f32[7,6,24,128]{3,2,1,0:T(8,128)S(1)}, u32[]{:S(2)}, u32[]{:S(2)}) collective-permute-start(f32[7,6,24,128]{3,2,1,0:T(8,128)S(1)} %get-tuple-element.37), channel_id=1, source_target_pairs={{0,8},{8,0},{16,24},{24,16},{32,40},{40,32},{48,56},{56,48},{64,72... | collective-permute-start | bytes 1548296 | tf_op jit(solution)/shard_map/ppermute | solution.py:470
  45.5 10.8 %collective-permute-start.3 = (f32[4,24,128]{2,1,0:T(8,128)S(1)}, f32[4,24,128]{2,1,0:T(8,128)S(1)}, u32[]{:S(2)}, u32[]{:S(2)}) collective-permute-start(f32[4,24,128]{2,1,0:T(8,128)S(1)} %get-tuple-element.38), channel_id=1, source_target_pairs={{16,32},{24,40},{32,16},{40,24},{48,64},{56,72},{64,48},{72,56},{8... | collective-permute-start | bytes 147464 | tf_op jit(solution)/shard_map/ppermute | solution.py:470
  54.2 6.2 %collective-permute-start.2 = (f32[4,24,128]{2,1,0:T(8,128)S(1)}, f32[4,24,128]{2,1,0:T(8,128)S(1)}, u32[]{:S(2)}, u32[]{:S(2)}) collective-permute-start(f32[4,24,128]{2,1,0:T(8,128)S(1)} %get-tuple-element.38), channel_id=1, source_target_pairs={{0,16},{8,24},{16,0},{24,8},{32,48},{40,56},{48,32},{56,40},{64,80... | collective-permute-start | bytes 147464 | tf_op jit(solution)/shard_map/ppermute | solution.py:470
  56.3 9.2 %collective-permute-start.4 = (f32[4,24,128]{2,1,0:T(8,128)S(1)}, f32[4,24,128]{2,1,0:T(8,128)S(1)}, u32[]{:S(2)}, u32[]{:S(2)}) collective-permute-start(f32[4,24,128]{2,1,0:T(8,128)S(1)} %collective-permute-done.3), channel_id=1, source_target_pairs={{0,16},{8,24},{16,0},{24,8},{32,48},{40,56},{48,32},{56,40},{64,80... | collective-permute-start | bytes 147464 | tf_op jit(solution)/shard_map/ppermute | solution.py:470
  60.4 9.3 %collective-permute-start.5 = (f32[4,24,128]{2,1,0:T(8,128)S(1)}, f32[4,24,128]{2,1,0:T(8,128)S(1)}, u32[]{:S(2)}, u32[]{:S(2)}) collective-permute-start(f32[4,24,128]{2,1,0:T(8,128)S(1)} %collective-permute-done.2), channel_id=1, source_target_pairs={{16,32},{24,40},{32,16},{40,24},{48,64},{56,72},{64,48},{72,56},{8... | collective-permute-start | bytes 147464 | tf_op jit(solution)/shard_map/ppermute | solution.py:470
  69.7 3.6 %collective-permute-start.6 = (f32[29,24,128]{2,1,0:T(8,128)S(1)}, f32[29,24,128]{2,1,0:T(8,128)S(1)}, u32[]{:S(2)}, u32[]{:S(2)}) collective-permute-start(f32[29,24,128]{2,1,0:T(8,128)S(1)} %constant_dynamic-update-slice_fusion.mine), channel_id=1, source_target_pairs={{0,8},{8,0},{16,24},{24,16},{32,40},{40,32},{48,56},{56,48},{64,72... | collective-permute-start | bytes 1069064 | tf_op jit(solution)/shard_map/ppermute | solution.py:470
  75.9 6.1 %collective-permute-start.7 = (f32[3,3,24,128]{3,2,1,0:T(8,128)S(1)}, f32[3,3,24,128]{3,2,1,0:T(8,128)S(1)}, u32[]{:S(2)}, u32[]{:S(2)}) collective-permute-start(f32[3,3,24,128]{3,2,1,0:T(8,128)S(1)} %get-tuple-element.43), channel_id=1, source_target_pairs={{8,16},{16,8},{24,32},{32,24},{40,48},{48,40},{56,64},{64,56},{72,... | collective-permute-start | bytes 331784 | tf_op jit(solution)/shard_map/ppermute | solution.py:470
  83.5 10.4 %collective-permute-start.8 = (f32[3,7,24,128]{3,2,1,0:T(8,128)S(1)}, f32[3,7,24,128]{3,2,1,0:T(8,128)S(1)}, u32[]{:S(2)}, u32[]{:S(2)}) collective-permute-start(f32[3,7,24,128]{3,2,1,0:T(8,128)S(1)} %get-tuple-element.50), channel_id=1, source_target_pairs={{8,16},{16,8},{24,32},{32,24},{40,48},{48,40},{56,64},{64,56},{72,... | collective-permute-start | bytes 774152 | tf_op jit(solution)/shard_map/ppermute | solution.py:470
  85.4 9.6 %collective-permute-start.9 = (f32[3,7,24,128]{3,2,1,0:T(8,128)S(1)}, f32[3,7,24,128]{3,2,1,0:T(8,128)S(1)}, u32[]{:S(2)}, u32[]{:S(2)}) collective-permute-start(f32[3,7,24,128]{3,2,1,0:T(8,128)S(1)} %get-tuple-element.51), channel_id=1, source_target_pairs={{0,8},{8,0},{16,24},{24,16},{32,40},{40,32},{48,56},{56,48},{64,72... | collective-permute-start | bytes 774152 | tf_op jit(solution)/shard_map/ppermute | solution.py:470
  95.2 12.2 %collective-permute-start.10 = (f32[3,11,24,128]{3,2,1,0:T(8,128)S(1)}, f32[3,11,24,128]{3,2,1,0:T(8,128)S(1)}, u32[]{:S(2)}, u32[]{:S(2)}) collective-permute-start(f32[3,11,24,128]{3,2,1,0:T(8,128)S(1)} %get-tuple-element.53), channel_id=1, source_target_pairs={{0,1},{1,0},{2,3},{3,2},{4,5},{5,4},{6,7},{7,6},{8,9},{9,8},{10,11... | collective-permute-start | bytes 1216520 | tf_op jit(solution)/shard_map/ppermute | solution.py:470
  97.7 9.7 %collective-permute-start.11 = (f32[3,11,24,128]{3,2,1,0:T(8,128)S(1)}, f32[3,11,24,128]{3,2,1,0:T(8,128)S(1)}, u32[]{:S(2)}, u32[]{:S(2)}) collective-permute-start(f32[3,11,24,128]{3,2,1,0:T(8,128)S(1)} %get-tuple-element.54), channel_id=1, source_target_pairs={{1,2},{2,1},{3,4},{4,3},{5,6},{6,5},{9,10},{10,9},{11,12},{12,11},... | collective-permute-start | bytes 1216520 | tf_op jit(solution)/shard_map/ppermute | solution.py:470
  112.2 9.3 %collective-permute-start.13 = (f32[4,24,128]{2,1,0:T(8,128)S(1)}, f32[4,24,128]{2,1,0:T(8,128)S(1)}, u32[]{:S(2)}, u32[]{:S(2)}) collective-permute-start(f32[4,24,128]{2,1,0:T(8,128)S(1)} %get-tuple-element.57), channel_id=1, source_target_pairs={{16,32},{24,40},{32,16},{40,24},{48,64},{56,72},{64,48},{72,56},{8... | collective-permute-start | bytes 147464 | tf_op jit(solution)/shard_map/ppermute | solution.py:470
  117.6 6.0 %collective-permute-start.12 = (f32[4,24,128]{2,1,0:T(8,128)S(1)}, f32[4,24,128]{2,1,0:T(8,128)S(1)}, u32[]{:S(2)}, u32[]{:S(2)}) collective-permute-start(f32[4,24,128]{2,1,0:T(8,128)S(1)} %get-tuple-element.57), channel_id=1, source_target_pairs={{0,16},{8,24},{16,0},{24,8},{32,48},{40,56},{48,32},{56,40},{64,80... | collective-permute-start | bytes 147464 | tf_op jit(solution)/shard_map/ppermute | solution.py:470
  121.5 7.4 %collective-permute-start.14 = (f32[4,24,128]{2,1,0:T(8,128)S(1)}, f32[4,24,128]{2,1,0:T(8,128)S(1)}, u32[]{:S(2)}, u32[]{:S(2)}) collective-permute-start(f32[4,24,128]{2,1,0:T(8,128)S(1)} %collective-permute-done.13), channel_id=1, source_target_pairs={{0,16},{8,24},{16,0},{24,8},{32,48},{40,56},{48,32},{56,40},{64,80... | collective-permute-start | bytes 147464 | tf_op jit(solution)/shard_map/ppermute | solution.py:470
  123.6 9.3 %collective-permute-start.15 = (f32[4,24,128]{2,1,0:T(8,128)S(1)}, f32[4,24,128]{2,1,0:T(8,128)S(1)}, u32[]{:S(2)}, u32[]{:S(2)}) collective-permute-start(f32[4,24,128]{2,1,0:T(8,128)S(1)} %collective-permute-done.12), channel_id=1, source_target_pairs={{16,32},{24,40},{32,16},{40,24},{48,64},{56,72},{64,48},{72,56},{8... | collective-permute-start | bytes 147464 | tf_op jit(solution)/shard_map/ppermute | solution.py:470
  132.9 3.6 %collective-permute-start.16 = (f32[29,24,128]{2,1,0:T(8,128)S(1)}, f32[29,24,128]{2,1,0:T(8,128)S(1)}, u32[]{:S(2)}, u32[]{:S(2)}) collective-permute-start(f32[29,24,128]{2,1,0:T(8,128)S(1)} %constant_dynamic-update-slice_fusion.6.mine), channel_id=1, source_target_pairs={{0,8},{8,0},{16,24},{24,16},{32,40},{40,32},{48,56},{56,48},{64,72... | collective-permute-start | bytes 1069064 | tf_op jit(solution)/shard_map/ppermute | solution.py:470
  139.2 6.1 %collective-permute-start.17 = (f32[3,3,24,128]{3,2,1,0:T(8,128)S(1)}, f32[3,3,24,128]{3,2,1,0:T(8,128)S(1)}, u32[]{:S(2)}, u32[]{:S(2)}) collective-permute-start(f32[3,3,24,128]{3,2,1,0:T(8,128)S(1)} %get-tuple-element.62), channel_id=1, source_target_pairs={{8,16},{16,8},{24,32},{32,24},{40,48},{48,40},{56,64},{64,56},{72,... | collective-permute-start | bytes 331784 | tf_op jit(solution)/shard_map/ppermute | solution.py:470

commit v9 on v8

--- a/solution.py
+++ b/solution.py
@@ -322,11 +322,17 @@
         tall[c, at] = value
 
     with_halo(position, own, first, second, store)
-    for c in range(C):
-        for r in range(half):
-            one, two = tall[c, r], pltpu.roll(tall[c, r + half], LANES // 2, 1)
-            to_first[c, r] = jnp.where(low, one, two)
-            to_second[c, r] = jnp.where(low, two, one)
+    tiles = ([], [])
+    for n in range(C * half):
+        one, other = tall[n // half, n % half], tall[n // half, n % half + half]
+        two = jnp.where(lane_index() < LANES // 2, pltpu.roll(other, 48, 1), pltpu.roll(other, 80, 1))
+        tiles[0].append(jnp.where(low, one, two))
+        tiles[1].append(jnp.where(low, two, one))
+    for target, some in ((to_first, tiles[0]), (to_second, tiles[1])):
+        whole = len(some) // 4 * 4
+        packed = [tile for n in range(0, whole, 4) for tile in squeeze(some[n : n + 4])] + some[whole:]
+        for n, tile in enumerate(packed):
+            target[n] = tile
 
 
 def second_down_kernel(tall, first, second, g0, d0, f0, d1, f1, v0, g1, v1, packed, edge, wide, field, field1):
@@ -338,9 +344,16 @@
     for c in range(C):
         for r in range(2 * half):
             wide[c, r, :, :LANES] = tall[c, r]
-        for r in range(half):
-            wide[c, r, :, LANES:] = jnp.where(low, first[c, r], second[c, r])
-            wide[c, r + half, :, LANES:] = pltpu.roll(jnp.where(low, second[c, r], first[c, r]), LANES // 2, 1)
+    whole = C * half // 4
+    sides = []
+    for ref in (first, second):
+        some = [tile for n in range(whole) for tile in unsqueeze([ref[3 * n + t] for t in range(3)])]
+        sides.append(some + [ref[n] for n in range(3 * whole, ref.shape[0])])
+    for n, (one, two) in enumerate(zip(*sides)):
+        c, r = n // half, n % half
+        wide[c, r, :, LANES:] = jnp.where(low, one, two)
+        other = jnp.where(low, two, one)
+        wide[c, r + half, :, LANES:] = jnp.where(lane_index() < LANES // 2, pltpu.roll(other, 48, 1), pltpu.roll(other, 80, 1))
     g, d, f, a, b = (g0, -HALO), (d0, -HALO), (f0, -HALO), (field, -HALO), (v0, -HALO)
     sweep(a, (wide, -halo), g, f, 0, -6, rows + 6)
     sweep(b, a, g, f, 0, -5, rows + 5)
@@ -532,7 +545,7 @@
     half = (rows + 2 * reach) // 2
     tall, first, second = call(
         side_kernel,
-        [(C, 2 * half, NZ, LANES)] + [(C, half, NZ, LANES)] * 2,
+        [(C, 2 * half, NZ, LANES)] + [(C * half - C * half // 4, NZ, LANES)] * 2,
         [],
         field,
         swap(second, "gx", False),

time: 168 us -> 168 us (level)
  waiting for transfers between devices: 35.1 us -> 31.9 us
  starting transfers between devices: 63 us -> 65.1 us
    ppermute x18, waiting for transfers between devices: 35.1 us -> 31.9 us  [swap(): return lax.ppermute(values, axis, pairs)]
    ppermute x18, starting transfers between devices: 63 us -> 65.1 us  [swap(): return lax.ppermute(values, axis, pairs)]
where the time goes in v9:
time: 168 us; the launch traced here: 165 us
  starting transfers between devices  65.1 us (39%)
  blocking collectives  45.8 us (27%)
  waiting for transfers between devices  31.9 us (19%)
  Pallas kernels  19.8 us (12%)
  local copies, waits for them, and re-layouts  1.93 us (1%)
    ppermute x18, starting transfers between devices, swap(): return lax.ppermute(values, axis, pairs)  65.1 us
    ppermute x18, waiting for transfers between devices, swap(): return lax.ppermute(values, axis, pairs)  31.9 us
    all_to_all x1, blocking collectives, shards(): taken = lax.all_to_all(sent, 'gz', 0, 0)  27.9 us
    pallas_call x10, Pallas kernels, call(): pl.pallas_call(kernel, out_shape=[shape(s) for s in outs], in_specs=[pl.B...  19.8 us
    all_to_all x1, blocking collectives, shards(): lax.all_to_all(sent, 'gz', 0, 0)  17.9 us
  transfers between devices with their start and end apart: 18, of which 13 were waited for; matrix products, arithmetic and copies ran while one was open for 0% of the time, Pallas kernels for 0%

profile of v9, /device:TPU:198, one launch (start us, length us, event | category | flops | bytes accessed | tf_op | source)
XLA Modules:
  0.0 164.8 jit_solution(17136977586773366607)
XLA Ops:
  0.0 0.0 copy-start
  0.0 1.0 copy-done
  1.0 0.0 copy-start.1
  1.0 0.9 copy-done.1
  1.9 0.2 pack_kernel.1
  2.0 27.9 %all_to_all.10.taken = f32[8,21,8,128]{3,2,1,0:T(8,128)S(1)} all-to-all(f32[8,21,8,128]{3,2,1,0:T(8,128)S(1)} %pack_kernel.1), channel_id=1, replica_groups=mesh['gx'=64,'gz'=8] {'gz'}, dimensions={0} | all-to-all | bytes 1376256 | tf_op jit(solution)/shard_map/all_to_all | solution.py:499
  29.9 0.5 unpack_kernel.1
  30.4 1.9 %collective-permute-start = (f32[7,6,24,128]{3,2,1,0:T(8,128)S(1)}, f32[7,6,24,128]{3,2,1,0:T(8,128)S(1)}, u32[]{:S(2)}, u32[]{:S(2)}) collective-permute-start(f32[7,6,24,128]{3,2,1,0:T(8,128)S(1)} %get-tuple-element.36), channel_id=1, source_target_pairs={{8,16},{16,8},{24,32},{32,24},{40,48},{48,40},{56,64},{64,56},{72,... | collective-permute-start | bytes 1548296 | tf_op jit(solution)/shard_map/ppermute | solution.py:483
  32.3 5.5 %collective-permute-start.1 = (f32[7,6,24,128]{3,2,1,0:T(8,128)S(1)}, f32[7,6,24,128]{3,2,1,0:T(8,128)S(1)}, u32[]{:S(2)}, u32[]{:S(2)}) collective-permute-start(f32[7,6,24,128]{3,2,1,0:T(8,128)S(1)} %get-tuple-element.37), channel_id=1, source_target_pairs={{0,8},{8,0},{16,24},{24,16},{32,40},{40,32},{48,56},{56,48},{64,72... | collective-permute-start | bytes 1548296 | tf_op jit(solution)/shard_map/ppermute | solution.py:483
  37.9 3.0 %collective-permute-done.second = f32[7,6,24,128]{3,2,1,0:T(8,128)S(1)} collective-permute-done((f32[7,6,24,128]{3,2,1,0:T(8,128)S(1)}, f32[7,6,24,128]{3,2,1,0:T(8,128)S(1)}, u32[]{:S(2)}, u32[]{:S(2)}) %collective-permute-start) | collective-permute-done | bytes 516128 | tf_op jit(solution)/shard_map/ppermute | solution.py:483
  40.8 0.0 collective-permute-done.1.first
  40.8 4.7 %first_down_kernel.1 = (f32[3,20,24,256]{3,2,1,0:T(8,128)S(1)}, f32[20,24,256]{2,1,0:T(8,128)S(1)}, f32[20,24,256]{2,1,0:T(8,128)S(1)}, f32[3,20,24,256]{3,2,1,0...) custom-call(f32[4,8,24,256]{3,2,1,0:T(8,128)S(1)} %get-tuple-element, ...), custom_call_target="tpu_custom_call" | custom-call | tf_op jit(solution)/shard_map/first_down_kernel/pallas_call | solution.py:464
  45.5 8.7 %collective-permute-start.3 = (f32[4,24,128]{2,1,0:T(8,128)S(1)}, f32[4,24,128]{2,1,0:T(8,128)S(1)}, u32[]{:S(2)}, u32[]{:S(2)}) collective-permute-start(f32[4,24,128]{2,1,0:T(8,128)S(1)} %get-tuple-element.38), channel_id=1, source_target_pairs={{16,32},{24,40},{32,16},{40,24},{48,64},{56,72},{64,48},{72,56},{8... | collective-permute-start | bytes 147464 | tf_op jit(solution)/shard_map/ppermute | solution.py:483
  54.2 1.9 %collective-permute-start.2 = (f32[4,24,128]{2,1,0:T(8,128)S(1)}, f32[4,24,128]{2,1,0:T(8,128)S(1)}, u32[]{:S(2)}, u32[]{:S(2)}) collective-permute-start(f32[4,24,128]{2,1,0:T(8,128)S(1)} %get-tuple-element.38), channel_id=1, source_target_pairs={{0,16},{8,24},{16,0},{24,8},{32,48},{40,56},{48,32},{56,40},{64,80... | collective-permute-start | bytes 147464 | tf_op jit(solution)/shard_map/ppermute | solution.py:483
  56.2 0.1 collective-permute-done.3
  56.3 3.8 %collective-permute-start.4 = (f32[4,24,128]{2,1,0:T(8,128)S(1)}, f32[4,24,128]{2,1,0:T(8,128)S(1)}, u32[]{:S(2)}, u32[]{:S(2)}) collective-permute-start(f32[4,24,128]{2,1,0:T(8,128)S(1)} %collective-permute-done.3), channel_id=1, source_target_pairs={{0,16},{8,24},{16,0},{24,8},{32,48},{40,56},{48,32},{56,40},{64,80... | collective-permute-start | bytes 147464 | tf_op jit(solution)/shard_map/ppermute | solution.py:483
  60.1 0.3 collective-permute-done.2
  60.4 5.0 %collective-permute-start.5 = (f32[4,24,128]{2,1,0:T(8,128)S(1)}, f32[4,24,128]{2,1,0:T(8,128)S(1)}, u32[]{:S(2)}, u32[]{:S(2)}) collective-permute-start(f32[4,24,128]{2,1,0:T(8,128)S(1)} %collective-permute-done.2), channel_id=1, source_target_pairs={{16,32},{24,40},{32,16},{40,24},{48,64},{56,72},{64,48},{72,56},{8... | collective-permute-start | bytes 147464 | tf_op jit(solution)/shard_map/ppermute | solution.py:483
  65.5 0.0 collective-permute-done.4
  65.5 4.2 %collective-permute-done.5 = f32[4,24,128]{2,1,0:T(8,128)S(1)} collective-permute-done((f32[4,24,128]{2,1,0:T(8,128)S(1)}, f32[4,24,128]{2,1,0:T(8,128)S(1)}, u32[]{:S(2)}, u32[]{:S(2)}) %collective-permute-start.5) | collective-permute-done | bytes 49184 | tf_op jit(solution)/shard_map/ppermute | solution.py:483
  69.7 1.9 %collective-permute-start.6 = (f32[29,24,128]{2,1,0:T(8,128)S(1)}, f32[29,24,128]{2,1,0:T(8,128)S(1)}, u32[]{:S(2)}, u32[]{:S(2)}) collective-permute-start(f32[29,24,128]{2,1,0:T(8,128)S(1)} %constant_dynamic-update-slice_fusion.mine), channel_id=1, source_target_pairs={{0,8},{8,0},{16,24},{24,16},{32,40},{40,32},{48,56},{56,48},{64,72... | collective-permute-start | bytes 1069064 | tf_op jit(solution)/shard_map/ppermute | solution.py:483
  71.7 1.6 collective-permute-done.6.other
  73.3 2.6 %coarse_kernel.2 = (f32[3,4,24,128]{3,2,1,0:T(8,128)S(1)}, f32[3,3,24,128]{3,2,1,0:T(8,128)S(1)}, f32[3,3,24,128]{3,2,1,0:T(8,128)S(1)}) custom-call(f32[29,24,128]{2,1,0:T(8,128)S(1)} %constant_dynamic-update-slice_fusion.mine, f32[29,24,128]{2,1,0:T(8,128)S(1)} %collective-permute-done.6.other, f32[3,8,24,128]{3,2,1,0:T(8,128)S(1)} %get-tuple-element.40.v1), custom_call_target="tpu_custom_call" | custom-call | tf_op jit(solution)/shard_map/coarse_kernel/pallas_call | solution.py:464
  75.9 1.9 %collective-permute-start.7 = (f32[3,3,24,128]{3,2,1,0:T(8,128)S(1)}, f32[3,3,24,128]{3,2,1,0:T(8,128)S(1)}, u32[]{:S(2)}, u32[]{:S(2)}) collective-permute-start(f32[3,3,24,128]{3,2,1,0:T(8,128)S(1)} %get-tuple-element.43), channel_id=1, source_target_pairs={{8,16},{16,8},{24,32},{32,24},{40,48},{48,40},{56,64},{64,56},{72,... | collective-permute-start | bytes 331784 | tf_op jit(solution)/shard_map/ppermute | solution.py:483
  77.9 4.1 %collective-permute-done.7.right = f32[3,3,24,128]{3,2,1,0:T(8,128)S(1)} collective-permute-done((f32[3,3,24,128]{3,2,1,0:T(8,128)S(1)}, f32[3,3,24,128]{3,2,1,0:T(8,128)S(1)}, u32[]{:S(2)}, u32[]{:S(2)}) %collective-permute-start.7) | collective-permute-done | bytes 110624 | tf_op jit(solution)/shard_map/ppermute | solution.py:483
  82.0 1.4 first_up_kernel.1
  83.5 1.9 %collective-permute-start.8 = (f32[3,7,24,128]{3,2,1,0:T(8,128)S(1)}, f32[3,7,24,128]{3,2,1,0:T(8,128)S(1)}, u32[]{:S(2)}, u32[]{:S(2)}) collective-permute-start(f32[3,7,24,128]{3,2,1,0:T(8,128)S(1)} %get-tuple-element.50), channel_id=1, source_target_pairs={{8,16},{16,8},{24,32},{32,24},{40,48},{48,40},{56,64},{64,56},{72,... | collective-permute-start | bytes 774152 | tf_op jit(solution)/shard_map/ppermute | solution.py:483
  85.4 8.5 %collective-permute-start.9 = (f32[3,7,24,128]{3,2,1,0:T(8,128)S(1)}, f32[3,7,24,128]{3,2,1,0:T(8,128)S(1)}, u32[]{:S(2)}, u32[]{:S(2)}) collective-permute-start(f32[3,7,24,128]{3,2,1,0:T(8,128)S(1)} %get-tuple-element.51), channel_id=1, source_target_pairs={{0,8},{8,0},{16,24},{24,16},{32,40},{40,32},{48,56},{56,48},{64,72... | collective-permute-start | bytes 774152 | tf_op jit(solution)/shard_map/ppermute | solution.py:483
  93.9 0.0 collective-permute-done.8.second
  93.9 1.1 collective-permute-done.9.first
  95.0 0.5 side_kernel.1
  95.5 2.5 %collective-permute-start.10 = (f32[25,24,128]{2,1,0:T(8,128)S(1)}, f32[25,24,128]{2,1,0:T(8,128)S(1)}, u32[]{:S(2)}, u32[]{:S(2)}) collective-permute-start(f32[25,24,128]{2,1,0:T(8,128)S(1)} %get-tuple-element.53), channel_id=1, source_target_pairs={{0,1},{1,0},{2,3},{3,2},{4,5},{5,4},{6,7},{7,6},{8,9},{9,8},{10,11... | collective-permute-start | bytes 921608 | tf_op jit(solution)/shard_map/ppermute | solution.py:483
  98.0 0.7 collective-permute-start.11
  98.7 6.9 %collective-permute-done.10.first = f32[25,24,128]{2,1,0:T(8,128)S(1)} collective-permute-done((f32[25,24,128]{2,1,0:T(8,128)S(1)}, f32[25,24,128]{2,1,0:T(8,128)S(1)}, u32[]{:S(2)}, u32[]{:S(2)}) %collective-permute-start.10) | collective-permute-done | bytes 307232 | tf_op jit(solution)/shard_map/ppermute | solution.py:483
  105.6 0.0 collective-permute-done.11.second
  105.6 5.0 %second_down_kernel.1 = (f32[3,20,24,256]{3,2,1,0:T(8,128)S(1)}, f32[3,8,24,128]{3,2,1,0:T(8,128)S(1)}, f32[3,8,24,128]{3,2,1,0:T(8,128)S(1)}, f32[4,24,128]{2,1,0:T(8,128)S(1)}, f32[9,24,128]{2,1,0:T(8,128)S(1)}) custom-call(f32[3,22,24,128]{3,2,1,0:T(8,128)S(1)} %get-tuple-element.52.tall, f32[25,24,128]{2,1,0:T(8,128)S(1)} %collective-permute-done.10.first, ...), custom_call_target="tpu_custom_call" | custom-call | tf_op jit(solution)/shard_map/second_down_kernel/pallas_call | solution.py:464
  110.6 6.5 %collective-permute-start.13 = (f32[4,24,128]{2,1,0:T(8,128)S(1)}, f32[4,24,128]{2,1,0:T(8,128)S(1)}, u32[]{:S(2)}, u32[]{:S(2)}) collective-permute-start(f32[4,24,128]{2,1,0:T(8,128)S(1)} %get-tuple-element.57), channel_id=1, source_target_pairs={{16,32},{24,40},{32,16},{40,24},{48,64},{56,72},{64,48},{72,56},{8... | collective-permute-start | bytes 147464 | tf_op jit(solution)/shard_map/ppermute | solution.py:483
  117.1 1.9 %collective-permute-start.12 = (f32[4,24,128]{2,1,0:T(8,128)S(1)}, f32[4,24,128]{2,1,0:T(8,128)S(1)}, u32[]{:S(2)}, u32[]{:S(2)}) collective-permute-start(f32[4,24,128]{2,1,0:T(8,128)S(1)} %get-tuple-element.57), channel_id=1, source_target_pairs={{0,16},{8,24},{16,0},{24,8},{32,48},{40,56},{48,32},{56,40},{64,80... | collective-permute-start | bytes 147464 | tf_op jit(solution)/shard_map/ppermute | solution.py:483
  119.1 0.9 collective-permute-done.13
  119.9 3.1 %collective-permute-start.14 = (f32[4,24,128]{2,1,0:T(8,128)S(1)}, f32[4,24,128]{2,1,0:T(8,128)S(1)}, u32[]{:S(2)}, u32[]{:S(2)}) collective-permute-start(f32[4,24,128]{2,1,0:T(8,128)S(1)} %collective-permute-done.13), channel_id=1, source_target_pairs={{0,16},{8,24},{16,0},{24,8},{32,48},{40,56},{48,32},{56,40},{64,80... | collective-permute-start | bytes 147464 | tf_op jit(solution)/shard_map/ppermute | solution.py:483
  123.0 0.1 collective-permute-done.12
  123.1 5.2 %collective-permute-start.15 = (f32[4,24,128]{2,1,0:T(8,128)S(1)}, f32[4,24,128]{2,1,0:T(8,128)S(1)}, u32[]{:S(2)}, u32[]{:S(2)}) collective-permute-start(f32[4,24,128]{2,1,0:T(8,128)S(1)} %collective-permute-done.12), channel_id=1, source_target_pairs={{16,32},{24,40},{32,16},{40,24},{48,64},{56,72},{64,48},{72,56},{8... | collective-permute-start | bytes 147464 | tf_op jit(solution)/shard_map/ppermute | solution.py:483
  128.4 0.0 collective-permute-done.14
  128.4 4.0 %collective-permute-done.15 = f32[4,24,128]{2,1,0:T(8,128)S(1)} collective-permute-done((f32[4,24,128]{2,1,0:T(8,128)S(1)}, f32[4,24,128]{2,1,0:T(8,128)S(1)}, u32[]{:S(2)}, u32[]{:S(2)}) %collective-permute-start.15) | collective-permute-done | bytes 49184 | tf_op jit(solution)/shard_map/ppermute | solution.py:483
  132.4 2.1 %collective-permute-start.16 = (f32[29,24,128]{2,1,0:T(8,128)S(1)}, f32[29,24,128]{2,1,0:T(8,128)S(1)}, u32[]{:S(2)}, u32[]{:S(2)}) collective-permute-start(f32[29,24,128]{2,1,0:T(8,128)S(1)} %constant_dynamic-update-slice_fusion.6.mine), channel_id=1, source_target_pairs={{0,8},{8,0},{16,24},{24,16},{32,40},{40,32},{48,56},{56,48},{64,72... | collective-permute-start | bytes 1069064 | tf_op jit(solution)/shard_map/ppermute | solution.py:483
  134.5 1.5 collective-permute-done.16.other
  136.0 2.6 %coarse_kernel.3 = (f32[3,4,24,128]{3,2,1,0:T(8,128)S(1)}, f32[3,3,24,128]{3,2,1,0:T(8,128)S(1)}, f32[3,3,24,128]{3,2,1,0:T(8,128)S(1)}) custom-call(f32[29,24,128]{2,1,0:T(8,128)S(1)} %constant_dynamic-update-slice_fusion.6.mine, f32[29,24,128]{2,1,0:T(8,128)S(1)} %collective-permute-done.16.other, f32[3,8,24,128]{3,2,1,0:T(8,128)S(1)} %get-tuple-element.59.v1), custom_call_target="tpu_custom_call" | custom-call | tf_op jit(solution)/shard_map/coarse_kernel/pallas_call | solution.py:464
  138.6 1.9 %collective-permute-start.17 = (f32[3,3,24,128]{3,2,1,0:T(8,128)S(1)}, f32[3,3,24,128]{3,2,1,0:T(8,128)S(1)}, u32[]{:S(2)}, u32[]{:S(2)}) collective-permute-start(f32[3,3,24,128]{3,2,1,0:T(8,128)S(1)} %get-tuple-element.62), channel_id=1, source_target_pairs={{8,16},{16,8},{24,32},{32,24},{40,48},{48,40},{56,64},{64,56},{72,... | collective-permute-start | bytes 331784 | tf_op jit(solution)/shard_map/ppermute | solution.py:483
  140.6 4.1 %collective-permute-done.17.right = f32[3,3,24,128]{3,2,1,0:T(8,128)S(1)} collective-permute-done((f32[3,3,24,128]{3,2,1,0:T(8,128)S(1)}, f32[3,3,24,128]{3,2,1,0:T(8,128)S(1)}, u32[]{:S(2)}, u32[]{:S(2)}) %collective-permute-start.17) | collective-permute-done | bytes 110624 | tf_op jit(solution)/shard_map/ppermute | solution.py:483
  144.7 1.5 last_up_kernel.1
  146.2 17.9 %all_to_all.11.taken = f32[8,9,8,128]{3,2,1,0:T(8,128)S(1)} all-to-all(f32[8,9,8,128]{3,2,1,0:T(8,128)S(1)} %last_up_kernel.1), channel_id=1, replica_groups=mesh['gx'=64,'gz'=8] {'gz'}, dimensions={0} | all-to-all | bytes 589824 | tf_op jit(solution)/shard_map/all_to_all | solution.py:578
  164.0 0.7 join_kernel.1
  (12 shorter events, 0.1 us)
Async XLA Ops:
  0.0 1.0 copy-start
  1.0 0.9 copy-start.1
  30.4 10.4 %collective-permute-start = (f32[7,6,24,128]{3,2,1,0:T(8,128)S(1)}, f32[7,6,24,128]{3,2,1,0:T(8,128)S(1)}, u32[]{:S(2)}, u32[]{:S(2)}) collective-permute-start(f32[7,6,24,128]{3,2,1,0:T(8,128)S(1)} %get-tuple-element.36), channel_id=1, source_target_pairs={{8,16},{16,8},{24,32},{32,24},{40,48},{48,40},{56,64},{64,56},{72,... | collective-permute-start | bytes 1548296 | tf_op jit(solution)/shard_map/ppermute | solution.py:483
  32.3 8.5 %collective-permute-start.1 = (f32[7,6,24,128]{3,2,1,0:T(8,128)S(1)}, f32[7,6,24,128]{3,2,1,0:T(8,128)S(1)}, u32[]{:S(2)}, u32[]{:S(2)}) collective-permute-start(f32[7,6,24,128]{3,2,1,0:T(8,128)S(1)} %get-tuple-element.37), channel_id=1, source_target_pairs={{0,8},{8,0},{16,24},{24,16},{32,40},{40,32},{48,56},{56,48},{64,72... | collective-permute-start | bytes 1548296 | tf_op jit(solution)/shard_map/ppermute | solution.py:483
  45.5 10.8 %collective-permute-start.3 = (f32[4,24,128]{2,1,0:T(8,128)S(1)}, f32[4,24,128]{2,1,0:T(8,128)S(1)}, u32[]{:S(2)}, u32[]{:S(2)}) collective-permute-start(f32[4,24,128]{2,1,0:T(8,128)S(1)} %get-tuple-element.38), channel_id=1, source_target_pairs={{16,32},{24,40},{32,16},{40,24},{48,64},{56,72},{64,48},{72,56},{8... | collective-permute-start | bytes 147464 | tf_op jit(solution)/shard_map/ppermute | solution.py:483
  54.2 6.2 %collective-permute-start.2 = (f32[4,24,128]{2,1,0:T(8,128)S(1)}, f32[4,24,128]{2,1,0:T(8,128)S(1)}, u32[]{:S(2)}, u32[]{:S(2)}) collective-permute-start(f32[4,24,128]{2,1,0:T(8,128)S(1)} %get-tuple-element.38), channel_id=1, source_target_pairs={{0,16},{8,24},{16,0},{24,8},{32,48},{40,56},{48,32},{56,40},{64,80... | collective-permute-start | bytes 147464 | tf_op jit(solution)/shard_map/ppermute | solution.py:483
  56.3 9.2 %collective-permute-start.4 = (f32[4,24,128]{2,1,0:T(8,128)S(1)}, f32[4,24,128]{2,1,0:T(8,128)S(1)}, u32[]{:S(2)}, u32[]{:S(2)}) collective-permute-start(f32[4,24,128]{2,1,0:T(8,128)S(1)} %collective-permute-done.3), channel_id=1, source_target_pairs={{0,16},{8,24},{16,0},{24,8},{32,48},{40,56},{48,32},{56,40},{64,80... | collective-permute-start | bytes 147464 | tf_op jit(solution)/shard_map/ppermute | solution.py:483
  60.4 9.3 %collective-permute-start.5 = (f32[4,24,128]{2,1,0:T(8,128)S(1)}, f32[4,24,128]{2,1,0:T(8,128)S(1)}, u32[]{:S(2)}, u32[]{:S(2)}) collective-permute-start(f32[4,24,128]{2,1,0:T(8,128)S(1)} %collective-permute-done.2), channel_id=1, source_target_pairs={{16,32},{24,40},{32,16},{40,24},{48,64},{56,72},{64,48},{72,56},{8... | collective-permute-start | bytes 147464 | tf_op jit(solution)/shard_map/ppermute | solution.py:483
  69.7 3.6 %collective-permute-start.6 = (f32[29,24,128]{2,1,0:T(8,128)S(1)}, f32[29,24,128]{2,1,0:T(8,128)S(1)}, u32[]{:S(2)}, u32[]{:S(2)}) collective-permute-start(f32[29,24,128]{2,1,0:T(8,128)S(1)} %constant_dynamic-update-slice_fusion.mine), channel_id=1, source_target_pairs={{0,8},{8,0},{16,24},{24,16},{32,40},{40,32},{48,56},{56,48},{64,72... | collective-permute-start | bytes 1069064 | tf_op jit(solution)/shard_map/ppermute | solution.py:483
  75.9 6.1 %collective-permute-start.7 = (f32[3,3,24,128]{3,2,1,0:T(8,128)S(1)}, f32[3,3,24,128]{3,2,1,0:T(8,128)S(1)}, u32[]{:S(2)}, u32[]{:S(2)}) collective-permute-start(f32[3,3,24,128]{3,2,1,0:T(8,128)S(1)} %get-tuple-element.43), channel_id=1, source_target_pairs={{8,16},{16,8},{24,32},{32,24},{40,48},{48,40},{56,64},{64,56},{72,... | collective-permute-start | bytes 331784 | tf_op jit(solution)/shard_map/ppermute | solution.py:483
  83.5 10.4 %collective-permute-start.8 = (f32[3,7,24,128]{3,2,1,0:T(8,128)S(1)}, f32[3,7,24,128]{3,2,1,0:T(8,128)S(1)}, u32[]{:S(2)}, u32[]{:S(2)}) collective-permute-start(f32[3,7,24,128]{3,2,1,0:T(8,128)S(1)} %get-tuple-element.50), channel_id=1, source_target_pairs={{8,16},{16,8},{24,32},{32,24},{40,48},{48,40},{56,64},{64,56},{72,... | collective-permute-start | bytes 774152 | tf_op jit(solution)/shard_map/ppermute | solution.py:483
  85.4 9.6 %collective-permute-start.9 = (f32[3,7,24,128]{3,2,1,0:T(8,128)S(1)}, f32[3,7,24,128]{3,2,1,0:T(8,128)S(1)}, u32[]{:S(2)}, u32[]{:S(2)}) collective-permute-start(f32[3,7,24,128]{3,2,1,0:T(8,128)S(1)} %get-tuple-element.51), channel_id=1, source_target_pairs={{0,8},{8,0},{16,24},{24,16},{32,40},{40,32},{48,56},{56,48},{64,72... | collective-permute-start | bytes 774152 | tf_op jit(solution)/shard_map/ppermute | solution.py:483
  95.5 10.0 %collective-permute-start.10 = (f32[25,24,128]{2,1,0:T(8,128)S(1)}, f32[25,24,128]{2,1,0:T(8,128)S(1)}, u32[]{:S(2)}, u32[]{:S(2)}) collective-permute-start(f32[25,24,128]{2,1,0:T(8,128)S(1)} %get-tuple-element.53), channel_id=1, source_target_pairs={{0,1},{1,0},{2,3},{3,2},{4,5},{5,4},{6,7},{7,6},{8,9},{9,8},{10,11... | collective-permute-start | bytes 921608 | tf_op jit(solution)/shard_map/ppermute | solution.py:483
  98.0 7.6 %collective-permute-start.11 = (f32[25,24,128]{2,1,0:T(8,128)S(1)}, f32[25,24,128]{2,1,0:T(8,128)S(1)}, u32[]{:S(2)}, u32[]{:S(2)}) collective-permute-start(f32[25,24,128]{2,1,0:T(8,128)S(1)} %get-tuple-element.54), channel_id=1, source_target_pairs={{1,2},{2,1},{3,4},{4,3},{5,6},{6,5},{9,10},{10,9},{11,12},{12,11},... | collective-permute-start | bytes 921608 | tf_op jit(solution)/shard_map/ppermute | solution.py:483
  110.6 9.3 %collective-permute-start.13 = (f32[4,24,128]{2,1,0:T(8,128)S(1)}, f32[4,24,128]{2,1,0:T(8,128)S(1)}, u32[]{:S(2)}, u32[]{:S(2)}) collective-permute-start(f32[4,24,128]{2,1,0:T(8,128)S(1)} %get-tuple-element.57), channel_id=1, source_target_pairs={{16,32},{24,40},{32,16},{40,24},{48,64},{56,72},{64,48},{72,56},{8... | collective-permute-start | bytes 147464 | tf_op jit(solution)/shard_map/ppermute | solution.py:483
  117.1 6.0 %collective-permute-start.12 = (f32[4,24,128]{2,1,0:T(8,128)S(1)}, f32[4,24,128]{2,1,0:T(8,128)S(1)}, u32[]{:S(2)}, u32[]{:S(2)}) collective-permute-start(f32[4,24,128]{2,1,0:T(8,128)S(1)} %get-tuple-element.57), channel_id=1, source_target_pairs={{0,16},{8,24},{16,0},{24,8},{32,48},{40,56},{48,32},{56,40},{64,80... | collective-permute-start | bytes 147464 | tf_op jit(solution)/shard_map/ppermute | solution.py:483
  119.9 8.5 %collective-permute-start.14 = (f32[4,24,128]{2,1,0:T(8,128)S(1)}, f32[4,24,128]{2,1,0:T(8,128)S(1)}, u32[]{:S(2)}, u32[]{:S(2)}) collective-permute-start(f32[4,24,128]{2,1,0:T(8,128)S(1)} %collective-permute-done.13), channel_id=1, source_target_pairs={{0,16},{8,24},{16,0},{24,8},{32,48},{40,56},{48,32},{56,40},{64,80... | collective-permute-start | bytes 147464 | tf_op jit(solution)/shard_map/ppermute | solution.py:483
  123.1 9.3 %collective-permute-start.15 = (f32[4,24,128]{2,1,0:T(8,128)S(1)}, f32[4,24,128]{2,1,0:T(8,128)S(1)}, u32[]{:S(2)}, u32[]{:S(2)}) collective-permute-start(f32[4,24,128]{2,1,0:T(8,128)S(1)} %collective-permute-done.12), channel_id=1, source_target_pairs={{16,32},{24,40},{32,16},{40,24},{48,64},{56,72},{64,48},{72,56},{8... | collective-permute-start | bytes 147464 | tf_op jit(solution)/shard_map/ppermute | solution.py:483
  132.4 3.6 %collective-permute-start.16 = (f32[29,24,128]{2,1,0:T(8,128)S(1)}, f32[29,24,128]{2,1,0:T(8,128)S(1)}, u32[]{:S(2)}, u32[]{:S(2)}) collective-permute-start(f32[29,24,128]{2,1,0:T(8,128)S(1)} %constant_dynamic-update-slice_fusion.6.mine), channel_id=1, source_target_pairs={{0,8},{8,0},{16,24},{24,16},{32,40},{40,32},{48,56},{56,48},{64,72... | collective-permute-start | bytes 1069064 | tf_op jit(solution)/shard_map/ppermute | solution.py:483
  138.6 6.1 %collective-permute-start.17 = (f32[3,3,24,128]{3,2,1,0:T(8,128)S(1)}, f32[3,3,24,128]{3,2,1,0:T(8,128)S(1)}, u32[]{:S(2)}, u32[]{:S(2)}) collective-permute-start(f32[3,3,24,128]{3,2,1,0:T(8,128)S(1)} %get-tuple-element.62), channel_id=1, source_target_pairs={{8,16},{16,8},{24,32},{32,24},{40,48},{48,40},{56,64},{64,56},{72,... | collective-permute-start | bytes 331784 | tf_op jit(solution)/shard_map/ppermute | solution.py:483

commit v10 on v9

--- a/solution.py
+++ b/solution.py
@@ -147,7 +147,7 @@
 
     for r in [*range(low - reach, low), *range(high, high + reach)]:
         body(Row(0, r))
-    each_row(low, high, whole, UNROLL[level])
+    each_row(low, high, whole, min(UNROLL[level], 5))
 
 
 def first_sweep(target, source, factor, level, low, high):

time: 168 us -> 168 us (level)
  no operation moved by 1% of the time
where the time goes in v10:
time: 168 us; the launch traced here: 165 us
  starting transfers between devices  65.1 us (39%)
  blocking collectives  45.8 us (27%)
  waiting for transfers between devices  31.9 us (19%)
  Pallas kernels  20.1 us (12%)
  local copies, waits for them, and re-layouts  1.93 us (1%)
    ppermute x18, starting transfers between devices, swap(): return lax.ppermute(values, axis, pairs)  65.1 us
    ppermute x18, waiting for transfers between devices, swap(): return lax.ppermute(values, axis, pairs)  31.9 us
    all_to_all x1, blocking collectives, shards(): taken = lax.all_to_all(sent, 'gz', 0, 0)  27.9 us
    pallas_call x10, Pallas kernels, call(): pl.pallas_call(kernel, out_shape=[shape(s) for s in outs], in_specs=[pl.B...  20.1 us
    all_to_all x1, blocking collectives, shards(): lax.all_to_all(sent, 'gz', 0, 0)  17.9 us
  transfers between devices with their start and end apart: 18, of which 13 were waited for; matrix products, arithmetic and copies ran while one was open for 0% of the time, Pallas kernels for 0%

profile of v10, /device:TPU:198, one launch (start us, length us, event | category | flops | bytes accessed | tf_op | source)
XLA Modules:
  0.0 165.1 jit_solution(4230940986785302383)
XLA Ops:
  0.0 0.0 copy-start
  0.0 1.0 copy-done
  1.0 0.0 copy-start.1
  1.0 0.9 copy-done.1
  1.9 0.2 pack_kernel.1
  2.0 27.9 %all_to_all.10.taken = f32[8,21,8,128]{3,2,1,0:T(8,128)S(1)} all-to-all(f32[8,21,8,128]{3,2,1,0:T(8,128)S(1)} %pack_kernel.1), channel_id=1, replica_groups=mesh['gx'=64,'gz'=8] {'gz'}, dimensions={0} | all-to-all | bytes 1376256 | tf_op jit(solution)/shard_map/all_to_all | solution.py:499
  29.9 0.5 unpack_kernel.1
  30.4 1.9 %collective-permute-start = (f32[7,6,24,128]{3,2,1,0:T(8,128)S(1)}, f32[7,6,24,128]{3,2,1,0:T(8,128)S(1)}, u32[]{:S(2)}, u32[]{:S(2)}) collective-permute-start(f32[7,6,24,128]{3,2,1,0:T(8,128)S(1)} %get-tuple-element.36), channel_id=1, source_target_pairs={{8,16},{16,8},{24,32},{32,24},{40,48},{48,40},{56,64},{64,56},{72,... | collective-permute-start | bytes 1548296 | tf_op jit(solution)/shard_map/ppermute | solution.py:483
  32.3 5.5 %collective-permute-start.1 = (f32[7,6,24,128]{3,2,1,0:T(8,128)S(1)}, f32[7,6,24,128]{3,2,1,0:T(8,128)S(1)}, u32[]{:S(2)}, u32[]{:S(2)}) collective-permute-start(f32[7,6,24,128]{3,2,1,0:T(8,128)S(1)} %get-tuple-element.37), channel_id=1, source_target_pairs={{0,8},{8,0},{16,24},{24,16},{32,40},{40,32},{48,56},{56,48},{64,72... | collective-permute-start | bytes 1548296 | tf_op jit(solution)/shard_map/ppermute | solution.py:483
  37.9 3.0 %collective-permute-done.second = f32[7,6,24,128]{3,2,1,0:T(8,128)S(1)} collective-permute-done((f32[7,6,24,128]{3,2,1,0:T(8,128)S(1)}, f32[7,6,24,128]{3,2,1,0:T(8,128)S(1)}, u32[]{:S(2)}, u32[]{:S(2)}) %collective-permute-start) | collective-permute-done | bytes 516128 | tf_op jit(solution)/shard_map/ppermute | solution.py:483
  40.8 0.0 collective-permute-done.1.first
  40.8 4.8 %first_down_kernel.1 = (f32[3,20,24,256]{3,2,1,0:T(8,128)S(1)}, f32[20,24,256]{2,1,0:T(8,128)S(1)}, f32[20,24,256]{2,1,0:T(8,128)S(1)}, f32[3,20,24,256]{3,2,1,0...) custom-call(f32[4,8,24,256]{3,2,1,0:T(8,128)S(1)} %get-tuple-element, ...), custom_call_target="tpu_custom_call" | custom-call | tf_op jit(solution)/shard_map/first_down_kernel/pallas_call | solution.py:464
  45.6 8.7 %collective-permute-start.3 = (f32[4,24,128]{2,1,0:T(8,128)S(1)}, f32[4,24,128]{2,1,0:T(8,128)S(1)}, u32[]{:S(2)}, u32[]{:S(2)}) collective-permute-start(f32[4,24,128]{2,1,0:T(8,128)S(1)} %get-tuple-element.38), channel_id=1, source_target_pairs={{16,32},{24,40},{32,16},{40,24},{48,64},{56,72},{64,48},{72,56},{8... | collective-permute-start | bytes 147464 | tf_op jit(solution)/shard_map/ppermute | solution.py:483
  54.4 1.9 %collective-permute-start.2 = (f32[4,24,128]{2,1,0:T(8,128)S(1)}, f32[4,24,128]{2,1,0:T(8,128)S(1)}, u32[]{:S(2)}, u32[]{:S(2)}) collective-permute-start(f32[4,24,128]{2,1,0:T(8,128)S(1)} %get-tuple-element.38), channel_id=1, source_target_pairs={{0,16},{8,24},{16,0},{24,8},{32,48},{40,56},{48,32},{56,40},{64,80... | collective-permute-start | bytes 147464 | tf_op jit(solution)/shard_map/ppermute | solution.py:483
  56.3 0.1 collective-permute-done.3
  56.4 3.8 %collective-permute-start.4 = (f32[4,24,128]{2,1,0:T(8,128)S(1)}, f32[4,24,128]{2,1,0:T(8,128)S(1)}, u32[]{:S(2)}, u32[]{:S(2)}) collective-permute-start(f32[4,24,128]{2,1,0:T(8,128)S(1)} %collective-permute-done.3), channel_id=1, source_target_pairs={{0,16},{8,24},{16,0},{24,8},{32,48},{40,56},{48,32},{56,40},{64,80... | collective-permute-start | bytes 147464 | tf_op jit(solution)/shard_map/ppermute | solution.py:483
  60.2 0.3 collective-permute-done.2
  60.6 5.0 %collective-permute-start.5 = (f32[4,24,128]{2,1,0:T(8,128)S(1)}, f32[4,24,128]{2,1,0:T(8,128)S(1)}, u32[]{:S(2)}, u32[]{:S(2)}) collective-permute-start(f32[4,24,128]{2,1,0:T(8,128)S(1)} %collective-permute-done.2), channel_id=1, source_target_pairs={{16,32},{24,40},{32,16},{40,24},{48,64},{56,72},{64,48},{72,56},{8... | collective-permute-start | bytes 147464 | tf_op jit(solution)/shard_map/ppermute | solution.py:483
  65.6 0.0 collective-permute-done.4
  65.6 4.2 %collective-permute-done.5 = f32[4,24,128]{2,1,0:T(8,128)S(1)} collective-permute-done((f32[4,24,128]{2,1,0:T(8,128)S(1)}, f32[4,24,128]{2,1,0:T(8,128)S(1)}, u32[]{:S(2)}, u32[]{:S(2)}) %collective-permute-start.5) | collective-permute-done | bytes 49184 | tf_op jit(solution)/shard_map/ppermute | solution.py:483
  69.9 1.9 %collective-permute-start.6 = (f32[29,24,128]{2,1,0:T(8,128)S(1)}, f32[29,24,128]{2,1,0:T(8,128)S(1)}, u32[]{:S(2)}, u32[]{:S(2)}) collective-permute-start(f32[29,24,128]{2,1,0:T(8,128)S(1)} %constant_dynamic-update-slice_fusion.mine), channel_id=1, source_target_pairs={{0,8},{8,0},{16,24},{24,16},{32,40},{40,32},{48,56},{56,48},{64,72... | collective-permute-start | bytes 1069064 | tf_op jit(solution)/shard_map/ppermute | solution.py:483
  71.8 1.6 collective-permute-done.6.other
  73.4 2.7 %coarse_kernel.2 = (f32[3,4,24,128]{3,2,1,0:T(8,128)S(1)}, f32[3,3,24,128]{3,2,1,0:T(8,128)S(1)}, f32[3,3,24,128]{3,2,1,0:T(8,128)S(1)}) custom-call(f32[29,24,128]{2,1,0:T(8,128)S(1)} %constant_dynamic-update-slice_fusion.mine, f32[29,24,128]{2,1,0:T(8,128)S(1)} %collective-permute-done.6.other, f32[3,8,24,128]{3,2,1,0:T(8,128)S(1)} %get-tuple-element.40.v1), custom_call_target="tpu_custom_call" | custom-call | tf_op jit(solution)/shard_map/coarse_kernel/pallas_call | solution.py:464
  76.2 1.9 %collective-permute-start.7 = (f32[3,3,24,128]{3,2,1,0:T(8,128)S(1)}, f32[3,3,24,128]{3,2,1,0:T(8,128)S(1)}, u32[]{:S(2)}, u32[]{:S(2)}) collective-permute-start(f32[3,3,24,128]{3,2,1,0:T(8,128)S(1)} %get-tuple-element.43), channel_id=1, source_target_pairs={{8,16},{16,8},{24,32},{32,24},{40,48},{48,40},{56,64},{64,56},{72,... | collective-permute-start | bytes 331784 | tf_op jit(solution)/shard_map/ppermute | solution.py:483
  78.1 4.1 %collective-permute-done.7.right = f32[3,3,24,128]{3,2,1,0:T(8,128)S(1)} collective-permute-done((f32[3,3,24,128]{3,2,1,0:T(8,128)S(1)}, f32[3,3,24,128]{3,2,1,0:T(8,128)S(1)}, u32[]{:S(2)}, u32[]{:S(2)}) %collective-permute-start.7) | collective-permute-done | bytes 110624 | tf_op jit(solution)/shard_map/ppermute | solution.py:483
  82.2 1.4 first_up_kernel.1
  83.7 1.9 %collective-permute-start.8 = (f32[3,7,24,128]{3,2,1,0:T(8,128)S(1)}, f32[3,7,24,128]{3,2,1,0:T(8,128)S(1)}, u32[]{:S(2)}, u32[]{:S(2)}) collective-permute-start(f32[3,7,24,128]{3,2,1,0:T(8,128)S(1)} %get-tuple-element.50), channel_id=1, source_target_pairs={{8,16},{16,8},{24,32},{32,24},{40,48},{48,40},{56,64},{64,56},{72,... | collective-permute-start | bytes 774152 | tf_op jit(solution)/shard_map/ppermute | solution.py:483
  85.6 8.5 %collective-permute-start.9 = (f32[3,7,24,128]{3,2,1,0:T(8,128)S(1)}, f32[3,7,24,128]{3,2,1,0:T(8,128)S(1)}, u32[]{:S(2)}, u32[]{:S(2)}) collective-permute-start(f32[3,7,24,128]{3,2,1,0:T(8,128)S(1)} %get-tuple-element.51), channel_id=1, source_target_pairs={{0,8},{8,0},{16,24},{24,16},{32,40},{40,32},{48,56},{56,48},{64,72... | collective-permute-start | bytes 774152 | tf_op jit(solution)/shard_map/ppermute | solution.py:483
  94.1 0.0 collective-permute-done.8.second
  94.1 1.1 collective-permute-done.9.first
  95.2 0.5 side_kernel.1
  95.8 2.5 %collective-permute-start.10 = (f32[25,24,128]{2,1,0:T(8,128)S(1)}, f32[25,24,128]{2,1,0:T(8,128)S(1)}, u32[]{:S(2)}, u32[]{:S(2)}) collective-permute-start(f32[25,24,128]{2,1,0:T(8,128)S(1)} %get-tuple-element.53), channel_id=1, source_target_pairs={{0,1},{1,0},{2,3},{3,2},{4,5},{5,4},{6,7},{7,6},{8,9},{9,8},{10,11... | collective-permute-start | bytes 921608 | tf_op jit(solution)/shard_map/ppermute | solution.py:483
  98.2 0.7 collective-permute-start.11
  98.9 6.9 %collective-permute-done.10.first = f32[25,24,128]{2,1,0:T(8,128)S(1)} collective-permute-done((f32[25,24,128]{2,1,0:T(8,128)S(1)}, f32[25,24,128]{2,1,0:T(8,128)S(1)}, u32[]{:S(2)}, u32[]{:S(2)}) %collective-permute-start.10) | collective-permute-done | bytes 307232 | tf_op jit(solution)/shard_map/ppermute | solution.py:483
  105.8 0.0 collective-permute-done.11.second
  105.8 5.0 %second_down_kernel.1 = (f32[3,20,24,256]{3,2,1,0:T(8,128)S(1)}, f32[3,8,24,128]{3,2,1,0:T(8,128)S(1)}, f32[3,8,24,128]{3,2,1,0:T(8,128)S(1)}, f32[4,24,128]{2,1,0:T(8,128)S(1)}, f32[9,24,128]{2,1,0:T(8,128)S(1)}) custom-call(f32[3,22,24,128]{3,2,1,0:T(8,128)S(1)} %get-tuple-element.52.tall, f32[25,24,128]{2,1,0:T(8,128)S(1)} %collective-permute-done.10.first, ...), custom_call_target="tpu_custom_call" | custom-call | tf_op jit(solution)/shard_map/second_down_kernel/pallas_call | solution.py:464
  110.9 6.5 %collective-permute-start.13 = (f32[4,24,128]{2,1,0:T(8,128)S(1)}, f32[4,24,128]{2,1,0:T(8,128)S(1)}, u32[]{:S(2)}, u32[]{:S(2)}) collective-permute-start(f32[4,24,128]{2,1,0:T(8,128)S(1)} %get-tuple-element.57), channel_id=1, source_target_pairs={{16,32},{24,40},{32,16},{40,24},{48,64},{56,72},{64,48},{72,56},{8... | collective-permute-start | bytes 147464 | tf_op jit(solution)/shard_map/ppermute | solution.py:483
  117.4 1.9 %collective-permute-start.12 = (f32[4,24,128]{2,1,0:T(8,128)S(1)}, f32[4,24,128]{2,1,0:T(8,128)S(1)}, u32[]{:S(2)}, u32[]{:S(2)}) collective-permute-start(f32[4,24,128]{2,1,0:T(8,128)S(1)} %get-tuple-element.57), channel_id=1, source_target_pairs={{0,16},{8,24},{16,0},{24,8},{32,48},{40,56},{48,32},{56,40},{64,80... | collective-permute-start | bytes 147464 | tf_op jit(solution)/shard_map/ppermute | solution.py:483
  119.3 0.9 collective-permute-done.13
  120.2 3.1 %collective-permute-start.14 = (f32[4,24,128]{2,1,0:T(8,128)S(1)}, f32[4,24,128]{2,1,0:T(8,128)S(1)}, u32[]{:S(2)}, u32[]{:S(2)}) collective-permute-start(f32[4,24,128]{2,1,0:T(8,128)S(1)} %collective-permute-done.13), channel_id=1, source_target_pairs={{0,16},{8,24},{16,0},{24,8},{32,48},{40,56},{48,32},{56,40},{64,80... | collective-permute-start | bytes 147464 | tf_op jit(solution)/shard_map/ppermute | solution.py:483
  123.2 0.1 collective-permute-done.12
  123.4 5.2 %collective-permute-start.15 = (f32[4,24,128]{2,1,0:T(8,128)S(1)}, f32[4,24,128]{2,1,0:T(8,128)S(1)}, u32[]{:S(2)}, u32[]{:S(2)}) collective-permute-start(f32[4,24,128]{2,1,0:T(8,128)S(1)} %collective-permute-done.12), channel_id=1, source_target_pairs={{16,32},{24,40},{32,16},{40,24},{48,64},{56,72},{64,48},{72,56},{8... | collective-permute-start | bytes 147464 | tf_op jit(solution)/shard_map/ppermute | solution.py:483
  128.6 0.0 collective-permute-done.14
  128.7 4.0 %collective-permute-done.15 = f32[4,24,128]{2,1,0:T(8,128)S(1)} collective-permute-done((f32[4,24,128]{2,1,0:T(8,128)S(1)}, f32[4,24,128]{2,1,0:T(8,128)S(1)}, u32[]{:S(2)}, u32[]{:S(2)}) %collective-permute-start.15) | collective-permute-done | bytes 49184 | tf_op jit(solution)/shard_map/ppermute | solution.py:483
  132.7 2.1 %collective-permute-start.16 = (f32[29,24,128]{2,1,0:T(8,128)S(1)}, f32[29,24,128]{2,1,0:T(8,128)S(1)}, u32[]{:S(2)}, u32[]{:S(2)}) collective-permute-start(f32[29,24,128]{2,1,0:T(8,128)S(1)} %constant_dynamic-update-slice_fusion.6.mine), channel_id=1, source_target_pairs={{0,8},{8,0},{16,24},{24,16},{32,40},{40,32},{48,56},{56,48},{64,72... | collective-permute-start | bytes 1069064 | tf_op jit(solution)/shard_map/ppermute | solution.py:483
  134.8 1.5 collective-permute-done.16.other
  136.2 2.7 %coarse_kernel.3 = (f32[3,4,24,128]{3,2,1,0:T(8,128)S(1)}, f32[3,3,24,128]{3,2,1,0:T(8,128)S(1)}, f32[3,3,24,128]{3,2,1,0:T(8,128)S(1)}) custom-call(f32[29,24,128]{2,1,0:T(8,128)S(1)} %constant_dynamic-update-slice_fusion.6.mine, f32[29,24,128]{2,1,0:T(8,128)S(1)} %collective-permute-done.16.other, f32[3,8,24,128]{3,2,1,0:T(8,128)S(1)} %get-tuple-element.59.v1), custom_call_target="tpu_custom_call" | custom-call | tf_op jit(solution)/shard_map/coarse_kernel/pallas_call | solution.py:464
  139.0 1.9 %collective-permute-start.17 = (f32[3,3,24,128]{3,2,1,0:T(8,128)S(1)}, f32[3,3,24,128]{3,2,1,0:T(8,128)S(1)}, u32[]{:S(2)}, u32[]{:S(2)}) collective-permute-start(f32[3,3,24,128]{3,2,1,0:T(8,128)S(1)} %get-tuple-element.62), channel_id=1, source_target_pairs={{8,16},{16,8},{24,32},{32,24},{40,48},{48,40},{56,64},{64,56},{72,... | collective-permute-start | bytes 331784 | tf_op jit(solution)/shard_map/ppermute | solution.py:483
  140.9 4.1 %collective-permute-done.17.right = f32[3,3,24,128]{3,2,1,0:T(8,128)S(1)} collective-permute-done((f32[3,3,24,128]{3,2,1,0:T(8,128)S(1)}, f32[3,3,24,128]{3,2,1,0:T(8,128)S(1)}, u32[]{:S(2)}, u32[]{:S(2)}) %collective-permute-start.17) | collective-permute-done | bytes 110624 | tf_op jit(solution)/shard_map/ppermute | solution.py:483
  145.0 1.5 last_up_kernel.1
  146.5 17.9 %all_to_all.11.taken = f32[8,9,8,128]{3,2,1,0:T(8,128)S(1)} all-to-all(f32[8,9,8,128]{3,2,1,0:T(8,128)S(1)} %last_up_kernel.1), channel_id=1, replica_groups=mesh['gx'=64,'gz'=8] {'gz'}, dimensions={0} | all-to-all | bytes 589824 | tf_op jit(solution)/shard_map/all_to_all | solution.py:578
  164.4 0.7 join_kernel.1
  (12 shorter events, 0.1 us)
Async XLA Ops:
  0.0 1.0 copy-start
  1.0 0.9 copy-start.1
  30.4 10.4 %collective-permute-start = (f32[7,6,24,128]{3,2,1,0:T(8,128)S(1)}, f32[7,6,24,128]{3,2,1,0:T(8,128)S(1)}, u32[]{:S(2)}, u32[]{:S(2)}) collective-permute-start(f32[7,6,24,128]{3,2,1,0:T(8,128)S(1)} %get-tuple-element.36), channel_id=1, source_target_pairs={{8,16},{16,8},{24,32},{32,24},{40,48},{48,40},{56,64},{64,56},{72,... | collective-permute-start | bytes 1548296 | tf_op jit(solution)/shard_map/ppermute | solution.py:483
  32.3 8.5 %collective-permute-start.1 = (f32[7,6,24,128]{3,2,1,0:T(8,128)S(1)}, f32[7,6,24,128]{3,2,1,0:T(8,128)S(1)}, u32[]{:S(2)}, u32[]{:S(2)}) collective-permute-start(f32[7,6,24,128]{3,2,1,0:T(8,128)S(1)} %get-tuple-element.37), channel_id=1, source_target_pairs={{0,8},{8,0},{16,24},{24,16},{32,40},{40,32},{48,56},{56,48},{64,72... | collective-permute-start | bytes 1548296 | tf_op jit(solution)/shard_map/ppermute | solution.py:483
  45.6 10.8 %collective-permute-start.3 = (f32[4,24,128]{2,1,0:T(8,128)S(1)}, f32[4,24,128]{2,1,0:T(8,128)S(1)}, u32[]{:S(2)}, u32[]{:S(2)}) collective-permute-start(f32[4,24,128]{2,1,0:T(8,128)S(1)} %get-tuple-element.38), channel_id=1, source_target_pairs={{16,32},{24,40},{32,16},{40,24},{48,64},{56,72},{64,48},{72,56},{8... | collective-permute-start | bytes 147464 | tf_op jit(solution)/shard_map/ppermute | solution.py:483
  54.4 6.2 %collective-permute-start.2 = (f32[4,24,128]{2,1,0:T(8,128)S(1)}, f32[4,24,128]{2,1,0:T(8,128)S(1)}, u32[]{:S(2)}, u32[]{:S(2)}) collective-permute-start(f32[4,24,128]{2,1,0:T(8,128)S(1)} %get-tuple-element.38), channel_id=1, source_target_pairs={{0,16},{8,24},{16,0},{24,8},{32,48},{40,56},{48,32},{56,40},{64,80... | collective-permute-start | bytes 147464 | tf_op jit(solution)/shard_map/ppermute | solution.py:483
  56.4 9.2 %collective-permute-start.4 = (f32[4,24,128]{2,1,0:T(8,128)S(1)}, f32[4,24,128]{2,1,0:T(8,128)S(1)}, u32[]{:S(2)}, u32[]{:S(2)}) collective-permute-start(f32[4,24,128]{2,1,0:T(8,128)S(1)} %collective-permute-done.3), channel_id=1, source_target_pairs={{0,16},{8,24},{16,0},{24,8},{32,48},{40,56},{48,32},{56,40},{64,80... | collective-permute-start | bytes 147464 | tf_op jit(solution)/shard_map/ppermute | solution.py:483
  60.6 9.3 %collective-permute-start.5 = (f32[4,24,128]{2,1,0:T(8,128)S(1)}, f32[4,24,128]{2,1,0:T(8,128)S(1)}, u32[]{:S(2)}, u32[]{:S(2)}) collective-permute-start(f32[4,24,128]{2,1,0:T(8,128)S(1)} %collective-permute-done.2), channel_id=1, source_target_pairs={{16,32},{24,40},{32,16},{40,24},{48,64},{56,72},{64,48},{72,56},{8... | collective-permute-start | bytes 147464 | tf_op jit(solution)/shard_map/ppermute | solution.py:483
  69.9 3.6 %collective-permute-start.6 = (f32[29,24,128]{2,1,0:T(8,128)S(1)}, f32[29,24,128]{2,1,0:T(8,128)S(1)}, u32[]{:S(2)}, u32[]{:S(2)}) collective-permute-start(f32[29,24,128]{2,1,0:T(8,128)S(1)} %constant_dynamic-update-slice_fusion.mine), channel_id=1, source_target_pairs={{0,8},{8,0},{16,24},{24,16},{32,40},{40,32},{48,56},{56,48},{64,72... | collective-permute-start | bytes 1069064 | tf_op jit(solution)/shard_map/ppermute | solution.py:483
  76.2 6.1 %collective-permute-start.7 = (f32[3,3,24,128]{3,2,1,0:T(8,128)S(1)}, f32[3,3,24,128]{3,2,1,0:T(8,128)S(1)}, u32[]{:S(2)}, u32[]{:S(2)}) collective-permute-start(f32[3,3,24,128]{3,2,1,0:T(8,128)S(1)} %get-tuple-element.43), channel_id=1, source_target_pairs={{8,16},{16,8},{24,32},{32,24},{40,48},{48,40},{56,64},{64,56},{72,... | collective-permute-start | bytes 331784 | tf_op jit(solution)/shard_map/ppermute | solution.py:483
  83.7 10.4 %collective-permute-start.8 = (f32[3,7,24,128]{3,2,1,0:T(8,128)S(1)}, f32[3,7,24,128]{3,2,1,0:T(8,128)S(1)}, u32[]{:S(2)}, u32[]{:S(2)}) collective-permute-start(f32[3,7,24,128]{3,2,1,0:T(8,128)S(1)} %get-tuple-element.50), channel_id=1, source_target_pairs={{8,16},{16,8},{24,32},{32,24},{40,48},{48,40},{56,64},{64,56},{72,... | collective-permute-start | bytes 774152 | tf_op jit(solution)/shard_map/ppermute | solution.py:483
  85.6 9.6 %collective-permute-start.9 = (f32[3,7,24,128]{3,2,1,0:T(8,128)S(1)}, f32[3,7,24,128]{3,2,1,0:T(8,128)S(1)}, u32[]{:S(2)}, u32[]{:S(2)}) collective-permute-start(f32[3,7,24,128]{3,2,1,0:T(8,128)S(1)} %get-tuple-element.51), channel_id=1, source_target_pairs={{0,8},{8,0},{16,24},{24,16},{32,40},{40,32},{48,56},{56,48},{64,72... | collective-permute-start | bytes 774152 | tf_op jit(solution)/shard_map/ppermute | solution.py:483
  95.8 10.0 %collective-permute-start.10 = (f32[25,24,128]{2,1,0:T(8,128)S(1)}, f32[25,24,128]{2,1,0:T(8,128)S(1)}, u32[]{:S(2)}, u32[]{:S(2)}) collective-permute-start(f32[25,24,128]{2,1,0:T(8,128)S(1)} %get-tuple-element.53), channel_id=1, source_target_pairs={{0,1},{1,0},{2,3},{3,2},{4,5},{5,4},{6,7},{7,6},{8,9},{9,8},{10,11... | collective-permute-start | bytes 921608 | tf_op jit(solution)/shard_map/ppermute | solution.py:483
  98.2 7.6 %collective-permute-start.11 = (f32[25,24,128]{2,1,0:T(8,128)S(1)}, f32[25,24,128]{2,1,0:T(8,128)S(1)}, u32[]{:S(2)}, u32[]{:S(2)}) collective-permute-start(f32[25,24,128]{2,1,0:T(8,128)S(1)} %get-tuple-element.54), channel_id=1, source_target_pairs={{1,2},{2,1},{3,4},{4,3},{5,6},{6,5},{9,10},{10,9},{11,12},{12,11},... | collective-permute-start | bytes 921608 | tf_op jit(solution)/shard_map/ppermute | solution.py:483
  110.9 9.3 %collective-permute-start.13 = (f32[4,24,128]{2,1,0:T(8,128)S(1)}, f32[4,24,128]{2,1,0:T(8,128)S(1)}, u32[]{:S(2)}, u32[]{:S(2)}) collective-permute-start(f32[4,24,128]{2,1,0:T(8,128)S(1)} %get-tuple-element.57), channel_id=1, source_target_pairs={{16,32},{24,40},{32,16},{40,24},{48,64},{56,72},{64,48},{72,56},{8... | collective-permute-start | bytes 147464 | tf_op jit(solution)/shard_map/ppermute | solution.py:483
  117.4 6.0 %collective-permute-start.12 = (f32[4,24,128]{2,1,0:T(8,128)S(1)}, f32[4,24,128]{2,1,0:T(8,128)S(1)}, u32[]{:S(2)}, u32[]{:S(2)}) collective-permute-start(f32[4,24,128]{2,1,0:T(8,128)S(1)} %get-tuple-element.57), channel_id=1, source_target_pairs={{0,16},{8,24},{16,0},{24,8},{32,48},{40,56},{48,32},{56,40},{64,80... | collective-permute-start | bytes 147464 | tf_op jit(solution)/shard_map/ppermute | solution.py:483
  120.2 8.5 %collective-permute-start.14 = (f32[4,24,128]{2,1,0:T(8,128)S(1)}, f32[4,24,128]{2,1,0:T(8,128)S(1)}, u32[]{:S(2)}, u32[]{:S(2)}) collective-permute-start(f32[4,24,128]{2,1,0:T(8,128)S(1)} %collective-permute-done.13), channel_id=1, source_target_pairs={{0,16},{8,24},{16,0},{24,8},{32,48},{40,56},{48,32},{56,40},{64,80... | collective-permute-start | bytes 147464 | tf_op jit(solution)/shard_map/ppermute | solution.py:483
  123.4 9.3 %collective-permute-start.15 = (f32[4,24,128]{2,1,0:T(8,128)S(1)}, f32[4,24,128]{2,1,0:T(8,128)S(1)}, u32[]{:S(2)}, u32[]{:S(2)}) collective-permute-start(f32[4,24,128]{2,1,0:T(8,128)S(1)} %collective-permute-done.12), channel_id=1, source_target_pairs={{16,32},{24,40},{32,16},{40,24},{48,64},{56,72},{64,48},{72,56},{8... | collective-permute-start | bytes 147464 | tf_op jit(solution)/shard_map/ppermute | solution.py:483
  132.7 3.6 %collective-permute-start.16 = (f32[29,24,128]{2,1,0:T(8,128)S(1)}, f32[29,24,128]{2,1,0:T(8,128)S(1)}, u32[]{:S(2)}, u32[]{:S(2)}) collective-permute-start(f32[29,24,128]{2,1,0:T(8,128)S(1)} %constant_dynamic-update-slice_fusion.6.mine), channel_id=1, source_target_pairs={{0,8},{8,0},{16,24},{24,16},{32,40},{40,32},{48,56},{56,48},{64,72... | collective-permute-start | bytes 1069064 | tf_op jit(solution)/shard_map/ppermute | solution.py:483
  139.0 6.1 %collective-permute-start.17 = (f32[3,3,24,128]{3,2,1,0:T(8,128)S(1)}, f32[3,3,24,128]{3,2,1,0:T(8,128)S(1)}, u32[]{:S(2)}, u32[]{:S(2)}) collective-permute-start(f32[3,3,24,128]{3,2,1,0:T(8,128)S(1)} %get-tuple-element.62), channel_id=1, source_target_pairs={{8,16},{16,8},{24,32},{32,24},{40,48},{48,40},{56,64},{64,56},{72,... | collective-permute-start | bytes 331784 | tf_op jit(solution)/shard_map/ppermute | solution.py:483
